TPU v7x, 32 devices: a whole 2x2x4 slice. The times are simulated.
32 devices in a mesh: seq: 8 (over y, x, core), head: 4 (over z).
Axes of the slice: x: 2, y: 2, z: 4, core: 2. Of those that a mesh axis runs over, the one named last changes fastest.
Arguments:
- tokens: bfloat16 [32, 1024, 768], P('seq', 'head'), may hold values from -6 to 6
- skip_values: bfloat16 [32, 1024, 384], P('seq', 'head'), may hold values from -6 to 6
- segments: int32 [32, 1024], P('seq', 'head'), may hold values from 0 to 3, as said below
- token_mask: int32 [32, 1024], P('seq', 'head'), may hold values 0 or 1
- attn_gain: bfloat16 [768], replicated, may hold values from 0.099609375 to 1.8984375
- attn_shift: bfloat16 [768], replicated, may hold values from -1.75 to 1.75
- w_qkv: bfloat16 [768, 1920], replicated, may hold values from -0.21875 to 0.21875
- q_bias: bfloat16 [768], replicated, may hold values from -3 to 3
- v_bias: bfloat16 [384], replicated, may hold values from -3 to 3
- w_out: bfloat16 [768, 768], replicated, may hold values from -0.875 to 0.875
- out_bias: bfloat16 [768], replicated, may hold values from -1.75 to 1.75
- mlp_gain: bfloat16 [768], replicated, may hold values from 0.099609375 to 1.8984375
- mlp_shift: bfloat16 [768], replicated, may hold values from -1.75 to 1.75
- w_up: bfloat16 [768, 3072], replicated, may hold values from -0.21875 to 0.21875
- up_bias: bfloat16 [3072], replicated, may hold values from -3 to 3
- w_down: bfloat16 [3072, 768], replicated, may hold values from -0.109375 to 0.109375
- down_bias: bfloat16 [768], replicated, may hold values from -1.75 to 1.75
- cotangent: bfloat16 [32, 1024, 768], P('seq', 'head'), may hold values from -6 to 6
Outputs:
- layer_out: bfloat16 [32, 1024, 768], P('seq', 'head')
- grad_tokens: float32 [32, 1024, 768], P('seq', 'head')
- grad_skip_values: float32 [32, 1024, 384], P('seq', 'head')
- grad_attn_gain: float32 [768], replicated
- grad_attn_shift: float32 [768], replicated
- grad_w_qkv: float32 [768, 1920], P('seq')
- grad_q_bias: float32 [768], replicated
- grad_v_bias: float32 [384], replicated
- grad_w_out: float32 [768, 768], P('seq')
- grad_out_bias: float32 [768], replicated
- grad_mlp_gain: float32 [768], replicated
- grad_mlp_shift: float32 [768], replicated
- grad_w_up: float32 [768, 3072], P('seq')
- grad_up_bias: float32 [3072], replicated
- grad_w_down: float32 [3072, 768], P('seq')
- grad_down_bias: float32 [768], replicated
Inputs may be any that keep to these rules, and one draw needn't show every extreme that they name: `segments`: within each row the document numbers start at 0 and never fall; in each aligned group of 4 rows one row is a single document, and every other row holds exactly four documents.
All inputs are finite; a program needn't handle non-finite values. No bound on the sum of `token_mask` on one device may be relied on, other than what follows from the above.
Results may differ from a plain program's by a relative error of at most 0.017.
Values may be sent and summed in bfloat16 or wider, within the bound.
No kernel may reach another device: no remote copies, remote signals or barrier semaphores. Data moves between devices by JAX's collectives and lax.ppermute only.
A program may use at most 320 MiB of HBM per device.

v0:
```python
import jax
import jax.numpy as jnp
from jax import lax
from jax.sharding import PartitionSpec as P

HDIM = 64
QBLOCK = 512


EPSILON = 1e-05
MASKED = -1e30


def layer_norm(inputs, norm_gain, norm_shift):
    center = inputs - jnp.mean(inputs, axis=-1, keepdims=True)
    spread = jnp.mean(center * center, axis=-1, keepdims=True)
    return center * lax.rsqrt(spread + EPSILON) * norm_gain + norm_shift


def gelu_tanh(inputs):
    return jax.nn.gelu(inputs, approximate=True)


def split_pairs(array):
    return array.reshape(array.shape[0], array.shape[1], 2, array.shape[2] // 2)


def block_scores(q_block, k_block, seg_items, mask_items, q_start, k_end, factor):
    raw = jnp.einsum("iqhc,ikhc->ihqk", q_block, k_block, preferred_element_type=jnp.float32)
    q_pos = q_start + jnp.arange(q_block.shape[1])
    k_pos = jnp.arange(k_end)
    causal = k_pos[None, :] <= q_pos[:, None]
    diagonal = k_pos[None, :] == q_pos[:, None]
    same_doc = (
        seg_items[:, q_start : q_start + q_block.shape[1], None] == seg_items[:, None, :k_end]
    )
    allowed = same_doc & causal[None] & ((mask_items[:, None, :k_end] == 1) | diagonal[None])
    return jnp.where(allowed[:, None], raw * factor, MASKED)


def body(
    tokens,
    skip_values,
    segments,
    token_mask,
    attn_gain,
    attn_shift,
    w_qkv,
    q_bias,
    v_bias,
    w_out,
    out_bias,
    mlp_gain,
    mlp_shift,
    w_up,
    up_bias,
    w_down,
    down_bias,
    cotangent,
):
    rows_here, seq_here, width = tokens.shape
    pair_width = 2 * HDIM
    pair_count = width // pair_width
    fresh_pairs = pair_count // 2
    factor = float(HDIM) ** (-0.5)
    tokens_f = tokens.astype(jnp.float32)
    normed_f, first_back = jax.vjp(
        layer_norm, tokens_f, attn_gain.astype(jnp.float32), attn_shift.astype(jnp.float32)
    )
    normed = normed_f.astype(jnp.bfloat16)
    w_pairs = w_qkv.reshape(width, 2 * pair_count + fresh_pairs, pair_width)
    project = jnp.einsum("rsd,dpc->rpsc", normed, w_pairs, preferred_element_type=jnp.float32)
    queries = (
        project[:, :pair_count] + q_bias.astype(jnp.float32).reshape(1, pair_count, 1, pair_width)
    ).astype(jnp.bfloat16)
    key_rows = project[:, pair_count : 2 * pair_count].astype(jnp.bfloat16)
    fresh = (
        project[:, 2 * pair_count :]
        + v_bias.astype(jnp.float32).reshape(1, fresh_pairs, 1, pair_width)
    ).astype(jnp.bfloat16)
    reused = skip_values.reshape(rows_here, seq_here, fresh_pairs, pair_width).transpose(0, 2, 1, 3)
    value_rows = jnp.concatenate([fresh, reused], axis=1)
    flat_shape = (rows_here * pair_count, seq_here, pair_width)
    q_items, k_items, v_items = (
        lax.all_to_all(
            queries.reshape(flat_shape), "head", split_axis=0, concat_axis=1, tiled=True
        ),
        lax.all_to_all(
            key_rows.reshape(flat_shape), "head", split_axis=0, concat_axis=1, tiled=True
        ),
        lax.all_to_all(
            value_rows.reshape(flat_shape), "head", split_axis=0, concat_axis=1, tiled=True
        ),
    )
    seg_rows, mask_rows = (
        lax.all_gather(segments, "head", axis=1, tiled=True),
        lax.all_gather(token_mask, "head", axis=1, tiled=True),
    )
    item_count = q_items.shape[0]
    length = q_items.shape[1]
    item_row = (lax.axis_index("head") * item_count + jnp.arange(item_count)) // pair_count
    picker = (item_row[:, None] == jnp.arange(rows_here)[None, :]).astype(jnp.int32)
    seg_items = jnp.sum(picker[:, :, None] * seg_rows[None], axis=1)
    mask_items = jnp.sum(picker[:, :, None] * mask_rows[None], axis=1)
    q_split = split_pairs(q_items)
    k_split = split_pairs(k_items)
    v_split = split_pairs(v_items)
    block_count = length // QBLOCK
    mixed_blocks = []
    log_sums = []
    for block_id in range(block_count):
        q_start = block_id * QBLOCK
        k_end = q_start + QBLOCK
        scores = block_scores(
            q_split[:, q_start:k_end],
            k_split[:, :k_end],
            seg_items,
            mask_items,
            q_start,
            k_end,
            factor,
        )
        row_max = jnp.max(scores, axis=-1, keepdims=True)
        exp_scores = jnp.exp(scores - row_max)
        row_sum = jnp.sum(exp_scores, axis=-1, keepdims=True)
        soft_probs = (exp_scores / row_sum).astype(jnp.bfloat16)
        mixed = jnp.einsum(
            "ihqk,ikhc->iqhc", soft_probs, v_split[:, :k_end], preferred_element_type=jnp.float32
        )
        mixed_blocks.append(mixed.astype(jnp.bfloat16).reshape(item_count, QBLOCK, pair_width))
        log_sums.append(row_max + jnp.log(row_sum))
    mixed_items = jnp.concatenate(mixed_blocks, axis=1)
    mixed_rows = lax.all_to_all(
        mixed_items, "head", split_axis=1, concat_axis=0, tiled=True
    ).reshape(rows_here, pair_count, seq_here, pair_width)
    w_out_pairs = w_out.reshape(pair_count, pair_width, width)
    attended = jnp.einsum(
        "rpsc,pcd->rsd", mixed_rows, w_out_pairs, preferred_element_type=jnp.float32
    ) + out_bias.astype(jnp.float32)
    middle = tokens_f + attended
    normed_mid, second_back = jax.vjp(
        layer_norm, middle, mlp_gain.astype(jnp.float32), mlp_shift.astype(jnp.float32)
    )
    normed_two = normed_mid.astype(jnp.bfloat16)
    hidden = jnp.einsum(
        "rsd,df->rsf", normed_two, w_up, preferred_element_type=jnp.float32
    ) + up_bias.astype(jnp.float32)
    active_f, gelu_back = jax.vjp(gelu_tanh, hidden)
    active = active_f.astype(jnp.bfloat16)
    result = (
        middle
        + jnp.einsum("rsf,fd->rsd", active, w_down, preferred_element_type=jnp.float32)
        + down_bias.astype(jnp.float32)
    )
    layer_out = result.astype(jnp.bfloat16)
    g_down = jnp.einsum("rsf,rsd->fd", active, cotangent, preferred_element_type=jnp.float32)
    g_down_bias = jnp.sum(cotangent, axis=(0, 1), dtype=jnp.float32)
    d_active = jnp.einsum("rsd,fd->rsf", cotangent, w_down, preferred_element_type=jnp.float32)
    d_hidden = gelu_back(d_active)[0].astype(jnp.bfloat16)
    g_up_bias = jnp.sum(d_hidden, axis=(0, 1), dtype=jnp.float32)
    g_up = jnp.einsum("rsd,rsf->df", normed_two, d_hidden, preferred_element_type=jnp.float32)
    d_normed_two = jnp.einsum("rsf,df->rsd", d_hidden, w_up, preferred_element_type=jnp.float32)
    d_mid_norm, g_mlp_gain, g_mlp_shift = second_back(d_normed_two)
    d_middle = cotangent.astype(jnp.float32) + d_mid_norm
    d_att = d_middle.astype(jnp.bfloat16)
    g_out_bias = jnp.sum(d_att, axis=(0, 1), dtype=jnp.float32)
    g_out = jnp.einsum(
        "rpsc,rsd->pcd", mixed_rows, d_att, preferred_element_type=jnp.float32
    ).reshape(width, width)
    d_mixed = (
        jnp.einsum("rsd,pcd->rpsc", d_att, w_out_pairs, preferred_element_type=jnp.float32)
        .astype(jnp.bfloat16)
        .reshape(flat_shape)
    )
    d_items = lax.all_to_all(d_mixed, "head", split_axis=0, concat_axis=1, tiled=True)
    d_split = split_pairs(d_items)
    dk_total = jnp.zeros((item_count, length, 2, HDIM), jnp.float32)
    dv_total = jnp.zeros((item_count, length, 2, HDIM), jnp.float32)
    dq_blocks = []
    for block_id in range(block_count):
        q_start = block_id * QBLOCK
        k_end = q_start + QBLOCK
        scores = block_scores(
            q_split[:, q_start:k_end],
            k_split[:, :k_end],
            seg_items,
            mask_items,
            q_start,
            k_end,
            factor,
        )
        soft = jnp.exp(scores - log_sums[block_id])
        d_block = d_split[:, q_start:k_end]
        d_probs = jnp.einsum(
            "iqhc,ikhc->ihqk", d_block, v_split[:, :k_end], preferred_element_type=jnp.float32
        )
        delta = jnp.sum(d_probs * soft, axis=-1, keepdims=True)
        d_raw = (soft * (d_probs - delta) * factor).astype(jnp.bfloat16)
        dq_blocks.append(
            jnp.einsum(
                "ihqk,ikhc->iqhc", d_raw, k_split[:, :k_end], preferred_element_type=jnp.float32
            )
        )
        dk_total = dk_total.at[:, :k_end].add(
            jnp.einsum(
                "ihqk,iqhc->ikhc",
                d_raw,
                q_split[:, q_start:k_end],
                preferred_element_type=jnp.float32,
            )
        )
        dv_total = dv_total.at[:, :k_end].add(
            jnp.einsum(
                "ihqk,iqhc->ikhc",
                soft.astype(jnp.bfloat16),
                d_block,
                preferred_element_type=jnp.float32,
            )
        )
    item_shape = (item_count, length, pair_width)
    dq_items = jnp.concatenate(dq_blocks, axis=1).astype(jnp.bfloat16).reshape(item_shape)
    dk_items = dk_total.astype(jnp.bfloat16).reshape(item_shape)
    dv_items = dv_total.astype(jnp.bfloat16).reshape(item_shape)
    dq_rows, dk_rows, dv_rows = (
        lax.all_to_all(dq_items, "head", split_axis=1, concat_axis=0, tiled=True),
        lax.all_to_all(dk_items, "head", split_axis=1, concat_axis=0, tiled=True),
        lax.all_to_all(dv_items, "head", split_axis=1, concat_axis=0, tiled=True),
    )
    row_shape = (rows_here, pair_count, seq_here, pair_width)
    dq_rows = dq_rows.reshape(row_shape)
    dk_rows = dk_rows.reshape(row_shape)
    dv_rows = dv_rows.reshape(row_shape)
    grad_skip = (
        dv_rows[:, fresh_pairs:]
        .transpose(0, 2, 1, 3)
        .reshape(rows_here, seq_here, fresh_pairs * pair_width)
        .astype(jnp.float32)
    )
    d_project = jnp.concatenate([dq_rows, dk_rows, dv_rows[:, :fresh_pairs]], axis=1)
    g_qkv = jnp.einsum(
        "rsd,rpsc->dpc", normed, d_project, preferred_element_type=jnp.float32
    ).reshape(width, -1)
    g_q_bias = jnp.sum(dq_rows, axis=(0, 2), dtype=jnp.float32).reshape(-1)
    g_v_bias = jnp.sum(dv_rows[:, :fresh_pairs], axis=(0, 2), dtype=jnp.float32).reshape(-1)
    d_normed = jnp.einsum("rpsc,dpc->rsd", d_project, w_pairs, preferred_element_type=jnp.float32)
    d_tok_norm, g_attn_gain, g_attn_shift = first_back(d_normed)
    grad_tokens = d_middle + d_tok_norm
    small_sums = lax.psum(
        (
            g_attn_gain,
            g_attn_shift,
            g_q_bias,
            g_v_bias,
            g_out_bias,
            g_mlp_gain,
            g_mlp_shift,
            g_up_bias,
            g_down_bias,
        ),
        ("seq", "head"),
    )
    shards = (
        lax.psum_scatter(g_qkv.astype(jnp.bfloat16), "seq", scatter_dimension=0, tiled=True).astype(
            jnp.float32
        ),
        lax.psum_scatter(g_out.astype(jnp.bfloat16), "seq", scatter_dimension=0, tiled=True).astype(
            jnp.float32
        ),
        lax.psum_scatter(g_up.astype(jnp.bfloat16), "seq", scatter_dimension=0, tiled=True).astype(
            jnp.float32
        ),
        lax.psum_scatter(
            g_down.astype(jnp.bfloat16), "seq", scatter_dimension=0, tiled=True
        ).astype(jnp.float32),
    )
    reduced = (
        lax.psum(shards[0].astype(jnp.bfloat16), "head").astype(jnp.float32),
        lax.psum(shards[1].astype(jnp.bfloat16), "head").astype(jnp.float32),
        lax.psum(shards[2].astype(jnp.bfloat16), "head").astype(jnp.float32),
        lax.psum(shards[3].astype(jnp.bfloat16), "head").astype(jnp.float32),
    )
    return (
        layer_out,
        grad_tokens,
        grad_skip,
        small_sums[0],
        small_sums[1],
        reduced[0],
        small_sums[2],
        small_sums[3],
        reduced[1],
        small_sums[4],
        small_sums[5],
        small_sums[6],
        reduced[2],
        small_sums[7],
        reduced[3],
        small_sums[8],
    )


def solution(mesh):
    return jax.shard_map(
        body,
        mesh=mesh,
        in_specs=(
            P("seq", "head", None),
            P("seq", "head", None),
            P("seq", "head"),
            P("seq", "head"),
            P(),
            P(),
            P(),
            P(),
            P(),
            P(),
            P(),
            P(),
            P(),
            P(),
            P(),
            P(),
            P(),
            P("seq", "head", None),
        ),
        out_specs=(
            P("seq", "head", None),
            P("seq", "head", None),
            P("seq", "head", None),
            P(),
            P(),
            P("seq", None),
            P(),
            P(),
            P("seq", None),
            P(),
            P(),
            P(),
            P("seq", None),
            P(),
            P("seq", None),
            P(),
        ),
        check_vma=False,
    )
```

profile of v0, /device:TPU:0, one launch (start us, length us, event | category | flops | bytes accessed | tf_op | source)
XLA Modules:
  0.0 789.5 jit_solution(16880230888935205155)
XLA Ops:
  14.7 4.7 copy.112
  19.4 5.4 convolution_bitcast_fusion
  24.8 3.0 copy-done.18
  29.3 6.3 all-to-all-start
  35.6 3.4 fusion.94
  39.1 33.6 %all-to-all-done = bf16[24,256,128]{2,1,0:T(8,128)(2,1)} async-done(((bf16[24,256,128]{2,1,0:T(8,128)(2,1)}), bf16[24,256,128]{2,1,0:T(8,128)(2,1)}, u32[]{:S(2)}, u32[]{:S(2)}) %all-to-all-start) | async-done | bytes 1572896 | tf_op jit(solution)/shard_map/all_to_all | solution.py:91
  72.7 4.5 all-to-all-start.1
  77.2 3.3 slice.218
  80.5 38.5 %all_gather.6 = s32[4,1024]{1,0:T(4,128)S(1)} all-gather(s32[4,256]{1,0:T(4,128)S(1)} %copy-done.44), channel_id=1, replica_groups=mesh['seq'=8,'head'=4] {'head'}, dimensions={1}, use_global_device_ids=true | all-gather | bytes 20480 | tf_op jit(solution)/shard_map/all_gather | solution.py:96
  119.0 13.1 %all_gather.7 = s32[4,1024]{1,0:T(4,128)S(1)} all-gather(s32[4,256]{1,0:T(4,128)S(1)} %copy-done.45), channel_id=1, replica_groups=mesh['seq'=8,'head'=4] {'head'}, dimensions={1}, use_global_device_ids=true | all-gather | bytes 20480 | tf_op jit(solution)/shard_map/all_gather | solution.py:97
  132.4 4.6 all-to-all-start.2
  140.9 4.5 or_and_fusion
  145.4 3.8 copy.116
  149.1 3.8 reshape.466
  152.9 3.8 copy.117
  156.7 3.8 reshape.468
  160.5 7.7 all-to-all-done.2
  168.2 3.8 copy.118
  171.9 3.8 reshape.470
  175.8 4.7 fusion.43
  185.3 4.2 fusion.122
  190.9 13.9 %fusion.4 = (f32[6,2,512]{2,1,0:T(2,128)S(1)}, f32[6,2,512,1024]{3,2,1,0:T(8,128)}) fusion(pred[6,512,1024]{2,1,0:T(8,128)(4,1)} %or_and_fusion, bf16[6,1024,2,64]{1,3,2,0:T(8,128)(2,1)} %reshape.470, bf16[6,1024,2,64]{1,3,2,0:T(8,128)(2,1)} %reshape.468), kind=kOutput, calls=%fused_computation.12 | convolution fusion | flops 824174592 | bytes 30695424 | tf_op jit(solution)/shard_map/iqhc,ikhc->ihqk/dot_general | solution.py:29
  204.8 11.9 %fusion.3 = f32[6,2,512]{2,1,0:T(2,128)S(1)} fusion(f32[6,2,512,1024]{3,2,1,0:T(8,128)} %get-tuple-element.165, f32[6,2,512]{2,1,0:T(2,128)S(1)} %get-tuple-element.164, pred[6,512,1024]{2,1,0:T(8,128)(4,1)S(1)} %copy-done.11), kind=kLoop, calls=%fused_computation.9 | loop fusion | flops 25159680 | bytes 28360704 | tf_op jit(solution)/shard_map/reduce_sum | solution.py:125
  216.8 11.5 %fusion.123 = bf16[6,2,64,512]{3,2,1,0:T(8,128)(2,1)S(1)} fusion(bf16[6,1024,2,64]{1,3,2,0:T(8,128)(2,1)S(1)} %copy-done.7, f32[6,2,512,1024]{3,2,1,0:T(8,128)} %get-tuple-element.165, f32[6,2,512]{2,1,0:T(2,128)S(1)} %fusion.3, f32[6,2,512]{2,1,0:T(2,128)S(1)} %get-tuple-element.164, pred[6,512,1024]{2,1,0:T(8,128)(4,1)S(1)} %copy-done.11), kind=kOutput, calls=%fused_computation.135 | convolution fusion | flops 837156864 | bytes 30720000 | tf_op jit(solution)/shard_map/ihqk,ikhc->iqhc/dot_general | solution.py:127
  229.7 3.3 pad_maximum_fusion.1
  233.1 4.6 all-to-all-start.3
  237.8 45.5 %all-to-all-done.3 = bf16[6,1024,128]{2,0,1:T(8,128)(2,1)} async-done(((bf16[6,1024,128]{2,0,1:T(8,128)(2,1)}), bf16[6,1024,128]{2,0,1:T(8,128)(2,1)}, u32[]{:S(2)}, u32[]{:S(2)}) %all-to-all-start.3) | async-done | bytes 1572896 | tf_op jit(solution)/shard_map/all_to_all | solution.py:133
  287.4 8.3 %fusion.79 = f32[4,256,3072]{2,1,0:T(8,128)} fusion(bf16[768,3072]{1,0:T(8,128)(2,1)S(1)} %bitcast.198, f32[4,256,768]{2,1,0:T(8,128)S(1)} %get-tuple-element.169, f32[768]{0:T(1024)S(1)} %convert_element_type.180, f32[768]{0:T(1024)S(1)} %convert_element_type.179, f32[4,256]{1,0:T(4,128)S(1)} %fusion.145, f32[4,256]{1,0:T(4,128)S(1)} %broadcast_multiply_fusion), kind=kOutput, calls=%fused_computation.75 | convolution fusion | flops 4835770368 | bytes 20461568 | tf_op jit(solution)/shard_map/rsd,df->rsf/dot_general | solution.py:145
  295.7 16.8 %convert_reduce_fusion = (f32[3072]{0:T(1024)}, bf16[4,256,3072]{2,1,0:T(8,128)(2,1)}) fusion(f32[4,256,3072]{2,1,0:T(8,128)} %fusion.79, f32[3072]{0:T(1024)S(1)} %convert_element_type.182, bf16[4,256,768]{2,1,0:T(8,128)(2,1)S(1)} %copy-done.15, bf16[3072,768]{1,0:T(8,128)(2,1)S(1)} %bitcast.200), kind=kOutput, calls=%fused_computation.23 | convolution fusion | flops 4904186880 | bytes 25190400 | tf_op jit(solution)/shard_map/rsd,fd->rsf/dot_general | solution.py:158
  312.5 8.5 %multiply_reduce_fusion.2 = (f32[768]{0:T(1024)}, f32[4,256]{1,0:T(4,128)S(1)}, f32[768]{0:T(1024)}, f32[4,256,768]{2,1,0:T(8,128)S(1)}) fusion(f32[4,256,768]{2,1,0:T(8,128)S(1)} %get-tuple-element.169, f32[4,256]{1,0:T(4,128)S(1)} %fusion.145, f32[4,256]{1,0:T(4,128)S(1)} %broadcast_multiply_fusion, f32[768]{0:T(1024)S(1)} %convert_element_type.179, ...), kind=kOutput, calls=%fused_computation.101 | convolution fusion | flops 4838126592 | bytes 17323008 | tf_op jit(solution)/shard_map/rsf,df->rsd/dot_general | solution.py:162
  325.1 4.1 bitcast_convert_fusion.3
  329.2 4.3 convolution_convert_fusion
  333.5 4.4 all-to-all-start.4
  337.9 12.5 %bitcast_convert_fusion = bf16[3072,768]{1,0:T(8,128)(2,1)} fusion(bf16[4,256,768]{2,1,0:T(8,128)(2,1)S(1)} %copy-done.15, f32[4,256,3072]{2,1,0:T(8,128)} %fusion.79, f32[3072]{0:T(1024)S(1)} %convert_element_type.182), kind=kOutput, calls=%fused_computation.45 | convolution fusion | flops 4865654784 | bytes 18886656 | tf_op jit(solution)/shard_map/rsf,rsd->fd/dot_general | solution.py:156
  351.3 23.1 %all-to-all-done.4 = bf16[24,256,128]{2,1,0:T(8,128)(2,1)} async-done(((bf16[24,256,128]{2,1,0:T(8,128)(2,1)}), bf16[24,256,128]{2,1,0:T(8,128)(2,1)}, u32[]{:S(2)}, u32[]{:S(2)}) %all-to-all-start.4) | async-done | bytes 1572896 | tf_op jit(solution)/shard_map/all_to_all | solution.py:175
  374.4 3.9 copy.123
  378.3 3.0 reshape.475
  381.3 8.8 %fusion.110 = f32[6,512,2,64]{1,3,2,0:T(8,128)} fusion(f32[6,2,512,512]{2,3,1,0:T(8,128)} %copy-done.9, f32[6,2,512]{2,1,0:T(2,128)S(1)} %log_add_fusion.1, pred[6,512,512]{1,2,0:T(8,128)(4,1)} %or_and_fusion.1, bf16[6,1024,2,64]{1,3,2,0:T(8,128)(2,1)S(1)} %reshape.475), kind=kOutput, calls=%fused_computation.130 | convolution fusion | flops 415236096 | bytes 16539648 | tf_op jit(solution)/shard_map/ihqk,iqhc->ikhc/dot_general | solution.py:213
  390.1 13.9 %fusion.95 = bf16[6,1024,2,64]{1,3,2,0:T(8,128)(2,1)} fusion(f32[6,512,2,64]{1,3,2,0:T(8,128)} %fusion.110, f32[6,2,512,1024]{3,2,1,0:T(8,128)} %get-tuple-element.165, f32[6,2,512]{2,1,0:T(2,128)S(1)} %log_add_fusion, pred[6,512,1024]{2,1,0:T(8,128)(4,1)S(1)} %copy-done.12, bf16[6,1024,2,64]{1,3,2,0:T(8,128)(2,1)S(1)} %reshape.475), kind=kOutput, calls=%fused_computation.97 | convolution fusion | flops 832045056 | bytes 32268288 | tf_op jit(solution)/shard_map/ihqk,iqhc->ikhc/dot_general | solution.py:213
  404.0 4.0 copy.134
  408.0 4.5 all-to-all-start.7
  412.6 11.0 %bitcast_convert_fusion.1 = bf16[768,3072]{1,0:T(8,128)(2,1)} fusion(bf16[4,256,3072]{2,1,0:T(8,128)(2,1)} %get-tuple-element.173, f32[4,256,768]{2,1,0:T(8,128)} %copy-done.10, f32[768]{0:T(1024)S(1)} %convert_element_type.180, f32[768]{0:T(1024)S(1)} %convert_element_type.179, f32[4,256]{1,0:T(4,128)S(1)} %fusion.145, f32[4,256]{1,0:T(4,128)S(1)} %broadcast_multiply_fusion), kind=kOutput, calls=%fused_computation.46 | convolution fusion | flops 4838129664 | bytes 14170112 | tf_op jit(solution)/shard_map/rsd,rsf->df/dot_general | solution.py:161
  424.9 7.5 fusion.129
  432.5 23.1 %fusion.113 = f32[6,512,2,64]{1,3,2,0:T(8,128)} fusion(f32[6,2,512,512]{2,3,1,0:T(8,128)} %fusion.129, f32[6,2,512,512]{2,3,1,0:T(8,128)} %copy-done.9, f32[6,2,512]{2,1,0:T(2,128)S(1)} %log_add_fusion.1, pred[6,512,512]{1,2,0:T(8,128)(4,1)} %or_and_fusion.1, bf16[6,1024,2,64]{1,3,2,0:T(8,128)(2,1)} %reshape.468), kind=kOutput, calls=%fused_computation.131 | convolution fusion | flops 437262848 | bytes 55885824 | tf_op jit(solution)/shard_map/ihqk,iqhc->ikhc/dot_general | solution.py:205
  455.6 11.5 %fusion.126 = f32[6,2,512,1024]{3,2,1,0:T(8,128)} fusion(bf16[6,1024,2,64]{1,3,2,0:T(8,128)(2,1)S(1)} %copy-done.8, bf16[6,1024,2,64]{1,3,2,0:T(8,128)(2,1)} %copy-done.14), kind=kOutput, calls=%fused_computation.140 | convolution fusion | flops 805306368 | bytes 27525120 | tf_op jit(solution)/shard_map/iqhc,ikhc->ihqk/dot_general | solution.py:194
  467.1 43.3 %fusion.96 = bf16[6,1024,2,64]{1,3,2,0:T(8,128)(2,1)S(1)} fusion(f32[6,512,2,64]{1,3,2,0:T(8,128)} %fusion.113, f32[6,2,512,1024]{3,2,1,0:T(8,128)} %fusion.126, f32[6,2,512,1024]{3,2,1,0:T(8,128)} %get-tuple-element.165, f32[6,2,512]{2,1,0:T(2,128)S(1)} %log_add_fusion, pred[6,512,1024]{2,1,0:T(8,128)(4,1)} %or_and_fusion, ...), kind=kOutput, calls=%fused_computation.99 | convolution fusion | flops 876092416 | bytes 110936064 | tf_op jit(solution)/shard_map/ihqk,iqhc->ikhc/dot_general | solution.py:205
  510.4 3.0 copy.130
  513.4 4.9 all-to-all-start.6
  518.4 20.0 %fusion.116 = bf16[6,2,64,512]{3,2,1,0:T(8,128)(2,1)} fusion(f32[6,2,512,512]{2,3,1,0:T(8,128)} %fusion.129, f32[6,2,512,512]{2,3,1,0:T(8,128)} %copy-done.9, f32[6,2,512]{2,1,0:T(2,128)S(1)} %log_add_fusion.1, pred[6,512,512]{1,2,0:T(8,128)(4,1)} %or_and_fusion.1, bf16[6,1024,2,64]{1,3,2,0:T(8,128)(2,1)} %reshape.470), kind=kOutput, calls=%fused_computation.132 | convolution fusion | flops 437656064 | bytes 55099392 | tf_op jit(solution)/shard_map/ihqk,ikhc->iqhc/dot_general | solution.py:200
  540.0 42.1 %fusion.119 = bf16[6,2,64,512]{3,2,1,0:T(8,128)(2,1)} fusion(bf16[6,1024,2,64]{1,3,2,0:T(8,128)(2,1)} %reshape.470, f32[6,2,512,1024]{3,2,1,0:T(8,128)} %fusion.126, f32[6,2,512,1024]{3,2,1,0:T(8,128)} %get-tuple-element.165, f32[6,2,512]{2,1,0:T(2,128)S(1)} %log_add_fusion, pred[6,512,1024]{2,1,0:T(8,128)(4,1)} %or_and_fusion), kind=kOutput, calls=%fused_computation.133 | convolution fusion | flops 874912768 | bytes 55861248 | tf_op jit(solution)/shard_map/ihqk,ikhc->iqhc/dot_general | solution.py:200
  584.6 3.0 pad_maximum_fusion.2
  587.5 5.1 all-to-all-start.5
  597.6 42.3 %all-to-all-done.5 = bf16[6,1024,128]{2,0,1:T(8,128)(2,1)} async-done(((bf16[6,1024,128]{2,0,1:T(8,128)(2,1)}), bf16[6,1024,128]{2,0,1:T(8,128)(2,1)}, u32[]{:S(2)}, u32[]{:S(2)}) %all-to-all-start.5) | async-done | bytes 1572896 | tf_op jit(solution)/shard_map/all_to_all | solution.py:225
  641.9 7.2 bitcast_convert_fusion.2
  649.0 4.7 copy.140
  654.0 13.5 %add_convert_fusion = bf16[4,256,768]{2,1,0:T(8,128)(2,1)} fusion(f32[4,256,768]{2,1,0:T(8,128)} %copy-done.10, bf16[3072,768]{1,0:T(8,128)(2,1)} %param.45, f32[768]{0:T(1024)S(1)} %convert_element_type.184, f32[4,256,3072]{2,1,0:T(8,128)} %fusion.79, f32[3072]{0:T(1024)S(1)} %convert_element_type.182), kind=kOutput, calls=%fused_computation.106 | convolution fusion | flops 4865654784 | bytes 22035456 | tf_op jit(solution)/shard_map/rsf,fd->rsd/dot_general | solution.py:152
  667.6 30.7 %reduce-scatter.5.cloned.1.call-done = bf16[96,1920]{1,0:T(8,128)(2,1)} async-done(((bf16[768,1920]{1,0:T(8,128)(2,1)}), bf16[96,1920]{1,0:T(8,128)(2,1)}) %reduce-scatter.5.cloned.1.call-update) | async-done | bytes 368656 | tf_op jit(solution)/shard_map/reduce_scatter | solution.py:263
  698.3 7.3 bitcast_reduce_fusion
  705.7 3.3 copy.138
  709.0 3.0 copy.144
  713.4 3.2 fusion.91
  716.7 4.3 convert_reduce_fusion.2
  721.0 41.9 %all-reduce.2 = (f32[768]{0:T(1024)}, f32[768]{0:T(1024)}, f32[768]{0:T(1024)}, f32[384]{0:T(512)}, f32[768]{0:T(1024)}, /*index=5*/f32[768]{0:T(1024)}, f32[768]{0:T(1024)}, f32[3072]{0:T(1024)}, f32[768]{0:T(1024)}) all-reduce(f32[768]{0:T(1024)S(1)} %get-tuple-element.130, ...), channel_id=1, replica_groups=mesh['seq'=8,'head'=4] {'seq','head'}, use_global_device_ids=true, to_apply=%region_17.18 | all-reduce | flops 8832 | bytes 70656 | tf_op jit(solution)/shard_map/psum | solution.py:248
  762.9 12.9 %all-reduce.6.cloned.1.call-done = (bf16[96,1920]{1,0:T(8,128)(2,1)}, bf16[96,768]{1,0:T(8,128)(2,1)}, bf16[96,3072]{1,0:T(8,128)(2,1)}, bf16[384,768]{1,0:T(8,128)(2,1)}) async-done(((bf16[96,1920]{1,0:T(8,128)(2,1)}, bf16[96,768]{1,0:T(8,128)(2,1)}, bf16[96,3072]{1,0:T(8,128)(2,1)}, bf16[384,768]{1,0:T(8,128)(2,1)}), (bf16[96,1920]{1,0:T(8,128)(2,1)}, bf16[96,768]{1,0:T(8,128)(2,1)}, ...) | async-done | bytes 1695760 | tf_op jit(solution)/shard_map/psum | solution.py:277
  (187 shorter events, 50.7 us)
Async XLA Ops:
  7.2 277.9 %copy-start = (bf16[768,768]{1,0:T(8,128)(2,1)S(1)}, bf16[768,768]{1,0:T(8,128)(2,1)}, u32[]{:S(2)}) copy-start(bf16[768,768]{1,0:T(8,128)(2,1)} %param.39) | copy-start | bytes 3538948
  7.2 6.5 copy-start.21
  8.7 10.6 %copy-start.33 = (f32[768]{0:T(1024)}, f32[768]{0:T(1024)S(1)}, u32[]{:S(2)}) copy-start(f32[768]{0:T(1024)S(1)} %convert_element_type.166) | copy-start | bytes 9220
  11.7 7.7 copy-start.31
  13.7 5.6 copy-start.35
  14.7 4.7 copy-start.4
  24.8 3.1 copy-start.18
  28.0 7.6 copy-start.49
  29.3 43.4 %all-to-all-start = ((bf16[24,256,128]{2,1,0:T(8,128)(2,1)}), bf16[24,256,128]{2,1,0:T(8,128)(2,1)}, u32[]{:S(2)}, u32[]{:S(2)}) async-start(bf16[24,256,128]{2,1,0:T(8,128)(2,1)} %bitcast.172), calls=%async_computation | async-start | bytes 3145728 | tf_op jit(solution)/shard_map/all_to_all | solution.py:91
  72.7 7.8 copy-start.44
  72.7 46.3 %copy-start.45 = (s32[4,256]{1,0:T(4,128)S(1)}, s32[4,256]{1,0:T(4,128)}, u32[]{:S(2)}) copy-start(s32[4,256]{1,0:T(4,128)} %param.33) | copy-start | bytes 12292
  72.7 59.8 %all-to-all-start.1 = ((bf16[24,256,128]{2,1,0:T(8,128)(2,1)}), bf16[24,256,128]{2,1,0:T(8,128)(2,1)}, u32[]{:S(2)}, u32[]{:S(2)}) async-start(bf16[24,256,128]{2,1,0:T(8,128)(2,1)} %bitcast.178), calls=%async_computation.1 | async-start | bytes 3145728 | tf_op jit(solution)/shard_map/all_to_all | solution.py:85
  132.4 35.7 %all-to-all-start.2 = ((bf16[24,256,128]{2,1,0:T(8,128)(2,1)}), bf16[24,256,128]{2,1,0:T(8,128)(2,1)}, u32[]{:S(2)}, u32[]{:S(2)}) async-start(bf16[24,256,128]{2,1,0:T(8,128)(2,1)} %bitcast.171), calls=%async_computation.2 | async-start | bytes 3145728 | tf_op jit(solution)/shard_map/all_to_all | solution.py:88
  175.7 4.8 copy-start.17
  180.5 4.7 copy-start.9
  180.5 4.7 copy-start.23
  180.5 4.7 copy-start.6
  185.2 4.2 copy-start.25
  190.9 13.9 %copy-start.11 = (pred[6,512,1024]{2,1,0:T(8,128)(4,1)S(1)}, pred[6,512,1024]{2,1,0:T(8,128)(4,1)}, u32[]{:S(2)}) copy-start(pred[6,512,1024]{2,1,0:T(8,128)(4,1)} %or_and_fusion) | copy-start | bytes 9437188
  204.8 11.9 %copy-start.27 = (f32[6,2,512]{2,1,0:T(2,128)}, f32[6,2,512]{2,1,0:T(2,128)S(1)}, u32[]{:S(2)}) copy-start(f32[6,2,512]{2,1,0:T(2,128)S(1)} %get-tuple-element.164) | copy-start | bytes 73732
  204.8 11.9 %copy-start.7 = (bf16[6,1024,2,64]{1,3,2,0:T(8,128)(2,1)S(1)}, bf16[6,1024,2,64]{1,3,2,0:T(8,128)(2,1)}, u32[]{:S(2)}) copy-start(bf16[6,1024,2,64]{1,3,2,0:T(8,128)(2,1)} %reshape.466) | copy-start | bytes 4718596
  216.8 11.5 %copy-start.29 = (f32[6,2,512]{2,1,0:T(2,128)}, f32[6,2,512]{2,1,0:T(2,128)S(1)}, u32[]{:S(2)}) copy-start(f32[6,2,512]{2,1,0:T(2,128)S(1)} %fusion.3) | copy-start | bytes 73732
  233.1 4.7 copy-start.50
  233.1 4.7 copy-start.51
  233.1 4.7 copy-start.52
  233.1 4.7 copy-start.43
  233.1 50.2 %all-to-all-start.3 = ((bf16[6,1024,128]{2,0,1:T(8,128)(2,1)}), bf16[6,1024,128]{2,0,1:T(8,128)(2,1)}, u32[]{:S(2)}, u32[]{:S(2)}) async-start(bf16[6,1024,128]{2,0,1:T(8,128)(2,1)} %pad_maximum_fusion.1), calls=%async_computation.3 | async-start | bytes 4194304 | tf_op jit(solution)/shard_map/all_to_all | solution.py:133
  237.7 429.9 %reduce-scatter.7.cloned.1.call-start = ((), (), s32[]{:S(2)}) async-start(), calls=%async_computation.13 | async-start | bytes 1327104 | tf_op jit(solution)/shard_map/reduce_scatter | solution.py:266
  285.1 2.2 slice-start
  285.1 2.3 slice-start.1
  285.1 10.6 %slice-start.2 = ((s8[4718592]{0:T(1024)(128)(4,1)}), s8[4194304]{0:T(1024)(128)(4,1)S(1)}, s32[]{:S(2)}) async-start(s8[4718592]{0:T(1024)(128)(4,1)} %bitcast.199), calls=%async_computation.19 | async-start | bytes 8388608
  286.7 34.3 %copy-start.10 = (f32[4,256,768]{2,1,0:T(8,128)}, f32[4,256,768]{2,1,0:T(8,128)S(1)}, u32[]{:S(2)}) copy-start(f32[4,256,768]{2,1,0:T(8,128)S(1)} %get-tuple-element.169) | copy-start | bytes 9437188
  287.4 8.3 %copy-start.15 = (bf16[4,256,768]{2,1,0:T(8,128)(2,1)S(1)}, bf16[4,256,768]{2,1,0:T(8,128)(2,1)}, u32[]{:S(2)}) copy-start(bf16[4,256,768]{2,1,0:T(8,128)(2,1)} %param.47) | copy-start | bytes 4718596
  287.4 8.3 %slice-start.3 = ((s8[4718592]{0:T(1024)(128)(4,1)}), s8[524288]{0:T(1024)(128)(4,1)S(1)}, s32[]{:S(2)}) async-start(s8[4718592]{0:T(1024)(128)(4,1)} %bitcast.199), calls=%async_computation.20 | async-start | bytes 1048576
  322.3 1.6 copy-start.2
  322.3 1.6 copy-start.37
  333.5 40.9 %all-to-all-start.4 = ((bf16[24,256,128]{2,1,0:T(8,128)(2,1)}), bf16[24,256,128]{2,1,0:T(8,128)(2,1)}, u32[]{:S(2)}, u32[]{:S(2)}) async-start(bf16[24,256,128]{2,1,0:T(8,128)(2,1)} %bitcast.189), calls=%async_computation.4 | async-start | bytes 3145728 | tf_op jit(solution)/shard_map/all_to_all | solution.py:175
  337.9 329.7 %reduce-scatter.11.cloned.1.call-start = ((), (), s32[]{:S(2)}) async-start(), calls=%async_computation.15 | async-start | bytes 5308416 | tf_op jit(solution)/shard_map/reduce_scatter | solution.py:272
  381.3 8.8 %copy-start.14 = (bf16[6,1024,2,64]{1,3,2,0:T(8,128)(2,1)}, bf16[6,1024,2,64]{1,3,2,0:T(8,128)(2,1)S(1)}, u32[]{:S(2)}) copy-start(bf16[6,1024,2,64]{1,3,2,0:T(8,128)(2,1)S(1)} %reshape.475) | copy-start | bytes 4718596
  381.3 8.8 %copy-start.12 = (pred[6,512,1024]{2,1,0:T(8,128)(4,1)S(1)}, pred[6,512,1024]{2,1,0:T(8,128)(4,1)}, u32[]{:S(2)}) copy-start(pred[6,512,1024]{2,1,0:T(8,128)(4,1)} %or_and_fusion) | copy-start | bytes 9437188
  408.0 105.4 %all-to-all-start.7 = ((bf16[6,1024,128]{2,0,1:T(8,128)(2,1)}), bf16[6,1024,128]{2,0,1:T(8,128)(2,1)}, u32[]{:S(2)}, u32[]{:S(2)}) async-start(bf16[6,1024,128]{2,0,1:T(8,128)(2,1)} %copy.134), calls=%async_computation.7 | async-start | bytes 4194304 | tf_op jit(solution)/shard_map/all_to_all | solution.py:227
  412.5 255.0 %reduce-scatter.9.cloned.1.call-start = ((), (), s32[]{:S(2)}) async-start(), calls=%async_computation.14 | async-start | bytes 5308416 | tf_op jit(solution)/shard_map/reduce_scatter | solution.py:269
  513.4 74.1 %all-to-all-start.6 = ((bf16[6,1024,128]{2,0,1:T(8,128)(2,1)}), bf16[6,1024,128]{2,0,1:T(8,128)(2,1)S(1)}, u32[]{:S(2)}, u32[]{:S(2)}) async-start(bf16[6,1024,128]{2,0,1:T(8,128)(2,1)} %copy.130), calls=%async_computation.6 | async-start | bytes 4194304 | tf_op jit(solution)/shard_map/all_to_all | solution.py:226
  587.5 52.3 %all-to-all-start.5 = ((bf16[6,1024,128]{2,0,1:T(8,128)(2,1)}), bf16[6,1024,128]{2,0,1:T(8,128)(2,1)}, u32[]{:S(2)}, u32[]{:S(2)}) async-start(bf16[6,1024,128]{2,0,1:T(8,128)(2,1)} %pad_maximum_fusion.2), calls=%async_computation.5 | async-start | bytes 4194304 | tf_op jit(solution)/shard_map/all_to_all | solution.py:225
  592.6 105.7 %reduce-scatter.5.cloned.1.call-start = ((), (), s32[]{:S(2)}) async-start(), calls=%async_computation.12 | async-start | bytes 3317760 | tf_op jit(solution)/shard_map/reduce_scatter | solution.py:263
  594.5 1.7 copy-start.13
  596.2 45.6 %copy-start.5 = (bf16[4,256,768]{2,1,0:T(8,128)(2,1)S(1)}, bf16[4,256,768]{2,1,0:T(8,128)(2,1)}, u32[]{:S(2)}) copy-start(bf16[4,256,768]{2,1,0:T(8,128)(2,1)} %param.30) | copy-start | bytes 4718596
  596.2 45.6 %copy-start.32 = (f32[4,256]{1,0:T(4,128)S(1)}, f32[4,256]{1,0:T(4,128)}, u32[]{:S(2)}) copy-start(f32[4,256]{1,0:T(4,128)} %copy-done.31) | copy-start | bytes 12292
  596.2 45.6 %copy-start.34 = (f32[768]{0:T(1024)S(1)}, f32[768]{0:T(1024)}, u32[]{:S(2)}) copy-start(f32[768]{0:T(1024)} %copy-done.33) | copy-start | bytes 9220
  596.2 45.7 %copy-start.36 = (f32[4,256]{1,0:T(4,128)S(1)}, f32[4,256]{1,0:T(4,128)}, u32[]{:S(2)}) copy-start(f32[4,256]{1,0:T(4,128)} %copy-done.35) | copy-start | bytes 12292
  596.2 45.7 %copy-start.46 = (f32[768]{0:T(1024)S(1)}, f32[768]{0:T(1024)}, u32[]{:S(2)}) copy-start(f32[768]{0:T(1024)} %convert_element_type.167) | copy-start | bytes 9220
  641.8 7.2 copy-start.19
  649.0 5.0 copy-start.53
  653.7 122.1 %all-reduce.6.cloned.1.call-start = ((), (), s32[]{:S(2)}) async-start(), calls=%async_computation.16 | async-start | bytes 3391488 | tf_op jit(solution)/shard_map/psum | solution.py:277
  705.7 7.7 copy-start.40
  712.0 4.7 copy-start.3
  712.0 4.7 copy-start.16
  712.0 4.7 copy-start.38
  716.7 4.3 copy-start.41
  716.7 4.3 copy-start.42
  716.7 4.3 copy-start.47
  716.7 4.3 copy-start.48
  716.7 66.0 %copy-start.1 = (bf16[768,768]{1,0:T(8,128)(2,1)S(1)}, bf16[768,768]{1,0:T(8,128)(2,1)}, u32[]{:S(2)}) copy-start(bf16[768,768]{1,0:T(8,128)(2,1)} %param.39) | copy-start | bytes 3538948
  775.8 5.8 copy-start.22
  (7 other events, 6.2 us)
Sparse Core Ops, SparseCore 0:
  329.3 35.8 reduce-scatter.6
  369.1 53.8 reduce-scatter.10
  426.4 53.8 reduce-scatter.8
  653.9 44.4 reduce-scatter.4
  701.0 74.7 all-reduce.5
where the time goes:
time: 797 us; the launch traced here: 789 us
  matrix products  305 us (38%)
  waiting for transfers between devices  196 us (25%)
  blocking collectives  93.5 us (12%)
  local copies, waits for them, and re-layouts  77.3 us (10%)
  other arithmetic  63.5 us (8%)
  starting transfers between devices  39.3 us (5%)
  between operations  14.9 us (2%)
    dot_general x2, matrix products, body(): jnp.einsum('ihqk,iqhc->ikhc', d_raw, q_split[:, q_start:k_end], preferred...  66.5 us
    dot_general x2, matrix products, body(): jnp.einsum('ihqk,ikhc->iqhc', d_raw, k_split[:, :k_end], preferred_elemen...  62.1 us
    all_to_all x1, waiting for transfers between devices, body(): lax.all_to_all(mixed_items, 'head', split_axis=1, concat_axis=0, tiled=True)  45.5 us
    all_to_all x1, waiting for transfers between devices, body(): lax.all_to_all(dq_items, 'head', split_axis=1, concat_axis=0, tiled=True)  42.3 us
    psum x1, blocking collectives, body(): lax.psum((g_attn_gain, g_attn_shift, g_q_bias, g_v_bias, g_out_bias, g_ml...  41.9 us
    all_gather x1, blocking collectives, body(): lax.all_gather(segments, 'head', axis=1, tiled=True)  38.5 us
    all_to_all x1, waiting for transfers between devices, body(): lax.all_to_all(value_rows.reshape(flat_shape), 'head', split_axis=0, conc...  33.6 us
    reduce_scatter x1, waiting for transfers between devices, body(): lax.psum_scatter(g_qkv.astype(jnp.bfloat16), 'seq', scatter_dimension=0,...  30.7 us
  transfers between devices with their start and end apart: 13, of which 7 were waited for; matrix products, arithmetic and copies ran while one was open for 39% of the time, Pallas kernels for 0%

commit v1 on v0

--- a/solution.py
+++ b/solution.py
@@ -1,9 +1,127 @@
-import jax
-import jax.numpy as jnp
+import functools
+import jax, jax.numpy as jnp
 from jax import lax
 from jax.sharding import PartitionSpec as P
-
+from jax.experimental import pallas as pl
+from jax.experimental.pallas import tpu as pltpu
 HDIM = 64
+BLK = 256
+LN2 = 0.6931471805599453
+LOG2E = 1.4426950408889634
+def nt(a,b): return lax.dot_general(a,b,(((1,),(1,)),((),())),preferred_element_type=jnp.float32)
+def nn(a,b): return lax.dot_general(a,b,(((1,),(0,)),((),())),preferred_element_type=jnp.float32)
+
+def fill_bias(code_ref, bias_ref):
+    length = code_ref.shape[1]
+    code = code_ref[...]
+    col = jnp.transpose(jnp.broadcast_to(code, (128, length)))
+    for i in range(length // BLK):
+        q_doc = col[i*BLK:(i+1)*BLK, :1] >> 1
+        for j in range(i + 1):
+            k_code = code[:, j*BLK:(j+1)*BLK]
+            same = q_doc == (k_code >> 1)
+            real = (k_code & 1) == 1
+            if i == j:
+                rows = lax.broadcasted_iota(jnp.int32, (BLK, BLK), 0)
+                cols = lax.broadcasted_iota(jnp.int32, (BLK, BLK), 1)
+                ok = same & (cols <= rows) & (real | (cols == rows))
+            else:
+                ok = same & real
+            bias_ref[i*BLK:(i+1)*BLK, j*BLK:(j+1)*BLK] = jnp.where(ok, 0.0, MASKED)
+
+def fwd_kernel(code_ref, q_ref, k_ref, v_ref, o_ref, lse_ref, bias_ref):
+    @pl.when(pl.program_id(0) == 0)
+    def _(): fill_bias(code_ref, bias_ref)
+    length = q_ref.shape[0]
+    first = lax.broadcasted_iota(jnp.int32, (length, 2*HDIM), 1) < HDIM
+    k_pair, v_pair = k_ref[...], v_ref[...]
+    zero = jnp.zeros_like(k_pair); one = jnp.ones_like(v_pair)
+    keys = (jnp.where(first, k_pair, zero), jnp.where(first, zero, k_pair))
+    vals = (jnp.where(first, v_pair, one), jnp.where(first, one, v_pair))
+    half = first[:BLK]
+    for i in range(length // BLK):
+        end = (i + 1) * BLK
+        q = q_ref[i*BLK:end, :]
+        outs, lses = [], []
+        for h in range(2):
+            s = nt(q, keys[h][:end]) + bias_ref[i*BLK:end, :end]
+            top = jnp.max(s, axis=1, keepdims=True)
+            p = jnp.exp2(s - top).astype(jnp.bfloat16)
+            mixed = nn(p, vals[h][:end])
+            total = pltpu.roll(mixed, HDIM, 1)
+            outs.append(mixed / total)
+            lses.append(top + jnp.log2(total))
+        o_ref[i*BLK:end, :] = jnp.where(half, outs[0], outs[1]).astype(o_ref.dtype)
+        lse_ref[i*BLK:end, :] = jnp.where(half, lses[0], lses[1])
+
+def bwd_kernel(code_ref, q_ref, k_ref, v_ref, o_ref, do_ref, lse_ref, dq_ref, dk_ref, dv_ref, bias_ref, dkt_ref, dvt_ref):
+    @pl.when(pl.program_id(0) == 0)
+    def _(): fill_bias(code_ref, bias_ref)
+    length = q_ref.shape[0]
+    first = lax.broadcasted_iota(jnp.int32, (length, 2*HDIM), 1) < HDIM
+    k_pair, v_pair = k_ref[...], v_ref[...]
+    zero = jnp.zeros_like(k_pair)
+    keys = (jnp.where(first, k_pair, zero), jnp.where(first, zero, k_pair))
+    vals = (jnp.where(first, v_pair, zero), jnp.where(first, zero, v_pair))
+    half = first[:BLK]
+    count = length // BLK
+    for i in reversed(range(count)):
+        end = (i + 1) * BLK
+        rows = slice(i*BLK, end)
+        q, do = q_ref[rows, :], do_ref[rows, :]
+        q_t, do_t = jnp.transpose(q), jnp.transpose(do)
+        prod = do.astype(jnp.float32) * o_ref[rows, :].astype(jnp.float32)
+        dq = None
+        for h in range(2):
+            lse = lse_ref[rows, h*HDIM:h*HDIM+1]
+            mine = half if h == 0 else ~half
+            delta = jnp.sum(jnp.where(mine, prod, 0.0), axis=1, keepdims=True)
+            p = jnp.exp2(nt(q, keys[h][:end]) + bias_ref[rows, :end] - lse)
+            dp = nt(do, vals[h][:end])
+            ds = (p * (dp - delta)).astype(jnp.bfloat16)
+            pb = p.astype(jnp.bfloat16)
+            part = nn(ds, keys[h][:end])
+            dq = part if dq is None else dq + part
+            hs = slice(h*HDIM, (h+1)*HDIM)
+            dv = nn(do_t[hs], pb)
+            dk = nn(q_t[hs], ds)
+            if i == count - 1:
+                dvt_ref[hs, :] = dv
+                dkt_ref[hs, :] = dk
+            else:
+                dvt_ref[hs, :end] += dv
+                dkt_ref[hs, :end] += dk
+        dq_ref[rows, :] = (dq * 0.125).astype(dq_ref.dtype)
+    dk_ref[...] = jnp.transpose(dkt_ref[...] * LN2).astype(dk_ref.dtype)
+    dv_ref[...] = jnp.transpose(dvt_ref[...]).astype(dv_ref.dtype)
+
+def attn_fwd(code, proj, values, q0, k0, v0, pairs, name):
+    length = proj.shape[0]
+    w = 2*HDIM
+    blk = lambda off: pl.BlockSpec((length, w), lambda p: (0, p + off))
+    flops = pairs * 2 * 2 * 2 * length * length * 256
+    return pl.pallas_call(fwd_kernel, grid=(pairs,), name=name,
+        in_specs=[pl.BlockSpec((1, length), lambda p: (0, 0)), blk(q0), blk(k0), blk(v0)],
+        out_specs=[blk(0), blk(0)],
+        out_shape=[jax.ShapeDtypeStruct((length, pairs*w), jnp.bfloat16), jax.ShapeDtypeStruct((length, pairs*w), jnp.float32)],
+        scratch_shapes=[pltpu.VMEM((length, length), jnp.float32)],
+        cost_estimate=pl.CostEstimate(flops=flops, bytes_accessed=pairs*length*w*12, transcendentals=0),
+        compiler_params=pltpu.CompilerParams(vmem_limit_bytes=48 << 20))(code, proj, proj, values)
+
+def attn_bwd(code, proj, values, o, do, lse, q0, k0, v0, o0, do0, pairs, name):
+    length = proj.shape[0]
+    w = 2*HDIM
+    blk = lambda off: pl.BlockSpec((length, w), lambda p: (0, p + off))
+    flops = pairs * 2 * 5 * 2 * length * length * 256
+    return pl.pallas_call(bwd_kernel, grid=(pairs,), name=name,
+        in_specs=[pl.BlockSpec((1, length), lambda p: (0, 0)), blk(q0), blk(k0), blk(v0), blk(o0), blk(do0), blk(0)],
+        out_specs=[blk(0)]*3,
+        out_shape=[jax.ShapeDtypeStruct((length, pairs*w), jnp.bfloat16)]*3,
+        scratch_shapes=[pltpu.VMEM((length, length), jnp.float32), pltpu.VMEM((w, length), jnp.float32), pltpu.VMEM((w, length), jnp.float32)],
+        cost_estimate=pl.CostEstimate(flops=flops, bytes_accessed=pairs*length*w*18, transcendentals=0),
+        compiler_params=pltpu.CompilerParams(vmem_limit_bytes=48 << 20))(code, proj, proj, values, o, do, lse)
+
+
 QBLOCK = 512
 
 
@@ -38,7 +156,7 @@
     return jnp.where(allowed[:, None], raw * factor, MASKED)
 
 
-def body(
+def spread_body(
     tokens,
     skip_values,
     segments,
@@ -299,9 +417,161 @@
     )
 
 
+Q_SCALE = LOG2E * HDIM ** -0.5
+
+
+def fits(sizes):
+    return sizes == (8, 4)
+
+
+def pick(array, index):
+    return lax.dynamic_index_in_dim(array, index, 0, keepdims=False)
+
+
+def swap(array, axis, count, bit):
+    return lax.ppermute(array, axis, [(i, i ^ bit) for i in range(count)])
+
+
+def trade(blocks, me, count):
+    return [
+        pick(blocks, me) if d == 0 else swap(pick(blocks, me ^ d), "head", count, d)
+        for d in range(count)
+    ]
+
+
+def settle(parts, me):
+    whole = jnp.zeros((len(parts),) + parts[0].shape, parts[0].dtype)
+    for d, part in enumerate(parts):
+        whole = lax.dynamic_update_index_in_dim(whole, part, me ^ d, 0)
+    return whole
+
+
+def row_body(
+    sizes,
+    tokens,
+    skip_values,
+    segments,
+    token_mask,
+    attn_gain,
+    attn_shift,
+    w_qkv,
+    q_bias,
+    v_bias,
+    w_out,
+    out_bias,
+    mlp_gain,
+    mlp_shift,
+    w_up,
+    up_bias,
+    w_down,
+    down_bias,
+    cotangent,
+):
+    n_head = sizes[1]
+    f32 = jnp.float32
+    me = lax.axis_index("head")
+    rows, part, width = tokens.shape
+    length = rows * part
+    fresh = width // 2
+    code = (segments * 2 + token_mask).reshape(rows, 1, part)
+    code_row = settle(trade(code, me, n_head), me).reshape(1, length)
+    x_row = settle(trade(tokens, me, n_head), me).reshape(length, width)
+    skip_values, x_row = lax.optimization_barrier((skip_values, x_row))
+    skip_row = settle(trade(skip_values, me, n_head), me).reshape(length, fresh)
+    cotangent, skip_gate = lax.optimization_barrier((cotangent, skip_row))
+    skip_row = skip_gate
+    dy = settle(trade(cotangent, me, n_head), me).reshape(length, width)
+
+    x_f = x_row.astype(f32)
+    normed_f, first_back = jax.vjp(layer_norm, x_f, attn_gain.astype(f32), attn_shift.astype(f32))
+    normed = normed_f.astype(jnp.bfloat16)
+    qkv_bias = jnp.concatenate([q_bias, jnp.zeros_like(q_bias), v_bias]).astype(f32)
+    scale = jnp.where(jnp.arange(w_qkv.shape[1]) < width, Q_SCALE, 1.0).astype(f32)
+    proj = ((nn(normed, w_qkv) + qkv_bias) * scale).astype(jnp.bfloat16)
+    o_a, lse_a = attn_fwd(code_row, proj, proj, 0, 6, 12, 3, "attn_fwd_a")
+    o_b, lse_b = attn_fwd(code_row, proj, skip_row, 3, 9, 0, 3, "attn_fwd_b")
+    mixed = jnp.concatenate([o_a, o_b], axis=1)
+    middle = x_f + nn(mixed, w_out) + out_bias.astype(f32)
+    normed_mid, second_back = jax.vjp(layer_norm, middle, mlp_gain.astype(f32), mlp_shift.astype(f32))
+    normed_two = normed_mid.astype(jnp.bfloat16)
+    hidden = nn(normed_two, w_up) + up_bias.astype(f32)
+    active_f, gelu_back = jax.vjp(gelu_tanh, hidden)
+    active = active_f.astype(jnp.bfloat16)
+    result = (middle + nn(active, w_down) + down_bias.astype(f32)).astype(jnp.bfloat16)
+    layer_out = settle(trade(result.reshape(rows, part, width), me, n_head), me)
+    g_down = jnp.einsum("sf,sd->fd", active, dy, preferred_element_type=f32)
+    g_down_bias = jnp.sum(dy, axis=0, dtype=f32)
+    d_hidden = gelu_back(nt(dy, w_down))[0].astype(jnp.bfloat16)
+    g_up_bias = jnp.sum(d_hidden, axis=0, dtype=f32)
+    g_up = jnp.einsum("sd,sf->df", normed_two, d_hidden, preferred_element_type=f32)
+    d_mid_norm, g_mlp_gain, g_mlp_shift = second_back(nt(d_hidden, w_up))
+    d_middle = dy.astype(f32) + d_mid_norm
+    d_att = d_middle.astype(jnp.bfloat16)
+    g_out_bias = jnp.sum(d_att, axis=0, dtype=f32)
+    g_out = jnp.einsum("sc,sd->cd", mixed, d_att, preferred_element_type=f32)
+    d_mixed = nt(d_att, w_out).astype(jnp.bfloat16)
+    dq_b, dk_b, dv_b = attn_bwd(
+        code_row, proj, skip_row, o_b, d_mixed, lse_b, 3, 9, 0, 0, 3, 3, "attn_bwd_b"
+    )
+    grad_skip = settle(trade(dv_b.reshape(rows, part, fresh), me, n_head), me).astype(f32)
+    dq_a, dk_a, dv_a = attn_bwd(
+        code_row, proj, proj, o_a, d_mixed, lse_a, 0, 6, 12, 0, 0, 3, "attn_bwd_a"
+    )
+    d_proj = jnp.concatenate([dq_a, dq_b, dk_a, dk_b, dv_a], axis=1)
+    d_normed = nt(d_proj, w_qkv)
+    d_tok_norm, g_attn_gain, g_attn_shift = first_back(d_normed)
+    grad_row = (d_middle + d_tok_norm).astype(jnp.bfloat16)
+    grad_tokens = settle(trade(grad_row.reshape(rows, part, width), me, n_head), me).astype(f32)
+    g_qkv = jnp.einsum("sd,sc->dc", normed, d_proj, preferred_element_type=f32)
+    g_proj_bias = jnp.sum(d_proj, axis=0, dtype=f32)
+    small = (
+        g_attn_gain,
+        g_attn_shift,
+        g_proj_bias[:width],
+        g_proj_bias[2 * width :],
+        g_out_bias,
+        g_mlp_gain,
+        g_mlp_shift,
+        g_up_bias,
+        g_down_bias,
+    )
+    packed = lax.psum(jnp.concatenate(small), ("seq", "head"))
+    sums = []
+    for entry in small:
+        sums.append(packed[: entry.shape[0]])
+        packed = packed[entry.shape[0] :]
+
+    def reduce(grad):
+        shard = lax.psum_scatter(
+            grad.astype(jnp.bfloat16), "seq", scatter_dimension=0, tiled=True
+        )
+        return lax.psum(shard, "head").astype(f32)
+
+    r_down, r_up, r_out, r_qkv = reduce(g_down), reduce(g_up), reduce(g_out), reduce(g_qkv)
+    return (
+        layer_out,
+        grad_tokens,
+        grad_skip,
+        sums[0],
+        sums[1],
+        r_qkv,
+        sums[2],
+        sums[3],
+        r_out,
+        sums[4],
+        sums[5],
+        sums[6],
+        r_up,
+        sums[7],
+        r_down,
+        sums[8],
+    )
+
+
 def solution(mesh):
+    sizes = (mesh.shape["seq"], mesh.shape["head"])
     return jax.shard_map(
-        body,
+        functools.partial(row_body, sizes) if fits(sizes) else spread_body,
         mesh=mesh,
         in_specs=(
             P("seq", "head", None),

time: 797 us -> 499 us (0.63)
  matrix products: 305 us -> 99.6 us
  Pallas kernels: 0 us -> 51.4 us
  blocking collectives: 93.5 us -> 43.4 us
  other arithmetic: 63.5 us -> 23.2 us
  local copies, waits for them, and re-layouts: 77.3 us -> 37.3 us
  waiting for transfers between devices: 196 us -> 175 us
    dot_general x24 -> x12, matrix products: 305 us -> 99.6 us  [the longest x4 33.9 us: nt(): lax.dot_general(a, b, (((1,), (1,)), ((), ())), preferred_element_type=jn...]
    all_to_all x8 -> x0, waiting for transfers between devices: 152 us -> none  [the longest x1 45.5 us: body(): lax.all_to_all(mixed_items, 'head', split_axis=1, concat_axis=0, tiled=True)]
    ppermute x0 -> x21, waiting for transfers between devices: none -> 86.9 us  [swap(): return lax.ppermute(array, axis, [(i, i ^ bit) for i in range(count)])]
    reduce_scatter x4, waiting for transfers between devices: 30.8 us -> 88.4 us  [reduce(): lax.psum_scatter(grad.astype(jnp.bfloat16), 'seq', scatter_dimension=0, t...]
    all_gather x2 -> x0, blocking collectives: 51.6 us -> none  [the longest x1 38.5 us: body(): lax.all_gather(segments, 'head', axis=1, tiled=True)]
    pallas_call x0 -> x4, Pallas kernels: none -> 51.4 us  [the longest x2 28 us: attn_bwd(): pl.pallas_call(bwd_kernel, grid=(pairs,), name=name, in_specs=[pl.BlockSp...]
    ppermute x0 -> x21, starting transfers between devices: none -> 44 us  [swap(): return lax.ppermute(array, axis, [(i, i ^ bit) for i in range(count)])]
    all_to_all x8 -> x0, starting transfers between devices: 38.9 us -> none  [the longest x1 6.33 us: body(): lax.all_to_all(value_rows.reshape(flat_shape), 'head', split_axis=0, conc...]
  transfers between devices with their start and end apart: 13 -> 26, of which waited for: 7 -> 8; matrix products, arithmetic and copies ran while one was open for 39% -> 21% of each run, Pallas kernels for 0% -> 10%
where the time goes in v1:
time: 499 us; the launch traced here: 489 us
  waiting for transfers between devices  175 us (35%)
  matrix products  99.6 us (20%)
  Pallas kernels  51.4 us (10%)
  starting transfers between devices  44.2 us (9%)
  blocking collectives  43.4 us (9%)
  local copies, waits for them, and re-layouts  37.3 us (7%)
  other arithmetic  23.2 us (5%)
  between operations  15 us (3%)
    reduce_scatter x4, waiting for transfers between devices, reduce(): lax.psum_scatter(grad.astype(jnp.bfloat16), 'seq', scatter_dimension=0, t...  88.4 us
    ppermute x21, waiting for transfers between devices, swap(): return lax.ppermute(array, axis, [(i, i ^ bit) for i in range(count)])  86.9 us
    ppermute x21, starting transfers between devices, swap(): return lax.ppermute(array, axis, [(i, i ^ bit) for i in range(count)])  44 us
    psum x1, blocking collectives, row_body(): packed = lax.psum(jnp.concatenate(small), ('seq', 'head'))  43.4 us
    dot_general x4, matrix products, nt(): lax.dot_general(a, b, (((1,), (1,)), ((), ())), preferred_element_type=jn...  33.9 us
    dot_general x4, matrix products, nn(): lax.dot_general(a, b, (((1,), (0,)), ((), ())), preferred_element_type=jn...  32.6 us
    pallas_call x2, Pallas kernels, attn_bwd(): pl.pallas_call(bwd_kernel, grid=(pairs,), name=name, in_specs=[pl.BlockSp...  28 us
    pallas_call x2, Pallas kernels, attn_fwd(): pl.pallas_call(fwd_kernel, grid=(pairs,), name=name, in_specs=[pl.BlockSp...  23.4 us
  transfers between devices with their start and end apart: 26, of which 8 were waited for; matrix products, arithmetic and copies ran while one was open for 21% of the time, Pallas kernels for 10%

profile of v1, /device:TPU:0, one launch (start us, length us, event | category | flops | bytes accessed | tf_op | source)
XLA Modules:
  0.0 489.4 jit_solution(11353468299351947029)
XLA Ops:
  7.4 1.2 broadcast.115.clone
  8.6 2.7 dynamic-slice_bitcast_fusion.9
  11.3 3.0 collective-permute-start
  14.3 2.6 collective-permute-start.1
  17.5 3.9 collective-permute-start.5
  21.6 10.4 %collective-permute-done.3 = s32[1,256]{1,0:T(1,128)S(1)} collective-permute-done((s32[1,256]{1,0:T(1,128)S(1)}, s32[1,256]{1,0:T(1,128)S(1)}, u32[]{:S(2)}, u32[]{:S(2)}) %collective-permute-start.3) | collective-permute-done | bytes 1056 | tf_op jit(solution)/shard_map/ppermute | solution.py:432
  32.0 2.6 collective-permute-start.2
  34.8 1.8 bitcast_dynamic-update-slice_fusion.11
  37.5 7.1 %collective-permute-done.2 = bf16[256,768]{1,0:T(8,128)(2,1)} collective-permute-done((bf16[256,768]{1,0:T(8,128)(2,1)}, bf16[256,768]{1,0:T(8,128)(2,1)}, u32[]{:S(2)}, u32[]{:S(2)}) %collective-permute-start.2) | collective-permute-done | bytes 393248 | tf_op jit(solution)/shard_map/ppermute | solution.py:432
  44.6 1.8 bitcast_dynamic-update-slice_fusion.9
  46.5 8.1 %collective-permute-start.6 = (bf16[256,384]{1,0:T(8,128)(2,1)S(1)}, bf16[256,384]{1,0:T(8,128)(2,1)S(1)}, u32[]{:S(2)}, u32[]{:S(2)}) collective-permute-start(bf16[256,384]{1,0:T(8,128)(2,1)S(1)} %get-tuple-element.81), channel_id=1, source_target_pairs={{0,1},{1,0},{2,3},{3,2},{4,5},{5,4},{6,7},{7,6},{8,9},{9,8},{10,11... | collective-permute-start | bytes 589832 | tf_op jit(solution)/shard_map/ppermute | solution.py:432
  55.7 1.4 collective-permute-start.8
  57.1 1.7 convert_reduce_fusion.2
  58.8 2.0 fusion.16
  60.8 7.0 %multiply_convert_fusion.1.q_ref.k_ref.v_ref = bf16[1024,1920]{1,0:T(8,128)(2,1)} fusion(f32[1920]{0:T(1024)S(1)} %fusion.20, f32[1920]{0:T(1024)S(1)} %maximum_convert_fusion, bf16[768,1920]{1,0:T(8,128)(2,1)S(1)} %copy-done, bf16[1024,768]{1,0:T(8,128)(2,1)} %bitcast.6, f32[768]{0:T(1024)S(1)} %convert_element_type.106, ...), kind=kOutput, calls=%fused_computation.12 | convolution fusion | flops 3030515712 | bytes 8483840 | tf_op jit(solution)/shard_map/dot_general | solution.py:12
  67.8 11.7 %attn_fwd_a.1 = (bf16[1024,384]{1,0:T(8,128)(2,1)S(1)}, f32[1024,384]{1,0:T(8,128)S(1)}) custom-call(s32[1,1024]{1,0:T(1,128)S(1)} %bitcast.110, bf16[1024,1920]{1,0:T(8,128)(2,1)} %multiply_convert_fusion.1.q_ref.k_ref.v_ref, bf16[1024,1920]{1,0:T(8,128)(2,1)} %multiply_convert_fusion.1.q_ref.k_ref.v_ref, ...), custom_call_target="tpu_custom_call" | custom-call | flops 6442450944 | bytes 4718592 | tf_op jit(solution)/shard_map/attn_fwd_a/pallas_call | solution.py:103
  80.0 2.2 copy-done.23
  83.3 2.0 collective-permute-start.13
  85.3 1.4 collective-permute-start.14
  86.7 11.7 %attn_fwd_b.1 = (bf16[1024,384]{1,0:T(8,128)(2,1)S(1)}, f32[1024,384]{1,0:T(8,128)S(1)}) custom-call(s32[1,1024]{1,0:T(1,128)S(1)} %bitcast.111, bf16[1024,1920]{1,0:T(8,128)(2,1)} %multiply_convert_fusion.1.q_ref.k_ref.v_ref, bf16[1024,1920]{1,0:T(8,128)(2,1)} %multiply_convert_fusion.1.q_ref.k_ref.v_ref, bf16[1024,384]{1,0:T(8,128)(2,1)S(1)} %bitcast.108), custom_call_target="tpu_custom_call" | custom-call | flops 6442450944 | bytes 4718592 | tf_op jit(solution)/shard_map/attn_fwd_b/pallas_call | solution.py:103
  98.6 3.9 fusion.32
  103.1 8.5 %fusion.27 = f32[1024,3072]{1,0:T(8,128)} fusion(bf16[768,3072]{1,0:T(8,128)(2,1)S(1)} %bitcast.123, f32[1024,768]{1,0:T(8,128)S(1)} %get-tuple-element.95, f32[768]{0:T(1024)S(1)} %convert_element_type.112, f32[768]{0:T(1024)S(1)} %convert_element_type.111, f32[1024]{0:T(1024)S(1)} %fusion.22, f32[1024]{0:T(1024)S(1)} %broadcast_multiply_fusion), kind=kOutput, calls=%fused_computation.123 | convolution fusion | flops 4835770368 | bytes 20461568 | tf_op jit(solution)/shard_map/dot_general | solution.py:12
  111.6 1.6 collective-permute-done.13
  113.2 17.0 %convert_reduce_fusion = (f32[3072]{0:T(1024)}, bf16[1024,3072]{1,0:T(8,128)(2,1)}) fusion(f32[1024,3072]{1,0:T(8,128)} %fusion.27, f32[3072]{0:T(1024)S(1)} %convert_element_type.114, bf16[1024,768]{1,0:T(8,128)(2,1)S(1)} %bitcast.114, bf16[3072,768]{1,0:T(8,128)(2,1)} %param.33), kind=kOutput, calls=%fused_computation.9 | convolution fusion | flops 4904186880 | bytes 25190400 | tf_op jit(solution)/shard_map/dot_general | solution.py:11
  130.3 9.1 %multiply_reduce_fusion = (f32[768]{0:T(1024)S(1)}, f32[1024]{0:T(1024)S(1)}, f32[768]{0:T(1024)S(1)}, f32[1024,768]{1,0:T(8,128)S(1)}) fusion(f32[1024,768]{1,0:T(8,128)S(1)} %get-tuple-element.95, f32[1024]{0:T(1024)S(1)} %fusion.22, f32[1024]{0:T(1024)S(1)} %broadcast_multiply_fusion, f32[768]{0:T(1024)S(1)} %convert_element_type.111, ...), kind=kOutput, calls=%fused_computation.34 | convolution fusion | flops 4838126592 | bytes 17323008 | tf_op jit(solution)/shard_map/dot_general | solution.py:11
  139.4 1.4 fusion.30
  141.4 1.1 copy-done.13
  143.0 2.6 convolution_convert_fusion.3.do_ref
  145.6 2.5 convolution_convert_fusion.4
  149.2 1.1 copy-done.8
  150.4 1.4 copy-done.9
  151.8 14.1 %attn_bwd_b.1 = (bf16[1024,384]{1,0:T(8,128)(2,1)S(1)}, bf16[1024,384]{1,0:T(8,128)(2,1)S(1)}, bf16[1024,384]{1,0:T(8,128)(2,1)S(1)}) custom-call(s32[1,1024]{1,0:T(1,128)S(1)} %bitcast.112, bf16[1024,1920]{1,0:T(8,128)(2,1)} %multiply_convert_fusion.1.q_ref.k_ref.v_ref, bf16[1024,1920]{1,0:T(8,128)(2,1)} %multiply_convert_fusion.1.q_ref.k_ref.v_ref, ...), custom_call_target="tpu_custom_call" | custom-call | flops 16106127360 | bytes 7077888 | tf_op jit(solution)/shard_map/attn_bwd_b/pallas_call | solution.py:116
  165.9 13.9 %attn_bwd_a.1 = (bf16[1024,384]{1,0:T(8,128)(2,1)S(1)}, bf16[1024,384]{1,0:T(8,128)(2,1)S(1)}, bf16[1024,384]{1,0:T(8,128)(2,1)S(1)}) custom-call(s32[1,1024]{1,0:T(1,128)S(1)} %bitcast.113, bf16[1024,1920]{1,0:T(8,128)(2,1)} %multiply_convert_fusion.1.q_ref.k_ref.v_ref, bf16[1024,1920]{1,0:T(8,128)(2,1)} %multiply_convert_fusion.1.q_ref.k_ref.v_ref, ...), custom_call_target="tpu_custom_call" | custom-call | flops 16106127360 | bytes 7077888 | tf_op jit(solution)/shard_map/attn_bwd_a/pallas_call | solution.py:116
  180.6 2.0 copy-done.20
  182.6 6.7 %convolution_convert_fusion.2 = bf16[768,1920]{1,0:T(8,128)(2,1)} fusion(bf16[1024,1920]{1,0:T(8,128)(2,1)S(1)} %constant_dynamic-update-slice_fusion.2, bf16[1024,768]{1,0:T(8,128)(2,1)} %bitcast.6, f32[768]{0:T(1024)S(1)} %convert_element_type.106, f32[768]{0:T(1024)S(1)} %convert_element_type.105, f32[1024]{0:T(1024)S(1)} %fusion.21, ...), kind=kOutput, calls=%fused_computation.26 | convolution fusion | flops 3026092032 | bytes 8468480 | tf_op jit(solution)/shard_map/sd,sc->dc/dot_general | solution.py:525
  189.3 10.9 %convolution_convert_fusion.1 = bf16[768,3072]{1,0:T(8,128)(2,1)} fusion(bf16[1024,3072]{1,0:T(8,128)(2,1)} %get-tuple-element.99, f32[1024,768]{1,0:T(8,128)} %copy-done.17, f32[768]{0:T(1024)S(1)} %convert_element_type.112, f32[768]{0:T(1024)S(1)} %convert_element_type.111, f32[1024]{0:T(1024)S(1)} %fusion.22, f32[1024]{0:T(1024)S(1)} %broadcast_multiply_fusion), kind=kOutput, calls=%fused_computation.14 | convolution fusion | flops 4838129664 | bytes 14170112 | tf_op jit(solution)/shard_map/sd,sf->df/dot_general | solution.py:506
  200.9 13.1 %convolution_convert_fusion = bf16[3072,768]{1,0:T(8,128)(2,1)} fusion(bf16[1024,768]{1,0:T(8,128)(2,1)} %bitcast.115, f32[1024,3072]{1,0:T(8,128)} %fusion.27, f32[3072]{0:T(1024)S(1)} %convert_element_type.114), kind=kOutput, calls=%fused_computation.13 | convolution fusion | flops 4865654784 | bytes 18886656 | tf_op jit(solution)/shard_map/sf,sd->fd/dot_general | solution.py:502
  214.1 13.2 %add_convert_fusion.1 = bf16[1024,768]{1,0:T(8,128)(2,1)S(1)} fusion(f32[1024,768]{1,0:T(8,128)} %copy-done.17, bf16[3072,768]{1,0:T(8,128)(2,1)} %param.33, f32[768]{0:T(1024)S(1)} %convert_element_type.116, f32[1024,3072]{1,0:T(8,128)} %fusion.27, f32[3072]{0:T(1024)S(1)} %convert_element_type.114), kind=kOutput, calls=%fused_computation.39 | convolution fusion | flops 4865654784 | bytes 22035456 | tf_op jit(solution)/shard_map/dot_general | solution.py:12
  227.3 1.2 broadcast.115.clone.1
  229.4 5.2 %collective-permute-start.9 = (bf16[256,768]{1,0:T(8,128)(2,1)S(1)}, bf16[256,768]{1,0:T(8,128)(2,1)S(1)}, u32[]{:S(2)}, u32[]{:S(2)}) collective-permute-start(bf16[256,768]{1,0:T(8,128)(2,1)S(1)} %get-tuple-element.69), channel_id=1, source_target_pairs={{0,1},{1,0},{2,3},{3,2},{4,5},{5,4},{6,7},{7,6},{8,9},{9,8},{10,11... | collective-permute-start | bytes 1179656 | tf_op jit(solution)/shard_map/ppermute | solution.py:432
  234.7 1.1 collective-permute-start.10
  235.8 1.5 collective-permute-start.11
  240.0 5.2 %fusion.28 = (f32[768]{0:T(1024)S(1)}, f32[1024]{0:T(1024)S(1)}, f32[1024,768]{1,0:T(8,128)S(1)}) fusion(f32[768]{0:T(1024)S(1)} %convert_element_type.105, f32[1024]{0:T(1024)S(1)} %broadcast_multiply_fusion.1, bf16[1024,768]{1,0:T(8,128)(2,1)} %bitcast.6, bf16[1024,1920]{1,0:T(8,128)(2,1)S(1)} %copy-done.21, bf16[768,1920]{1,0:T(8,128)(2,1)S(1)} %copy-done), kind=kOutput, calls=%fused_computation.124 | convolution fusion | flops 3024615680 | bytes 11614208 | tf_op jit(solution)/shard_map/dot_general | solution.py:11
  245.2 3.0 fusion.15
  248.2 2.8 add_convert_fusion
  252.2 1.1 copy-done.18
  256.2 8.3 %collective-permute-done.10 = bf16[256,768]{1,0:T(8,128)(2,1)S(1)} collective-permute-done((bf16[256,768]{1,0:T(8,128)(2,1)S(1)}, bf16[256,768]{1,0:T(8,128)(2,1)S(1)}, u32[]{:S(2)}, u32[]{:S(2)}) %collective-permute-start.10) | collective-permute-done | bytes 393248 | tf_op jit(solution)/shard_map/ppermute | solution.py:432
  266.1 31.1 %reduce-scatter.9.cloned.1.call-done = bf16[96,3072]{1,0:T(8,128)(2,1)} async-done(((bf16[768,3072]{1,0:T(8,128)(2,1)}), bf16[96,3072]{1,0:T(8,128)(2,1)}) %reduce-scatter.9.cloned.1.call-update) | async-done | bytes 589840 | tf_op jit(solution)/shard_map/reduce_scatter | solution.py:545
  297.2 57.2 %reduce-scatter.11.cloned.1.call-done = bf16[384,768]{1,0:T(8,128)(2,1)} async-done(((bf16[3072,768]{1,0:T(8,128)(2,1)}), bf16[384,768]{1,0:T(8,128)(2,1)}) %reduce-scatter.11.cloned.1.call-update) | async-done | bytes 589840 | tf_op jit(solution)/shard_map/reduce_scatter | solution.py:545
  354.5 1.3 constant_dynamic-update-slice_fusion.10
  355.8 43.4 %psum.35 = f32[8832]{0:T(1024)} all-reduce(f32[8832]{0:T(1024)} %constant_dynamic-update-slice_fusion.10), channel_id=1, replica_groups=mesh['seq'=8,'head'=4] {'seq','head'}, use_global_device_ids=true, to_apply=%region_16.17 | all-reduce | flops 8832 | bytes 70656 | tf_op jit(solution)/shard_map/psum | solution.py:538
  399.2 1.4 slice.74
  400.6 1.3 slice.70
  401.9 2.6 collective-permute-start.19
  404.5 1.7 collective-permute-start.20
  406.1 1.4 fusion.31
  407.6 2.2 collective-permute-start.17
  409.8 1.6 bitcast_dynamic-update-slice_fusion.14
  411.4 33.4 %collective-permute-done.19 = bf16[256,384]{1,0:T(8,128)(2,1)S(1)} collective-permute-done((bf16[256,384]{1,0:T(8,128)(2,1)}, bf16[256,384]{1,0:T(8,128)(2,1)S(1)}, u32[]{:S(2)}, u32[]{:S(2)}) %collective-permute-start.19) | collective-permute-done | bytes 196640 | tf_op jit(solution)/shard_map/ppermute | solution.py:432
  446.2 2.4 convert_element_type.124
  448.6 26.0 %collective-permute-done.16 = bf16[256,768]{1,0:T(8,128)(2,1)S(1)} collective-permute-done((bf16[256,768]{1,0:T(8,128)(2,1)}, bf16[256,768]{1,0:T(8,128)(2,1)S(1)}, u32[]{:S(2)}, u32[]{:S(2)}) %collective-permute-start.16) | collective-permute-done | bytes 393248 | tf_op jit(solution)/shard_map/ppermute | solution.py:432
  474.7 1.9 convert_element_type.123
  476.7 2.2 convert_element_type.134
  478.9 2.2 convert_element_type.136
  (196 shorter events, 21.2 us)
Async XLA Ops:
  7.2 53.6 %copy-start = (bf16[768,1920]{1,0:T(8,128)(2,1)S(1)}, bf16[768,1920]{1,0:T(8,128)(2,1)}, u32[]{:S(2)}) copy-start(bf16[768,1920]{1,0:T(8,128)(2,1)} %param.24) | copy-start | bytes 8847364
  7.2 9.7 %copy-start.34 = (s32[4,256]{1,0:T(4,128)S(1)}, s32[4,256]{1,0:T(4,128)}, u32[]{:S(2)}) copy-start(s32[4,256]{1,0:T(4,128)} %param.20) | copy-start | bytes 12292
  7.2 9.7 %copy-start.33 = (s32[4,256]{1,0:T(4,128)S(1)}, s32[4,256]{1,0:T(4,128)}, u32[]{:S(2)}) copy-start(s32[4,256]{1,0:T(4,128)} %param.21) | copy-start | bytes 12292
  7.2 14.2 %copy-start.41 = (bf16[768]{0:T(1024)(128)(2,1)S(1)}, bf16[768]{0:T(1024)(128)(2,1)}, u32[]{:S(2)}) copy-start(bf16[768]{0:T(1024)(128)(2,1)} %param.25) | copy-start | bytes 4612
  7.2 14.2 %copy-start.42 = (bf16[384]{0:T(512)(128)(2,1)S(1)}, bf16[384]{0:T(512)(128)(2,1)}, u32[]{:S(2)}) copy-start(bf16[384]{0:T(512)(128)(2,1)} %param.26) | copy-start | bytes 2308
  7.2 14.2 %copy-start.35 = (bf16[768]{0:T(1024)(128)(2,1)S(1)}, bf16[768]{0:T(1024)(128)(2,1)}, u32[]{:S(2)}) copy-start(bf16[768]{0:T(1024)(128)(2,1)} %param.22) | copy-start | bytes 4612
  7.2 14.2 %copy-start.36 = (bf16[768]{0:T(1024)(128)(2,1)S(1)}, bf16[768]{0:T(1024)(128)(2,1)}, u32[]{:S(2)}) copy-start(bf16[768]{0:T(1024)(128)(2,1)} %param.23) | copy-start | bytes 4612
  7.3 14.2 %copy-start.37 = (bf16[768]{0:T(1024)(128)(2,1)S(1)}, bf16[768]{0:T(1024)(128)(2,1)}, u32[]{:S(2)}) copy-start(bf16[768]{0:T(1024)(128)(2,1)} %param.28) | copy-start | bytes 4612
  7.3 14.2 %copy-start.38 = (bf16[768]{0:T(1024)(128)(2,1)S(1)}, bf16[768]{0:T(1024)(128)(2,1)}, u32[]{:S(2)}) copy-start(bf16[768]{0:T(1024)(128)(2,1)} %param.29) | copy-start | bytes 4612
  7.3 14.2 %copy-start.39 = (bf16[768]{0:T(1024)(128)(2,1)S(1)}, bf16[768]{0:T(1024)(128)(2,1)}, u32[]{:S(2)}) copy-start(bf16[768]{0:T(1024)(128)(2,1)} %param.30) | copy-start | bytes 4612
  7.3 14.2 %copy-start.32 = (bf16[3072]{0:T(1024)(128)(2,1)S(1)}, bf16[3072]{0:T(1024)(128)(2,1)}, u32[]{:S(2)}) copy-start(bf16[3072]{0:T(1024)(128)(2,1)} %param.32) | copy-start | bytes 18436
  7.3 258.8 %reduce-scatter.7.cloned.1.call-start = ((), (), s32[]{:S(2)}) async-start(), calls=%async_computation.5 | async-start | bytes 1327104 | tf_op jit(solution)/shard_map/reduce_scatter | solution.py:545
  11.3 23.6 %collective-permute-start = (bf16[256,768]{1,0:T(8,128)(2,1)}, bf16[256,768]{1,0:T(8,128)(2,1)}, u32[]{:S(2)}, u32[]{:S(2)}) collective-permute-start(bf16[256,768]{1,0:T(8,128)(2,1)} %get-tuple-element.72), channel_id=1, source_target_pairs={{0,1},{1,0},{2,3},{3,2},{4,5},{5,4},{6,7},{7,6},{8,9},{9,8},{10,11... | collective-permute-start | bytes 1179656 | tf_op jit(solution)/shard_map/ppermute | solution.py:432
  14.3 22.4 %collective-permute-start.1 = (bf16[256,768]{1,0:T(8,128)(2,1)}, bf16[256,768]{1,0:T(8,128)(2,1)S(1)}, u32[]{:S(2)}, u32[]{:S(2)}) collective-permute-start(bf16[256,768]{1,0:T(8,128)(2,1)} %get-tuple-element.74), channel_id=1, source_target_pairs={{0,2},{1,3},{2,0},{3,1},{4,6},{5,7},{6,4},{7,5},{8,10},{9,11},{10,... | collective-permute-start | bytes 1179656 | tf_op jit(solution)/shard_map/ppermute | solution.py:432
  16.9 15.1 %collective-permute-start.3 = (s32[1,256]{1,0:T(1,128)S(1)}, s32[1,256]{1,0:T(1,128)S(1)}, u32[]{:S(2)}, u32[]{:S(2)}) collective-permute-start(s32[1,256]{1,0:T(1,128)S(1)} %get-tuple-element.92), channel_id=1, source_target_pairs={{0,1},{1,0},{2,3},{3,2},{4,5},{5,4},{6,7},{7,6},{8,9},{9,8},{10,11... | collective-permute-start | bytes 3080 | tf_op jit(solution)/shard_map/ppermute | solution.py:432
  17.4 17.3 %collective-permute-start.4 = (s32[1,256]{1,0:T(1,128)S(1)}, s32[1,256]{1,0:T(1,128)S(1)}, u32[]{:S(2)}, u32[]{:S(2)}) collective-permute-start(s32[1,256]{1,0:T(1,128)S(1)} %get-tuple-element.91), channel_id=1, source_target_pairs={{0,2},{1,3},{2,0},{3,1},{4,6},{5,7},{6,4},{7,5},{8,10},{9,11},{10,... | collective-permute-start | bytes 3080 | tf_op jit(solution)/shard_map/ppermute | solution.py:432
  17.5 17.3 %collective-permute-start.5 = (s32[1,256]{1,0:T(1,128)S(1)}, s32[1,256]{1,0:T(1,128)S(1)}, u32[]{:S(2)}, u32[]{:S(2)}) collective-permute-start(s32[1,256]{1,0:T(1,128)S(1)} %get-tuple-element.90), channel_id=1, source_target_pairs={{0,3},{1,2},{2,1},{3,0},{4,7},{5,6},{6,5},{7,4},{8,11},{9,10},{10,... | collective-permute-start | bytes 3080 | tf_op jit(solution)/shard_map/ppermute | solution.py:432
  32.0 12.5 %collective-permute-start.2 = (bf16[256,768]{1,0:T(8,128)(2,1)}, bf16[256,768]{1,0:T(8,128)(2,1)}, u32[]{:S(2)}, u32[]{:S(2)}) collective-permute-start(bf16[256,768]{1,0:T(8,128)(2,1)} %get-tuple-element.71), channel_id=1, source_target_pairs={{0,3},{1,2},{2,1},{3,0},{4,7},{5,6},{6,5},{7,4},{8,11},{9,10},{10,... | collective-permute-start | bytes 1179656 | tf_op jit(solution)/shard_map/ppermute | solution.py:432
  34.8 11.6 %copy-start.24 = (bf16[4,256,384]{2,1,0:T(8,128)(2,1)S(1)}, bf16[4,256,384]{2,1,0:T(8,128)(2,1)}, u32[]{:S(2)}) copy-start(bf16[4,256,384]{2,1,0:T(8,128)(2,1)} %param.19) | copy-start | bytes 2359300
  46.5 33.2 %collective-permute-start.6 = (bf16[256,384]{1,0:T(8,128)(2,1)S(1)}, bf16[256,384]{1,0:T(8,128)(2,1)S(1)}, u32[]{:S(2)}, u32[]{:S(2)}) collective-permute-start(bf16[256,384]{1,0:T(8,128)(2,1)S(1)} %get-tuple-element.81), channel_id=1, source_target_pairs={{0,1},{1,0},{2,3},{3,2},{4,5},{5,4},{6,7},{7,6},{8,9},{9,8},{10,11... | collective-permute-start | bytes 589832 | tf_op jit(solution)/shard_map/ppermute | solution.py:432
  54.6 25.1 %collective-permute-start.7 = (bf16[256,384]{1,0:T(8,128)(2,1)S(1)}, bf16[256,384]{1,0:T(8,128)(2,1)S(1)}, u32[]{:S(2)}, u32[]{:S(2)}) collective-permute-start(bf16[256,384]{1,0:T(8,128)(2,1)S(1)} %get-tuple-element.80), channel_id=1, source_target_pairs={{0,2},{1,3},{2,0},{3,1},{4,6},{5,7},{6,4},{7,5},{8,10},{9,11},{10,... | collective-permute-start | bytes 589832 | tf_op jit(solution)/shard_map/ppermute | solution.py:432
  55.7 24.1 %collective-permute-start.8 = (bf16[256,384]{1,0:T(8,128)(2,1)S(1)}, bf16[256,384]{1,0:T(8,128)(2,1)S(1)}, u32[]{:S(2)}, u32[]{:S(2)}) collective-permute-start(bf16[256,384]{1,0:T(8,128)(2,1)S(1)} %get-tuple-element.79), channel_id=1, source_target_pairs={{0,3},{1,2},{2,1},{3,0},{4,7},{5,6},{6,5},{7,4},{8,11},{9,10},{10,... | collective-permute-start | bytes 589832 | tf_op jit(solution)/shard_map/ppermute | solution.py:432
  60.8 7.1 %copy-start.27 = (f32[1024]{0:T(1024)}, f32[1024]{0:T(1024)S(1)}, u32[]{:S(2)}) copy-start(f32[1024]{0:T(1024)S(1)} %fusion.16) | copy-start | bytes 12292
  79.6 2.7 copy-start.1
  79.6 2.7 copy-start.11
  79.6 2.5 copy-start.23
  79.9 18.5 %copy-start.7 = (bf16[4,256,384]{2,1,0:T(8,128)(2,1)}, bf16[4,256,384]{2,1,0:T(8,128)(2,1)S(1)}, u32[]{:S(2)}) copy-start(bf16[4,256,384]{2,1,0:T(8,128)(2,1)S(1)} %bitcast_dynamic-update-slice_fusion.15) | copy-start | bytes 2359300
  82.3 29.3 %collective-permute-start.12 = (bf16[256,768]{1,0:T(8,128)(2,1)S(1)}, bf16[256,768]{1,0:T(8,128)(2,1)S(1)}, u32[]{:S(2)}, u32[]{:S(2)}) collective-permute-start(bf16[256,768]{1,0:T(8,128)(2,1)S(1)} %get-tuple-element.65), channel_id=1, source_target_pairs={{0,1},{1,0},{2,3},{3,2},{4,5},{5,4},{6,7},{7,6},{8,9},{9,8},{10,11... | collective-permute-start | bytes 1179656 | tf_op jit(solution)/shard_map/ppermute | solution.py:432
  83.3 29.8 %collective-permute-start.13 = (bf16[256,768]{1,0:T(8,128)(2,1)S(1)}, bf16[256,768]{1,0:T(8,128)(2,1)S(1)}, u32[]{:S(2)}, u32[]{:S(2)}) collective-permute-start(bf16[256,768]{1,0:T(8,128)(2,1)S(1)} %get-tuple-element.64), channel_id=1, source_target_pairs={{0,2},{1,3},{2,0},{3,1},{4,6},{5,7},{6,4},{7,5},{8,10},{9,11},{10,... | collective-permute-start | bytes 1179656 | tf_op jit(solution)/shard_map/ppermute | solution.py:432
  85.3 13.3 %copy-start.43 = (bf16[768,768]{1,0:T(8,128)(2,1)S(1)}, bf16[768,768]{1,0:T(8,128)(2,1)}, u32[]{:S(2)}) copy-start(bf16[768,768]{1,0:T(8,128)(2,1)} %param.27) | copy-start | bytes 3538948
  85.3 27.9 %collective-permute-start.14 = (bf16[256,768]{1,0:T(8,128)(2,1)S(1)}, bf16[256,768]{1,0:T(8,128)(2,1)S(1)}, u32[]{:S(2)}, u32[]{:S(2)}) collective-permute-start(bf16[256,768]{1,0:T(8,128)(2,1)S(1)} %get-tuple-element.63), channel_id=1, source_target_pairs={{0,3},{1,2},{2,1},{3,0},{4,7},{5,6},{6,5},{7,4},{8,11},{9,10},{10,... | collective-permute-start | bytes 1179656 | tf_op jit(solution)/shard_map/ppermute | solution.py:432
  98.4 4.1 copy-start.5
  98.4 4.1 copy-start.12
  98.4 4.6 slice-start
  98.6 4.4 slice-start.1
  102.5 36.9 %copy-start.17 = (f32[1024,768]{1,0:T(8,128)}, f32[1024,768]{1,0:T(8,128)S(1)}, u32[]{:S(2)}) copy-start(f32[1024,768]{1,0:T(8,128)S(1)} %get-tuple-element.95) | copy-start | bytes 9437188
  113.2 27.6 %copy-start.15 = (bf16[4,256,768]{2,1,0:T(8,128)(2,1)}, bf16[4,256,768]{2,1,0:T(8,128)(2,1)S(1)}, u32[]{:S(2)}) copy-start(bf16[4,256,768]{2,1,0:T(8,128)(2,1)S(1)} %bitcast_dynamic-update-slice_fusion.3) | copy-start | bytes 4718596
  140.8 2.2 copy-start.44
  148.0 118.0 %reduce-scatter.5.cloned.1.call-start = ((), (), s32[]{:S(2)}) async-start(), calls=%async_computation.4 | async-start | bytes 3317760 | tf_op jit(solution)/shard_map/reduce_scatter | solution.py:545
  151.8 14.1 %copy-start.2 = (bf16[1024,384]{1,0:T(8,128)(2,1)S(1)}, bf16[1024,384]{1,0:T(8,128)(2,1)}, u32[]{:S(2)}) copy-start(bf16[1024,384]{1,0:T(8,128)(2,1)} %copy-done.1) | copy-start | bytes 2359300
  151.8 14.1 %copy-start.10 = (bf16[1024,768]{1,0:T(8,128)(2,1)S(1)}, bf16[1024,768]{1,0:T(8,128)(2,1)}, u32[]{:S(2)}) copy-start(bf16[1024,768]{1,0:T(8,128)(2,1)} %convolution_convert_fusion.3.do_ref) | copy-start | bytes 4718596
  165.9 13.9 %copy-start.3 = (bf16[1024,384]{1,0:T(8,128)(2,1)}, bf16[1024,384]{1,0:T(8,128)(2,1)S(1)}, u32[]{:S(2)}) copy-start(bf16[1024,384]{1,0:T(8,128)(2,1)S(1)} %get-tuple-element.43) | copy-start | bytes 2359300
  189.3 107.9 %reduce-scatter.9.cloned.1.call-start = ((), (), s32[]{:S(2)}) async-start(), calls=%async_computation.6 | async-start | bytes 5308416 | tf_op jit(solution)/shard_map/reduce_scatter | solution.py:545
  200.3 154.2 %reduce-scatter.11.cloned.1.call-start = ((), (), s32[]{:S(2)}) async-start(), calls=%async_computation.7 | async-start | bytes 5308416 | tf_op jit(solution)/shard_map/reduce_scatter | solution.py:545
  214.1 262.6 %all-reduce.3.cloned.1.call-start = ((), (), s32[]{:S(2)}) async-start(), calls=%async_computation.8 | async-start | bytes 3391488 | tf_op jit(solution)/shard_map/psum | solution.py:548
  227.3 10.0 %copy-start.4 = (bf16[1024,384]{1,0:T(8,128)(2,1)S(1)}, bf16[1024,384]{1,0:T(8,128)(2,1)}, u32[]{:S(2)}) copy-start(bf16[1024,384]{1,0:T(8,128)(2,1)} %copy-done.3) | copy-start | bytes 2359300
  228.6 11.4 %copy-start.21 = (bf16[1024,1920]{1,0:T(8,128)(2,1)S(1)}, bf16[1024,1920]{1,0:T(8,128)(2,1)}, u32[]{:S(2)}) copy-start(bf16[1024,1920]{1,0:T(8,128)(2,1)} %copy-done.20) | copy-start | bytes 11796484
  229.4 25.6 %collective-permute-start.9 = (bf16[256,768]{1,0:T(8,128)(2,1)S(1)}, bf16[256,768]{1,0:T(8,128)(2,1)S(1)}, u32[]{:S(2)}, u32[]{:S(2)}) collective-permute-start(bf16[256,768]{1,0:T(8,128)(2,1)S(1)} %get-tuple-element.69), channel_id=1, source_target_pairs={{0,1},{1,0},{2,3},{3,2},{4,5},{5,4},{6,7},{7,6},{8,9},{9,8},{10,11... | collective-permute-start | bytes 1179656 | tf_op jit(solution)/shard_map/ppermute | solution.py:432
  234.7 29.9 %collective-permute-start.10 = (bf16[256,768]{1,0:T(8,128)(2,1)S(1)}, bf16[256,768]{1,0:T(8,128)(2,1)S(1)}, u32[]{:S(2)}, u32[]{:S(2)}) collective-permute-start(bf16[256,768]{1,0:T(8,128)(2,1)S(1)} %get-tuple-element.68), channel_id=1, source_target_pairs={{0,2},{1,3},{2,0},{3,1},{4,6},{5,7},{6,4},{7,5},{8,10},{9,11},{10,... | collective-permute-start | bytes 1179656 | tf_op jit(solution)/shard_map/ppermute | solution.py:432
  235.8 29.5 %collective-permute-start.11 = (bf16[256,768]{1,0:T(8,128)(2,1)S(1)}, bf16[256,768]{1,0:T(8,128)(2,1)S(1)}, u32[]{:S(2)}, u32[]{:S(2)}) collective-permute-start(bf16[256,768]{1,0:T(8,128)(2,1)S(1)} %get-tuple-element.67), channel_id=1, source_target_pairs={{0,3},{1,2},{2,1},{3,0},{4,7},{5,6},{6,5},{7,4},{8,11},{9,10},{10,... | collective-permute-start | bytes 1179656 | tf_op jit(solution)/shard_map/ppermute | solution.py:432
  239.0 6.1 %copy-start.28 = (f32[1024]{0:T(1024)S(1)}, f32[1024]{0:T(1024)}, u32[]{:S(2)}) copy-start(f32[1024]{0:T(1024)} %copy-done.27) | copy-start | bytes 12292
  239.0 168.5 %collective-permute-start.18 = (bf16[256,384]{1,0:T(8,128)(2,1)}, bf16[256,384]{1,0:T(8,128)(2,1)}, u32[]{:S(2)}, u32[]{:S(2)}) collective-permute-start(bf16[256,384]{1,0:T(8,128)(2,1)} %get-tuple-element.77), channel_id=1, source_target_pairs={{0,1},{1,0},{2,3},{3,2},{4,5},{5,4},{6,7},{7,6},{8,9},{9,8},{10,11... | collective-permute-start | bytes 589832 | tf_op jit(solution)/shard_map/ppermute | solution.py:432
  245.1 3.0 copy-start.14
  245.1 3.0 copy-start.16
  251.0 3.4 copy-start.29
  253.3 195.3 %collective-permute-start.15 = (bf16[256,768]{1,0:T(8,128)(2,1)}, bf16[256,768]{1,0:T(8,128)(2,1)S(1)}, u32[]{:S(2)}, u32[]{:S(2)}) collective-permute-start(bf16[256,768]{1,0:T(8,128)(2,1)} %get-tuple-element.61), channel_id=1, source_target_pairs={{0,1},{1,0},{2,3},{3,2},{4,5},{5,4},{6,7},{7,6},{8,9},{9,8},{10,11... | collective-permute-start | bytes 1179656 | tf_op jit(solution)/shard_map/ppermute | solution.py:432
  256.2 9.1 %copy-start.30 = (f32[8832]{0:T(1024)}, f32[8832]{0:T(1024)S(1)}, u32[]{:S(2)}) copy-start(f32[8832]{0:T(1024)S(1)} %constant_dynamic-update-slice_fusion.11) | copy-start | bytes 105988
  399.2 49.4 %copy-start.19 = (bf16[4,256,768]{2,1,0:T(8,128)(2,1)S(1)}, bf16[4,256,768]{2,1,0:T(8,128)(2,1)}, u32[]{:S(2)}) copy-start(bf16[4,256,768]{2,1,0:T(8,128)(2,1)} %copy-done.18) | copy-start | bytes 4718596
  401.9 42.9 %collective-permute-start.19 = (bf16[256,384]{1,0:T(8,128)(2,1)}, bf16[256,384]{1,0:T(8,128)(2,1)S(1)}, u32[]{:S(2)}, u32[]{:S(2)}) collective-permute-start(bf16[256,384]{1,0:T(8,128)(2,1)} %get-tuple-element.76), channel_id=1, source_target_pairs={{0,2},{1,3},{2,0},{3,1},{4,6},{5,7},{6,4},{7,5},{8,10},{9,11},{10,... | collective-permute-start | bytes 589832 | tf_op jit(solution)/shard_map/ppermute | solution.py:432
  404.5 41.1 %collective-permute-start.20 = (bf16[256,384]{1,0:T(8,128)(2,1)S(1)}, bf16[256,384]{1,0:T(8,128)(2,1)S(1)}, u32[]{:S(2)}, u32[]{:S(2)}) collective-permute-start(bf16[256,384]{1,0:T(8,128)(2,1)S(1)} %get-tuple-element.75), channel_id=1, source_target_pairs={{0,3},{1,2},{2,1},{3,0},{4,7},{5,6},{6,5},{7,4},{8,11},{9,10},{10,... | collective-permute-start | bytes 589832 | tf_op jit(solution)/shard_map/ppermute | solution.py:432
  406.1 68.5 %collective-permute-start.16 = (bf16[256,768]{1,0:T(8,128)(2,1)}, bf16[256,768]{1,0:T(8,128)(2,1)S(1)}, u32[]{:S(2)}, u32[]{:S(2)}) collective-permute-start(bf16[256,768]{1,0:T(8,128)(2,1)} %get-tuple-element.60), channel_id=1, source_target_pairs={{0,2},{1,3},{2,0},{3,1},{4,6},{5,7},{6,4},{7,5},{8,10},{9,11},{10,... | collective-permute-start | bytes 1179656 | tf_op jit(solution)/shard_map/ppermute | solution.py:432
  407.6 67.1 %collective-permute-start.17 = (bf16[256,768]{1,0:T(8,128)(2,1)}, bf16[256,768]{1,0:T(8,128)(2,1)S(1)}, u32[]{:S(2)}, u32[]{:S(2)}) collective-permute-start(bf16[256,768]{1,0:T(8,128)(2,1)} %get-tuple-element.59), channel_id=1, source_target_pairs={{0,3},{1,2},{2,1},{3,0},{4,7},{5,6},{6,5},{7,4},{8,11},{9,10},{10,... | collective-permute-start | bytes 1179656 | tf_op jit(solution)/shard_map/ppermute | solution.py:432
  476.7 4.4 copy-start.25
  476.7 5.3 %copy-start.26 = (bf16[96,768]{1,0:T(8,128)(2,1)S(1)}, bf16[96,768]{1,0:T(8,128)(2,1)}, u32[]{:S(2)}) copy-start(bf16[96,768]{1,0:T(8,128)(2,1)} %get-tuple-element.52) | copy-start | bytes 442372
  (9 other events, 11.9 us)
Sparse Core Ops, SparseCore 0:
  148.2 41.4 reduce-scatter.6
  193.5 45.9 reduce-scatter.4
  243.3 53.8 reduce-scatter.8
  300.5 53.8 reduce-scatter.10
  357.1 114.4 all-reduce.2

commit v2 on v0

--- a/solution.py
+++ b/solution.py
@@ -1,9 +1,559 @@
+import functools
+
 import jax
 import jax.numpy as jnp
 from jax import lax
+from jax.experimental import pallas as pl
+from jax.experimental.pallas import tpu as pltpu
 from jax.sharding import PartitionSpec as P
 
 HDIM = 64
+PAIR = 2 * HDIM
+BLK = 256
+LN2 = 0.6931471805599453
+LOG2E = 1.4426950408889634
+Q_SCALE = LOG2E * HDIM**-0.5
+BF16 = jnp.bfloat16
+F32 = jnp.float32
+VMEM_BYTES = 56 << 20
+
+
+def dot(left, right, left_dim, right_dim):
+    return lax.dot_general(
+        left, right, (((left_dim,), (right_dim,)), ((), ())), preferred_element_type=F32
+    )
+
+
+def nn(left, right):
+    return dot(left, right, 1, 0)
+
+
+def nt(left, right):
+    return dot(left, right, 1, 1)
+
+
+def tn(left, right):
+    return dot(left, right, 0, 0)
+
+
+def call(kernel, name, grid, in_specs, out_specs, out_shape, scratch=(), flops=0, moved=0, aliases=None):
+    return pl.pallas_call(
+        kernel,
+        name=name,
+        grid_spec=pltpu.PrefetchScalarGridSpec(
+            num_scalar_prefetch=1,
+            grid=grid,
+            in_specs=in_specs,
+            out_specs=out_specs,
+            scratch_shapes=list(scratch),
+        ),
+        out_shape=out_shape,
+        input_output_aliases=aliases or {},
+        cost_estimate=pl.CostEstimate(flops=flops, bytes_accessed=moved, transcendentals=0),
+        compiler_params=pltpu.CompilerParams(vmem_limit_bytes=VMEM_BYTES),
+    )
+
+
+def shape(dims, dtype=BF16):
+    return jax.ShapeDtypeStruct(dims, dtype)
+
+
+def whole(dims):
+    return pl.BlockSpec(dims, lambda *_: (0,) * len(dims))
+
+
+def standardize(values):
+    center = values - jnp.mean(values, axis=1, keepdims=True)
+    rate = lax.rsqrt(jnp.mean(center * center, axis=1, keepdims=True) + EPSILON)
+    return center * rate, rate
+
+
+def standardize_back(grad, unit, rate):
+    mean_grad = jnp.mean(grad, axis=1, keepdims=True)
+    mean_dot = jnp.mean(grad * unit, axis=1, keepdims=True)
+    return rate * (grad - mean_grad - unit * mean_dot)
+
+
+def column_sums(values):
+    return jnp.sum(values, axis=0, keepdims=True)
+
+
+def block_rows(place, d, size):
+    return pl.ds(pl.multiple_of((place ^ d) * size, size), size)
+
+
+def project_kernel(at_ref, x_ref, gain_ref, shift_ref, w_ref, bias_ref, scale_ref, *refs):
+    row_ref, normed_ref, proj_ref = refs[-3:]
+    unit, _ = standardize(x_ref[...].astype(F32))
+    normed = (unit * gain_ref[...] + shift_ref[...]).astype(BF16)
+    row_ref[...] = x_ref[...]
+    normed_ref[...] = normed
+    proj_ref[...] = ((nn(normed, w_ref[...]) + bias_ref[...]) * scale_ref[...]).astype(BF16)
+
+
+def project(at, piece, gain, shift, w, bias, scale, length, so_far):
+    part, width = piece.shape
+    cols = w.shape[1]
+    block = lambda n: pl.BlockSpec((part, n), lambda i, at: (at[0], 0))
+    held = [pl.BlockSpec(memory_space=pl.ANY)] * len(so_far)
+    return call(
+        project_kernel,
+        "project",
+        (1,),
+        [whole((part, width)), whole((1, width)), whole((1, width)), whole((width, cols)), whole((1, cols)), whole((1, cols))]
+        + held,
+        [block(width), block(width), block(cols)],
+        [shape((length, width)), shape((length, width)), shape((length, cols))],
+        flops=2 * part * width * cols,
+        moved=2 * (part * (3 * width + cols) + width * cols),
+        aliases={7 + n: n for n in range(len(so_far))},
+    )(at, piece, gain, shift, w, bias, scale, *so_far)
+
+
+def fill_bias(code_ref, bias_ref):
+    length = code_ref.shape[1]
+    code = code_ref[...]
+    column = jnp.transpose(jnp.broadcast_to(code, (128, length)))
+    for i in range(length // BLK):
+        q_doc = column[i * BLK : (i + 1) * BLK, :1] >> 1
+        for j in range(i + 1):
+            k_code = code[:, j * BLK : (j + 1) * BLK]
+            same = q_doc == (k_code >> 1)
+            real = (k_code & 1) == 1
+            if i == j:
+                row_at = lax.broadcasted_iota(jnp.int32, (BLK, BLK), 0)
+                col_at = lax.broadcasted_iota(jnp.int32, (BLK, BLK), 1)
+                allowed = same & (col_at <= row_at) & (real | (col_at == row_at))
+            else:
+                allowed = same & real
+            bias_ref[i * BLK : (i + 1) * BLK, j * BLK : (j + 1) * BLK] = jnp.where(allowed, 0.0, MASKED)
+
+
+def halves(pair, other):
+    first = lax.broadcasted_iota(jnp.int32, pair.shape, 1) < HDIM
+    return jnp.where(first, pair, other), jnp.where(first, other, pair)
+
+
+def gather_values(me_ref, v_refs, value_ref):
+    if len(v_refs) == 1:
+        return v_refs[0][...]
+    for d, ref in enumerate(v_refs):
+        value_ref[block_rows(me_ref[0], d, ref.shape[0]), :] = ref[...]
+    return value_ref[...]
+
+
+def forward_kernel(count, me_ref, code_ref, q_ref, k_ref, *refs):
+    v_refs, (o_ref, lse_ref, bias_ref, value_ref) = refs[:count], refs[count:]
+
+    @pl.when(pl.program_id(0) == 0)
+    def _():
+        fill_bias(code_ref, bias_ref)
+
+    length = q_ref.shape[0]
+    v_pair = gather_values(me_ref, v_refs, value_ref)
+    k_pair = k_ref[...]
+    keys = halves(k_pair, jnp.zeros_like(k_pair))
+    vals = halves(v_pair, jnp.ones_like(v_pair))
+    first = lax.broadcasted_iota(jnp.int32, (BLK, PAIR), 1) < HDIM
+    for i in range(length // BLK):
+        end = (i + 1) * BLK
+        rows = slice(i * BLK, end)
+        q = q_ref[rows, :]
+        outs, lses = [], []
+        for h in range(2):
+            scores = nt(q, keys[h][:end]) + bias_ref[rows, :end]
+            top = jnp.max(scores, axis=1, keepdims=True)
+            weights = jnp.exp2(scores - top).astype(BF16)
+            mixed = nn(weights, vals[h][:end])
+            total = pltpu.roll(mixed, HDIM, 1)
+            outs.append(mixed / total)
+            lses.append(top + jnp.log2(total))
+        o_ref[rows, :] = jnp.where(first, outs[0], outs[1]).astype(BF16)
+        lse_ref[rows, :] = jnp.where(first, lses[0], lses[1])
+
+
+def backward_kernel(count, me_ref, code_ref, q_ref, k_ref, *refs):
+    v_refs = refs[:count]
+    o_ref, do_ref, lse_ref = refs[count : count + 3]
+    outs = refs[count + 3 :]
+    d_ref = outs[0]
+    piece_refs = outs[1 : len(outs) - 4]
+    bias_ref, value_ref, dkt_ref, dvt_ref = outs[-4:]
+
+    @pl.when(pl.program_id(0) == 0)
+    def _():
+        fill_bias(code_ref, bias_ref)
+
+    length = q_ref.shape[0]
+    v_pair = gather_values(me_ref, v_refs, value_ref)
+    k_pair = k_ref[...]
+    zero = jnp.zeros_like(k_pair)
+    keys = halves(k_pair, zero)
+    vals = halves(v_pair, zero)
+    first = lax.broadcasted_iota(jnp.int32, (BLK, PAIR), 1) < HDIM
+    blocks = length // BLK
+    for i in reversed(range(blocks)):
+        end = (i + 1) * BLK
+        rows = slice(i * BLK, end)
+        q, do = q_ref[rows, :], do_ref[rows, :]
+        q_t, do_t = jnp.transpose(q), jnp.transpose(do)
+        prod = do.astype(F32) * o_ref[rows, :].astype(F32)
+        dq = None
+        for h in range(2):
+            head = slice(h * HDIM, (h + 1) * HDIM)
+            lse = lse_ref[rows, h * HDIM : h * HDIM + 1]
+            mine = first if h == 0 else ~first
+            delta = jnp.sum(jnp.where(mine, prod, 0.0), axis=1, keepdims=True)
+            probs = jnp.exp2(nt(q, keys[h][:end]) + bias_ref[rows, :end] - lse)
+            d_scores = (probs * (nt(do, vals[h][:end]) - delta)).astype(BF16)
+            part = nn(d_scores, keys[h][:end])
+            dq = part if dq is None else dq + part
+            dv = nn(do_t[head], probs.astype(BF16))
+            dk = nn(q_t[head], d_scores)
+            if i == blocks - 1:
+                dvt_ref[head, :] = dv
+                dkt_ref[head, :] = dk
+            else:
+                dvt_ref[head, :end] += dv
+                dkt_ref[head, :end] += dk
+        d_ref[0, rows, :] = (dq * HDIM**-0.5).astype(BF16)
+    d_ref[1] = jnp.transpose(dkt_ref[...] * LN2).astype(BF16)
+    dv = jnp.transpose(dvt_ref[...]).astype(BF16)
+    if piece_refs:
+        value_ref[...] = dv
+        for d, ref in enumerate(piece_refs):
+            ref[...] = value_ref[block_rows(me_ref[0], d, ref.shape[0]), :]
+    else:
+        d_ref[2] = dv
+
+
+def pair_specs(length, offset):
+    return pl.BlockSpec((length, PAIR), lambda p, me: (0, p + offset))
+
+
+def value_specs(values, length, offset):
+    if len(values) == 1:
+        return [pair_specs(length, offset)]
+    return [pl.BlockSpec((v.shape[0], PAIR), lambda p, me: (0, p)) for v in values]
+
+
+def attend(me, code, proj, values, q_at, k_at, v_at, pairs, name):
+    length = proj.shape[0]
+    return call(
+        functools.partial(forward_kernel, len(values)),
+        name,
+        (pairs,),
+        [whole((1, length)), pair_specs(length, q_at), pair_specs(length, k_at)]
+        + value_specs(values, length, v_at),
+        [pair_specs(length, 0)] * 2,
+        [shape((length, pairs * PAIR)), shape((length, pairs * PAIR), F32)],
+        [pltpu.VMEM((length, length), F32), pltpu.VMEM((length, PAIR), BF16)],
+        flops=pairs * 24 * length * length * PAIR,
+        moved=pairs * length * PAIR * 12,
+    )(me, code, proj, proj, *values)
+
+
+def attend_back(me, code, proj, values, o, do, lse, q_at, k_at, v_at, do_at, pairs, name):
+    length = proj.shape[0]
+    split = len(values) > 1
+    part = length // 4
+    outs = [pl.BlockSpec((2 if split else 3, length, PAIR), lambda p, me: (0, 0, p))]
+    shapes = [shape((2 if split else 3, length, pairs * PAIR))]
+    if split:
+        outs += [pl.BlockSpec((v.shape[0], PAIR), lambda p, me: (0, p)) for v in values]
+        shapes += [shape((v.shape[0], pairs * PAIR)) for v in values]
+    return call(
+        functools.partial(backward_kernel, len(values)),
+        name,
+        (pairs,),
+        [whole((1, length)), pair_specs(length, q_at), pair_specs(length, k_at)]
+        + value_specs(values, length, v_at)
+        + [pair_specs(length, 0), pair_specs(length, do_at), pair_specs(length, 0)],
+        outs,
+        shapes,
+        [
+            pltpu.VMEM((length, length), F32),
+            pltpu.VMEM((length, PAIR), BF16),
+            pltpu.VMEM((PAIR, length), F32),
+            pltpu.VMEM((PAIR, length), F32),
+        ],
+        flops=pairs * 30 * length * length * PAIR,
+        moved=pairs * length * PAIR * 18,
+    )(me, code, proj, proj, *values, o, do, lse)
+
+
+def mlp_kernel(
+    me_ref, x_ref, oa_ref, ob_ref, wo_ref, ob_bias_ref, gain_ref, shift_ref, wu_ref, ub_ref, wd_ref, db_ref,
+    middle_ref, normed_ref, act_ref, slope_ref, y0_ref, y1_ref, y2_ref, y3_ref, acc_ref,
+):
+    @pl.when(pl.program_id(0) == 0)
+    def _():
+        half = oa_ref.shape[1]
+        middle = (
+            x_ref[...].astype(F32)
+            + nn(oa_ref[...], wo_ref[:half, :])
+            + nn(ob_ref[...], wo_ref[half:, :])
+            + ob_bias_ref[...]
+        )
+        middle_ref[...] = middle
+        unit, _ = standardize(middle)
+        normed_ref[...] = (unit * gain_ref[...] + shift_ref[...]).astype(BF16)
+        acc_ref[...] = middle + db_ref[...]
+
+    pre = nn(normed_ref[...], wu_ref[...]) + ub_ref[...]
+    square = pre * pre
+    curve = jnp.tanh(pre * (GELU_A + (GELU_A * GELU_B) * square))
+    half_up = 0.5 + 0.5 * curve
+    act = (pre * half_up).astype(BF16)
+    act_ref[...] = act
+    slope = half_up + 0.5 * pre * (1.0 - curve * curve) * (GELU_A + (3.0 * GELU_A * GELU_B) * square)
+    slope_ref[...] = slope.astype(BF16)
+    acc_ref[...] += nn(act, wd_ref[...])
+
+    @pl.when(pl.program_id(0) == pl.num_programs(0) - 1)
+    def _():
+        for d, ref in enumerate((y0_ref, y1_ref, y2_ref, y3_ref)):
+            ref[...] = acc_ref[block_rows(me_ref[0], d, ref.shape[0]), :].astype(BF16)
+
+
+GELU_A = 0.7978845608028654
+GELU_B = 0.044715
+
+
+def mlp(me, x, o_a, o_b, w_out, out_bias, gain, shift, w_up, up_bias, w_down, down_bias, chunk):
+    length, width = x.shape
+    ff = w_up.shape[1]
+    part = length // 4
+    vec = whole((1, width))
+    cols = pl.BlockSpec((length, chunk), lambda c, me: (0, c))
+    return call(
+        mlp_kernel,
+        "mlp",
+        (ff // chunk,),
+        [
+            whole((length, width)), whole(o_a.shape), whole(o_b.shape), whole((width, width)), vec, vec, vec,
+            pl.BlockSpec((width, chunk), lambda c, me: (0, c)),
+            pl.BlockSpec((1, chunk), lambda c, me: (0, c)),
+            pl.BlockSpec((chunk, width), lambda c, me: (c, 0)),
+            vec,
+        ],
+        [whole((length, width))] * 2 + [cols, cols] + [whole((part, width))] * 4,
+        [shape((length, width), F32), shape((length, width)), shape((length, ff)), shape((length, ff))]
+        + [shape((part, width))] * 4,
+        [pltpu.VMEM((length, width), F32)],
+        flops=2 * length * width * (width + 2 * ff),
+        moved=length * (width * 12 + ff * 4) + 4 * width * ff,
+    )(me, x, o_a, o_b, w_out, out_bias, gain, shift, w_up, up_bias, w_down, down_bias)
+
+
+def step_chunk(step, core):
+    return 2 * (step % 4) + jnp.where(step < 4, 1 - core, core)
+
+
+def down_kernel(at_ref, d0_ref, d1_ref, d2_ref, d3_ref, act_ref, dy_ref, bias_ref, send_ref, keep_ref):
+    @pl.when(pl.program_id(0) == 0)
+    def _():
+        for d, ref in enumerate((d0_ref, d1_ref, d2_ref, d3_ref)):
+            dy_ref[block_rows(at_ref[0], d, ref.shape[0]), :] = ref[...]
+        bias_ref[...] = column_sums(dy_ref[...].astype(F32))
+
+    grad = tn(act_ref[...], dy_ref[...]).astype(BF16)
+
+    @pl.when(pl.program_id(0) < 4)
+    def _():
+        send_ref[0] = grad
+
+    @pl.when(pl.program_id(0) >= 4)
+    def _():
+        keep_ref[0] = grad
+
+
+def down_grad(at, pieces, act):
+    part, width = pieces[0].shape
+    length, ff = act.shape
+    chunk = ff // 8
+    return call(
+        down_kernel,
+        "down_grad",
+        (8,),
+        [whole((part, width))] * 4
+        + [pl.BlockSpec((length, chunk), lambda s, at: (0, step_chunk(s, at[1])))],
+        [
+            whole((length, width)),
+            whole((1, width)),
+            pl.BlockSpec((1, chunk, width), lambda s, at: (jnp.minimum(s, 3), 0, 0)),
+            pl.BlockSpec((1, chunk, width), lambda s, at: (jnp.maximum(s - 4, 0), 0, 0)),
+        ],
+        [shape((length, width)), shape((1, width), F32), shape((4, chunk, width)), shape((4, chunk, width))],
+        flops=2 * length * width * ff,
+        moved=2 * (length * ff + 2 * length * width + width * ff),
+    )(at, *pieces, act)
+
+
+def split_store(grad, core, stage_ref, send_ref, keep_ref, lead):
+    stage_ref[...] = grad.astype(BF16).reshape(stage_ref.shape)
+    for j in range(4):
+        send_ref[(j,) + lead] = stage_ref[j, 1 - core]
+        keep_ref[(j,) + lead] = stage_ref[j, core]
+
+
+def mlp_back_kernel(
+    at_ref, dy_ref, normed_ref, act_slope_ref, wd_ref, wu_ref, middle_ref, gain_ref, oa_ref, ob_ref, wo_ref,
+    up_bias_ref, send_ref, keep_ref, d_att_ref, d_o_ref, sums_ref, out_send_ref, out_keep_ref, acc_ref, stage_ref, out_stage_ref,
+):
+    step = pl.program_id(0)
+    core = at_ref[1]
+    d_pre = (nt(dy_ref[...], wd_ref[...]) * act_slope_ref[...].astype(F32)).astype(BF16)
+    up_bias_ref[...] = column_sums(d_pre.astype(F32))
+    split_store(tn(normed_ref[...], d_pre), core, stage_ref, send_ref, keep_ref, (0,))
+    d_normed = nt(d_pre, wu_ref[...])
+
+    @pl.when(step == 0)
+    def _():
+        acc_ref[...] = d_normed
+
+    @pl.when(step > 0)
+    def _():
+        acc_ref[...] += d_normed
+
+    @pl.when(step == pl.num_programs(0) - 1)
+    def _():
+        total = acc_ref[...]
+        unit, rate = standardize(middle_ref[...])
+        sums_ref[0:1, :] = column_sums(total * unit)
+        sums_ref[1:2, :] = column_sums(total)
+        d_middle = dy_ref[...].astype(F32) + standardize_back(total * gain_ref[...], unit, rate)
+        d_att = d_middle.astype(BF16)
+        d_att_ref[...] = d_att
+        sums_ref[2:3, :] = column_sums(d_att.astype(F32))
+        d_o_ref[...] = nt(d_att, wo_ref[...]).astype(BF16)
+        grad = jnp.concatenate([tn(oa_ref[...], d_att), tn(ob_ref[...], d_att)], axis=0)
+        split_store(grad, core, out_stage_ref, out_send_ref, out_keep_ref, ())
+
+
+def mlp_back(at, dy, normed, slope, w_down, w_up, middle, gain, o_a, o_b, w_out):
+    length, width = dy.shape
+    ff = slope.shape[1]
+    chunk = ff // 8
+    rows = width // 8
+    full = whole((length, width))
+    shards = pl.BlockSpec((4, 1, rows, chunk), lambda c, at: (0, c, 0, 0))
+    return call(
+        mlp_back_kernel,
+        "mlp_back",
+        (8,),
+        [
+            full, full,
+            pl.BlockSpec((length, chunk), lambda c, at: (0, c)),
+            pl.BlockSpec((chunk, width), lambda c, at: (c, 0)),
+            pl.BlockSpec((width, chunk), lambda c, at: (0, c)),
+            full, whole((1, width)), whole(o_a.shape), whole(o_b.shape), whole((width, width)),
+        ],
+        [
+            pl.BlockSpec((1, chunk), lambda c, at: (0, c)), shards, shards, full, full,
+            whole((8, width)), whole((4, rows, width)), whole((4, rows, width)),
+        ],
+        [
+            shape((1, ff), F32), shape((4, 8, rows, chunk)), shape((4, 8, rows, chunk)), shape((length, width)),
+            shape((length, width)), shape((8, width), F32), shape((4, rows, width)), shape((4, rows, width)),
+        ],
+        [
+            pltpu.VMEM((length, width), F32),
+            pltpu.VMEM((4, 2, rows, chunk), BF16),
+            pltpu.VMEM((4, 2, rows, width), BF16),
+        ],
+        flops=2 * length * width * (3 * ff + 2 * width),
+        moved=2 * length * (6 * width + ff) + 6 * width * ff,
+    )(at, dy, normed, slope, w_down, w_up, middle, gain, o_a, o_b, w_out)
+
+
+def qkv_grad_kernel(at_ref, normed_ref, d_ref, bias_ref, send_ref, keep_ref, stage_ref):
+    grad = d_ref[0]
+    bias_ref[0] = column_sums(grad.astype(F32))
+    split_store(tn(normed_ref[...], grad), at_ref[1], stage_ref, send_ref, keep_ref, (0,))
+
+
+def qkv_grad(at, normed, d_heads, name):
+    length, width = normed.shape
+    count, _, chunk = d_heads.shape
+    rows = width // 8
+    shards = pl.BlockSpec((4, 1, rows, chunk), lambda c, at: (0, c, 0, 0))
+    return call(
+        qkv_grad_kernel,
+        name,
+        (count,),
+        [whole((length, width)), pl.BlockSpec((1, length, chunk), lambda c, at: (c, 0, 0))],
+        [pl.BlockSpec((1, 1, chunk), lambda c, at: (c, 0, 0)), shards, shards],
+        [shape((count, 1, chunk), F32), shape((4, count, rows, chunk)), shape((4, count, rows, chunk))],
+        [pltpu.VMEM((4, 2, rows, chunk), BF16)],
+        flops=2 * count * length * width * chunk,
+        moved=2 * (length * width + count * chunk * (length + width)),
+    )(at, normed, d_heads)
+
+
+def token_grad_kernel(at_ref, da_ref, db_ref, w_ref, x_ref, gain_ref, d_att_ref, sums_ref, y0_ref, y1_ref, y2_ref, y3_ref, acc_ref):
+    step = pl.program_id(0)
+
+    @pl.when(step == 0)
+    def _():
+        acc_ref[...] = nt(da_ref[0], w_ref[...])
+
+    for s in range(1, 5):
+        d_ref = da_ref if s % 2 == 0 else db_ref
+
+        @pl.when(step == s)
+        def _():
+            acc_ref[...] += nt(d_ref[s // 2], w_ref[...])
+
+    @pl.when(step == 4)
+    def _():
+        total = acc_ref[...]
+        unit, rate = standardize(x_ref[...].astype(F32))
+        sums_ref[0:1, :] = column_sums(total * unit)
+        sums_ref[1:2, :] = column_sums(total)
+        acc_ref[...] = d_att_ref[...].astype(F32) + standardize_back(total * gain_ref[...], unit, rate)
+        for d, ref in enumerate((y0_ref, y1_ref, y2_ref, y3_ref)):
+            ref[...] = acc_ref[block_rows(at_ref[0], d, ref.shape[0]), :].astype(BF16)
+
+
+def token_grad(at, d_a, d_b, w_qkv, x, gain, d_att):
+    length, width = x.shape
+    chunk = d_a.shape[2]
+    part = length // 4
+    full = whole((length, width))
+    return call(
+        token_grad_kernel,
+        "token_grad",
+        (5,),
+        [whole(d_a.shape), whole(d_b.shape), pl.BlockSpec((width, chunk), lambda c, at: (0, c)), full, whole((1, width)), full],
+        [whole((8, width))] + [whole((part, width))] * 4,
+        [shape((8, width), F32)] + [shape((part, width))] * 4,
+        [pltpu.VMEM((length, width), F32)],
+        flops=10 * length * width * chunk,
+        moved=2 * length * (5 * chunk + 3 * width) + 10 * width * chunk,
+    )(at, d_a, d_b, w_qkv, x, gain, d_att)
+
+
+def settle_kernel(at_ref, *refs):
+    out_ref = refs[-1]
+    for d, ref in enumerate(refs[:-1]):
+        out_ref[at_ref[0] ^ d] = ref[...].astype(out_ref.dtype)
+
+
+def settle(at, pieces, dtype, name):
+    part, width = pieces[0].shape
+    rows = part // 4
+    return call(
+        settle_kernel,
+        name,
+        (4,),
+        [pl.BlockSpec((rows, width), lambda i, at: (i, 0))] * 4,
+        pl.BlockSpec((4, rows, width), lambda i, at: (0, i, 0)),
+        shape((4, part, width), dtype),
+        moved=4 * part * width * 6,
+    )(at, *pieces)
+
+
 QBLOCK = 512
 
 
@@ -38,7 +588,7 @@
     return jnp.where(allowed[:, None], raw * factor, MASKED)
 
 
-def body(
+def spread_body(
     tokens,
     skip_values,
     segments,
@@ -299,9 +849,205 @@
     )
 
 
+def pick(array, index):
+    return lax.dynamic_index_in_dim(array, index, 0, keepdims=False)
+
+
+def swap(array, axis, count, bit):
+    return lax.ppermute(array, axis, [(i, i ^ bit) for i in range(count)])
+
+
+def trade(pieces):
+    return [pieces[0]] + [swap(pieces[d], "head", 4, d) for d in (1, 2, 3)]
+
+
+def deal(array, me):
+    return [pick(array, me ^ d) for d in range(4)]
+
+
+def arrange(pieces, me):
+    return [lax.select_n(me, *(pieces[q ^ m] for m in range(4))) for q in range(4)]
+
+
+def add_up(parts):
+    total = parts[0].astype(F32)
+    for part in parts[1:]:
+        total = total + part.astype(F32)
+    return total.astype(BF16)
+
+
+def across_cores(send):
+    return swap(send, "seq", 8, 1)
+
+
+def plane_pieces(pairs, plane):
+    return [
+        jnp.concatenate([add_up([pick(a, plane ^ d), pick(b, plane ^ d)]) for a, b in pairs], axis=0)
+        for d in range(4)
+    ]
+
+
+def across_plane(pieces):
+    return [pieces[0]] + [swap(pieces[d], "seq", 8, 2 * d) for d in (1, 2, 3)]
+
+
+def gate(first, second):
+    return lax.optimization_barrier((first, second))
+
+
+def fits(sizes):
+    return sizes == (8, 4)
+
+
+def row_body(
+    tokens,
+    skip_values,
+    segments,
+    token_mask,
+    attn_gain,
+    attn_shift,
+    w_qkv,
+    q_bias,
+    v_bias,
+    w_out,
+    out_bias,
+    mlp_gain,
+    mlp_shift,
+    w_up,
+    up_bias,
+    w_down,
+    down_bias,
+    cotangent,
+):
+    me = lax.axis_index("head")
+    seq = lax.axis_index("seq")
+    core, plane = seq & 1, seq >> 1
+    at = jnp.stack([me, core]).astype(jnp.int32)
+    rows, part, width = tokens.shape
+    length = rows * part
+    fresh = width // 2
+    ff = w_up.shape[1]
+    row = lambda v: v.astype(F32).reshape(1, -1)
+    qkv_bias = row(jnp.concatenate([q_bias, jnp.zeros_like(q_bias), v_bias]))
+    scale = row(jnp.where(jnp.arange(w_qkv.shape[1]) < width, Q_SCALE, 1.0))
+
+    code = (segments * 2 + token_mask).reshape(rows, 1, part)
+    strip = width // 8
+
+    x_pieces = trade(deal(tokens, me))
+    so_far = ()
+    for d in range(4):
+        so_far = project(
+            (me ^ d)[None], x_pieces[d], row(attn_gain), row(attn_shift), w_qkv, qkv_bias, scale, length, so_far
+        )
+    x, normed, proj = so_far
+    (code, skip_values), x_pieces = gate((code, skip_values), x_pieces)
+    code_row = jnp.concatenate(arrange(trade(deal(code, me)), me), axis=1)
+    skip = trade(deal(skip_values, me))
+
+    o_a, lse_a = attend(at, code_row, proj, [proj], 0, 6, 12, 3, "attend_a")
+    (o_a, skip), cotangent = gate((o_a, skip), cotangent)
+    dy_pieces = trade(deal(cotangent, me))
+    o_b, lse_b = attend(at, code_row, proj, skip, 3, 9, 0, 3, "attend_b")
+    middle, normed_two, act, slope, *y_pieces = mlp(
+        at, x, o_a, o_b, w_out, row(out_bias), row(mlp_gain), row(mlp_shift), w_up, row(up_bias), w_down, row(down_bias), 384
+    )
+    dy_pieces, y_pieces = gate(dy_pieces, y_pieces)
+    y_got = trade(y_pieces)
+    dy, g_down_bias, down_send, down_keep = down_grad(at, dy_pieces, act)
+    dy, down_send = gate(dy, down_send)
+    down_got = across_cores(down_send)
+    g_up_bias, up_send, up_keep, d_att, d_o, mlp_sums, out_send, out_keep = mlp_back(
+        at, dy, normed_two, slope, w_down, w_up, middle, row(mlp_gain), o_a, o_b, w_out
+    )
+    down_pieces = plane_pieces([(down_got, down_keep)], plane)
+    (d_o, up_send, out_send), (down_pieces, y_got) = gate((d_o, up_send, out_send), (down_pieces, y_got))
+    up_got = across_cores(up_send)
+    out_got = across_cores(out_send)
+    down_parts = across_plane(down_pieces)
+    d_b, *skip_grads = attend_back(at, code_row, proj, skip, o_b, d_o, lse_b, 3, 9, 0, 3, 3, "attend_back_b")
+    b_bias, b_send, b_keep = qkv_grad(at, normed, d_b, "qkv_grad_b")
+    down_quarters = deal(add_up(down_parts).reshape(4, -1, width), me)
+    up_pieces = plane_pieces([(up_got, up_keep)], plane)
+    (d_o, b_send), (down_quarters, up_pieces, skip_grads) = gate((d_o, b_send), (down_quarters, up_pieces, skip_grads))
+    b_got = across_cores(b_send)
+    up_parts = across_plane(up_pieces)
+    down_got = trade(down_quarters)
+    skip_got = trade(skip_grads)
+    (d_a,) = attend_back(at, code_row, proj, [proj], o_a, d_o, lse_a, 0, 6, 12, 0, 3, "attend_back_a")
+    down_own = add_up(down_got)
+    (d_a, b_got), (down_own, skip_got) = gate((d_a, b_got), (down_own, skip_got))
+    down_all = trade([down_own] * 4)
+    token_sums, *x_grads = token_grad(at, d_a, d_b, w_qkv, x, row(attn_gain), d_att)
+    (d_a, x_grads), down_all = gate((d_a, x_grads), down_all)
+    x_got = trade(x_grads)
+    a_bias, a_send, a_keep = qkv_grad(at, normed, d_a, "qkv_grad_a")
+    a_got = across_cores(a_send)
+
+    two = lambda v: v.reshape(4, strip, 2, fresh).transpose(0, 2, 1, 3)
+    rest_pieces = plane_pieces([(two(out_got), two(out_keep)), (b_got, b_keep), (a_got, a_keep)], plane)
+    rest_parts = across_plane(rest_pieces)
+    up = add_up(up_parts)
+    up_quarters = up.reshape(4, -1, strip, fresh)
+    rest = add_up(rest_parts)
+    by_rows = lambda v: v.reshape(v.shape[0], 4, -1, fresh).transpose(1, 0, 2, 3)
+    rest_quarters = by_rows(rest)
+    up_own = add_up(trade(deal(up_quarters, me)))
+    r_up = arrange(trade([up_own] * 4), me)
+    rest_own = add_up(trade(deal(rest_quarters, me)))
+    rest = jnp.concatenate(arrange(trade([rest_own] * 4), me), axis=1).astype(F32)
+
+    layer_out = settle(at, y_got, BF16, "settle_out")
+    grad_skip = settle(at, skip_got, F32, "settle_skip")
+    grad_tokens = settle(at, x_got, F32, "settle_tokens")
+    r_down = jnp.concatenate(arrange(down_all, me), axis=0).astype(F32)
+    r_up = jnp.concatenate([q[i] for q in r_up for i in range(2)], axis=1).astype(F32)
+    r_out = jnp.concatenate([rest[0], rest[1]], axis=1)
+    r_qkv = jnp.concatenate([rest[4], rest[2], rest[5], rest[3], rest[6]], axis=1)
+
+    small = (
+        token_sums[0],
+        token_sums[1],
+        jnp.concatenate([a_bias[0, 0], b_bias[0, 0]]),
+        a_bias[2, 0],
+        mlp_sums[2],
+        mlp_sums[0],
+        mlp_sums[1],
+        g_up_bias[0],
+        g_down_bias[0],
+    )
+    packed = jnp.concatenate(small).reshape(-1, 128)
+    for axis, count, bit in (("seq", 8, 1), ("seq", 8, 2), ("seq", 8, 4), ("head", 4, 1), ("head", 4, 3)):
+        packed = packed + swap(packed, axis, count, bit)
+    packed = packed.reshape(-1)
+    sums = []
+    for entry in small:
+        sums.append(packed[: entry.shape[0]])
+        packed = packed[entry.shape[0] :]
+    return (
+        layer_out,
+        grad_tokens,
+        grad_skip,
+        sums[0],
+        sums[1],
+        r_qkv,
+        sums[2],
+        sums[3],
+        r_out,
+        sums[4],
+        sums[5],
+        sums[6],
+        r_up,
+        sums[7],
+        r_down,
+        sums[8],
+    )
+
+
 def solution(mesh):
+    sizes = (mesh.shape["seq"], mesh.shape["head"])
     return jax.shard_map(
-        body,
+        row_body if fits(sizes) else spread_body,
         mesh=mesh,
         in_specs=(
             P("seq", "head", None),

time: 797 us -> 391 us (0.49)
  matrix products: 305 us -> 0 us
  Pallas kernels: 0 us -> 188 us
  waiting for transfers between devices: 196 us -> 79.7 us
  blocking collectives: 93.5 us -> 0 us
  local copies, waits for them, and re-layouts: 77.3 us -> 22.8 us
  other arithmetic: 63.5 us -> 13.6 us
  starting transfers between devices: 39.3 us -> 78.9 us
  between operations: 14.9 us -> 2.12 us
    dot_general x24 -> x0, matrix products: 305 us -> none  [the longest x2 66.5 us: body(): jnp.einsum('ihqk,iqhc->ikhc', d_raw, q_split[:, q_start:k_end], preferred...]
    pallas_call x0 -> x17, Pallas kernels: none -> 188 us  [the longest x1 35.9 us: mlp_back(): call(mlp_back_kernel, 'mlp_back', (8,), [full, full, pl.BlockSpec((length...]
    all_to_all x8 -> x0, waiting for transfers between devices: 152 us -> none  [the longest x1 45.5 us: body(): lax.all_to_all(mixed_items, 'head', split_axis=1, concat_axis=0, tiled=True)]
    ppermute x0 -> x58, waiting for transfers between devices: none -> 79.7 us  [swap(): return lax.ppermute(array, axis, [(i, i ^ bit) for i in range(count)])]
    ppermute x0 -> x58, starting transfers between devices: none -> 78.9 us  [swap(): return lax.ppermute(array, axis, [(i, i ^ bit) for i in range(count)])]
    all_gather x2 -> x0, blocking collectives: 51.6 us -> none  [the longest x1 38.5 us: body(): lax.all_gather(segments, 'head', axis=1, tiled=True)]
    psum x1 -> x0, blocking collectives: 41.9 us -> none  [body(): lax.psum((g_attn_gain, g_attn_shift, g_q_bias, g_v_bias, g_out_bias, g_ml...]
    all_to_all x8 -> x0, starting transfers between devices: 38.9 us -> none  [the longest x1 6.33 us: body(): lax.all_to_all(value_rows.reshape(flat_shape), 'head', split_axis=0, conc...]
  transfers between devices with their start and end apart: 13 -> 58, of which waited for: 7 -> 14; matrix products, arithmetic and copies ran while one was open for 39% -> 7% of each run, Pallas kernels for 0% -> 45%
where the time goes in v2:
time: 391 us; the launch traced here: 385 us
  Pallas kernels  188 us (48%)
  waiting for transfers between devices  79.7 us (20%)
  starting transfers between devices  78.9 us (20%)
  local copies, waits for them, and re-layouts  22.8 us (6%)
  other arithmetic  13.6 us (3%)
    ppermute x58, waiting for transfers between devices, swap(): return lax.ppermute(array, axis, [(i, i ^ bit) for i in range(count)])  79.7 us
    ppermute x58, starting transfers between devices, swap(): return lax.ppermute(array, axis, [(i, i ^ bit) for i in range(count)])  78.9 us
    pallas_call x1, Pallas kernels, mlp_back(): call(mlp_back_kernel, 'mlp_back', (8,), [full, full, pl.BlockSpec((length...  35.9 us
    pallas_call x2, Pallas kernels, attend_back(): call(functools.partial(backward_kernel, len(values)), name, (pairs,), [wh...  30.6 us
    pallas_call x1, Pallas kernels, mlp(): call(mlp_kernel, 'mlp', (ff // chunk,), [whole((length, width)), whole(o_...  27.6 us
    pallas_call x2, Pallas kernels, attend(): call(functools.partial(forward_kernel, len(values)), name, (pairs,), [who...  26.9 us
    pallas_call x4, Pallas kernels, project(): call(project_kernel, 'project', (1,), [whole((part, width)), whole((1, wi...  16.5 us
    pallas_call x3, Pallas kernels, settle(): call(settle_kernel, name, (4,), [pl.BlockSpec((rows, width), lambda i, at...  13.1 us
  transfers between devices with their start and end apart: 58, of which 14 were waited for; matrix products, arithmetic and copies ran while one was open for 7% of the time, Pallas kernels for 45%

profile of v2, /device:TPU:0, one launch (start us, length us, event | category | flops | bytes accessed | tf_op | source)
XLA Modules:
  0.0 385.0 jit_solution(11110660795489552830)
XLA Ops:
  0.8 2.2 dynamic-slice_bitcast_fusion.4
  3.0 3.0 collective-permute-start
  6.0 2.6 collective-permute-start.1
  14.0 4.2 %project.4 = (bf16[1024,768]{1,0:T(8,128)(2,1)}, bf16[1024,768]{1,0:T(8,128)(2,1)}, bf16[1024,1920]{1,0:T(8,128)(2,1)}) custom-call(s32[1]{0:T(128)} %bitcast.at_ref, bf16[256,768]{1,0:T(8,128)(2,1)} %get-tuple-element.263.x_ref, f32[1,768]{1,0:T(1,128)} %reshape.275.gain_ref, f32[1,768]{1,0:T(1,128)} %reshape.277.shift_ref, bf16[768,1920]{1,0:T(8,128)(2,1)} %w_ref.9, ...), custom_call_target="tpu_custom_call" | custom-call | flops 754974720 | bytes 5111808 | tf_op jit(solution)/shard_map/project/pallas_call | solution.py:99
  18.8 4.0 %collective-permute-done.x_ref = bf16[256,768]{1,0:T(8,128)(2,1)S(1)} collective-permute-done((bf16[256,768]{1,0:T(8,128)(2,1)S(1)}, bf16[256,768]{1,0:T(8,128)(2,1)S(1)}, u32[]{:S(2)}, u32[]{:S(2)}) %collective-permute-start) | collective-permute-done | bytes 393248 | tf_op jit(solution)/shard_map/ppermute | solution.py:857
  22.8 13.0 %collective-permute-done.1.x_ref = bf16[256,768]{1,0:T(8,128)(2,1)S(1)} collective-permute-done((bf16[256,768]{1,0:T(8,128)(2,1)S(1)}, bf16[256,768]{1,0:T(8,128)(2,1)S(1)}, u32[]{:S(2)}, u32[]{:S(2)}) %collective-permute-start.1) | collective-permute-done | bytes 393248 | tf_op jit(solution)/shard_map/ppermute | solution.py:857
  35.9 7.6 %collective-permute-start.3 = (s32[1,256]{1,0:T(1,128)S(1)}, s32[1,256]{1,0:T(1,128)S(1)}, u32[]{:S(2)}, u32[]{:S(2)}) collective-permute-start(s32[1,256]{1,0:T(1,128)S(1)} %get-tuple-element.316), channel_id=1, source_target_pairs={{0,1},{1,0},{2,3},{3,2},{4,5},{5,4},{6,7},{7,6},{8,9},{9,8},{10,11... | collective-permute-start | bytes 3080 | tf_op jit(solution)/shard_map/ppermute | solution.py:857
  47.7 2.0 collective-permute-start.7
  49.7 4.1 %project.5 = (bf16[1024,768]{1,0:T(8,128)(2,1)}, bf16[1024,768]{1,0:T(8,128)(2,1)}, bf16[1024,1920]{1,0:T(8,128)(2,1)}) custom-call(s32[1]{0:T(128)} %bitcast.13.at_ref, bf16[256,768]{1,0:T(8,128)(2,1)} %copy-done.12, f32[1,768]{1,0:T(1,128)} %reshape.275.gain_ref, ...), custom_call_target="tpu_custom_call", output_to_operand_aliasing={{0}: (7, {}), {1}: (8, {}), {2}: (9, {})} | custom-call | flops 754974720 | bytes 5111808 | tf_op jit(solution)/shard_map/project/pallas_call | solution.py:99
  53.9 4.1 %project.6 = (bf16[1024,768]{1,0:T(8,128)(2,1)}, bf16[1024,768]{1,0:T(8,128)(2,1)}, bf16[1024,1920]{1,0:T(8,128)(2,1)}) custom-call(s32[1]{0:T(128)} %bitcast.12.at_ref, bf16[256,768]{1,0:T(8,128)(2,1)} %copy-done.11, f32[1,768]{1,0:T(1,128)} %reshape.275.gain_ref, ...), custom_call_target="tpu_custom_call", output_to_operand_aliasing={{0}: (7, {}), {1}: (8, {}), {2}: (9, {})} | custom-call | flops 754974720 | bytes 5111808 | tf_op jit(solution)/shard_map/project/pallas_call | solution.py:99
  57.9 4.1 %project.7 = (bf16[1024,768]{1,0:T(8,128)(2,1)}, bf16[1024,768]{1,0:T(8,128)(2,1)}, bf16[1024,1920]{1,0:T(8,128)(2,1)}) custom-call(s32[1]{0:T(128)} %bitcast.11.at_ref, bf16[256,768]{1,0:T(8,128)(2,1)} %copy-done.10, f32[1,768]{1,0:T(1,128)} %reshape.275.gain_ref, ...), custom_call_target="tpu_custom_call", output_to_operand_aliasing={{0}: (7, {}), {1}: (8, {}), {2}: (9, {})} | custom-call | flops 754974720 | bytes 5111808 | tf_op jit(solution)/shard_map/project/pallas_call | solution.py:99
  64.0 13.8 %attend_a.1 = (bf16[1024,384]{1,0:T(8,128)(2,1)}, f32[1024,384]{1,0:T(8,128)}) custom-call(s32[2]{0:T(128)} %pad_add_fusion.1.me_ref.at_ref, s32[1,1024]{1,0:T(1,128)} %pad_add_fusion.code_ref, bf16[1024,1920]{1,0:T(8,128)(2,1)} %get-tuple-element.137.q_ref.k_ref.refs_0_, bf16[1024,1920]{1,0:T(8,128)(2,1)} %get-tuple-element.137.q_ref.k_ref.refs_0_, ...), custom_call_target="tpu_custom_call" | custom-call | flops 9663676416 | bytes 4718592 | tf_op jit(solution)/shard_map/attend_a/pallas_call | solution.py:242
  79.9 1.4 collective-permute-start.11
  82.3 13.1 %attend_b.1 = (bf16[1024,384]{1,0:T(8,128)(2,1)}, f32[1024,384]{1,0:T(8,128)}) custom-call(s32[2]{0:T(128)} %pad_add_fusion.1.me_ref.at_ref, s32[1,1024]{1,0:T(1,128)} %pad_add_fusion.code_ref, bf16[1024,1920]{1,0:T(8,128)(2,1)} %get-tuple-element.137.q_ref.k_ref.refs_0_, bf16[1024,1920]{1,0:T(8,128)(2,1)} %get-tuple-element.137.q_ref.k_ref.refs_0_, ...), custom_call_target="tpu_custom_call" | custom-call | flops 9663676416 | bytes 4718592 | tf_op jit(solution)/shard_map/attend_b/pallas_call | solution.py:242
  95.4 27.6 %mlp.1 = (f32[1024,768]{1,0:T(8,128)}, bf16[1024,768]{1,0:T(8,128)(2,1)}, bf16[1024,3072]{1,0:T(8,128)(2,1)}, bf16[1024,3072]{1,0:T(8,128)(2,1)}, bf16[256,768]{...) custom-call(s32[2]{0:T(128)} %pad_add_fusion.1.me_ref.at_ref, ...), custom_call_target="tpu_custom_call" | custom-call | flops 10871635968 | bytes 31457280 | tf_op jit(solution)/shard_map/mlp/pallas_call | solution.py:329
  124.1 13.0 %down_grad.1 = (bf16[1024,768]{1,0:T(8,128)(2,1)}, f32[1,768]{1,0:T(1,128)}, bf16[4,384,768]{2,1,0:T(8,128)(2,1)}, bf16[4,384,768]{2,1,0:T(8,128)(2,1)}) custom-call(s32[2]{0:T(128)} %pad_add_fusion.1.me_ref.at_ref, bf16[256,768]{1,0:T(8,128)(2,1)} %get-tuple-element.152.d0_ref, bf16[256,768]{1,0:T(8,128)(2,1)} %copy-done.43, bf16[256,768]{1,0:T(8,128)(2,1)} %copy-done.41, ...), custom_call_target="tpu_custom_call" | custom-call | flops 4831838208 | bytes 14155776 | tf_op jit(solution)/shard_map/down_grad/pallas_call | solution.py:375
  138.2 2.0 collective-permute-start.14
  141.6 35.9 %mlp_back.1 = (f32[1,3072]{1,0:T(1,128)}, bf16[4,8,96,384]{3,2,1,0:T(8,128)(2,1)}, bf16[4,8,96,384]{3,2,1,0:T(8,128)(2,1)}, bf16[1024,768]{1,0:T(8,128)(2,1)}, b...) custom-call(s32[2]{0:T(128)} %pad_add_fusion.1.me_ref.at_ref, ...), custom_call_target="tpu_custom_call" | custom-call | flops 16911433728 | bytes 29884416 | tf_op jit(solution)/shard_map/mlp_back/pallas_call | solution.py:441
  177.6 2.0 reshape.271
  181.7 3.3 fusion.3
  185.1 1.6 collective-permute-start.16
  186.6 1.5 collective-permute-start.17
  188.6 15.3 %attend_back_b.1 = (bf16[2,1024,384]{2,1,0:T(8,128)(2,1)}, bf16[256,384]{1,0:T(8,128)(2,1)}, bf16[256,384]{1,0:T(8,128)(2,1)}, bf16[256,384]{1,0:T(8,128)(2,1)}, bf16[256,384]{1,0:T(8,128)(2,1)}) custom-call(s32[2]{0:T(128)} %pad_add_fusion.1.me_ref.at_ref, s32[1,1024]{1,0:T(1,128)} %pad_add_fusion.code_ref, ...), custom_call_target="tpu_custom_call" | custom-call | flops 12079595520 | bytes 7077888 | tf_op jit(solution)/shard_map/attend_back_b/pallas_call | solution.py:265
  203.9 4.3 %settle_out.1 = bf16[4,256,768]{2,1,0:T(8,128)(2,1)} custom-call(s32[2]{0:T(128)} %pad_add_fusion.1.me_ref.at_ref, bf16[256,768]{1,0:T(8,128)(2,1)} %get-tuple-element.172.refs_0_, bf16[256,768]{1,0:T(8,128)(2,1)} %collective-permute-done.13.refs_1_, bf16[256,768]{1,0:T(8,128)(2,1)} %collective-permute-done.14.refs_2_, ...), custom_call_target="tpu_custom_call" | custom-call | bytes 4718592 | tf_op jit(solution)/shard_map/settle_out/pallas_call | solution.py:546
  208.2 5.3 %qkv_grad_b.1 = (f32[2,1,384]{2,1,0:T(1,128)}, bf16[4,2,96,384]{3,2,1,0:T(8,128)(2,1)}, bf16[4,2,96,384]{3,2,1,0:T(8,128)(2,1)}) custom-call(s32[2]{0:T(128)} %pad_add_fusion.1.me_ref.at_ref, bf16[1024,768]{1,0:T(8,128)(2,1)} %get-tuple-element.177.normed_ref, bf16[2,1024,384]{2,1,0:T(8,128)(2,1)} %get-tuple-element.179.d_ref.db_ref), custom_call_target="tpu_custom_call" | custom-call | flops 1207959552 | bytes 4325376 | tf_op jit(solution)/shard_map/qkv_grad_b/pallas_call | solution.py:481
  214.8 1.8 reshape.270
  216.6 1.7 add_convert_fusion.5
  221.1 2.9 collective-permute-start.22
  224.0 1.4 collective-permute-start.23
  225.5 5.0 %collective-permute-done.21 = bf16[96,768]{1,0:T(8,128)(2,1)S(1)} collective-permute-done((bf16[96,768]{1,0:T(8,128)(2,1)S(1)}, bf16[96,768]{1,0:T(8,128)(2,1)S(1)}, u32[]{:S(2)}, u32[]{:S(2)}) %collective-permute-start.21) | collective-permute-done | bytes 147488 | tf_op jit(solution)/shard_map/ppermute | solution.py:857
  230.5 4.5 %collective-permute-done.22 = bf16[96,768]{1,0:T(8,128)(2,1)S(1)} collective-permute-done((bf16[96,768]{1,0:T(8,128)(2,1)S(1)}, bf16[96,768]{1,0:T(8,128)(2,1)S(1)}, u32[]{:S(2)}, u32[]{:S(2)}) %collective-permute-start.22) | collective-permute-done | bytes 147488 | tf_op jit(solution)/shard_map/ppermute | solution.py:857
  235.0 1.5 collective-permute-start.49
  236.5 1.6 collective-permute-start.50
  238.2 2.5 collective-permute-start.51
  240.6 15.3 %attend_back_a.1.da_ref.d_ref = bf16[3,1024,384]{2,1,0:T(8,128)(2,1)} custom-call(s32[2]{0:T(128)} %pad_add_fusion.1.me_ref.at_ref, s32[1,1024]{1,0:T(1,128)} %pad_add_fusion.code_ref, bf16[1024,1920]{1,0:T(8,128)(2,1)} %get-tuple-element.137.q_ref.k_ref.refs_0_, bf16[1024,1920]{1,0:T(8,128)(2,1)} %get-tuple-element.137.q_ref.k_ref.refs_0_, ...), custom_call_target="tpu_custom_call" | custom-call | flops 12079595520 | bytes 7077888 | tf_op jit(solution)/shard_map/attend_back_a/pallas_call | solution.py:265
  256.0 2.1 collective-permute-start.26
  258.2 5.6 %collective-permute-done.26.refs_3_ = bf16[256,384]{1,0:T(8,128)(2,1)S(1)} collective-permute-done((bf16[256,384]{1,0:T(8,128)(2,1)S(1)}, bf16[256,384]{1,0:T(8,128)(2,1)S(1)}, u32[]{:S(2)}, u32[]{:S(2)}) %collective-permute-start.26) | collective-permute-done | bytes 196640 | tf_op jit(solution)/shard_map/ppermute | solution.py:857
  263.8 3.2 collective-permute-start.27
  268.3 1.4 collective-permute-start.29
  271.0 2.1 collective-permute-start.53
  273.2 12.2 %token_grad.1 = (f32[8,768]{1,0:T(8,128)}, bf16[256,768]{1,0:T(8,128)(2,1)}, bf16[256,768]{1,0:T(8,128)(2,1)}, bf16[256,768]{1,0:T(8,128)(2,1)}, bf16[256,768]{1,0:T(8,128)(2,1)}) custom-call(s32[2]{0:T(128)} %pad_add_fusion.1.me_ref.at_ref, bf16[3,1024,384]{2,1,0:T(8,128)(2,1)} %attend_back_a.1.da_ref.d_ref, ...), custom_call_target="tpu_custom_call" | custom-call | flops 3019898880 | bytes 11599872 | tf_op jit(solution)/shard_map/token_grad/pallas_call | solution.py:524
  286.2 1.5 collective-permute-start.54
  287.7 6.8 %qkv_grad_a.1 = (f32[3,1,384]{2,1,0:T(1,128)}, bf16[4,3,96,384]{3,2,1,0:T(8,128)(2,1)}, bf16[4,3,96,384]{3,2,1,0:T(8,128)(2,1)}) custom-call(s32[2]{0:T(128)} %pad_add_fusion.1.me_ref.at_ref, bf16[1024,768]{1,0:T(8,128)(2,1)} %get-tuple-element.177.normed_ref, bf16[3,1024,384]{2,1,0:T(8,128)(2,1)} %attend_back_a.1.da_ref.d_ref), custom_call_target="tpu_custom_call" | custom-call | flops 1811939328 | bytes 5701632 | tf_op jit(solution)/shard_map/qkv_grad_a/pallas_call | solution.py:481
  295.6 4.1 %settle_skip.1 = f32[4,256,384]{2,1,0:T(8,128)} custom-call(s32[2]{0:T(128)} %pad_add_fusion.1.me_ref.at_ref, bf16[256,384]{1,0:T(8,128)(2,1)} %get-tuple-element.213.refs_0_, bf16[256,384]{1,0:T(8,128)(2,1)} %copy-done.16, bf16[256,384]{1,0:T(8,128)(2,1)} %copy-done.17, bf16[256,384]{1,0:T(8,128)(2,1)} %copy-done.18), custom_call_target="tpu_custom_call" | custom-call | bytes 2359296 | tf_op jit(solution)/shard_map/settle_skip/pallas_call | solution.py:546
  300.4 2.9 collective-permute-start.56
  303.3 1.4 collective-permute-start.57
  304.7 1.6 collective-permute-start.35
  306.4 2.4 collective-permute-done.35
  309.9 4.8 %collective-permute-done.36 = f32[69,128]{1,0:T(8,128)S(1)} collective-permute-done((f32[69,128]{1,0:T(8,128)S(1)}, f32[69,128]{1,0:T(8,128)S(1)}, u32[]{:S(2)}, u32[]{:S(2)}) %collective-permute-start.36) | collective-permute-done | bytes 35360 | tf_op jit(solution)/shard_map/ppermute | solution.py:857
  314.7 2.2 collective-permute-start.37
  317.4 1.7 collective-permute-start.40
  319.2 1.6 collective-permute-start.41
  322.4 4.3 %collective-permute-done.37 = f32[69,128]{1,0:T(8,128)S(1)} collective-permute-done((f32[69,128]{1,0:T(8,128)S(1)}, f32[69,128]{1,0:T(8,128)S(1)}, u32[]{:S(2)}, u32[]{:S(2)}) %collective-permute-start.37) | collective-permute-done | bytes 35360 | tf_op jit(solution)/shard_map/ppermute | solution.py:857
  327.4 4.8 %collective-permute-done.40 = bf16[7,96,384]{2,1,0:T(8,128)(2,1)S(1)} collective-permute-done((bf16[7,96,384]{2,1,0:T(8,128)(2,1)S(1)}, bf16[7,96,384]{2,1,0:T(8,128)(2,1)S(1)}, u32[]{:S(2)}, u32[]{:S(2)}) %collective-permute-start.40) | collective-permute-done | bytes 516128 | tf_op jit(solution)/shard_map/ppermute | solution.py:857
  332.1 11.2 %collective-permute-done.41 = bf16[7,96,384]{2,1,0:T(8,128)(2,1)S(1)} collective-permute-done((bf16[7,96,384]{2,1,0:T(8,128)(2,1)S(1)}, bf16[7,96,384]{2,1,0:T(8,128)(2,1)S(1)}, u32[]{:S(2)}, u32[]{:S(2)}) %collective-permute-start.41) | collective-permute-done | bytes 516128 | tf_op jit(solution)/shard_map/ppermute | solution.py:857
  344.6 1.6 collective-permute-start.44
  346.1 2.0 collective-permute-start.45
  348.7 2.6 collective-permute-done.43
  351.3 1.9 collective-permute-start.32
  353.3 10.8 %collective-permute-done.44 = bf16[7,24,384]{2,1,0:T(8,128)(2,1)S(1)} collective-permute-done((bf16[7,24,384]{2,1,0:T(8,128)(2,1)S(1)}, bf16[7,24,384]{2,1,0:T(8,128)(2,1)S(1)}, u32[]{:S(2)}, u32[]{:S(2)}) %collective-permute-start.44) | collective-permute-done | bytes 129056 | tf_op jit(solution)/shard_map/ppermute | solution.py:857
  364.2 3.4 collective-permute-start.46
  368.0 2.0 collective-permute-start.48
  372.1 4.6 %settle_tokens.1 = f32[4,256,768]{2,1,0:T(8,128)} custom-call(s32[2]{0:T(128)} %pad_add_fusion.1.me_ref.at_ref, bf16[256,768]{1,0:T(8,128)(2,1)} %get-tuple-element.209.refs_0_, bf16[256,768]{1,0:T(8,128)(2,1)} %copy-done.13, bf16[256,768]{1,0:T(8,128)(2,1)} %copy-done.14, bf16[256,768]{1,0:T(8,128)(2,1)} %copy-done.15), custom_call_target="tpu_custom_call" | custom-call | bytes 4718592 | tf_op jit(solution)/shard_map/settle_tokens/pallas_call | solution.py:546
  376.7 6.6 %collective-permute-done.47 = bf16[7,24,384]{2,1,0:T(8,128)(2,1)S(1)} collective-permute-done((bf16[7,24,384]{2,1,0:T(8,128)(2,1)S(1)}, bf16[7,24,384]{2,1,0:T(8,128)(2,1)S(1)}, u32[]{:S(2)}, u32[]{:S(2)}) %collective-permute-start.47) | collective-permute-done | bytes 129056 | tf_op jit(solution)/shard_map/ppermute | solution.py:857
  (257 shorter events, 40.3 us)
Async XLA Ops:
  3.0 19.8 %collective-permute-start = (bf16[256,768]{1,0:T(8,128)(2,1)S(1)}, bf16[256,768]{1,0:T(8,128)(2,1)S(1)}, u32[]{:S(2)}, u32[]{:S(2)}) collective-permute-start(bf16[256,768]{1,0:T(8,128)(2,1)S(1)} %get-tuple-element.262), channel_id=1, source_target_pairs={{0,1},{1,0},{2,3},{3,2},{4,5},{5,4},{6,7},{7,6},{8,9},{9,8},{10,11... | collective-permute-start | bytes 1179656 | tf_op jit(solution)/shard_map/ppermute | solution.py:857
  6.0 29.8 %collective-permute-start.1 = (bf16[256,768]{1,0:T(8,128)(2,1)S(1)}, bf16[256,768]{1,0:T(8,128)(2,1)S(1)}, u32[]{:S(2)}, u32[]{:S(2)}) collective-permute-start(bf16[256,768]{1,0:T(8,128)(2,1)S(1)} %get-tuple-element.264), channel_id=1, source_target_pairs={{0,2},{1,3},{2,0},{3,1},{4,6},{5,7},{6,4},{7,5},{8,10},{9,11},{10,... | collective-permute-start | bytes 1179656 | tf_op jit(solution)/shard_map/ppermute | solution.py:857
  8.6 27.2 %collective-permute-start.2 = (bf16[256,768]{1,0:T(8,128)(2,1)S(1)}, bf16[256,768]{1,0:T(8,128)(2,1)S(1)}, u32[]{:S(2)}, u32[]{:S(2)}) collective-permute-start(bf16[256,768]{1,0:T(8,128)(2,1)S(1)} %get-tuple-element.261), channel_id=1, source_target_pairs={{0,3},{1,2},{2,1},{3,0},{4,7},{5,6},{6,5},{7,4},{8,11},{9,10},{10,... | collective-permute-start | bytes 1179656 | tf_op jit(solution)/shard_map/ppermute | solution.py:857
  14.0 32.0 %copy-start.4 = (bf16[4,256,384]{2,1,0:T(8,128)(2,1)S(1)}, bf16[4,256,384]{2,1,0:T(8,128)(2,1)}, u32[]{:S(2)}) copy-start(bf16[4,256,384]{2,1,0:T(8,128)(2,1)} %param.19) | copy-start | bytes 2359300
  22.8 26.9 %copy-start.12 = (bf16[256,768]{1,0:T(8,128)(2,1)}, bf16[256,768]{1,0:T(8,128)(2,1)S(1)}, u32[]{:S(2)}) copy-start(bf16[256,768]{1,0:T(8,128)(2,1)S(1)} %collective-permute-done.x_ref) | copy-start | bytes 1179652
  35.8 18.0 %copy-start.11 = (bf16[256,768]{1,0:T(8,128)(2,1)}, bf16[256,768]{1,0:T(8,128)(2,1)S(1)}, u32[]{:S(2)}) copy-start(bf16[256,768]{1,0:T(8,128)(2,1)S(1)} %collective-permute-done.1.x_ref) | copy-start | bytes 1179652
  35.8 18.0 %copy-start.10 = (bf16[256,768]{1,0:T(8,128)(2,1)}, bf16[256,768]{1,0:T(8,128)(2,1)S(1)}, u32[]{:S(2)}) copy-start(bf16[256,768]{1,0:T(8,128)(2,1)S(1)} %collective-permute-done.2.x_ref) | copy-start | bytes 1179652
  35.9 26.2 %collective-permute-start.3 = (s32[1,256]{1,0:T(1,128)S(1)}, s32[1,256]{1,0:T(1,128)S(1)}, u32[]{:S(2)}, u32[]{:S(2)}) collective-permute-start(s32[1,256]{1,0:T(1,128)S(1)} %get-tuple-element.316), channel_id=1, source_target_pairs={{0,1},{1,0},{2,3},{3,2},{4,5},{5,4},{6,7},{7,6},{8,9},{9,8},{10,11... | collective-permute-start | bytes 3080 | tf_op jit(solution)/shard_map/ppermute | solution.py:857
  43.5 19.9 %collective-permute-start.4 = (s32[1,256]{1,0:T(1,128)S(1)}, s32[1,256]{1,0:T(1,128)S(1)}, u32[]{:S(2)}, u32[]{:S(2)}) collective-permute-start(s32[1,256]{1,0:T(1,128)S(1)} %get-tuple-element.318), channel_id=1, source_target_pairs={{0,2},{1,3},{2,0},{3,1},{4,6},{5,7},{6,4},{7,5},{8,10},{9,11},{10,... | collective-permute-start | bytes 3080 | tf_op jit(solution)/shard_map/ppermute | solution.py:857
  44.6 18.9 %collective-permute-start.5 = (s32[1,256]{1,0:T(1,128)S(1)}, s32[1,256]{1,0:T(1,128)S(1)}, u32[]{:S(2)}, u32[]{:S(2)}) collective-permute-start(s32[1,256]{1,0:T(1,128)S(1)} %get-tuple-element.317), channel_id=1, source_target_pairs={{0,3},{1,2},{2,1},{3,0},{4,7},{5,6},{6,5},{7,4},{8,11},{9,10},{10,... | collective-permute-start | bytes 3080 | tf_op jit(solution)/shard_map/ppermute | solution.py:857
  46.7 31.1 %collective-permute-start.6 = (bf16[256,384]{1,0:T(8,128)(2,1)S(1)}, bf16[256,384]{1,0:T(8,128)(2,1)S(1)}, u32[]{:S(2)}, u32[]{:S(2)}) collective-permute-start(bf16[256,384]{1,0:T(8,128)(2,1)S(1)} %get-tuple-element.273), channel_id=1, source_target_pairs={{0,1},{1,0},{2,3},{3,2},{4,5},{5,4},{6,7},{7,6},{8,9},{9,8},{10,11... | collective-permute-start | bytes 589832 | tf_op jit(solution)/shard_map/ppermute | solution.py:857
  47.7 30.1 %collective-permute-start.7 = (bf16[256,384]{1,0:T(8,128)(2,1)S(1)}, bf16[256,384]{1,0:T(8,128)(2,1)S(1)}, u32[]{:S(2)}, u32[]{:S(2)}) collective-permute-start(bf16[256,384]{1,0:T(8,128)(2,1)S(1)} %get-tuple-element.272), channel_id=1, source_target_pairs={{0,2},{1,3},{2,0},{3,1},{4,6},{5,7},{6,4},{7,5},{8,10},{9,11},{10,... | collective-permute-start | bytes 589832 | tf_op jit(solution)/shard_map/ppermute | solution.py:857
  62.0 15.8 %collective-permute-start.8 = (bf16[256,384]{1,0:T(8,128)(2,1)S(1)}, bf16[256,384]{1,0:T(8,128)(2,1)S(1)}, u32[]{:S(2)}, u32[]{:S(2)}) collective-permute-start(bf16[256,384]{1,0:T(8,128)(2,1)S(1)} %get-tuple-element.271), channel_id=1, source_target_pairs={{0,3},{1,2},{2,1},{3,0},{4,7},{5,6},{6,5},{7,4},{8,11},{9,10},{10,... | collective-permute-start | bytes 589832 | tf_op jit(solution)/shard_map/ppermute | solution.py:857
  78.8 44.3 %collective-permute-start.10 = (bf16[256,768]{1,0:T(8,128)(2,1)S(1)}, bf16[256,768]{1,0:T(8,128)(2,1)S(1)}, u32[]{:S(2)}, u32[]{:S(2)}) collective-permute-start(bf16[256,768]{1,0:T(8,128)(2,1)S(1)} %get-tuple-element.258), channel_id=1, source_target_pairs={{0,2},{1,3},{2,0},{3,1},{4,6},{5,7},{6,4},{7,5},{8,10},{9,11},{10,... | collective-permute-start | bytes 1179656 | tf_op jit(solution)/shard_map/ppermute | solution.py:857
  79.9 43.1 %collective-permute-start.11 = (bf16[256,768]{1,0:T(8,128)(2,1)S(1)}, bf16[256,768]{1,0:T(8,128)(2,1)S(1)}, u32[]{:S(2)}, u32[]{:S(2)}) collective-permute-start(bf16[256,768]{1,0:T(8,128)(2,1)S(1)} %get-tuple-element.257), channel_id=1, source_target_pairs={{0,3},{1,2},{2,1},{3,0},{4,7},{5,6},{6,5},{7,4},{8,11},{9,10},{10,... | collective-permute-start | bytes 1179656 | tf_op jit(solution)/shard_map/ppermute | solution.py:857
  81.4 41.7 %collective-permute-start.9 = (bf16[256,768]{1,0:T(8,128)(2,1)S(1)}, bf16[256,768]{1,0:T(8,128)(2,1)S(1)}, u32[]{:S(2)}, u32[]{:S(2)}) collective-permute-start(bf16[256,768]{1,0:T(8,128)(2,1)S(1)} %get-tuple-element.259), channel_id=1, source_target_pairs={{0,1},{1,0},{2,3},{3,2},{4,5},{5,4},{6,7},{7,6},{8,9},{9,8},{10,11... | collective-permute-start | bytes 1179656 | tf_op jit(solution)/shard_map/ppermute | solution.py:857
  137.1 44.6 %collective-permute-start.12 = (bf16[4,384,768]{2,1,0:T(8,128)(2,1)}, bf16[4,384,768]{2,1,0:T(8,128)(2,1)}, u32[]{:S(2)}, u32[]{:S(2)}) collective-permute-start(bf16[4,384,768]{2,1,0:T(8,128)(2,1)} %get-tuple-element.166), channel_id=1, source_target_pairs={{0,4},{4,0},{8,12},{12,8},{16,20},{20,16},{24,28},{28,24},{1,5},{5... | collective-permute-start | bytes 7077896 | tf_op jit(solution)/shard_map/ppermute | solution.py:857
  137.2 47.8 %collective-permute-start.13 = (bf16[256,768]{1,0:T(8,128)(2,1)}, bf16[256,768]{1,0:T(8,128)(2,1)}, u32[]{:S(2)}, u32[]{:S(2)}) collective-permute-start(bf16[256,768]{1,0:T(8,128)(2,1)} %get-tuple-element.169), channel_id=1, source_target_pairs={{0,1},{1,0},{2,3},{3,2},{4,5},{5,4},{6,7},{7,6},{8,9},{9,8},{10,11... | collective-permute-start | bytes 1179656 | tf_op jit(solution)/shard_map/ppermute | solution.py:857
  138.2 46.7 %collective-permute-start.14 = (bf16[256,768]{1,0:T(8,128)(2,1)}, bf16[256,768]{1,0:T(8,128)(2,1)}, u32[]{:S(2)}, u32[]{:S(2)}) collective-permute-start(bf16[256,768]{1,0:T(8,128)(2,1)} %get-tuple-element.170), channel_id=1, source_target_pairs={{0,2},{1,3},{2,0},{3,1},{4,6},{5,7},{6,4},{7,5},{8,10},{9,11},{10,... | collective-permute-start | bytes 1179656 | tf_op jit(solution)/shard_map/ppermute | solution.py:857
  140.2 44.8 %collective-permute-start.15 = (bf16[256,768]{1,0:T(8,128)(2,1)}, bf16[256,768]{1,0:T(8,128)(2,1)}, u32[]{:S(2)}, u32[]{:S(2)}) collective-permute-start(bf16[256,768]{1,0:T(8,128)(2,1)} %get-tuple-element.171), channel_id=1, source_target_pairs={{0,3},{1,2},{2,1},{3,0},{4,7},{5,6},{6,5},{7,4},{8,11},{9,10},{10,... | collective-permute-start | bytes 1179656 | tf_op jit(solution)/shard_map/ppermute | solution.py:857
  185.0 34.5 %collective-permute-start.19 = (bf16[4,8,96,384]{3,2,1,0:T(8,128)(2,1)}, bf16[4,8,96,384]{3,2,1,0:T(8,128)(2,1)S(1)}, u32[]{:S(2)}, u32[]{:S(2)}) collective-permute-start(bf16[4,8,96,384]{3,2,1,0:T(8,128)(2,1)} %get-tuple-element.185), channel_id=1, source_target_pairs={{0,4},{4,0},{8,12},{12,8},{16,20},{20,16},{24,28},{28,24},{1,5},{5... | collective-permute-start | bytes 7077896 | tf_op jit(solution)/shard_map/ppermute | solution.py:857
  185.1 31.5 %collective-permute-start.16 = (bf16[384,768]{1,0:T(8,128)(2,1)}, bf16[384,768]{1,0:T(8,128)(2,1)}, u32[]{:S(2)}, u32[]{:S(2)}) collective-permute-start(bf16[384,768]{1,0:T(8,128)(2,1)} %get-tuple-element.182), channel_id=1, source_target_pairs={{0,8},{4,12},{8,0},{12,4},{16,24},{20,28},{24,16},{28,20},{1,9},{5... | collective-permute-start | bytes 1769480 | tf_op jit(solution)/shard_map/ppermute | solution.py:857
  186.6 30.0 %collective-permute-start.17 = (bf16[384,768]{1,0:T(8,128)(2,1)}, bf16[384,768]{1,0:T(8,128)(2,1)}, u32[]{:S(2)}, u32[]{:S(2)}) collective-permute-start(bf16[384,768]{1,0:T(8,128)(2,1)} %get-tuple-element.183), channel_id=1, source_target_pairs={{0,16},{4,20},{8,24},{12,28},{16,0},{20,4},{24,8},{28,12},{1,17},{... | collective-permute-start | bytes 1769480 | tf_op jit(solution)/shard_map/ppermute | solution.py:857
  188.1 28.5 %collective-permute-start.18 = (bf16[384,768]{1,0:T(8,128)(2,1)}, bf16[384,768]{1,0:T(8,128)(2,1)}, u32[]{:S(2)}, u32[]{:S(2)}) collective-permute-start(bf16[384,768]{1,0:T(8,128)(2,1)} %get-tuple-element.184), channel_id=1, source_target_pairs={{0,24},{4,28},{8,16},{12,20},{16,8},{20,12},{24,0},{28,4},{1,25},{... | collective-permute-start | bytes 1769480 | tf_op jit(solution)/shard_map/ppermute | solution.py:857
  188.6 26.2 %collective-permute-start.38 = (bf16[4,96,768]{2,1,0:T(8,128)(2,1)S(1)}, bf16[4,96,768]{2,1,0:T(8,128)(2,1)}, u32[]{:S(2)}, u32[]{:S(2)}) collective-permute-start(bf16[4,96,768]{2,1,0:T(8,128)(2,1)S(1)} %copy-done.37), channel_id=1, source_target_pairs={{0,4},{4,0},{8,12},{12,8},{16,20},{20,16},{24,28},{28,24},{1,5},{5... | collective-permute-start | bytes 1769480 | tf_op jit(solution)/shard_map/ppermute | solution.py:857
  220.9 9.6 %collective-permute-start.21 = (bf16[96,768]{1,0:T(8,128)(2,1)S(1)}, bf16[96,768]{1,0:T(8,128)(2,1)S(1)}, u32[]{:S(2)}, u32[]{:S(2)}) collective-permute-start(bf16[96,768]{1,0:T(8,128)(2,1)S(1)} %get-tuple-element.195), channel_id=1, source_target_pairs={{0,1},{1,0},{2,3},{3,2},{4,5},{5,4},{6,7},{7,6},{8,9},{9,8},{10,11... | collective-permute-start | bytes 442376 | tf_op jit(solution)/shard_map/ppermute | solution.py:857
  221.1 14.0 %collective-permute-start.22 = (bf16[96,768]{1,0:T(8,128)(2,1)S(1)}, bf16[96,768]{1,0:T(8,128)(2,1)S(1)}, u32[]{:S(2)}, u32[]{:S(2)}) collective-permute-start(bf16[96,768]{1,0:T(8,128)(2,1)S(1)} %get-tuple-element.196), channel_id=1, source_target_pairs={{0,2},{1,3},{2,0},{3,1},{4,6},{5,7},{6,4},{7,5},{8,10},{9,11},{10,... | collective-permute-start | bytes 442376 | tf_op jit(solution)/shard_map/ppermute | solution.py:857
  224.0 12.5 %collective-permute-start.23 = (bf16[96,768]{1,0:T(8,128)(2,1)S(1)}, bf16[96,768]{1,0:T(8,128)(2,1)S(1)}, u32[]{:S(2)}, u32[]{:S(2)}) collective-permute-start(bf16[96,768]{1,0:T(8,128)(2,1)S(1)} %get-tuple-element.197), channel_id=1, source_target_pairs={{0,3},{1,2},{2,1},{3,0},{4,7},{5,6},{6,5},{7,4},{8,11},{9,10},{10,... | collective-permute-start | bytes 442376 | tf_op jit(solution)/shard_map/ppermute | solution.py:857
  225.4 12.8 %collective-permute-start.24 = (bf16[256,384]{1,0:T(8,128)(2,1)S(1)}, bf16[256,384]{1,0:T(8,128)(2,1)S(1)}, u32[]{:S(2)}, u32[]{:S(2)}) collective-permute-start(bf16[256,384]{1,0:T(8,128)(2,1)S(1)} %copy-done.48), channel_id=1, source_target_pairs={{0,1},{1,0},{2,3},{3,2},{4,5},{5,4},{6,7},{7,6},{8,9},{9,8},{10,11... | collective-permute-start | bytes 589832 | tf_op jit(solution)/shard_map/ppermute | solution.py:857
  225.4 38.4 %collective-permute-start.20 = (bf16[4,2,96,384]{3,2,1,0:T(8,128)(2,1)S(1)}, bf16[4,2,96,384]{3,2,1,0:T(8,128)(2,1)S(1)}, u32[]{:S(2)}, u32[]{:S(2)}) collective-permute-start(bf16[4,2,96,384]{3,2,1,0:T(8,128)(2,1)S(1)} %copy-done.36), channel_id=1, source_target_pairs={{0,4},{4,0},{8,12},{12,8},{16,20},{20,16},{24,28},{28,24},{1,5},{5... | collective-permute-start | bytes 1769480 | tf_op jit(solution)/shard_map/ppermute | solution.py:857
  230.5 25.5 %collective-permute-start.25 = (bf16[256,384]{1,0:T(8,128)(2,1)}, bf16[256,384]{1,0:T(8,128)(2,1)S(1)}, u32[]{:S(2)}, u32[]{:S(2)}) collective-permute-start(bf16[256,384]{1,0:T(8,128)(2,1)} %get-tuple-element.200), channel_id=1, source_target_pairs={{0,2},{1,3},{2,0},{3,1},{4,6},{5,7},{6,4},{7,5},{8,10},{9,11},{10,... | collective-permute-start | bytes 589832 | tf_op jit(solution)/shard_map/ppermute | solution.py:857
  235.0 33.3 %collective-permute-start.49 = (bf16[8,96,384]{2,1,0:T(8,128)(2,1)S(1)}, bf16[8,96,384]{2,1,0:T(8,128)(2,1)S(1)}, u32[]{:S(2)}, u32[]{:S(2)}) collective-permute-start(bf16[8,96,384]{2,1,0:T(8,128)(2,1)S(1)} %get-tuple-element.231), channel_id=1, source_target_pairs={{0,8},{4,12},{8,0},{12,4},{16,24},{20,28},{24,16},{28,20},{1,9},{5... | collective-permute-start | bytes 1769480 | tf_op jit(solution)/shard_map/ppermute | solution.py:857
  236.5 33.2 %collective-permute-start.50 = (bf16[8,96,384]{2,1,0:T(8,128)(2,1)S(1)}, bf16[8,96,384]{2,1,0:T(8,128)(2,1)S(1)}, u32[]{:S(2)}, u32[]{:S(2)}) collective-permute-start(bf16[8,96,384]{2,1,0:T(8,128)(2,1)S(1)} %get-tuple-element.232), channel_id=1, source_target_pairs={{0,16},{4,20},{8,24},{12,28},{16,0},{20,4},{24,8},{28,12},{1,17},{... | collective-permute-start | bytes 1769480 | tf_op jit(solution)/shard_map/ppermute | solution.py:857
  238.2 17.8 %copy-start.16 = (bf16[256,384]{1,0:T(8,128)(2,1)}, bf16[256,384]{1,0:T(8,128)(2,1)S(1)}, u32[]{:S(2)}) copy-start(bf16[256,384]{1,0:T(8,128)(2,1)S(1)} %collective-permute-done.24.refs_1_) | copy-start | bytes 589828
  238.2 31.6 %collective-permute-start.51 = (bf16[8,96,384]{2,1,0:T(8,128)(2,1)S(1)}, bf16[8,96,384]{2,1,0:T(8,128)(2,1)S(1)}, u32[]{:S(2)}, u32[]{:S(2)}) collective-permute-start(bf16[8,96,384]{2,1,0:T(8,128)(2,1)S(1)} %get-tuple-element.233), channel_id=1, source_target_pairs={{0,24},{4,28},{8,16},{12,20},{16,8},{20,12},{24,0},{28,4},{1,25},{... | collective-permute-start | bytes 1769480 | tf_op jit(solution)/shard_map/ppermute | solution.py:857
  240.6 15.4 %copy-start.47 = (bf16[256,384]{1,0:T(8,128)(2,1)S(1)}, bf16[256,384]{1,0:T(8,128)(2,1)}, u32[]{:S(2)}) copy-start(bf16[256,384]{1,0:T(8,128)(2,1)} %get-tuple-element.201) | copy-start | bytes 589828
  256.0 7.8 %collective-permute-start.26 = (bf16[256,384]{1,0:T(8,128)(2,1)S(1)}, bf16[256,384]{1,0:T(8,128)(2,1)S(1)}, u32[]{:S(2)}, u32[]{:S(2)}) collective-permute-start(bf16[256,384]{1,0:T(8,128)(2,1)S(1)} %copy-done.47), channel_id=1, source_target_pairs={{0,3},{1,2},{2,1},{3,0},{4,7},{5,6},{6,5},{7,4},{8,11},{9,10},{10,... | collective-permute-start | bytes 589832 | tf_op jit(solution)/shard_map/ppermute | solution.py:857
  263.8 22.4 %collective-permute-start.27 = (bf16[96,768]{1,0:T(8,128)(2,1)S(1)}, bf16[96,768]{1,0:T(8,128)(2,1)S(1)}, u32[]{:S(2)}, u32[]{:S(2)}) collective-permute-start(bf16[96,768]{1,0:T(8,128)(2,1)S(1)} %add_convert_fusion.23), channel_id=1, source_target_pairs={{0,1},{1,0},{2,3},{3,2},{4,5},{5,4},{6,7},{7,6},{8,9},{9,8},{10,11... | collective-permute-start | bytes 442376 | tf_op jit(solution)/shard_map/ppermute | solution.py:857
  267.1 20.6 %collective-permute-start.28 = (bf16[96,768]{1,0:T(8,128)(2,1)S(1)}, bf16[96,768]{1,0:T(8,128)(2,1)S(1)}, u32[]{:S(2)}, u32[]{:S(2)}) collective-permute-start(bf16[96,768]{1,0:T(8,128)(2,1)S(1)} %add_convert_fusion.23), channel_id=1, source_target_pairs={{0,2},{1,3},{2,0},{3,1},{4,6},{5,7},{6,4},{7,5},{8,10},{9,11},{10,... | collective-permute-start | bytes 442376 | tf_op jit(solution)/shard_map/ppermute | solution.py:857
  268.3 19.4 %collective-permute-start.29 = (bf16[96,768]{1,0:T(8,128)(2,1)S(1)}, bf16[96,768]{1,0:T(8,128)(2,1)S(1)}, u32[]{:S(2)}, u32[]{:S(2)}) collective-permute-start(bf16[96,768]{1,0:T(8,128)(2,1)S(1)} %add_convert_fusion.23), channel_id=1, source_target_pairs={{0,3},{1,2},{2,1},{3,0},{4,7},{5,6},{6,5},{7,4},{8,11},{9,10},{10,... | collective-permute-start | bytes 442376 | tf_op jit(solution)/shard_map/ppermute | solution.py:857
  270.1 30.0 %collective-permute-start.52 = (bf16[2,96,384]{2,1,0:T(8,128)(2,1)S(1)}, bf16[2,96,384]{2,1,0:T(8,128)(2,1)S(1)}, u32[]{:S(2)}, u32[]{:S(2)}) collective-permute-start(bf16[2,96,384]{2,1,0:T(8,128)(2,1)S(1)} %get-tuple-element.283), channel_id=1, source_target_pairs={{0,1},{1,0},{2,3},{3,2},{4,5},{5,4},{6,7},{7,6},{8,9},{9,8},{10,11... | collective-permute-start | bytes 442376 | tf_op jit(solution)/shard_map/ppermute | solution.py:857
  271.0 29.1 %collective-permute-start.53 = (bf16[2,96,384]{2,1,0:T(8,128)(2,1)S(1)}, bf16[2,96,384]{2,1,0:T(8,128)(2,1)S(1)}, u32[]{:S(2)}, u32[]{:S(2)}) collective-permute-start(bf16[2,96,384]{2,1,0:T(8,128)(2,1)S(1)} %get-tuple-element.285), channel_id=1, source_target_pairs={{0,2},{1,3},{2,0},{3,1},{4,6},{5,7},{6,4},{7,5},{8,10},{9,11},{10,... | collective-permute-start | bytes 442376 | tf_op jit(solution)/shard_map/ppermute | solution.py:857
  286.2 13.9 %collective-permute-start.54 = (bf16[2,96,384]{2,1,0:T(8,128)(2,1)S(1)}, bf16[2,96,384]{2,1,0:T(8,128)(2,1)S(1)}, u32[]{:S(2)}, u32[]{:S(2)}) collective-permute-start(bf16[2,96,384]{2,1,0:T(8,128)(2,1)S(1)} %get-tuple-element.284), channel_id=1, source_target_pairs={{0,3},{1,2},{2,1},{3,0},{4,7},{5,6},{6,5},{7,4},{8,11},{9,10},{10,... | collective-permute-start | bytes 442376 | tf_op jit(solution)/shard_map/ppermute | solution.py:857
  295.3 4.4 %collective-permute-start.33 = (f32[69,128]{1,0:T(8,128)S(1)}, f32[69,128]{1,0:T(8,128)S(1)}, u32[]{:S(2)}, u32[]{:S(2)}) collective-permute-start(f32[69,128]{1,0:T(8,128)S(1)} %bitcast.211), channel_id=1, source_target_pairs={{0,4},{4,0},{8,12},{12,8},{16,20},{20,16},{24,28},{28,24},{1,5},{5... | collective-permute-start | bytes 105992 | tf_op jit(solution)/shard_map/ppermute | solution.py:857
  299.7 5.0 %collective-permute-start.34 = (f32[69,128]{1,0:T(8,128)S(1)}, f32[69,128]{1,0:T(8,128)S(1)}, u32[]{:S(2)}, u32[]{:S(2)}) collective-permute-start(f32[69,128]{1,0:T(8,128)S(1)} %bitcast_add_fusion), channel_id=1, source_target_pairs={{0,8},{4,12},{8,0},{12,4},{16,24},{20,28},{24,16},{28,20},{1,9},{5... | collective-permute-start | bytes 105992 | tf_op jit(solution)/shard_map/ppermute | solution.py:857
  300.2 14.4 %collective-permute-start.55 = (bf16[2,96,384]{2,1,0:T(8,128)(2,1)S(1)}, bf16[2,96,384]{2,1,0:T(8,128)(2,1)S(1)}, u32[]{:S(2)}, u32[]{:S(2)}) collective-permute-start(bf16[2,96,384]{2,1,0:T(8,128)(2,1)S(1)} %fusion.10), channel_id=1, source_target_pairs={{0,1},{1,0},{2,3},{3,2},{4,5},{5,4},{6,7},{7,6},{8,9},{9,8},{10,11... | collective-permute-start | bytes 442376 | tf_op jit(solution)/shard_map/ppermute | solution.py:857
  300.4 16.5 %collective-permute-start.56 = (bf16[2,96,384]{2,1,0:T(8,128)(2,1)S(1)}, bf16[2,96,384]{2,1,0:T(8,128)(2,1)S(1)}, u32[]{:S(2)}, u32[]{:S(2)}) collective-permute-start(bf16[2,96,384]{2,1,0:T(8,128)(2,1)S(1)} %fusion.10), channel_id=1, source_target_pairs={{0,2},{1,3},{2,0},{3,1},{4,6},{5,7},{6,4},{7,5},{8,10},{9,11},{10,... | collective-permute-start | bytes 442376 | tf_op jit(solution)/shard_map/ppermute | solution.py:857
  303.3 13.5 %collective-permute-start.57 = (bf16[2,96,384]{2,1,0:T(8,128)(2,1)S(1)}, bf16[2,96,384]{2,1,0:T(8,128)(2,1)S(1)}, u32[]{:S(2)}, u32[]{:S(2)}) collective-permute-start(bf16[2,96,384]{2,1,0:T(8,128)(2,1)S(1)} %fusion.10), channel_id=1, source_target_pairs={{0,3},{1,2},{2,1},{3,0},{4,7},{5,6},{6,5},{7,4},{8,11},{9,10},{10,... | collective-permute-start | bytes 442376 | tf_op jit(solution)/shard_map/ppermute | solution.py:857
  304.7 12.4 %collective-permute-start.39 = (bf16[4,3,96,384]{3,2,1,0:T(8,128)(2,1)S(1)}, bf16[4,3,96,384]{3,2,1,0:T(8,128)(2,1)S(1)}, u32[]{:S(2)}, u32[]{:S(2)}) collective-permute-start(bf16[4,3,96,384]{3,2,1,0:T(8,128)(2,1)S(1)} %copy-done.35), channel_id=1, source_target_pairs={{0,4},{4,0},{8,12},{12,8},{16,20},{20,16},{24,28},{28,24},{1,5},{5... | collective-permute-start | bytes 2654216 | tf_op jit(solution)/shard_map/ppermute | solution.py:857
  304.7 4.0 %collective-permute-start.35 = (f32[69,128]{1,0:T(8,128)S(1)}, f32[69,128]{1,0:T(8,128)S(1)}, u32[]{:S(2)}, u32[]{:S(2)}) collective-permute-start(f32[69,128]{1,0:T(8,128)S(1)} %fusion.45), channel_id=1, source_target_pairs={{0,16},{4,20},{8,24},{12,28},{16,0},{20,4},{24,8},{28,12},{1,17},{... | collective-permute-start | bytes 105992 | tf_op jit(solution)/shard_map/ppermute | solution.py:857
  308.7 5.9 %collective-permute-start.36 = (f32[69,128]{1,0:T(8,128)S(1)}, f32[69,128]{1,0:T(8,128)S(1)}, u32[]{:S(2)}, u32[]{:S(2)}) collective-permute-start(f32[69,128]{1,0:T(8,128)S(1)} %add.274), channel_id=1, source_target_pairs={{0,1},{1,0},{2,3},{3,2},{4,5},{5,4},{6,7},{7,6},{8,9},{9,8},{10,11... | collective-permute-start | bytes 105992 | tf_op jit(solution)/shard_map/ppermute | solution.py:857
  314.6 53.4 %collective-permute-start.30 = (bf16[256,768]{1,0:T(8,128)(2,1)S(1)}, bf16[256,768]{1,0:T(8,128)(2,1)S(1)}, u32[]{:S(2)}, u32[]{:S(2)}) collective-permute-start(bf16[256,768]{1,0:T(8,128)(2,1)S(1)} %copy-done.40), channel_id=1, source_target_pairs={{0,1},{1,0},{2,3},{3,2},{4,5},{5,4},{6,7},{7,6},{8,9},{9,8},{10,11... | collective-permute-start | bytes 1179656 | tf_op jit(solution)/shard_map/ppermute | solution.py:857
  314.7 12.1 %collective-permute-start.37 = (f32[69,128]{1,0:T(8,128)S(1)}, f32[69,128]{1,0:T(8,128)S(1)}, u32[]{:S(2)}, u32[]{:S(2)}) collective-permute-start(f32[69,128]{1,0:T(8,128)S(1)} %add.275), channel_id=1, source_target_pairs={{0,3},{1,2},{2,1},{3,0},{4,7},{5,6},{6,5},{7,4},{8,11},{9,10},{10,... | collective-permute-start | bytes 105992 | tf_op jit(solution)/shard_map/ppermute | solution.py:857
  317.4 14.7 %collective-permute-start.40 = (bf16[7,96,384]{2,1,0:T(8,128)(2,1)S(1)}, bf16[7,96,384]{2,1,0:T(8,128)(2,1)S(1)}, u32[]{:S(2)}, u32[]{:S(2)}) collective-permute-start(bf16[7,96,384]{2,1,0:T(8,128)(2,1)S(1)} %pad_maximum_fusion), channel_id=1, source_target_pairs={{0,8},{4,12},{8,0},{12,4},{16,24},{20,28},{24,16},{28,20},{1,9},{5... | collective-permute-start | bytes 1548296 | tf_op jit(solution)/shard_map/ppermute | solution.py:857
  319.2 24.1 %collective-permute-start.41 = (bf16[7,96,384]{2,1,0:T(8,128)(2,1)S(1)}, bf16[7,96,384]{2,1,0:T(8,128)(2,1)S(1)}, u32[]{:S(2)}, u32[]{:S(2)}) collective-permute-start(bf16[7,96,384]{2,1,0:T(8,128)(2,1)S(1)} %pad_maximum_fusion.1), channel_id=1, source_target_pairs={{0,16},{4,20},{8,24},{12,28},{16,0},{20,4},{24,8},{28,12},{1,17},{... | collective-permute-start | bytes 1548296 | tf_op jit(solution)/shard_map/ppermute | solution.py:857
  320.9 22.5 %collective-permute-start.42 = (bf16[7,96,384]{2,1,0:T(8,128)(2,1)S(1)}, bf16[7,96,384]{2,1,0:T(8,128)(2,1)S(1)}, u32[]{:S(2)}, u32[]{:S(2)}) collective-permute-start(bf16[7,96,384]{2,1,0:T(8,128)(2,1)S(1)} %pad_maximum_fusion.2), channel_id=1, source_target_pairs={{0,24},{4,28},{8,16},{12,20},{16,8},{20,12},{24,0},{28,4},{1,25},{... | collective-permute-start | bytes 1548296 | tf_op jit(solution)/shard_map/ppermute | solution.py:857
  326.7 43.9 %collective-permute-start.31 = (bf16[256,768]{1,0:T(8,128)(2,1)S(1)}, bf16[256,768]{1,0:T(8,128)(2,1)S(1)}, u32[]{:S(2)}, u32[]{:S(2)}) collective-permute-start(bf16[256,768]{1,0:T(8,128)(2,1)S(1)} %copy-done.39), channel_id=1, source_target_pairs={{0,2},{1,3},{2,0},{3,1},{4,6},{5,7},{6,4},{7,5},{8,10},{9,11},{10,... | collective-permute-start | bytes 1179656 | tf_op jit(solution)/shard_map/ppermute | solution.py:857
  343.7 7.6 %collective-permute-start.43 = (bf16[7,24,384]{2,1,0:T(8,128)(2,1)S(1)}, bf16[7,24,384]{2,1,0:T(8,128)(2,1)S(1)}, u32[]{:S(2)}, u32[]{:S(2)}) collective-permute-start(bf16[7,24,384]{2,1,0:T(8,128)(2,1)S(1)} %get-tuple-element.302), channel_id=1, source_target_pairs={{0,1},{1,0},{2,3},{3,2},{4,5},{5,4},{6,7},{7,6},{8,9},{9,8},{10,11... | collective-permute-start | bytes 387080 | tf_op jit(solution)/shard_map/ppermute | solution.py:857
  344.6 19.5 %collective-permute-start.44 = (bf16[7,24,384]{2,1,0:T(8,128)(2,1)S(1)}, bf16[7,24,384]{2,1,0:T(8,128)(2,1)S(1)}, u32[]{:S(2)}, u32[]{:S(2)}) collective-permute-start(bf16[7,24,384]{2,1,0:T(8,128)(2,1)S(1)} %get-tuple-element.304), channel_id=1, source_target_pairs={{0,2},{1,3},{2,0},{3,1},{4,6},{5,7},{6,4},{7,5},{8,10},{9,11},{10,... | collective-permute-start | bytes 387080 | tf_op jit(solution)/shard_map/ppermute | solution.py:857
  346.1 17.9 %collective-permute-start.45 = (bf16[7,24,384]{2,1,0:T(8,128)(2,1)S(1)}, bf16[7,24,384]{2,1,0:T(8,128)(2,1)S(1)}, u32[]{:S(2)}, u32[]{:S(2)}) collective-permute-start(bf16[7,24,384]{2,1,0:T(8,128)(2,1)S(1)} %get-tuple-element.303), channel_id=1, source_target_pairs={{0,3},{1,2},{2,1},{3,0},{4,7},{5,6},{6,5},{7,4},{8,11},{9,10},{10,... | collective-permute-start | bytes 387080 | tf_op jit(solution)/shard_map/ppermute | solution.py:857
  351.3 19.2 %collective-permute-start.32 = (bf16[256,768]{1,0:T(8,128)(2,1)S(1)}, bf16[256,768]{1,0:T(8,128)(2,1)S(1)}, u32[]{:S(2)}, u32[]{:S(2)}) collective-permute-start(bf16[256,768]{1,0:T(8,128)(2,1)S(1)} %copy-done.38), channel_id=1, source_target_pairs={{0,3},{1,2},{2,1},{3,0},{4,7},{5,6},{6,5},{7,4},{8,11},{9,10},{10,... | collective-permute-start | bytes 1179656 | tf_op jit(solution)/shard_map/ppermute | solution.py:857
  364.2 12.6 %collective-permute-start.46 = (bf16[7,24,384]{2,1,0:T(8,128)(2,1)S(1)}, bf16[7,24,384]{2,1,0:T(8,128)(2,1)S(1)}, u32[]{:S(2)}, u32[]{:S(2)}) collective-permute-start(bf16[7,24,384]{2,1,0:T(8,128)(2,1)S(1)} %fusion.13), channel_id=1, source_target_pairs={{0,1},{1,0},{2,3},{3,2},{4,5},{5,4},{6,7},{7,6},{8,9},{9,8},{10,11... | collective-permute-start | bytes 387080 | tf_op jit(solution)/shard_map/ppermute | solution.py:857
  367.5 15.7 %collective-permute-start.47 = (bf16[7,24,384]{2,1,0:T(8,128)(2,1)S(1)}, bf16[7,24,384]{2,1,0:T(8,128)(2,1)S(1)}, u32[]{:S(2)}, u32[]{:S(2)}) collective-permute-start(bf16[7,24,384]{2,1,0:T(8,128)(2,1)S(1)} %fusion.13), channel_id=1, source_target_pairs={{0,2},{1,3},{2,0},{3,1},{4,6},{5,7},{6,4},{7,5},{8,10},{9,11},{10,... | collective-permute-start | bytes 387080 | tf_op jit(solution)/shard_map/ppermute | solution.py:857
  368.0 15.3 %collective-permute-start.48 = (bf16[7,24,384]{2,1,0:T(8,128)(2,1)S(1)}, bf16[7,24,384]{2,1,0:T(8,128)(2,1)S(1)}, u32[]{:S(2)}, u32[]{:S(2)}) collective-permute-start(bf16[7,24,384]{2,1,0:T(8,128)(2,1)S(1)} %fusion.13), channel_id=1, source_target_pairs={{0,3},{1,2},{2,1},{3,0},{4,7},{5,6},{6,5},{7,4},{8,11},{9,10},{10,... | collective-permute-start | bytes 387080 | tf_op jit(solution)/shard_map/ppermute | solution.py:857
  (43 other events, 251.9 us)

commit v3 on v0

--- a/solution.py
+++ b/solution.py
@@ -1,9 +1,527 @@
+import functools
+
 import jax
 import jax.numpy as jnp
 from jax import lax
+from jax.experimental import pallas as pl
+from jax.experimental.pallas import tpu as pltpu
 from jax.sharding import PartitionSpec as P
 
 HDIM = 64
+PAIR = 2 * HDIM
+BLK = 256
+LN2 = 0.6931471805599453
+LOG2E = 1.4426950408889634
+Q_SCALE = LOG2E * HDIM**-0.5
+BF16 = jnp.bfloat16
+F32 = jnp.float32
+VMEM_BYTES = 56 << 20
+CODE_ROWS = 16
+ATTN_GAIN, ATTN_SHIFT, OUT_BIAS, MLP_GAIN, MLP_SHIFT, DOWN_BIAS = (slice(n, n + 1) for n in range(6))
+
+
+def dot(left, right, left_dim, right_dim):
+    return lax.dot_general(
+        left, right, (((left_dim,), (right_dim,)), ((), ())), preferred_element_type=F32
+    )
+
+
+def nn(left, right):
+    return dot(left, right, 1, 0)
+
+
+def nt(left, right):
+    return dot(left, right, 1, 1)
+
+
+def tn(left, right):
+    return dot(left, right, 0, 0)
+
+
+def call(kernel, name, grid, in_specs, out_specs, out_shape, scratch=(), flops=0, moved=0, aliases=None):
+    return pl.pallas_call(
+        kernel,
+        name=name,
+        grid_spec=pltpu.PrefetchScalarGridSpec(
+            num_scalar_prefetch=1,
+            grid=grid,
+            in_specs=in_specs,
+            out_specs=out_specs,
+            scratch_shapes=list(scratch),
+        ),
+        out_shape=out_shape,
+        input_output_aliases=aliases or {},
+        cost_estimate=pl.CostEstimate(flops=flops, bytes_accessed=moved, transcendentals=0),
+        compiler_params=pltpu.CompilerParams(vmem_limit_bytes=VMEM_BYTES),
+    )
+
+
+def shape(dims, dtype=BF16):
+    return jax.ShapeDtypeStruct(dims, dtype)
+
+
+def whole(dims):
+    return pl.BlockSpec(dims, lambda *_: (0,) * len(dims))
+
+
+def once(dims):
+    return pl.BlockSpec(dims, lambda *_: (0,) * len(dims), pipeline_mode=pl.Buffered(1))
+
+
+def standardize(values):
+    center = values - jnp.mean(values, axis=1, keepdims=True)
+    rate = lax.rsqrt(jnp.mean(center * center, axis=1, keepdims=True) + EPSILON)
+    return center * rate, rate
+
+
+def standardize_back(grad, unit, rate):
+    mean_grad = jnp.mean(grad, axis=1, keepdims=True)
+    mean_dot = jnp.mean(grad * unit, axis=1, keepdims=True)
+    return rate * (grad - mean_grad - unit * mean_dot)
+
+
+def column_sums(values):
+    return jnp.sum(values, axis=0, keepdims=True)
+
+
+def ways(core):
+    return 0, 1 + 2 * core, 3 - 2 * core, 2
+
+
+def block_rows(place, d, size):
+    return pl.ds(pl.multiple_of((place ^ d) * size, size), size)
+
+
+def each_way(at_ref, refs):
+    return [(block_rows(at_ref[0], d, ref.shape[0]), ref) for d, ref in zip(ways(at_ref[1]), refs)]
+
+
+def deal_out(at_ref, source_ref, own_ref, away_ref, far_ref):
+    place, part = at_ref[0], own_ref.shape[0]
+    own, near, far, across = (source_ref[block_rows(place, d, part), :] for d in ways(at_ref[1]))
+    own_ref[...] = own.astype(own_ref.dtype)
+    away_ref[0] = near.astype(own_ref.dtype)
+    away_ref[1] = across.astype(own_ref.dtype)
+    far_ref[...] = far.astype(own_ref.dtype)
+
+
+def piece_specs(pieces, rows, cols, at=lambda *index: (0, 0)):
+    specs, arrays = [], []
+    for piece in pieces:
+        if isinstance(piece, tuple):
+            array, number = piece
+            specs.append(pl.BlockSpec((None, rows, cols), lambda *index, n=number: (n,) + at(*index)))
+        else:
+            array = piece
+            specs.append(pl.BlockSpec((rows, cols), at))
+        arrays.append(array)
+    return specs, arrays
+
+
+def project_kernel(at_ref, x_ref, vec_ref, w_ref, affine_ref, *refs):
+    row_ref, normed_ref, proj_ref, code_ref = refs[-4:]
+    part = row_ref.shape[0]
+    tokens = x_ref[:part, :]
+    unit, _ = standardize(tokens.astype(F32))
+    normed = (unit * vec_ref[ATTN_GAIN] + vec_ref[ATTN_SHIFT]).astype(BF16)
+    row_ref[...] = tokens
+    normed_ref[...] = normed
+    proj_ref[...] = ((nn(normed, w_ref[...]) + affine_ref[0:1, :]) * affine_ref[1:2, :]).astype(BF16)
+    code_ref[...] = x_ref[part : part + CODE_ROWS, :part].astype(F32)[:8].astype(jnp.int32)
+
+
+def project(at, way, piece, vecs, w, affine, length, so_far):
+    part, width = length // 4, piece.shape[1]
+    cols = w.shape[1]
+    place = lambda at: at[0] ^ ways(at[1])[way]
+    block = lambda n: pl.BlockSpec((part, n), lambda i, at: (place(at), 0))
+    held = [pl.BlockSpec(memory_space=pl.ANY)] * len(so_far)
+    return call(
+        project_kernel,
+        "project",
+        (1,),
+        [whole((part + CODE_ROWS, width)), whole(vecs.shape), whole((width, cols)), whole(affine.shape)] + held,
+        [block(width), block(width), block(cols), pl.BlockSpec((8, part), lambda i, at: (0, place(at)))],
+        [shape((length, width)), shape((length, width)), shape((length, cols)), shape((8, length), jnp.int32)],
+        flops=2 * part * width * cols,
+        moved=2 * (part * (3 * width + cols) + width * cols),
+        aliases={5 + n: n for n in range(len(so_far))},
+    )(at, piece, vecs, w, affine, *so_far)
+
+
+def fill_bias(code_ref, bias_ref):
+    length = code_ref.shape[1]
+    code = code_ref[0:1, :]
+    column = jnp.transpose(jnp.broadcast_to(code, (128, length)))
+    for i in range(length // BLK):
+        q_doc = column[i * BLK : (i + 1) * BLK, :1] >> 1
+        for j in range(i + 1):
+            k_code = code[:, j * BLK : (j + 1) * BLK]
+            same = q_doc == (k_code >> 1)
+            real = (k_code & 1) == 1
+            if i == j:
+                row_at = lax.broadcasted_iota(jnp.int32, (BLK, BLK), 0)
+                col_at = lax.broadcasted_iota(jnp.int32, (BLK, BLK), 1)
+                allowed = same & (col_at <= row_at) & (real | (col_at == row_at))
+            else:
+                allowed = same & real
+            bias_ref[i * BLK : (i + 1) * BLK, j * BLK : (j + 1) * BLK] = jnp.where(allowed, 0.0, MASKED)
+
+
+def halves(pair, other):
+    first = lax.broadcasted_iota(jnp.int32, pair.shape, 1) < HDIM
+    return jnp.where(first, pair, other), jnp.where(first, other, pair)
+
+
+def gather_values(me_ref, v_refs, value_ref):
+    if len(v_refs) == 1:
+        return v_refs[0][...]
+    for rows, ref in each_way(me_ref, v_refs):
+        value_ref[rows, :] = ref[...]
+    return value_ref[...]
+
+
+def forward_kernel(count, me_ref, code_ref, q_ref, k_ref, *refs):
+    v_refs, (o_ref, lse_ref, bias_ref, value_ref) = refs[:count], refs[count:]
+
+    @pl.when(pl.program_id(0) == 0)
+    def _():
+        fill_bias(code_ref, bias_ref)
+
+    length = q_ref.shape[0]
+    v_pair = gather_values(me_ref, v_refs, value_ref)
+    k_pair = k_ref[...]
+    keys = halves(k_pair, jnp.zeros_like(k_pair))
+    vals = halves(v_pair, jnp.ones_like(v_pair))
+    first = lax.broadcasted_iota(jnp.int32, (BLK, PAIR), 1) < HDIM
+    for i in range(length // BLK):
+        end = (i + 1) * BLK
+        rows = slice(i * BLK, end)
+        q = q_ref[rows, :]
+        outs, lses = [], []
+        for h in range(2):
+            scores = nt(q, keys[h][:end]) + bias_ref[rows, :end]
+            top = jnp.max(scores, axis=1, keepdims=True)
+            weights = jnp.exp2(scores - top).astype(BF16)
+            mixed = nn(weights, vals[h][:end])
+            total = pltpu.roll(mixed, HDIM, 1)
+            outs.append(mixed / total)
+            lses.append(top + jnp.log2(total))
+        o_ref[rows, :] = jnp.where(first, outs[0], outs[1]).astype(BF16)
+        lse_ref[rows, :] = jnp.where(first, lses[0], lses[1])
+
+
+def backward_kernel(count, first_call, last_call, split, me_ref, code_ref, q_ref, k_ref, *refs):
+    refs = list(refs)
+    take = lambda n: [refs.pop(0) for _ in range(n)]
+    v_refs = take(count)
+    o_ref, do_ref, lse_ref, normed_ref = take(4)
+    w_refs = take(2 if split else 3)
+    before_ref = None if first_call else take(1)[0]
+    x_ref, vec_ref, d_att_ref = take(3) if last_call else (None, None, None)
+    send_ref, keep_ref, bias_sums_ref = take(3)
+    piece_refs = take(3) if split else []
+    if last_call:
+        *y_refs, sums_ref = take(4)
+    else:
+        (after_ref,) = take(1)
+    bias_ref, value_ref, dkt_ref, dvt_ref, d_ref, w_ref, acc_ref, stage_ref = refs
+    step = pl.program_id(0)
+    lane = lambda n: slice(n * PAIR, (n + 1) * PAIR)
+
+    @pl.when(step == 0)
+    def _():
+        fill_bias(code_ref, bias_ref)
+        acc_ref[...] = jnp.zeros_like(acc_ref) if first_call else before_ref[...]
+
+    length = q_ref.shape[0]
+    v_pair = gather_values(me_ref, v_refs, value_ref)
+    k_pair = k_ref[...]
+    zero = jnp.zeros_like(k_pair)
+    keys = halves(k_pair, zero)
+    vals = halves(v_pair, zero)
+    first = lax.broadcasted_iota(jnp.int32, (BLK, PAIR), 1) < HDIM
+    blocks = length // BLK
+    for i in reversed(range(blocks)):
+        end = (i + 1) * BLK
+        rows = slice(i * BLK, end)
+        q, do = q_ref[rows, :], do_ref[rows, :]
+        q_t, do_t = jnp.transpose(q), jnp.transpose(do)
+        prod = do.astype(F32) * o_ref[rows, :].astype(F32)
+        dq = None
+        for h in range(2):
+            head = slice(h * HDIM, (h + 1) * HDIM)
+            lse = lse_ref[rows, h * HDIM : h * HDIM + 1]
+            mine = first if h == 0 else ~first
+            delta = jnp.sum(jnp.where(mine, prod, 0.0), axis=1, keepdims=True)
+            probs = jnp.exp2(nt(q, keys[h][:end]) + bias_ref[rows, :end] - lse)
+            d_scores = (probs * (nt(do, vals[h][:end]) - delta)).astype(BF16)
+            part = nn(d_scores, keys[h][:end])
+            dq = part if dq is None else dq + part
+            dv = nn(do_t[head], probs.astype(BF16))
+            dk = nn(q_t[head], d_scores)
+            if i == blocks - 1:
+                dvt_ref[head, :] = dv
+                dkt_ref[head, :] = dk
+            else:
+                dvt_ref[head, :end] += dv
+                dkt_ref[head, :end] += dk
+        d_ref[rows, lane(0)] = (dq * HDIM**-0.5).astype(BF16)
+    d_ref[:, lane(1)] = jnp.transpose(dkt_ref[...] * LN2).astype(BF16)
+    dv = jnp.transpose(dvt_ref[...]).astype(BF16)
+    if split:
+        value_ref[...] = dv
+        deal_out(me_ref, value_ref, *piece_refs)
+    else:
+        d_ref[:, lane(2)] = dv
+    for n, ref in enumerate(w_refs):
+        w_ref[:, lane(n)] = ref[...]
+    grad = d_ref[...]
+    bias_sums_ref[0] = column_sums(grad.astype(F32))
+    acc_ref[...] += nt(grad, w_ref[...])
+    store_units(tn(normed_ref[...], grad), me_ref[1], stage_ref, send_ref, keep_ref, (0,))
+
+    @pl.when(step == pl.num_programs(0) - 1)
+    def _():
+        if last_call:
+            total = acc_ref[...]
+            unit, rate = standardize(x_ref[...].astype(F32))
+            sums_ref[0:1, :] = column_sums(total * unit)
+            sums_ref[1:2, :] = column_sums(total)
+            acc_ref[...] = d_att_ref[...].astype(F32) + standardize_back(total * vec_ref[ATTN_GAIN], unit, rate)
+            deal_out(me_ref, acc_ref, *y_refs)
+        else:
+            after_ref[...] = acc_ref[...]
+
+
+def pair_specs(length, offset):
+    return pl.BlockSpec((length, PAIR), lambda p, me: (0, p + offset))
+
+
+def value_specs(values, length, offset):
+    if len(values) == 1:
+        return [pair_specs(length, offset)], values
+    return piece_specs(values, length // 4, PAIR, lambda p, me: (0, p))
+
+
+def attend(me, code, proj, values, q_at, k_at, v_at, pairs, name):
+    length = proj.shape[0]
+    v_specs, v_arrays = value_specs(values, length, v_at)
+    return call(
+        functools.partial(forward_kernel, len(values)),
+        name,
+        (pairs,),
+        [whole((8, length)), pair_specs(length, q_at), pair_specs(length, k_at)]
+        + v_specs,
+        [pair_specs(length, 0)] * 2,
+        [shape((length, pairs * PAIR)), shape((length, pairs * PAIR), F32)],
+        [pltpu.VMEM((length, length), F32), pltpu.VMEM((length, PAIR), BF16)],
+        flops=pairs * 24 * length * length * PAIR,
+        moved=pairs * length * PAIR * 12,
+    )(me, code, proj, proj, *v_arrays)
+
+
+def attend_back(at, code, proj, values, o, do, lse, normed, w, pair, pairs, o_at, before, last, name):
+    length, width = normed.shape
+    count = width // PAIR
+    split = len(values) > 1
+    units = 2 if split else 3
+    cols = units * PAIR
+    strip, part = width // 8, length // 4
+    full = once((length, width))
+    v_specs, v_arrays = value_specs(values, length, 2 * count + pair)
+    w_spec = lambda offset: pl.BlockSpec((width, PAIR), lambda p, at: (0, p + offset))
+    grads = pl.BlockSpec((4, 1, units, strip, PAIR), lambda p, at: (0, p, 0, 0, 0))
+    in_specs = (
+        [whole((8, length)), pair_specs(length, pair), pair_specs(length, count + pair)]
+        + v_specs
+        + [pair_specs(length, o_at), pair_specs(length, pair), pair_specs(length, o_at), full]
+        + [w_spec(n * count + pair) for n in range(units)]
+    )
+    args = [code, proj, proj, *v_arrays, o, do, lse, normed] + [w] * units
+    out_specs = [grads, grads, pl.BlockSpec((1, 1, cols), lambda p, at: (p, 0, 0))]
+    out_shape = [shape((4, pairs, units, strip, PAIR))] * 2 + [shape((pairs, 1, cols), F32)]
+    if before is not None:
+        in_specs.append(full)
+        args.append(before)
+    if last is not None:
+        in_specs += [full, once(last[1].shape), full]
+        args += last
+    if split:
+        one = pl.BlockSpec((part, PAIR), lambda p, at: (0, p))
+        out_specs += [one, pl.BlockSpec((2, part, PAIR), lambda p, at: (0, 0, p)), one]
+        out_shape += [shape((part, pairs * PAIR)), shape((2, part, pairs * PAIR)), shape((part, pairs * PAIR))]
+    if last is not None:
+        out_specs += [once((part, width)), once((2, part, width)), once((part, width)), once((8, width))]
+        out_shape += [shape((part, width)), shape((2, part, width)), shape((part, width)), shape((8, width), F32)]
+    else:
+        out_specs.append(full)
+        out_shape.append(shape((length, width), F32))
+    return call(
+        functools.partial(backward_kernel, len(values), before is None, last is not None, split),
+        name,
+        (pairs,),
+        in_specs,
+        out_specs,
+        out_shape,
+        [
+            pltpu.VMEM((length, length), F32),
+            pltpu.VMEM((length, PAIR), BF16),
+            pltpu.VMEM((PAIR, length), F32),
+            pltpu.VMEM((PAIR, length), F32),
+            pltpu.VMEM((length, cols), BF16),
+            pltpu.VMEM((width, cols), BF16),
+            pltpu.VMEM((length, width), F32),
+            pltpu.VMEM((4, 2, strip, cols), BF16),
+        ],
+        flops=pairs * (30 * length * length * PAIR + 4 * length * width * cols),
+        moved=pairs * length * PAIR * 18 + 12 * length * width,
+    )(at, *args)
+
+
+GELU_A = 0.7978845608028654
+GELU_B = 0.044715
+
+
+def split_store(grad, core, stage_ref, send_ref, keep_ref, lead):
+    stage_ref[...] = grad.astype(BF16).reshape(stage_ref.shape)
+    for j in range(4):
+        send_ref[(j,) + lead] = stage_ref[j, 1 - core]
+        keep_ref[(j,) + lead] = stage_ref[j, core]
+
+
+def store_units(grad, core, stage_ref, send_ref, keep_ref, lead):
+    stage_ref[...] = grad.astype(BF16).reshape(stage_ref.shape)
+    for u in range(stage_ref.shape[3] // PAIR):
+        lanes = slice(u * PAIR, (u + 1) * PAIR)
+        for j in range(4):
+            send_ref[(j,) + lead + (u,)] = stage_ref[j, 1 - core, :, lanes]
+            keep_ref[(j,) + lead + (u,)] = stage_ref[j, core, :, lanes]
+
+
+def feed_kernel(
+    at_ref, x_ref, oa_ref, ob_ref, d0_ref, d1_ref, d2_ref, d3_ref, wo_ref, vec_ref,
+    wu_ref, ub_ref, wd_ref,
+    y_own_ref, y_away_ref, y_far_ref, down_send_ref, down_keep_ref, up_send_ref, up_keep_ref, up_bias_ref,
+    d_att_ref, d_o_ref, sums_ref, out_send_ref, out_keep_ref,
+    dy_ref, middle_ref, normed_ref, y_ref, acc_ref, down_stage_ref, up_stage_ref, out_stage_ref,
+):
+    step = pl.program_id(0)
+    core = at_ref[1]
+
+    @pl.when(step == 0)
+    def _():
+        for rows, ref in each_way(at_ref, (d0_ref, d1_ref, d2_ref, d3_ref)):
+            dy_ref[rows, :] = ref[...]
+        half = oa_ref.shape[1]
+        middle = (
+            x_ref[...].astype(F32)
+            + nn(oa_ref[...], wo_ref[:half, :])
+            + nn(ob_ref[...], wo_ref[half:, :])
+            + vec_ref[OUT_BIAS]
+        )
+        middle_ref[...] = middle
+        unit, _ = standardize(middle)
+        normed_ref[...] = (unit * vec_ref[MLP_GAIN] + vec_ref[MLP_SHIFT]).astype(BF16)
+        y_ref[...] = middle + vec_ref[DOWN_BIAS]
+        acc_ref[...] = jnp.zeros_like(acc_ref)
+
+    dy = dy_ref[...]
+    pre = nn(normed_ref[...], wu_ref[...]) + ub_ref[...]
+    d_act = nt(dy, wd_ref[...])
+    square = pre * pre
+    curve = jnp.tanh(pre * (GELU_A + (GELU_A * GELU_B) * square))
+    half_up = 0.5 + 0.5 * curve
+    act = (pre * half_up).astype(BF16)
+    bend = (0.5 * GELU_A) + (1.5 * GELU_A * GELU_B) * square
+    d_pre = (d_act * (half_up + pre * bend * (1.0 - curve * curve))).astype(BF16)
+    y_ref[...] += nn(act, wd_ref[...])
+    down_stage_ref[...] = tn(act, dy).astype(BF16).reshape(down_stage_ref.shape)
+    down_send_ref[0] = down_stage_ref[1 - core]
+    down_keep_ref[0] = down_stage_ref[core]
+    up_bias_ref[...] = column_sums(d_pre.astype(F32))
+    acc_ref[...] += nt(d_pre, wu_ref[...])
+    split_store(tn(normed_ref[...], d_pre), core, up_stage_ref, up_send_ref, up_keep_ref, (0,))
+
+    @pl.when(step == pl.num_programs(0) - 1)
+    def _():
+        deal_out(at_ref, y_ref, y_own_ref, y_away_ref, y_far_ref)
+        total = acc_ref[...]
+        unit, rate = standardize(middle_ref[...])
+        dy_f = dy_ref[...].astype(F32)
+        sums_ref[0:1, :] = column_sums(total * unit)
+        sums_ref[1:2, :] = column_sums(total)
+        d_att = (dy_f + standardize_back(total * vec_ref[MLP_GAIN], unit, rate)).astype(BF16)
+        d_att_ref[...] = d_att
+        sums_ref[2:3, :] = column_sums(d_att.astype(F32))
+        sums_ref[3:4, :] = column_sums(dy_f)
+        d_o_ref[...] = nt(d_att, wo_ref[...]).astype(BF16)
+        grad = jnp.concatenate([tn(oa_ref[...], d_att), tn(ob_ref[...], d_att)], axis=0)
+        store_units(grad, core, out_stage_ref, out_send_ref, out_keep_ref, ())
+
+
+def feed(at, x, o_a, o_b, dy_pieces, w_out, vecs, w_up, up_bias, w_down):
+    length, width = x.shape
+    ff = w_up.shape[1]
+    part = length // 4
+    strip, shard, chunk, units = width // 8, ff // 8, ff // 4, width // PAIR
+    down = pl.BlockSpec((1, shard, width), lambda c, at: (c, 0, 0))
+    up = pl.BlockSpec((4, 1, strip, chunk), lambda c, at: (0, c, 0, 0))
+    cols = pl.BlockSpec((1, chunk), lambda c, at: (0, c))
+    full = once((length, width))
+    dy_specs, dy_arrays = piece_specs(dy_pieces, part, width)
+    return call(
+        feed_kernel,
+        "feed",
+        (4,),
+        [full, once(o_a.shape), once(o_b.shape)] + dy_specs + [once((width, width)), once(vecs.shape)]
+        + [
+            pl.BlockSpec((width, chunk), lambda c, at: (0, c)),
+            cols,
+            pl.BlockSpec((chunk, width), lambda c, at: (c, 0)),
+        ],
+        [once((part, width)), once((2, part, width)), once((part, width)), down, down, up, up, cols, full, full, once((8, width)), once((4, units, strip, PAIR)), once((4, units, strip, PAIR))],
+        [shape((part, width)), shape((2, part, width)), shape((part, width))]
+        + [shape((4, shard, width))] * 2
+        + [shape((4, 4, strip, chunk))] * 2
+        + [shape((1, ff), F32), shape((length, width)), shape((length, width)), shape((8, width), F32)]
+        + [shape((4, units, strip, PAIR))] * 2,
+        [
+            pltpu.VMEM((length, width), BF16),
+            pltpu.VMEM((length, width), F32),
+            pltpu.VMEM((length, width), BF16),
+            pltpu.VMEM((length, width), F32),
+            pltpu.VMEM((length, width), F32),
+            pltpu.VMEM((2, shard, width), BF16),
+            pltpu.VMEM((4, 2, strip, chunk), BF16),
+            pltpu.VMEM((4, 2, strip, width), BF16),
+        ],
+        flops=2 * length * width * (6 * ff + 3 * width),
+        moved=2 * (length * width * 7 + 4 * width * ff + 3 * width * width),
+    )(at, x, o_a, o_b, *dy_arrays, w_out, vecs, w_up, up_bias, w_down)
+
+
+def settle_kernel(at_ref, *refs):
+    out_ref = refs[-1]
+    for d, ref in zip(ways(at_ref[1]), refs[:-1]):
+        out_ref[at_ref[0] ^ d] = ref[...].astype(out_ref.dtype)
+
+
+def settle(at, pieces, dtype, name):
+    part, width = pieces[0].shape
+    rows = part // 2
+    specs, arrays = piece_specs(pieces, rows, width, lambda i, at: (i, 0))
+    return call(
+        settle_kernel,
+        name,
+        (2,),
+        specs,
+        pl.BlockSpec((4, rows, width), lambda i, at: (0, i, 0)),
+        shape((4, part, width), dtype),
+        moved=4 * part * width * 6,
+    )(at, *arrays)
+
+
 QBLOCK = 512
 
 
@@ -38,7 +556,7 @@
     return jnp.where(allowed[:, None], raw * factor, MASKED)
 
 
-def body(
+def spread_body(
     tokens,
     skip_values,
     segments,
@@ -299,9 +817,282 @@
     )
 
 
+def pick(array, index):
+    return lax.dynamic_index_in_dim(array, index, 0, keepdims=False)
+
+
+def gate(first, second):
+    return lax.optimization_barrier((first, second))
+
+
+def add_up(parts):
+    total = parts[0].astype(F32)
+    for part in parts[1:]:
+        total = total + part.astype(F32)
+    return total.astype(BF16)
+
+
+def across_cores(array):
+    return lax.ppermute(array, "seq", [(i, i ^ 1) for i in range(8)])
+
+
+def group_swap(array, core_zero, core_one):
+    pairs = [(4 * s + z, 4 * s + (z ^ (core_one if s & 1 else core_zero))) for s in range(8) for z in range(4)]
+    return lax.ppermute(array, ("seq", "head"), pairs)
+
+
+def near_swap(array):
+    return group_swap(array, 1, 3)
+
+
+def far_swap(array):
+    return group_swap(array, 3, 1)
+
+
+def across_swap(array):
+    return group_swap(array, 2, 2)
+
+
+def plane_swap(array, core_zero, core_one):
+    return lax.ppermute(array, "seq", [(s, s ^ (core_one if s & 1 else core_zero)) for s in range(8)])
+
+
+def first_hop(array):
+    return plane_swap(array, 2, 4)
+
+
+def second_hop(array):
+    return plane_swap(array, 4, 2)
+
+
+def plane_first(pairs, plane, core):
+    bit = 1 + core
+    away, stay = [], []
+    for other in range(2):
+        at = (plane & bit) | (other * (3 - bit))
+        stay.append(jnp.concatenate([add_up([pick(a, at), pick(b, at)]) for a, b in pairs]))
+        away.append(jnp.concatenate([add_up([pick(a, at ^ bit), pick(b, at ^ bit)]) for a, b in pairs]))
+    return jnp.stack(away), jnp.stack(stay)
+
+
+def plane_second(got, keep, plane, core):
+    mine = jnp.where(plane & (2 - core) > 0, 1, 0)
+    both = lambda at: add_up([pick(got, at), pick(keep, at)])
+    return both(1 - mine), both(mine)
+
+
+def group_first(blocks, me, core):
+    near, far = 1 + 2 * core, 3 - 2 * core
+    take = lambda d: pick(blocks, me ^ d)
+    return jnp.stack([take(near), take(2)]), jnp.stack([take(0), take(far)])
+
+
+def by_owner(own, far, near, me, core):
+    one, three = jnp.where(core == 0, near[0], far), jnp.where(core == 0, far, near[0])
+    by_distance = [own, one, near[1], three]
+    return [lax.select_n(me, *(by_distance[q ^ m] for m in range(4))) for q in range(4)]
+
+
+def fits(sizes):
+    return sizes == (8, 4)
+
+
+def row_body(
+    tokens,
+    skip_values,
+    segments,
+    token_mask,
+    attn_gain,
+    attn_shift,
+    w_qkv,
+    q_bias,
+    v_bias,
+    w_out,
+    out_bias,
+    mlp_gain,
+    mlp_shift,
+    w_up,
+    up_bias,
+    w_down,
+    down_bias,
+    cotangent,
+):
+    me = lax.axis_index("head")
+    seq = lax.axis_index("seq")
+    core, plane = seq & 1, seq >> 1
+    near, far = 1 + 2 * core, 3 - 2 * core
+    at = jnp.stack([me, core]).astype(jnp.int32)
+    rows, part, width = tokens.shape
+    length = rows * part
+    fresh = width // 2
+    ff = w_up.shape[1]
+    strip = width // 8
+    up_row = up_bias.astype(F32).reshape(1, ff)
+    vecs = jnp.stack([attn_gain, attn_shift, out_bias, mlp_gain, mlp_shift, down_bias, down_bias, down_bias]).astype(F32)
+    qkv_bias = jnp.concatenate([q_bias, jnp.zeros_like(q_bias), v_bias]).astype(F32)
+    scale = jnp.where(jnp.arange(w_qkv.shape[1]) < width, Q_SCALE, 1.0).astype(F32)
+    affine = jnp.stack([qkv_bias, scale])
+
+    def forward(array, got):
+        return jnp.stack([array, got[1]])
+
+    code = (segments * 2 + token_mask).astype(BF16)
+    code = jnp.broadcast_to(jnp.pad(code, ((0, 0), (0, width - part)))[:, None], (rows, CODE_ROWS, width))
+    tokens_at = lambda d: jnp.concatenate([pick(tokens, me ^ d), pick(code, me ^ d)])
+    pro = lambda way, piece, so_far: project(at, way, piece, vecs, w_qkv, affine, length, so_far)
+    near_x = near_swap(tokens_at(near))
+    far_x = far_swap(tokens_at(far))
+    across_x = across_swap(tokens_at(2))
+    so_far = pro(0, tokens_at(0), ())
+    so_far = pro(1, near_x, so_far)
+    so_far = pro(2, far_x, so_far)
+    (across_x, so_far), (skip_values, cotangent) = gate((across_x, so_far), (skip_values, cotangent))
+    skip_across = across_swap(pick(skip_values, me ^ 2))
+    skip_near = near_swap(pick(skip_values, me ^ near))
+    skip_far = far_swap(pick(skip_values, me ^ far))
+    dy_across = across_swap(pick(cotangent, me ^ 2))
+    dy_near = near_swap(pick(cotangent, me ^ near))
+    x, normed, proj, code_row = pro(3, across_x, so_far)
+    skip = [pick(skip_values, me), skip_near, skip_far, skip_across]
+
+    from_a = attend(at, code_row, proj, [proj], 0, 6, 12, 3, "attend_a")
+    (o_a, lse_a, skip), cotangent = gate((*from_a, skip), cotangent)
+    dy_far = far_swap(pick(cotangent, me ^ far))
+    o_b, lse_b = attend(at, code_row, proj, skip, 3, 9, 0, 3, "attend_b")
+    dy = [pick(cotangent, me), dy_near, dy_far, dy_across]
+    fed = feed(at, x, o_a, o_b, dy, w_out, vecs, w_up, up_row, w_down)
+    y_own, y_away, y_far, down_send, down_keep, up_send, up_keep, g_up_bias, d_att, d_o, mlp_sums, out_send, out_keep = fed
+    down_got = across_cores(down_send)
+    up_got = across_cores(up_send)
+    y_got = near_swap(y_away)
+    out_got = across_cores(out_send)
+    from_b = attend_back(
+        at, code_row, proj, skip, o_b, d_o, lse_b, normed, w_qkv, 3, 3, 0, None, None, "attend_back_b"
+    )
+    from_b, (down_got, up_got, y_got, out_got) = gate(from_b, (down_got, up_got, y_got, out_got))
+    b_send, b_keep, b_bias, s_own, s_away, s_far, d_normed = from_b
+    lines = lambda v: v.reshape(4, -1, strip, width)
+    big_away, big_stay = plane_first([(up_got, up_keep), (lines(down_got), lines(down_keep))], plane, core)
+    y_last = forward(y_far, y_got)
+    (d_normed, s_away, b_send), (big_away, big_stay, y_last) = gate((d_normed, s_away, b_send), (big_away, big_stay, y_last))
+    big_got = first_hop(big_away)
+    y_last = far_swap(y_last)
+    s_got = near_swap(s_away)
+    b_got = across_cores(b_send)
+    from_a = attend_back(
+        at, code_row, proj, [proj], o_a, d_o, lse_a, normed, w_qkv, 0, 3, 0, d_normed, [x, vecs, d_att], "attend_back_a"
+    )
+    from_a, (big_got, y_last, s_got, b_got) = gate(from_a, (big_got, y_last, s_got, b_got))
+    a_send, a_keep, a_bias, x_own, x_away, x_far, token_sums = from_a
+
+    q_sums = jnp.concatenate([v[:, 0, :PAIR].reshape(-1) for v in (a_bias, b_bias)])
+    v_sums = a_bias[:, 0, 2 * PAIR :].reshape(-1)
+    small = (
+        token_sums[0],
+        token_sums[1],
+        q_sums,
+        v_sums,
+        mlp_sums[2],
+        mlp_sums[0],
+        mlp_sums[1],
+        g_up_bias[0],
+        mlp_sums[3],
+    )
+    packed = jnp.concatenate(small).reshape(-1, 128)
+    units = lambda v: v.reshape(4, -1, strip, PAIR)
+
+    x_across = across_swap(x_away[1])
+    a_got = across_cores(a_send)
+    big_send, big_stay = plane_second(big_got, big_stay, plane, core)
+    big_got = second_hop(big_send)
+    small_got = across_cores(packed)
+    s_last = far_swap(forward(s_far, s_got))
+
+    (big_got, a_got, x_away, x_far), (x_across, small_got, s_last) = gate(
+        (big_got, a_got, x_away, x_far), (x_across, small_got, s_last)
+    )
+    x_near = near_swap(x_away[0])
+    x_far = far_swap(x_far)
+    big = add_up([big_got, big_stay]).reshape(2, 4, strip, width).transpose(1, 0, 2, 3)
+    big_send, big_keep = group_first(big, me, core)
+    big_got = near_swap(big_send)
+    rest_away, rest_stay = plane_first(
+        [(out_got, out_keep), (units(b_got), units(b_keep)), (units(a_got), units(a_keep))], plane, core
+    )
+    rest_got = first_hop(rest_away)
+    packed = packed + small_got
+    small_got = plane_swap(packed, 2, 2)
+
+    rest_got, (small_got, x_near, x_far) = gate(rest_got, (small_got, x_near, x_far))
+    rest_send, rest_stay = plane_second(rest_got, rest_stay, plane, core)
+    rest_got = second_hop(rest_send)
+    packed = packed + small_got
+    small_got = plane_swap(packed, 4, 4)
+
+    big_got, (rest_got, small_got) = gate(big_got, (rest_got, small_got))
+    rest = add_up([rest_got, rest_stay]).reshape(-1, 4, strip // 4, PAIR).transpose(1, 0, 2, 3)
+    rest_send, rest_keep = group_first(rest, me, core)
+    rest_got = near_swap(rest_send)
+    big_sum = add_up([big_got, big_keep])
+    big_got = far_swap(big_sum[1])
+    packed = packed + small_got
+    small_got = group_swap(packed, 1, 1)
+
+    big_got, rest_got = gate(big_got, rest_got)
+    rest_sum = add_up([rest_got, rest_keep])
+    rest_got = far_swap(rest_sum[1])
+    big_own = add_up([big_got, big_sum[0]])
+    big_far = far_swap(big_own)
+
+    (big_far, rest_got), small_got = gate((big_far, rest_got), small_got)
+    rest_own = add_up([rest_got, rest_sum[0]])
+    rest_far = far_swap(rest_own)
+    packed = packed + small_got
+    small_got = group_swap(packed, 3, 3)
+    big_near = near_swap(jnp.stack([big_own, big_far]))
+    rest_near = near_swap(jnp.stack([rest_own, rest_far]))
+    packed = (packed + small_got).reshape(-1)
+
+    layer_out = settle(at, [y_own, (y_got, 0), (y_last, 0), (y_last, 1)], BF16, "settle_out")
+    grad_skip = settle(at, [s_own, (s_got, 0), (s_last, 0), (s_last, 1)], F32, "settle_skip")
+    grad_tokens = settle(at, [x_own, x_near, x_far, x_across], F32, "settle_tokens")
+    big = by_owner(big_own, big_far, big_near, me, core)
+    rest = jnp.concatenate(by_owner(rest_own, rest_far, rest_near, me, core), axis=1).astype(F32)
+    r_up = jnp.concatenate([q[0] for q in big], axis=1).astype(F32)
+    r_down = jnp.concatenate([q[1] for q in big], axis=0).astype(F32)
+    count = width // PAIR
+    r_out = jnp.concatenate([rest[u] for u in range(count)], axis=1)
+    unit_of = lambda p, n: rest[count + (p - count // 2) * 2 + n] if p >= count // 2 else rest[2 * count + 3 * p + n]
+    order = [unit_of(p, n) for n in range(2) for p in range(count)] + [unit_of(p, 2) for p in range(count // 2)]
+    r_qkv = jnp.concatenate(order, axis=1)
+    sums = []
+    for entry in small:
+        sums.append(packed[: entry.shape[0]])
+        packed = packed[entry.shape[0] :]
+    return (
+        layer_out,
+        grad_tokens,
+        grad_skip,
+        sums[0],
+        sums[1],
+        r_qkv,
+        sums[2],
+        sums[3],
+        r_out,
+        sums[4],
+        sums[5],
+        sums[6],
+        r_up,
+        sums[7],
+        r_down,
+        sums[8],
+    )
+
+
 def solution(mesh):
+    sizes = (mesh.shape["seq"], mesh.shape["head"])
     return jax.shard_map(
-        body,
+        row_body if fits(sizes) else spread_body,
         mesh=mesh,
         in_specs=(
             P("seq", "head", None),

time: 797 us -> 336 us (0.42)
  matrix products: 305 us -> 0 us
  Pallas kernels: 0 us -> 153 us
  waiting for transfers between devices: 196 us -> 99.5 us
  blocking collectives: 93.5 us -> 0 us
  local copies, waits for them, and re-layouts: 77.3 us -> 12.9 us
  other arithmetic: 63.5 us -> 18 us
  between operations: 14.9 us -> 2.17 us
    dot_general x24 -> x0, matrix products: 305 us -> none  [the longest x2 66.5 us: body(): jnp.einsum('ihqk,iqhc->ikhc', d_raw, q_split[:, q_start:k_end], preferred...]
    pallas_call x0 -> x12, Pallas kernels: none -> 153 us  [the longest x1 48.4 us: feed(): call(feed_kernel, 'feed', (4,), [full, once(o_a.shape), once(o_b.shape)]...]
    all_to_all x8 -> x0, waiting for transfers between devices: 152 us -> none  [the longest x1 45.5 us: body(): lax.all_to_all(mixed_items, 'head', split_axis=1, concat_axis=0, tiled=True)]
    ppermute x0 -> x38, waiting for transfers between devices: none -> 99.5 us  [the longest x26 98.6 us: group_swap(): return lax.ppermute(array, ('seq', 'head'), pairs)]
    all_gather x2 -> x0, blocking collectives: 51.6 us -> none  [the longest x1 38.5 us: body(): lax.all_gather(segments, 'head', axis=1, tiled=True)]
    ppermute x0 -> x38, starting transfers between devices: none -> 45.9 us  [the longest x26 37.6 us: group_swap(): return lax.ppermute(array, ('seq', 'head'), pairs)]
    psum x1 -> x0, blocking collectives: 41.9 us -> none  [body(): lax.psum((g_attn_gain, g_attn_shift, g_q_bias, g_v_bias, g_out_bias, g_ml...]
    all_to_all x8 -> x0, starting transfers between devices: 38.9 us -> none  [the longest x1 6.33 us: body(): lax.all_to_all(value_rows.reshape(flat_shape), 'head', split_axis=0, conc...]
  transfers between devices with their start and end apart: 13 -> 38, of which waited for: 7 -> 14; matrix products, arithmetic and copies ran while one was open for 39% -> 4% of each run, Pallas kernels for 0% -> 31%
where the time goes in v3:
time: 336 us; the launch traced here: 331 us
  Pallas kernels  153 us (46%)
  waiting for transfers between devices  99.5 us (30%)
  starting transfers between devices  45.9 us (14%)
  other arithmetic  18 us (5%)
  local copies, waits for them, and re-layouts  12.9 us (4%)
    ppermute x26, waiting for transfers between devices, group_swap(): return lax.ppermute(array, ('seq', 'head'), pairs)  98.6 us
    pallas_call x1, Pallas kernels, feed(): call(feed_kernel, 'feed', (4,), [full, once(o_a.shape), once(o_b.shape)]...  48.4 us
    pallas_call x2, Pallas kernels, attend_back(): call(functools.partial(backward_kernel, len(values), before is None, last...  48.3 us
    ppermute x26, starting transfers between devices, group_swap(): return lax.ppermute(array, ('seq', 'head'), pairs)  37.6 us
    pallas_call x2, Pallas kernels, attend(): call(functools.partial(forward_kernel, len(values)), name, (pairs,), [who...  26.7 us
    pallas_call x4, Pallas kernels, project(): call(project_kernel, 'project', (1,), [whole((part + CODE_ROWS, width)),...  19.6 us
    pallas_call x3, Pallas kernels, settle(): call(settle_kernel, name, (2,), specs, pl.BlockSpec((4, rows, width), lam...  9.66 us
    convert_element_type x12, other arithmetic, add_up(): return total.astype(BF16)  8.26 us
  transfers between devices with their start and end apart: 38, of which 14 were waited for; matrix products, arithmetic and copies ran while one was open for 4% of the time, Pallas kernels for 31%

profile of v3, /device:TPU:0, one launch (start us, length us, event | category | flops | bytes accessed | tf_op | source)
XLA Modules:
  0.0 331.0 jit_solution(15386240940717496836)
XLA Ops:
  1.4 1.5 dynamic-slice_bitcast_fusion.4
  3.0 3.1 collective-permute-start.2
  6.2 2.5 collective-permute-start.1
  9.0 0.8 pad_maximum_fusion.9.x_ref
  12.4 4.9 %project.4 = (bf16[1024,768]{1,0:T(8,128)(2,1)}, bf16[1024,768]{1,0:T(8,128)(2,1)}, bf16[1024,1920]{1,0:T(8,128)(2,1)}, s32[8,1024]{1,0:T(8,128)}) custom-call(s32[2]{0:T(128)} %pad_add_fusion.at_ref.me_ref, bf16[272,768]{1,0:T(8,128)(2,1)} %pad_maximum_fusion.9.x_ref, f32[8,768]{1,0:T(8,128)} %convert_element_type.427.vec_ref.refs_10_, ...), custom_call_target="tpu_custom_call" | custom-call | flops 754974720 | bytes 5111808 | tf_op jit(solution)/shard_map/project/pallas_call | solution.py:139
  17.3 2.8 collective-permute-done.2.x_ref
  20.1 0.8 copy-done.16
  20.9 4.9 %project.5 = (bf16[1024,768]{1,0:T(8,128)(2,1)}, bf16[1024,768]{1,0:T(8,128)(2,1)}, bf16[1024,1920]{1,0:T(8,128)(2,1)}, s32[8,1024]{1,0:T(8,128)}) custom-call(s32[2]{0:T(128)} %pad_add_fusion.at_ref.me_ref, bf16[272,768]{1,0:T(8,128)(2,1)} %copy-done.16, ...), custom_call_target="tpu_custom_call", output_to_operand_aliasing={{0}: (5, {}), {1}: (6, {}), {2}: (7, {}), {3}: (8, {})} | custom-call | flops 754974720 | bytes 5111808 | tf_op jit(solution)/shard_map/project/pallas_call | solution.py:139
  25.7 2.4 collective-permute-done.1.x_ref
  28.1 0.8 copy-done.15
  28.9 5.0 %project.6 = (bf16[1024,768]{1,0:T(8,128)(2,1)}, bf16[1024,768]{1,0:T(8,128)(2,1)}, bf16[1024,1920]{1,0:T(8,128)(2,1)}, s32[8,1024]{1,0:T(8,128)}) custom-call(s32[2]{0:T(128)} %pad_add_fusion.at_ref.me_ref, bf16[272,768]{1,0:T(8,128)(2,1)} %copy-done.15, ...), custom_call_target="tpu_custom_call", output_to_operand_aliasing={{0}: (5, {}), {1}: (6, {}), {2}: (7, {}), {3}: (8, {})} | custom-call | flops 754974720 | bytes 5111808 | tf_op jit(solution)/shard_map/project/pallas_call | solution.py:139
  33.8 9.9 %collective-permute-done.x_ref = bf16[272,768]{1,0:T(8,128)(2,1)S(1)} collective-permute-done((bf16[272,768]{1,0:T(8,128)(2,1)S(1)}, bf16[272,768]{1,0:T(8,128)(2,1)S(1)}, u32[]{:S(2)}, u32[]{:S(2)}) %collective-permute-start) | collective-permute-done | bytes 417824 | tf_op jit(solution)/shard_map/ppermute | solution.py:841
  43.7 0.8 dynamic-slice_bitcast_fusion.12
  44.5 2.5 collective-permute-start.4
  47.0 1.0 collective-permute-start.5
  48.1 1.0 collective-permute-start.6
  49.1 2.1 collective-permute-start.8
  51.2 4.9 %project.7 = (bf16[1024,768]{1,0:T(8,128)(2,1)}, bf16[1024,768]{1,0:T(8,128)(2,1)}, bf16[1024,1920]{1,0:T(8,128)(2,1)}, s32[8,1024]{1,0:T(8,128)}) custom-call(s32[2]{0:T(128)} %pad_add_fusion.at_ref.me_ref, bf16[272,768]{1,0:T(8,128)(2,1)} %copy-done.14, ...), custom_call_target="tpu_custom_call", output_to_operand_aliasing={{0}: (5, {}), {1}: (6, {}), {2}: (7, {}), {3}: (8, {})} | custom-call | flops 754974720 | bytes 5111808 | tf_op jit(solution)/shard_map/project/pallas_call | solution.py:139
  56.1 13.6 %attend_a.1 = (bf16[1024,384]{1,0:T(8,128)(2,1)}, f32[1024,384]{1,0:T(8,128)}) custom-call(s32[2]{0:T(128)} %pad_add_fusion.at_ref.me_ref, s32[8,1024]{1,0:T(8,128)} %get-tuple-element.142.code_ref, bf16[1024,1920]{1,0:T(8,128)(2,1)} %get-tuple-element.143.q_ref.k_ref.refs_0_, bf16[1024,1920]{1,0:T(8,128)(2,1)} %get-tuple-element.143.q_ref.k_ref.refs_0_, ...), custom_call_target="tpu_custom_call" | custom-call | flops 9663676416 | bytes 4718592 | tf_op jit(solution)/shard_map/attend_a/pallas_call | solution.py:310
  69.7 8.3 %collective-permute-done.5.refs_3_ = bf16[256,384]{1,0:T(8,128)(2,1)S(1)} collective-permute-done((bf16[256,384]{1,0:T(8,128)(2,1)S(1)}, bf16[256,384]{1,0:T(8,128)(2,1)S(1)}, u32[]{:S(2)}, u32[]{:S(2)}) %collective-permute-start.5) | collective-permute-done | bytes 196640 | tf_op jit(solution)/shard_map/ppermute | solution.py:841
  78.0 0.8 dynamic-slice_bitcast_fusion.1
  78.8 1.7 collective-permute-start.7
  80.5 13.1 %attend_b.1 = (bf16[1024,384]{1,0:T(8,128)(2,1)}, f32[1024,384]{1,0:T(8,128)}) custom-call(s32[2]{0:T(128)} %pad_add_fusion.at_ref.me_ref, s32[8,1024]{1,0:T(8,128)} %get-tuple-element.142.code_ref, bf16[1024,1920]{1,0:T(8,128)(2,1)} %get-tuple-element.143.q_ref.k_ref.refs_0_, bf16[1024,1920]{1,0:T(8,128)(2,1)} %get-tuple-element.143.q_ref.k_ref.refs_0_, ...), custom_call_target="tpu_custom_call" | custom-call | flops 9663676416 | bytes 4718592 | tf_op jit(solution)/shard_map/attend_b/pallas_call | solution.py:310
  94.7 48.4 %feed.1 = (bf16[256,768]{1,0:T(8,128)(2,1)}, bf16[2,256,768]{2,1,0:T(8,128)(2,1)}, bf16[256,768]{1,0:T(8,128)(2,1)}, bf16[4,384,768]{2,1,0:T(8,128)(2,1)}, bf16[...) custom-call(s32[2]{0:T(128)} %pad_add_fusion.at_ref.me_ref, ...), custom_call_target="tpu_custom_call" | custom-call | flops 32614907904 | bytes 33423360 | tf_op jit(solution)/shard_map/feed/pallas_call | solution.py:473
  143.7 3.0 collective-permute-start.11
  146.7 20.6 %attend_back_b.1 = (bf16[4,3,2,96,128]{4,3,2,1,0:T(8,128)(2,1)}, bf16[4,3,2,96,128]{4,3,2,1,0:T(8,128)(2,1)}, f32[3,1,256]{2,1,0:T(1,128)}, bf16[256,384]{1,0:T(...) custom-call(s32[2]{0:T(128)} %pad_add_fusion.at_ref.me_ref, ...), custom_call_target="tpu_custom_call" | custom-call | flops 14495514624 | bytes 16515072 | tf_op jit(solution)/shard_map/attend_back_b/pallas_call | solution.py:360
  167.4 0.8 copy-done.12
  168.5 1.4 copy-done.1
  169.8 3.3 fusion.8
  173.8 1.7 pad_maximum_fusion
  175.5 1.5 collective-permute-start.13
  177.0 1.5 collective-permute-start.14
  179.1 27.7 %attend_back_a.1 = (bf16[4,3,3,96,128]{4,3,2,1,0:T(8,128)(2,1)}, bf16[4,3,3,96,128]{4,3,2,1,0:T(8,128)(2,1)}, f32[3,1,384]{2,1,0:T(1,128)}, bf16[256,768]{1,0:T(...) custom-call(s32[2]{0:T(128)} %pad_add_fusion.at_ref.me_ref, ...), custom_call_target="tpu_custom_call" | custom-call | flops 15703474176 | bytes 16515072 | tf_op jit(solution)/shard_map/attend_back_a/pallas_call | solution.py:360
  207.8 1.9 collective-permute-start.21
  209.7 0.8 slice_reduce_fusion.4
  210.6 1.7 fusion.1
  212.3 1.6 collective-permute-start.17
  214.0 1.1 collective-permute-start.19
  215.7 0.8 collective-permute-done.20
  216.5 5.2 %collective-permute-done.21.refs_2_.refs_3_ = bf16[2,256,384]{2,1,0:T(8,128)(2,1)S(1)} collective-permute-done((bf16[2,256,384]{2,1,0:T(8,128)(2,1)S(1)}, bf16[2,256,384]{2,1,0:T(8,128)(2,1)S(1)}, u32[]{:S(2)}, u32[]{:S(2)}) %collective-permute-start.21) | collective-permute-done | bytes 393248 | tf_op jit(solution)/shard_map/ppermute | solution.py:841
  221.7 15.8 %collective-permute-done.19.refs_3_ = bf16[256,768]{1,0:T(8,128)(2,1)S(1)} collective-permute-done((bf16[256,768]{1,0:T(8,128)(2,1)S(1)}, bf16[256,768]{1,0:T(8,128)(2,1)S(1)}, u32[]{:S(2)}, u32[]{:S(2)}) %collective-permute-start.19) | collective-permute-done | bytes 393248 | tf_op jit(solution)/shard_map/ppermute | solution.py:841
  238.7 1.6 collective-permute-start.22
  240.4 2.5 collective-permute-start.25
  242.9 1.7 fusion
  244.8 1.1 collective-permute-start.26
  246.0 13.1 %collective-permute-done.24.refs_1_ = bf16[256,768]{1,0:T(8,128)(2,1)S(1)} collective-permute-done((bf16[256,768]{1,0:T(8,128)(2,1)S(1)}, bf16[256,768]{1,0:T(8,128)(2,1)S(1)}, u32[]{:S(2)}, u32[]{:S(2)}) %collective-permute-start.24) | collective-permute-done | bytes 393248 | tf_op jit(solution)/shard_map/ppermute | solution.py:841
  259.1 2.3 collective-permute-done.25.refs_2_
  261.6 1.6 collective-permute-start.27
  263.8 9.0 %collective-permute-done.26 = bf16[2,2,96,768]{3,2,1,0:T(8,128)(2,1)S(1)} collective-permute-done((bf16[2,2,96,768]{3,2,1,0:T(8,128)(2,1)S(1)}, bf16[2,2,96,768]{3,2,1,0:T(8,128)(2,1)S(1)}, u32[]{:S(2)}, u32[]{:S(2)}) %collective-permute-start.26) | collective-permute-done | bytes 589856 | tf_op jit(solution)/shard_map/ppermute | solution.py:841
  273.4 1.7 collective-permute-start.29
  275.2 12.2 %collective-permute-done.30 = bf16[2,21,24,128]{3,2,1,0:T(8,128)(2,1)S(1)} collective-permute-done((bf16[2,21,24,128]{3,2,1,0:T(8,128)(2,1)S(1)}, bf16[2,21,24,128]{3,2,1,0:T(8,128)(2,1)S(1)}, u32[]{:S(2)}, u32[]{:S(2)}) %collective-permute-start.30) | collective-permute-done | bytes 258080 | tf_op jit(solution)/shard_map/ppermute | solution.py:841
  287.5 2.2 collective-permute-start.31
  289.8 1.8 collective-permute-start.32
  291.6 3.1 settle_out.1
  294.7 2.9 settle_skip.1
  297.6 3.7 %settle_tokens.1 = f32[4,256,768]{2,1,0:T(8,128)} custom-call(s32[2]{0:T(128)} %pad_add_fusion.at_ref.me_ref, bf16[256,768]{1,0:T(8,128)(2,1)} %get-tuple-element.194.refs_0_, bf16[256,768]{1,0:T(8,128)(2,1)} %copy-done.18, bf16[256,768]{1,0:T(8,128)(2,1)} %copy-done.19, bf16[256,768]{1,0:T(8,128)(2,1)} %copy-done.17), custom_call_target="tpu_custom_call" | custom-call | bytes 4718592 | tf_op jit(solution)/shard_map/settle_tokens/pallas_call | solution.py:514
  301.3 2.1 collective-permute-start.37
  303.4 2.1 collective-permute-start.34
  305.5 1.8 collective-permute-start.35
  307.3 11.4 %collective-permute-done.34 = f32[69,128]{1,0:T(8,128)S(1)} collective-permute-done((f32[69,128]{1,0:T(8,128)S(1)}, f32[69,128]{1,0:T(8,128)S(1)}, u32[]{:S(2)}, u32[]{:S(2)}) %collective-permute-start.34) | collective-permute-done | bytes 35360 | tf_op jit(solution)/shard_map/ppermute | solution.py:841
  319.3 0.8 collective-permute-done.35
  321.4 5.4 %collective-permute-done.36 = bf16[2,21,24,128]{3,2,1,0:T(8,128)(2,1)S(1)} collective-permute-done((bf16[2,21,24,128]{3,2,1,0:T(8,128)(2,1)S(1)}, bf16[2,21,24,128]{3,2,1,0:T(8,128)(2,1)S(1)}, u32[]{:S(2)}, u32[]{:S(2)}) %collective-permute-start.36) | collective-permute-done | bytes 258080 | tf_op jit(solution)/shard_map/ppermute | solution.py:841
  328.5 1.1 maximum_convert_fusion.1
  329.6 1.1 maximum_convert_fusion
  (231 shorter events, 15.1 us)
Async XLA Ops:
  2.9 6.1 %copy-start.28 = (bf16[768]{0:T(1024)(128)(2,1)S(1)}, bf16[768]{0:T(1024)(128)(2,1)}, u32[]{:S(2)}) copy-start(bf16[768]{0:T(1024)(128)(2,1)} %param.25) | copy-start | bytes 4612
  2.9 6.1 %copy-start.35 = (bf16[384]{0:T(512)(128)(2,1)S(1)}, bf16[384]{0:T(512)(128)(2,1)}, u32[]{:S(2)}) copy-start(bf16[384]{0:T(512)(128)(2,1)} %param.26) | copy-start | bytes 2308
  3.0 17.2 %collective-permute-start.2 = (bf16[272,768]{1,0:T(8,128)(2,1)S(1)}, bf16[272,768]{1,0:T(8,128)(2,1)S(1)}, u32[]{:S(2)}, u32[]{:S(2)}) collective-permute-start(bf16[272,768]{1,0:T(8,128)(2,1)S(1)} %pad_maximum_fusion.8), channel_id=1, source_target_pairs={{0,1},{1,0},{2,3},{3,2},{4,7},{5,6},{6,5},{7,4},{8,9},{9,8},{10,11... | collective-permute-start | bytes 1253384 | tf_op jit(solution)/shard_map/ppermute | solution.py:841
  6.1 4.4 %copy-start.29 = (bf16[768]{0:T(1024)(128)(2,1)S(1)}, bf16[768]{0:T(1024)(128)(2,1)}, u32[]{:S(2)}) copy-start(bf16[768]{0:T(1024)(128)(2,1)} %param.22) | copy-start | bytes 4612
  6.1 4.4 %copy-start.30 = (bf16[768]{0:T(1024)(128)(2,1)S(1)}, bf16[768]{0:T(1024)(128)(2,1)}, u32[]{:S(2)}) copy-start(bf16[768]{0:T(1024)(128)(2,1)} %param.23) | copy-start | bytes 4612
  6.1 4.4 %copy-start.31 = (bf16[768]{0:T(1024)(128)(2,1)S(1)}, bf16[768]{0:T(1024)(128)(2,1)}, u32[]{:S(2)}) copy-start(bf16[768]{0:T(1024)(128)(2,1)} %param.28) | copy-start | bytes 4612
  6.1 4.4 %copy-start.32 = (bf16[768]{0:T(1024)(128)(2,1)S(1)}, bf16[768]{0:T(1024)(128)(2,1)}, u32[]{:S(2)}) copy-start(bf16[768]{0:T(1024)(128)(2,1)} %param.29) | copy-start | bytes 4612
  6.1 4.4 %copy-start.33 = (bf16[768]{0:T(1024)(128)(2,1)S(1)}, bf16[768]{0:T(1024)(128)(2,1)}, u32[]{:S(2)}) copy-start(bf16[768]{0:T(1024)(128)(2,1)} %param.30) | copy-start | bytes 4612
  6.1 4.4 %copy-start.34 = (bf16[768]{0:T(1024)(128)(2,1)S(1)}, bf16[768]{0:T(1024)(128)(2,1)}, u32[]{:S(2)}) copy-start(bf16[768]{0:T(1024)(128)(2,1)} %param.34) | copy-start | bytes 4612
  6.1 5.1 %copy-start.25 = (bf16[3072]{0:T(1024)(128)(2,1)S(1)}, bf16[3072]{0:T(1024)(128)(2,1)}, u32[]{:S(2)}) copy-start(bf16[3072]{0:T(1024)(128)(2,1)} %param.32) | copy-start | bytes 18436
  6.2 21.9 %collective-permute-start.1 = (bf16[272,768]{1,0:T(8,128)(2,1)S(1)}, bf16[272,768]{1,0:T(8,128)(2,1)S(1)}, u32[]{:S(2)}, u32[]{:S(2)}) collective-permute-start(bf16[272,768]{1,0:T(8,128)(2,1)S(1)} %pad_maximum_fusion.7), channel_id=1, source_target_pairs={{0,3},{1,2},{2,1},{3,0},{4,5},{5,4},{6,7},{7,6},{8,11},{9,10},{10,... | collective-permute-start | bytes 1253384 | tf_op jit(solution)/shard_map/ppermute | solution.py:841
  8.7 35.0 %collective-permute-start = (bf16[272,768]{1,0:T(8,128)(2,1)S(1)}, bf16[272,768]{1,0:T(8,128)(2,1)S(1)}, u32[]{:S(2)}, u32[]{:S(2)}) collective-permute-start(bf16[272,768]{1,0:T(8,128)(2,1)S(1)} %pad_maximum_fusion.6), channel_id=1, source_target_pairs={{0,2},{1,3},{2,0},{3,1},{4,6},{5,7},{6,4},{7,5},{8,10},{9,11},{10,... | collective-permute-start | bytes 1253384 | tf_op jit(solution)/shard_map/ppermute | solution.py:841
  28.9 14.9 %copy-start.8 = (bf16[4,256,384]{2,1,0:T(8,128)(2,1)S(1)}, bf16[4,256,384]{2,1,0:T(8,128)(2,1)}, u32[]{:S(2)}) copy-start(bf16[4,256,384]{2,1,0:T(8,128)(2,1)} %param.19) | copy-start | bytes 2359300
  33.8 14.2 %copy-start.5 = (bf16[4,256,768]{2,1,0:T(8,128)(2,1)S(1)}, bf16[4,256,768]{2,1,0:T(8,128)(2,1)}, u32[]{:S(2)}) copy-start(bf16[4,256,768]{2,1,0:T(8,128)(2,1)} %param.35) | copy-start | bytes 4718596
  43.7 4.4 %copy-start.14 = (bf16[272,768]{1,0:T(8,128)(2,1)}, bf16[272,768]{1,0:T(8,128)(2,1)S(1)}, u32[]{:S(2)}) copy-start(bf16[272,768]{1,0:T(8,128)(2,1)S(1)} %collective-permute-done.x_ref) | copy-start | bytes 1253380
  44.5 25.1 %collective-permute-start.3 = (bf16[256,384]{1,0:T(8,128)(2,1)S(1)}, bf16[256,384]{1,0:T(8,128)(2,1)S(1)}, u32[]{:S(2)}, u32[]{:S(2)}) collective-permute-start(bf16[256,384]{1,0:T(8,128)(2,1)S(1)} %get-tuple-element.299), channel_id=1, source_target_pairs={{0,1},{1,0},{2,3},{3,2},{4,7},{5,6},{6,5},{7,4},{8,9},{9,8},{10,11... | collective-permute-start | bytes 589832 | tf_op jit(solution)/shard_map/ppermute | solution.py:841
  44.5 25.1 %collective-permute-start.4 = (bf16[256,384]{1,0:T(8,128)(2,1)S(1)}, bf16[256,384]{1,0:T(8,128)(2,1)S(1)}, u32[]{:S(2)}, u32[]{:S(2)}) collective-permute-start(bf16[256,384]{1,0:T(8,128)(2,1)S(1)} %get-tuple-element.298), channel_id=1, source_target_pairs={{0,3},{1,2},{2,1},{3,0},{4,5},{5,4},{6,7},{7,6},{8,11},{9,10},{10,... | collective-permute-start | bytes 589832 | tf_op jit(solution)/shard_map/ppermute | solution.py:841
  47.0 31.0 %collective-permute-start.5 = (bf16[256,384]{1,0:T(8,128)(2,1)S(1)}, bf16[256,384]{1,0:T(8,128)(2,1)S(1)}, u32[]{:S(2)}, u32[]{:S(2)}) collective-permute-start(bf16[256,384]{1,0:T(8,128)(2,1)S(1)} %get-tuple-element.297), channel_id=1, source_target_pairs={{0,2},{1,3},{2,0},{3,1},{4,6},{5,7},{6,4},{7,5},{8,10},{9,11},{10,... | collective-permute-start | bytes 589832 | tf_op jit(solution)/shard_map/ppermute | solution.py:841
  48.1 45.5 %collective-permute-start.6 = (bf16[256,768]{1,0:T(8,128)(2,1)S(1)}, bf16[256,768]{1,0:T(8,128)(2,1)S(1)}, u32[]{:S(2)}, u32[]{:S(2)}) collective-permute-start(bf16[256,768]{1,0:T(8,128)(2,1)S(1)} %get-tuple-element.263), channel_id=1, source_target_pairs={{0,1},{1,0},{2,3},{3,2},{4,7},{5,6},{6,5},{7,4},{8,9},{9,8},{10,11... | collective-permute-start | bytes 1179656 | tf_op jit(solution)/shard_map/ppermute | solution.py:841
  49.1 44.6 %collective-permute-start.8 = (bf16[256,768]{1,0:T(8,128)(2,1)S(1)}, bf16[256,768]{1,0:T(8,128)(2,1)S(1)}, u32[]{:S(2)}, u32[]{:S(2)}) collective-permute-start(bf16[256,768]{1,0:T(8,128)(2,1)S(1)} %get-tuple-element.262), channel_id=1, source_target_pairs={{0,2},{1,3},{2,0},{3,1},{4,6},{5,7},{6,4},{7,5},{8,10},{9,11},{10,... | collective-permute-start | bytes 1179656 | tf_op jit(solution)/shard_map/ppermute | solution.py:841
  69.6 10.9 %copy-start.42 = (bf16[256,384]{1,0:T(8,128)(2,1)}, bf16[256,384]{1,0:T(8,128)(2,1)S(1)}, u32[]{:S(2)}) copy-start(bf16[256,384]{1,0:T(8,128)(2,1)S(1)} %collective-permute-done.3.refs_1_) | copy-start | bytes 589828
  69.7 10.8 %copy-start.43 = (bf16[256,384]{1,0:T(8,128)(2,1)}, bf16[256,384]{1,0:T(8,128)(2,1)S(1)}, u32[]{:S(2)}) copy-start(bf16[256,384]{1,0:T(8,128)(2,1)S(1)} %collective-permute-done.4.refs_2_) | copy-start | bytes 589828
  78.8 14.9 %collective-permute-start.7 = (bf16[256,768]{1,0:T(8,128)(2,1)S(1)}, bf16[256,768]{1,0:T(8,128)(2,1)S(1)}, u32[]{:S(2)}, u32[]{:S(2)}) collective-permute-start(bf16[256,768]{1,0:T(8,128)(2,1)S(1)} %get-tuple-element.264), channel_id=1, source_target_pairs={{0,3},{1,2},{2,1},{3,0},{4,5},{5,4},{6,7},{7,6},{8,11},{9,10},{10,... | collective-permute-start | bytes 1179656 | tf_op jit(solution)/shard_map/ppermute | solution.py:841
  143.1 24.3 %collective-permute-start.10 = (bf16[4,4,96,768]{3,2,1,0:T(8,128)(2,1)}, bf16[4,4,96,768]{3,2,1,0:T(8,128)(2,1)S(1)}, u32[]{:S(2)}, u32[]{:S(2)}) collective-permute-start(bf16[4,4,96,768]{3,2,1,0:T(8,128)(2,1)} %get-tuple-element.167), channel_id=1, source_target_pairs={{0,4},{4,0},{8,12},{12,8},{16,20},{20,16},{24,28},{28,24},{1,5},{5... | collective-permute-start | bytes 7077896 | tf_op jit(solution)/shard_map/ppermute | solution.py:836
  143.2 24.2 %collective-permute-start.9 = (bf16[4,384,768]{2,1,0:T(8,128)(2,1)}, bf16[4,384,768]{2,1,0:T(8,128)(2,1)}, u32[]{:S(2)}, u32[]{:S(2)}) collective-permute-start(bf16[4,384,768]{2,1,0:T(8,128)(2,1)} %get-tuple-element.166), channel_id=1, source_target_pairs={{0,4},{4,0},{8,12},{12,8},{16,20},{20,16},{24,28},{28,24},{1,5},{5... | collective-permute-start | bytes 7077896 | tf_op jit(solution)/shard_map/ppermute | solution.py:836
  143.7 23.7 %collective-permute-start.11 = (bf16[2,256,768]{2,1,0:T(8,128)(2,1)}, bf16[2,256,768]{2,1,0:T(8,128)(2,1)S(1)}, u32[]{:S(2)}, u32[]{:S(2)}) collective-permute-start(bf16[2,256,768]{2,1,0:T(8,128)(2,1)} %get-tuple-element.168), channel_id=1, source_target_pairs={{0,1},{1,0},{2,3},{3,2},{4,7},{5,6},{6,5},{7,4},{8,9},{9,8},{10,11... | collective-permute-start | bytes 2359304 | tf_op jit(solution)/shard_map/ppermute | solution.py:841
  146.7 20.6 %collective-permute-start.12 = (bf16[4,6,96,128]{3,2,1,0:T(8,128)(2,1)}, bf16[4,6,96,128]{3,2,1,0:T(8,128)(2,1)S(1)}, u32[]{:S(2)}, u32[]{:S(2)}) collective-permute-start(bf16[4,6,96,128]{3,2,1,0:T(8,128)(2,1)} %get-tuple-element.169), channel_id=1, source_target_pairs={{0,4},{4,0},{8,12},{12,8},{16,20},{20,16},{24,28},{28,24},{1,5},{5... | collective-permute-start | bytes 1769480 | tf_op jit(solution)/shard_map/ppermute | solution.py:836
  146.7 21.5 %copy-start.20 = (bf16[256,768]{1,0:T(8,128)(2,1)S(1)}, bf16[256,768]{1,0:T(8,128)(2,1)}, u32[]{:S(2)}) copy-start(bf16[256,768]{1,0:T(8,128)(2,1)} %get-tuple-element.179) | copy-start | bytes 1179652
  146.7 21.7 %copy-start.2 = (bf16[4,4,96,768]{3,2,1,0:T(8,128)(2,1)S(1)}, bf16[4,4,96,768]{3,2,1,0:T(8,128)(2,1)}, u32[]{:S(2)}) copy-start(bf16[4,4,96,768]{3,2,1,0:T(8,128)(2,1)} %get-tuple-element.176) | copy-start | bytes 7077892
  175.5 31.6 %collective-permute-start.13 = (bf16[2,8,96,768]{3,2,1,0:T(8,128)(2,1)}, bf16[2,8,96,768]{3,2,1,0:T(8,128)(2,1)}, u32[]{:S(2)}, u32[]{:S(2)}) collective-permute-start(bf16[2,8,96,768]{3,2,1,0:T(8,128)(2,1)} %pad_maximum_fusion), channel_id=1, source_target_pairs={{0,8},{4,20},{8,0},{12,28},{16,24},{20,4},{24,16},{28,12},{1,9},{5... | collective-permute-start | bytes 7077896 | tf_op jit(solution)/shard_map/ppermute | solution.py:857
  177.0 30.0 %collective-permute-start.14 = (bf16[2,256,768]{2,1,0:T(8,128)(2,1)S(1)}, bf16[2,256,768]{2,1,0:T(8,128)(2,1)S(1)}, u32[]{:S(2)}, u32[]{:S(2)}) collective-permute-start(bf16[2,256,768]{2,1,0:T(8,128)(2,1)S(1)} %pad_maximum_fusion.3), channel_id=1, source_target_pairs={{0,3},{1,2},{2,1},{3,0},{4,5},{5,4},{6,7},{7,6},{8,11},{9,10},{10,... | collective-permute-start | bytes 2359304 | tf_op jit(solution)/shard_map/ppermute | solution.py:841
  178.5 28.5 %collective-permute-start.16 = (bf16[4,3,2,96,128]{4,3,2,1,0:T(8,128)(2,1)}, bf16[4,3,2,96,128]{4,3,2,1,0:T(8,128)(2,1)S(1)}, u32[]{:S(2)}, u32[]{:S(2)}) collective-permute-start(bf16[4,3,2,96,128]{4,3,2,1,0:T(8,128)(2,1)} %get-tuple-element.192), channel_id=1, source_target_pairs={{0,4},{4,0},{8,12},{12,8},{16,20},{20,16},{24,28},{28,24},{1,5},{5... | collective-permute-start | bytes 1769480 | tf_op jit(solution)/shard_map/ppermute | solution.py:836
  178.5 28.5 %collective-permute-start.15 = (bf16[2,256,384]{2,1,0:T(8,128)(2,1)}, bf16[2,256,384]{2,1,0:T(8,128)(2,1)S(1)}, u32[]{:S(2)}, u32[]{:S(2)}) collective-permute-start(bf16[2,256,384]{2,1,0:T(8,128)(2,1)} %get-tuple-element.191), channel_id=1, source_target_pairs={{0,1},{1,0},{2,3},{3,2},{4,7},{5,6},{6,5},{7,4},{8,9},{9,8},{10,11... | collective-permute-start | bytes 1179656 | tf_op jit(solution)/shard_map/ppermute | solution.py:841
  179.1 27.7 %copy-start.36 = (f32[3,1,256]{2,1,0:T(1,128)S(1)}, f32[3,1,256]{2,1,0:T(1,128)}, u32[]{:S(2)}) copy-start(f32[3,1,256]{2,1,0:T(1,128)} %get-tuple-element.206) | copy-start | bytes 9220
  179.1 27.7 %copy-start.11 = (bf16[4,6,96,128]{3,2,1,0:T(8,128)(2,1)S(1)}, bf16[4,6,96,128]{3,2,1,0:T(8,128)(2,1)}, u32[]{:S(2)}) copy-start(bf16[4,6,96,128]{3,2,1,0:T(8,128)(2,1)} %get-tuple-element.196) | copy-start | bytes 1769476
  179.1 27.7 %copy-start.13 = (bf16[4,6,96,128]{3,2,1,0:T(8,128)(2,1)S(1)}, bf16[4,6,96,128]{3,2,1,0:T(8,128)(2,1)}, u32[]{:S(2)}) copy-start(bf16[4,6,96,128]{3,2,1,0:T(8,128)(2,1)} %copy-done.12) | copy-start | bytes 1769476
  207.0 5.3 %copy-start.6 = (bf16[2,256,384]{2,1,0:T(8,128)(2,1)}, bf16[2,256,384]{2,1,0:T(8,128)(2,1)S(1)}, u32[]{:S(2)}) copy-start(bf16[2,256,384]{2,1,0:T(8,128)(2,1)S(1)} %collective-permute-done.15.refs_1_) | copy-start | bytes 1179652
  207.1 5.3 %copy-start = (bf16[2,256,768]{2,1,0:T(8,128)(2,1)}, bf16[2,256,768]{2,1,0:T(8,128)(2,1)S(1)}, u32[]{:S(2)}) copy-start(bf16[2,256,768]{2,1,0:T(8,128)(2,1)S(1)} %collective-permute-done.14.refs_2_.refs_3_) | copy-start | bytes 2359300
  207.8 14.0 %collective-permute-start.21 = (bf16[2,256,384]{2,1,0:T(8,128)(2,1)S(1)}, bf16[2,256,384]{2,1,0:T(8,128)(2,1)S(1)}, u32[]{:S(2)}, u32[]{:S(2)}) collective-permute-start(bf16[2,256,384]{2,1,0:T(8,128)(2,1)S(1)} %pad_maximum_fusion.10), channel_id=1, source_target_pairs={{0,3},{1,2},{2,1},{3,0},{4,5},{5,4},{6,7},{7,6},{8,11},{9,10},{10,... | collective-permute-start | bytes 1179656 | tf_op jit(solution)/shard_map/ppermute | solution.py:841
  210.6 4.6 %copy-start.22 = (f32[1,3072]{1,0:T(1,128)S(1)}, f32[1,3072]{1,0:T(1,128)}, u32[]{:S(2)}) copy-start(f32[1,3072]{1,0:T(1,128)} %get-tuple-element.208) | copy-start | bytes 36868
  212.3 25.2 %collective-permute-start.17 = (bf16[8,96,768]{2,1,0:T(8,128)(2,1)S(1)}, bf16[8,96,768]{2,1,0:T(8,128)(2,1)S(1)}, u32[]{:S(2)}, u32[]{:S(2)}) collective-permute-start(bf16[8,96,768]{2,1,0:T(8,128)(2,1)S(1)} %fusion.1), channel_id=1, source_target_pairs={{0,16},{4,12},{8,24},{12,4},{16,0},{20,28},{24,8},{28,20},{1,17},{... | collective-permute-start | bytes 3538952 | tf_op jit(solution)/shard_map/ppermute | solution.py:857
  213.9 23.6 %collective-permute-start.18 = (bf16[4,3,3,96,128]{4,3,2,1,0:T(8,128)(2,1)S(1)}, bf16[4,3,3,96,128]{4,3,2,1,0:T(8,128)(2,1)S(1)}, u32[]{:S(2)}, u32[]{:S(2)}) collective-permute-start(bf16[4,3,3,96,128]{4,3,2,1,0:T(8,128)(2,1)S(1)} %copy-done.37), channel_id=1, source_target_pairs={{0,4},{4,0},{8,12},{12,8},{16,20},{20,16},{24,28},{28,24},{1,5},{5... | collective-permute-start | bytes 2654216 | tf_op jit(solution)/shard_map/ppermute | solution.py:836
  214.0 24.2 %copy-start.7 = (bf16[4,3,3,96,128]{4,3,2,1,0:T(8,128)(2,1)S(1)}, bf16[4,3,3,96,128]{4,3,2,1,0:T(8,128)(2,1)}, u32[]{:S(2)}) copy-start(bf16[4,3,3,96,128]{4,3,2,1,0:T(8,128)(2,1)} %get-tuple-element.212) | copy-start | bytes 2654212
  214.0 23.6 %collective-permute-start.19 = (bf16[256,768]{1,0:T(8,128)(2,1)S(1)}, bf16[256,768]{1,0:T(8,128)(2,1)S(1)}, u32[]{:S(2)}, u32[]{:S(2)}) collective-permute-start(bf16[256,768]{1,0:T(8,128)(2,1)S(1)} %slice_bitcast_fusion.1), channel_id=1, source_target_pairs={{0,2},{1,3},{2,0},{3,1},{4,6},{5,7},{6,4},{7,5},{8,10},{9,11},{10,... | collective-permute-start | bytes 1179656 | tf_op jit(solution)/shard_map/ppermute | solution.py:841
  215.2 1.3 collective-permute-start.20
  221.7 16.7 %copy-start.4 = (bf16[2,256,384]{2,1,0:T(8,128)(2,1)}, bf16[2,256,384]{2,1,0:T(8,128)(2,1)S(1)}, u32[]{:S(2)}) copy-start(bf16[2,256,384]{2,1,0:T(8,128)(2,1)S(1)} %collective-permute-done.21.refs_2_.refs_3_) | copy-start | bytes 1179652
  237.6 8.4 %collective-permute-start.23 = (f32[69,128]{1,0:T(8,128)S(1)}, f32[69,128]{1,0:T(8,128)S(1)}, u32[]{:S(2)}, u32[]{:S(2)}) collective-permute-start(f32[69,128]{1,0:T(8,128)S(1)} %bitcast_add_fusion), channel_id=1, source_target_pairs={{0,8},{4,12},{8,0},{12,4},{16,24},{20,28},{24,16},{28,20},{1,9},{5... | collective-permute-start | bytes 105992 | tf_op jit(solution)/shard_map/ppermute | solution.py:857
  238.7 22.6 %collective-permute-start.22 = (bf16[2,21,96,128]{3,2,1,0:T(8,128)(2,1)S(1)}, bf16[2,21,96,128]{3,2,1,0:T(8,128)(2,1)S(1)}, u32[]{:S(2)}, u32[]{:S(2)}) collective-permute-start(bf16[2,21,96,128]{3,2,1,0:T(8,128)(2,1)S(1)} %pad_maximum_fusion.2), channel_id=1, source_target_pairs={{0,8},{4,20},{8,0},{12,28},{16,24},{20,4},{24,16},{28,12},{1,9},{5... | collective-permute-start | bytes 3096584 | tf_op jit(solution)/shard_map/ppermute | solution.py:857
  240.3 18.8 %collective-permute-start.24 = (bf16[256,768]{1,0:T(8,128)(2,1)S(1)}, bf16[256,768]{1,0:T(8,128)(2,1)S(1)}, u32[]{:S(2)}, u32[]{:S(2)}) collective-permute-start(bf16[256,768]{1,0:T(8,128)(2,1)S(1)} %slice_bitcast_fusion), channel_id=1, source_target_pairs={{0,1},{1,0},{2,3},{3,2},{4,7},{5,6},{6,5},{7,4},{8,9},{9,8},{10,11... | collective-permute-start | bytes 1179656 | tf_op jit(solution)/shard_map/ppermute | solution.py:841
  240.4 20.9 %collective-permute-start.25 = (bf16[256,768]{1,0:T(8,128)(2,1)S(1)}, bf16[256,768]{1,0:T(8,128)(2,1)S(1)}, u32[]{:S(2)}, u32[]{:S(2)}) collective-permute-start(bf16[256,768]{1,0:T(8,128)(2,1)S(1)} %copy-done.38), channel_id=1, source_target_pairs={{0,3},{1,2},{2,1},{3,0},{4,5},{5,4},{6,7},{7,6},{8,11},{9,10},{10,... | collective-permute-start | bytes 1179656 | tf_op jit(solution)/shard_map/ppermute | solution.py:841
  244.8 28.0 %collective-permute-start.26 = (bf16[2,2,96,768]{3,2,1,0:T(8,128)(2,1)S(1)}, bf16[2,2,96,768]{3,2,1,0:T(8,128)(2,1)S(1)}, u32[]{:S(2)}, u32[]{:S(2)}) collective-permute-start(bf16[2,2,96,768]{3,2,1,0:T(8,128)(2,1)S(1)} %pad_maximum_fusion.4), channel_id=1, source_target_pairs={{0,1},{1,0},{2,3},{3,2},{4,7},{5,6},{6,5},{7,4},{8,9},{9,8},{10,11... | collective-permute-start | bytes 1769480 | tf_op jit(solution)/shard_map/ppermute | solution.py:841
  259.1 14.1 %copy-start.18 = (bf16[256,768]{1,0:T(8,128)(2,1)}, bf16[256,768]{1,0:T(8,128)(2,1)S(1)}, u32[]{:S(2)}) copy-start(bf16[256,768]{1,0:T(8,128)(2,1)S(1)} %collective-permute-done.24.refs_1_) | copy-start | bytes 1179652
  261.3 11.8 %copy-start.19 = (bf16[256,768]{1,0:T(8,128)(2,1)}, bf16[256,768]{1,0:T(8,128)(2,1)S(1)}, u32[]{:S(2)}) copy-start(bf16[256,768]{1,0:T(8,128)(2,1)S(1)} %collective-permute-done.25.refs_2_) | copy-start | bytes 1179652
  261.6 11.2 %collective-permute-start.27 = (bf16[21,96,128]{2,1,0:T(8,128)(2,1)S(1)}, bf16[21,96,128]{2,1,0:T(8,128)(2,1)S(1)}, u32[]{:S(2)}, u32[]{:S(2)}) collective-permute-start(bf16[21,96,128]{2,1,0:T(8,128)(2,1)S(1)} %fusion.13), channel_id=1, source_target_pairs={{0,16},{4,12},{8,24},{12,4},{16,0},{20,28},{24,8},{28,20},{1,17},{... | collective-permute-start | bytes 1548296 | tf_op jit(solution)/shard_map/ppermute | solution.py:857
  263.2 9.5 %collective-permute-start.28 = (f32[69,128]{1,0:T(8,128)S(1)}, f32[69,128]{1,0:T(8,128)S(1)}, u32[]{:S(2)}, u32[]{:S(2)}) collective-permute-start(f32[69,128]{1,0:T(8,128)S(1)} %fusion.57), channel_id=1, source_target_pairs={{0,16},{4,20},{8,24},{12,28},{16,0},{20,4},{24,8},{28,12},{1,17},{... | collective-permute-start | bytes 105992 | tf_op jit(solution)/shard_map/ppermute | solution.py:857
  273.4 14.0 %collective-permute-start.29 = (bf16[2,96,768]{2,1,0:T(8,128)(2,1)S(1)}, bf16[2,96,768]{2,1,0:T(8,128)(2,1)S(1)}, u32[]{:S(2)}, u32[]{:S(2)}) collective-permute-start(bf16[2,96,768]{2,1,0:T(8,128)(2,1)S(1)} %slice_bitcast_fusion.5), channel_id=1, source_target_pairs={{0,3},{1,2},{2,1},{3,0},{4,5},{5,4},{6,7},{7,6},{8,11},{9,10},{10,... | collective-permute-start | bytes 884744 | tf_op jit(solution)/shard_map/ppermute | solution.py:841
  275.1 12.3 %collective-permute-start.30 = (bf16[2,21,24,128]{3,2,1,0:T(8,128)(2,1)S(1)}, bf16[2,21,24,128]{3,2,1,0:T(8,128)(2,1)S(1)}, u32[]{:S(2)}, u32[]{:S(2)}) collective-permute-start(bf16[2,21,24,128]{3,2,1,0:T(8,128)(2,1)S(1)} %pad_maximum_fusion.11), channel_id=1, source_target_pairs={{0,1},{1,0},{2,3},{3,2},{4,7},{5,6},{6,5},{7,4},{8,9},{9,8},{10,11... | collective-permute-start | bytes 774152 | tf_op jit(solution)/shard_map/ppermute | solution.py:841
  287.5 13.8 %collective-permute-start.31 = (bf16[2,96,768]{2,1,0:T(8,128)(2,1)S(1)}, bf16[2,96,768]{2,1,0:T(8,128)(2,1)S(1)}, u32[]{:S(2)}, u32[]{:S(2)}) collective-permute-start(bf16[2,96,768]{2,1,0:T(8,128)(2,1)S(1)} %fusion.12), channel_id=1, source_target_pairs={{0,3},{1,2},{2,1},{3,0},{4,5},{5,4},{6,7},{7,6},{8,11},{9,10},{10,... | collective-permute-start | bytes 884744 | tf_op jit(solution)/shard_map/ppermute | solution.py:841
  289.8 11.5 %collective-permute-start.32 = (bf16[21,24,128]{2,1,0:T(8,128)(2,1)S(1)}, bf16[21,24,128]{2,1,0:T(8,128)(2,1)S(1)}, u32[]{:S(2)}, u32[]{:S(2)}) collective-permute-start(bf16[21,24,128]{2,1,0:T(8,128)(2,1)S(1)} %slice_bitcast_fusion.17), channel_id=1, source_target_pairs={{0,3},{1,2},{2,1},{3,0},{4,5},{5,4},{6,7},{7,6},{8,11},{9,10},{10,... | collective-permute-start | bytes 387080 | tf_op jit(solution)/shard_map/ppermute | solution.py:841
  291.5 9.7 %collective-permute-start.33 = (f32[69,128]{1,0:T(8,128)S(1)}, f32[69,128]{1,0:T(8,128)S(1)}, u32[]{:S(2)}, u32[]{:S(2)}) collective-permute-start(f32[69,128]{1,0:T(8,128)S(1)} %add.282), channel_id=1, source_target_pairs={{0,1},{1,0},{2,3},{3,2},{4,5},{5,4},{6,7},{7,6},{8,9},{9,8},{10,11... | collective-permute-start | bytes 105992 | tf_op jit(solution)/shard_map/ppermute | solution.py:841
  301.3 26.2 %collective-permute-start.37 = (bf16[2,2,96,768]{3,2,1,0:T(8,128)(2,1)S(1)}, bf16[2,2,96,768]{3,2,1,0:T(8,128)(2,1)S(1)}, u32[]{:S(2)}, u32[]{:S(2)}) collective-permute-start(bf16[2,2,96,768]{3,2,1,0:T(8,128)(2,1)S(1)} %pad_maximum_fusion.5), channel_id=1, source_target_pairs={{0,1},{1,0},{2,3},{3,2},{4,7},{5,6},{6,5},{7,4},{8,9},{9,8},{10,11... | collective-permute-start | bytes 1769480 | tf_op jit(solution)/shard_map/ppermute | solution.py:841
  303.4 15.3 %collective-permute-start.34 = (f32[69,128]{1,0:T(8,128)S(1)}, f32[69,128]{1,0:T(8,128)S(1)}, u32[]{:S(2)}, u32[]{:S(2)}) collective-permute-start(f32[69,128]{1,0:T(8,128)S(1)} %add.288), channel_id=1, source_target_pairs={{0,3},{1,2},{2,1},{3,0},{4,7},{5,6},{6,5},{7,4},{8,11},{9,10},{10,... | collective-permute-start | bytes 105992 | tf_op jit(solution)/shard_map/ppermute | solution.py:841
  305.5 14.5 %collective-permute-start.35 = (bf16[21,24,128]{2,1,0:T(8,128)(2,1)S(1)}, bf16[21,24,128]{2,1,0:T(8,128)(2,1)S(1)}, u32[]{:S(2)}, u32[]{:S(2)}) collective-permute-start(bf16[21,24,128]{2,1,0:T(8,128)(2,1)S(1)} %fusion.17), channel_id=1, source_target_pairs={{0,3},{1,2},{2,1},{3,0},{4,5},{5,4},{6,7},{7,6},{8,11},{9,10},{10,... | collective-permute-start | bytes 387080 | tf_op jit(solution)/shard_map/ppermute | solution.py:841
  320.1 6.7 %collective-permute-start.36 = (bf16[2,21,24,128]{3,2,1,0:T(8,128)(2,1)S(1)}, bf16[2,21,24,128]{3,2,1,0:T(8,128)(2,1)S(1)}, u32[]{:S(2)}, u32[]{:S(2)}) collective-permute-start(bf16[2,21,24,128]{3,2,1,0:T(8,128)(2,1)S(1)} %pad_maximum_fusion.12), channel_id=1, source_target_pairs={{0,1},{1,0},{2,3},{3,2},{4,7},{5,6},{6,5},{7,4},{8,9},{9,8},{10,11... | collective-permute-start | bytes 774152 | tf_op jit(solution)/shard_map/ppermute | solution.py:841
  (19 other events, 32.4 us)

commit v4 on v3

--- a/solution.py
+++ b/solution.py
@@ -17,6 +17,7 @@
 F32 = jnp.float32
 VMEM_BYTES = 56 << 20
 CODE_ROWS = 16
+GAIN_ROWS, Q_ROWS, V_ROWS, SUM_ROWS = 6, 12, 18, 72
 ATTN_GAIN, ATTN_SHIFT, OUT_BIAS, MLP_GAIN, MLP_SHIFT, DOWN_BIAS = (slice(n, n + 1) for n in range(6))
 
 
@@ -218,11 +219,13 @@
     o_ref, do_ref, lse_ref, normed_ref = take(4)
     w_refs = take(2 if split else 3)
     before_ref = None if first_call else take(1)[0]
-    x_ref, vec_ref, d_att_ref = take(3) if last_call else (None, None, None)
-    send_ref, keep_ref, bias_sums_ref = take(3)
+    if last_call:
+        x_ref, vec_ref, d_att_ref, mlp_sums_ref, up_sums_ref, other_sums_ref = take(6)
+    send_ref, keep_ref = take(2)
+    bias_sums_ref = None if last_call else take(1)[0]
     piece_refs = take(3) if split else []
     if last_call:
-        *y_refs, sums_ref = take(4)
+        *y_refs, packed_ref = take(4)
     else:
         (after_ref,) = take(1)
     bias_ref, value_ref, dkt_ref, dvt_ref, d_ref, w_ref, acc_ref, stage_ref = refs
@@ -277,17 +280,30 @@
     for n, ref in enumerate(w_refs):
         w_ref[:, lane(n)] = ref[...]
     grad = d_ref[...]
-    bias_sums_ref[0] = column_sums(grad.astype(F32))
+    sums = column_sums(grad.astype(F32))
+    if last_call:
+        packed_ref[pl.ds(Q_ROWS + step, 1), :] = sums[:, lane(0)]
+        packed_ref[pl.ds(V_ROWS + step, 1), :] = sums[:, lane(2)]
+    else:
+        bias_sums_ref[0] = sums
     acc_ref[...] += nt(grad, w_ref[...])
-    store_units(tn(normed_ref[...], grad), me_ref[1], stage_ref, send_ref, keep_ref, (0,))
+    store_units(tn(normed_ref[...], grad), me_ref, stage_ref, send_ref, keep_ref, (0,))
 
     @pl.when(step == pl.num_programs(0) - 1)
     def _():
         if last_call:
             total = acc_ref[...]
             unit, rate = standardize(x_ref[...].astype(F32))
-            sums_ref[0:1, :] = column_sums(total * unit)
-            sums_ref[1:2, :] = column_sums(total)
+            rows_of = lambda ref, row: [ref[row : row + 1, lane(n)] for n in range(ref.shape[1] // PAIR)]
+            for first_row, vector in ((0, column_sums(total * unit)), (GAIN_ROWS, column_sums(total))):
+                for n in range(GAIN_ROWS):
+                    packed_ref[first_row + n : first_row + n + 1, :] = vector[:, lane(n)]
+            others = [other_sums_ref[p, :, lane(0)] for p in range(other_sums_ref.shape[0])]
+            tail_rows = rows_of(mlp_sums_ref, 2) + rows_of(mlp_sums_ref, 0) + rows_of(mlp_sums_ref, 1)
+            tail_rows += rows_of(up_sums_ref, 0) + rows_of(mlp_sums_ref, 3)
+            for first_row, values in ((Q_ROWS + len(others), others), (V_ROWS + len(others), tail_rows)):
+                for n, value in enumerate(values):
+                    packed_ref[first_row + n : first_row + n + 1, :] = value
             acc_ref[...] = d_att_ref[...].astype(F32) + standardize_back(total * vec_ref[ATTN_GAIN], unit, rate)
             deal_out(me_ref, acc_ref, *y_refs)
         else:
@@ -339,21 +355,24 @@
         + [w_spec(n * count + pair) for n in range(units)]
     )
     args = [code, proj, proj, *v_arrays, o, do, lse, normed] + [w] * units
-    out_specs = [grads, grads, pl.BlockSpec((1, 1, cols), lambda p, at: (p, 0, 0))]
-    out_shape = [shape((4, pairs, units, strip, PAIR))] * 2 + [shape((pairs, 1, cols), F32)]
+    out_specs = [grads, grads]
+    out_shape = [shape((4, pairs, units, strip, PAIR))] * 2
+    if last is None:
+        out_specs.append(pl.BlockSpec((1, 1, cols), lambda p, at: (p, 0, 0)))
+        out_shape.append(shape((pairs, 1, cols), F32))
     if before is not None:
         in_specs.append(full)
         args.append(before)
     if last is not None:
-        in_specs += [full, once(last[1].shape), full]
+        in_specs += [full, once(last[1].shape), full] + [once(v.shape) for v in last[3:]]
         args += last
     if split:
         one = pl.BlockSpec((part, PAIR), lambda p, at: (0, p))
         out_specs += [one, pl.BlockSpec((2, part, PAIR), lambda p, at: (0, 0, p)), one]
         out_shape += [shape((part, pairs * PAIR)), shape((2, part, pairs * PAIR)), shape((part, pairs * PAIR))]
     if last is not None:
-        out_specs += [once((part, width)), once((2, part, width)), once((part, width)), once((8, width))]
-        out_shape += [shape((part, width)), shape((2, part, width)), shape((part, width)), shape((8, width), F32)]
+        out_specs += [once((part, width)), once((2, part, width)), once((part, width)), once((SUM_ROWS, PAIR))]
+        out_shape += [shape((part, width)), shape((2, part, width)), shape((part, width)), shape((SUM_ROWS, PAIR), F32)]
     else:
         out_specs.append(full)
         out_shape.append(shape((length, width), F32))
@@ -383,20 +402,30 @@
 GELU_B = 0.044715
 
 
-def split_store(grad, core, stage_ref, send_ref, keep_ref, lead):
+def plane_order(core):
+    return 3, 1 + core, 2 - core, 0
+
+
+def plane_place(chip, core):
+    return jnp.where(chip == 3, 0, jnp.where(chip == 0, 3, jnp.where(chip == 1 + core, 1, 2)))
+
+
+def split_store(grad, at_ref, stage_ref, send_ref, keep_ref, lead):
+    core, chip = at_ref[1], at_ref[2]
     stage_ref[...] = grad.astype(BF16).reshape(stage_ref.shape)
-    for j in range(4):
-        send_ref[(j,) + lead] = stage_ref[j, 1 - core]
-        keep_ref[(j,) + lead] = stage_ref[j, core]
-
-
-def store_units(grad, core, stage_ref, send_ref, keep_ref, lead):
+    for j, (theirs, mine) in enumerate(zip(plane_order(1 - core), plane_order(core))):
+        send_ref[(j,) + lead] = stage_ref[chip ^ theirs, 1 - core]
+        keep_ref[(j,) + lead] = stage_ref[chip ^ mine, core]
+
+
+def store_units(grad, at_ref, stage_ref, send_ref, keep_ref, lead):
+    core, chip = at_ref[1], at_ref[2]
     stage_ref[...] = grad.astype(BF16).reshape(stage_ref.shape)
     for u in range(stage_ref.shape[3] // PAIR):
         lanes = slice(u * PAIR, (u + 1) * PAIR)
-        for j in range(4):
-            send_ref[(j,) + lead + (u,)] = stage_ref[j, 1 - core, :, lanes]
-            keep_ref[(j,) + lead + (u,)] = stage_ref[j, core, :, lanes]
+        for j, (theirs, mine) in enumerate(zip(plane_order(1 - core), plane_order(core))):
+            send_ref[(j,) + lead + (u,)] = stage_ref[chip ^ theirs, 1 - core, :, lanes]
+            keep_ref[(j,) + lead + (u,)] = stage_ref[chip ^ mine, core, :, lanes]
 
 
 def feed_kernel(
@@ -441,7 +470,7 @@
     down_keep_ref[0] = down_stage_ref[core]
     up_bias_ref[...] = column_sums(d_pre.astype(F32))
     acc_ref[...] += nt(d_pre, wu_ref[...])
-    split_store(tn(normed_ref[...], d_pre), core, up_stage_ref, up_send_ref, up_keep_ref, (0,))
+    split_store(tn(normed_ref[...], d_pre), at_ref, up_stage_ref, up_send_ref, up_keep_ref, (0,))
 
     @pl.when(step == pl.num_programs(0) - 1)
     def _():
@@ -457,7 +486,7 @@
         sums_ref[3:4, :] = column_sums(dy_f)
         d_o_ref[...] = nt(d_att, wo_ref[...]).astype(BF16)
         grad = jnp.concatenate([tn(oa_ref[...], d_att), tn(ob_ref[...], d_att)], axis=0)
-        store_units(grad, core, out_stage_ref, out_send_ref, out_keep_ref, ())
+        store_units(grad, at_ref, out_stage_ref, out_send_ref, out_keep_ref, ())
 
 
 def feed(at, x, o_a, o_b, dy_pieces, w_out, vecs, w_up, up_bias, w_down):
@@ -465,7 +494,8 @@
     ff = w_up.shape[1]
     part = length // 4
     strip, shard, chunk, units = width // 8, ff // 8, ff // 4, width // PAIR
-    down = pl.BlockSpec((1, shard, width), lambda c, at: (c, 0, 0))
+    down_send = pl.BlockSpec((1, shard, width), lambda c, at: (plane_place(c ^ at[2], 1 - at[1]), 0, 0))
+    down_keep = pl.BlockSpec((1, shard, width), lambda c, at: (plane_place(c ^ at[2], at[1]), 0, 0))
     up = pl.BlockSpec((4, 1, strip, chunk), lambda c, at: (0, c, 0, 0))
     cols = pl.BlockSpec((1, chunk), lambda c, at: (0, c))
     full = once((length, width))
@@ -480,7 +510,7 @@
             cols,
             pl.BlockSpec((chunk, width), lambda c, at: (c, 0)),
         ],
-        [once((part, width)), once((2, part, width)), once((part, width)), down, down, up, up, cols, full, full, once((8, width)), once((4, units, strip, PAIR)), once((4, units, strip, PAIR))],
+        [once((part, width)), once((2, part, width)), once((part, width)), down_send, down_keep, up, up, cols, full, full, once((8, width)), once((4, units, strip, PAIR)), once((4, units, strip, PAIR))],
         [shape((part, width)), shape((2, part, width)), shape((part, width))]
         + [shape((4, shard, width))] * 2
         + [shape((4, 4, strip, chunk))] * 2
@@ -825,6 +855,10 @@
     return lax.optimization_barrier((first, second))
 
 
+def after(value, *others):
+    return lax.optimization_barrier((value, *others))[0]
+
+
 def add_up(parts):
     total = parts[0].astype(F32)
     for part in parts[1:]:
@@ -865,20 +899,12 @@
     return plane_swap(array, 4, 2)
 
 
-def plane_first(pairs, plane, core):
-    bit = 1 + core
-    away, stay = [], []
-    for other in range(2):
-        at = (plane & bit) | (other * (3 - bit))
-        stay.append(jnp.concatenate([add_up([pick(a, at), pick(b, at)]) for a, b in pairs]))
-        away.append(jnp.concatenate([add_up([pick(a, at ^ bit), pick(b, at ^ bit)]) for a, b in pairs]))
-    return jnp.stack(away), jnp.stack(stay)
-
-
-def plane_second(got, keep, plane, core):
-    mine = jnp.where(plane & (2 - core) > 0, 1, 0)
-    both = lambda at: add_up([pick(got, at), pick(keep, at)])
-    return both(1 - mine), both(mine)
+def plane_away(pairs):
+    return jnp.concatenate([add_up([a[:2], b[:2]]) for a, b in pairs], axis=1)
+
+
+def plane_stay(pairs):
+    return jnp.concatenate([add_up([a[2:], b[2:]]) for a, b in pairs], axis=1)
 
 
 def group_first(blocks, me, core):
@@ -921,7 +947,7 @@
     seq = lax.axis_index("seq")
     core, plane = seq & 1, seq >> 1
     near, far = 1 + 2 * core, 3 - 2 * core
-    at = jnp.stack([me, core]).astype(jnp.int32)
+    at = jnp.stack([me, core, plane]).astype(jnp.int32)
     rows, part, width = tokens.shape
     length = rows * part
     fresh = width // 2
@@ -940,9 +966,10 @@
     code = jnp.broadcast_to(jnp.pad(code, ((0, 0), (0, width - part)))[:, None], (rows, CODE_ROWS, width))
     tokens_at = lambda d: jnp.concatenate([pick(tokens, me ^ d), pick(code, me ^ d)])
     pro = lambda way, piece, so_far: project(at, way, piece, vecs, w_qkv, affine, length, so_far)
-    near_x = near_swap(tokens_at(near))
-    far_x = far_swap(tokens_at(far))
-    across_x = across_swap(tokens_at(2))
+    near_x = tokens_at(near)
+    far_x = after(tokens_at(far), near_x)
+    across_x = after(tokens_at(2), far_x)
+    near_x, far_x, across_x = near_swap(near_x), far_swap(far_x), across_swap(across_x)
     so_far = pro(0, tokens_at(0), ())
     so_far = pro(1, near_x, so_far)
     so_far = pro(2, far_x, so_far)
@@ -972,92 +999,73 @@
     from_b, (down_got, up_got, y_got, out_got) = gate(from_b, (down_got, up_got, y_got, out_got))
     b_send, b_keep, b_bias, s_own, s_away, s_far, d_normed = from_b
     lines = lambda v: v.reshape(4, -1, strip, width)
-    big_away, big_stay = plane_first([(up_got, up_keep), (lines(down_got), lines(down_keep))], plane, core)
+    big_pairs = [(up_got, up_keep), (lines(down_got), lines(down_keep))]
+    big_away = plane_away(big_pairs)
     y_last = forward(y_far, y_got)
-    (d_normed, s_away, b_send), (big_away, big_stay, y_last) = gate((d_normed, s_away, b_send), (big_away, big_stay, y_last))
+    (d_normed, s_away, b_send), (big_away, y_last) = gate((d_normed, s_away, b_send), (big_away, y_last))
     big_got = first_hop(big_away)
     y_last = far_swap(y_last)
     s_got = near_swap(s_away)
     b_got = across_cores(b_send)
     from_a = attend_back(
-        at, code_row, proj, [proj], o_a, d_o, lse_a, normed, w_qkv, 0, 3, 0, d_normed, [x, vecs, d_att], "attend_back_a"
+        at, code_row, proj, [proj], o_a, d_o, lse_a, normed, w_qkv, 0, 3, 0, d_normed,
+        [x, vecs, d_att, mlp_sums, g_up_bias, b_bias], "attend_back_a"
     )
     from_a, (big_got, y_last, s_got, b_got) = gate(from_a, (big_got, y_last, s_got, b_got))
-    a_send, a_keep, a_bias, x_own, x_away, x_far, token_sums = from_a
-
-    q_sums = jnp.concatenate([v[:, 0, :PAIR].reshape(-1) for v in (a_bias, b_bias)])
-    v_sums = a_bias[:, 0, 2 * PAIR :].reshape(-1)
-    small = (
-        token_sums[0],
-        token_sums[1],
-        q_sums,
-        v_sums,
-        mlp_sums[2],
-        mlp_sums[0],
-        mlp_sums[1],
-        g_up_bias[0],
-        mlp_sums[3],
-    )
-    packed = jnp.concatenate(small).reshape(-1, 128)
+    a_send, a_keep, x_own, x_away, x_far, packed = from_a
+
     units = lambda v: v.reshape(4, -1, strip, PAIR)
 
-    x_across = across_swap(x_away[1])
-    a_got = across_cores(a_send)
-    big_send, big_stay = plane_second(big_got, big_stay, plane, core)
-    big_got = second_hop(big_send)
-    small_got = across_cores(packed)
     s_last = far_swap(forward(s_far, s_got))
-
-    (big_got, a_got, x_away, x_far), (x_across, small_got, s_last) = gate(
-        (big_got, a_got, x_away, x_far), (x_across, small_got, s_last)
-    )
     x_near = near_swap(x_away[0])
     x_far = far_swap(x_far)
-    big = add_up([big_got, big_stay]).reshape(2, 4, strip, width).transpose(1, 0, 2, 3)
+    a_got = across_cores(a_send)
+    big_half = add_up([big_got, plane_stay(big_pairs)])
+    big_got = second_hop(big_half[0])
+    layer_out = settle(at, [y_own, (y_got, 0), (y_last, 0), (y_last, 1)], BF16, "settle_out")
+    (big_got, a_got, packed, x_away), (layer_out, s_last, x_near, x_far) = gate(
+        (big_got, a_got, packed, x_away), (layer_out, s_last, x_near, x_far)
+    )
+
+    x_across = across_swap(x_away[1])
+    grad_skip = settle(at, [s_own, (s_got, 0), (s_last, 0), (s_last, 1)], F32, "settle_skip")
+    rest_pairs = [(out_got, out_keep), (units(b_got), units(b_keep)), (units(a_got), units(a_keep))]
+    rest_got = first_hop(plane_away(rest_pairs))
+    small_got = group_swap(packed, 1, 1)
+    big = add_up([big_got, big_half[1]]).reshape(2, 4, strip, width).transpose(1, 0, 2, 3)
     big_send, big_keep = group_first(big, me, core)
+    (big_send, rest_got), (x_across, small_got, grad_skip) = gate((big_send, rest_got), (x_across, small_got, grad_skip))
+
     big_got = near_swap(big_send)
-    rest_away, rest_stay = plane_first(
-        [(out_got, out_keep), (units(b_got), units(b_keep)), (units(a_got), units(a_keep))], plane, core
-    )
-    rest_got = first_hop(rest_away)
     packed = packed + small_got
-    small_got = plane_swap(packed, 2, 2)
-
-    rest_got, (small_got, x_near, x_far) = gate(rest_got, (small_got, x_near, x_far))
-    rest_send, rest_stay = plane_second(rest_got, rest_stay, plane, core)
-    rest_got = second_hop(rest_send)
-    packed = packed + small_got
-    small_got = plane_swap(packed, 4, 4)
-
-    big_got, (rest_got, small_got) = gate(big_got, (rest_got, small_got))
-    rest = add_up([rest_got, rest_stay]).reshape(-1, 4, strip // 4, PAIR).transpose(1, 0, 2, 3)
+    small_got = group_swap(packed, 3, 3)
+    rest_half = add_up([rest_got, plane_stay(rest_pairs)])
+    rest_got = second_hop(rest_half[0])
+    rest = add_up([rest_got, rest_half[1]]).reshape(-1, 4, strip // 4, PAIR).transpose(1, 0, 2, 3)
     rest_send, rest_keep = group_first(rest, me, core)
     rest_got = near_swap(rest_send)
-    big_sum = add_up([big_got, big_keep])
+    grad_tokens = settle(at, [x_own, x_near, x_far, x_across], F32, "settle_tokens")
+
+    big_sum = add_up([after(big_got, rest_send, grad_tokens), big_keep])
     big_got = far_swap(big_sum[1])
-    packed = packed + small_got
-    small_got = group_swap(packed, 1, 1)
-
-    big_got, rest_got = gate(big_got, rest_got)
-    rest_sum = add_up([rest_got, rest_keep])
+    packed = packed + after(small_got, big_sum)
+    small_got = across_cores(packed)
+    rest_sum = add_up([after(rest_got, big_sum), rest_keep])
     rest_got = far_swap(rest_sum[1])
-    big_own = add_up([big_got, big_sum[0]])
+    big_own = add_up([after(big_got, rest_sum), big_sum[0]])
     big_far = far_swap(big_own)
-
-    (big_far, rest_got), small_got = gate((big_far, rest_got), small_got)
-    rest_own = add_up([rest_got, rest_sum[0]])
+    packed = packed + after(small_got, big_own)
+    small_got = plane_swap(packed, 2, 2)
+    rest_own = add_up([after(rest_got, big_own), rest_sum[0]])
     rest_far = far_swap(rest_own)
-    packed = packed + small_got
-    small_got = group_swap(packed, 3, 3)
-    big_near = near_swap(jnp.stack([big_own, big_far]))
+    big_near = near_swap(jnp.stack([big_own, after(big_far, rest_own)]))
+    packed = packed + after(small_got, rest_own)
+    small_got = plane_swap(packed, 4, 4)
     rest_near = near_swap(jnp.stack([rest_own, rest_far]))
     packed = (packed + small_got).reshape(-1)
 
-    layer_out = settle(at, [y_own, (y_got, 0), (y_last, 0), (y_last, 1)], BF16, "settle_out")
-    grad_skip = settle(at, [s_own, (s_got, 0), (s_last, 0), (s_last, 1)], F32, "settle_skip")
-    grad_tokens = settle(at, [x_own, x_near, x_far, x_across], F32, "settle_tokens")
+    rest = jnp.concatenate(by_owner(rest_own, rest_far, rest_near, me, core), axis=1).astype(F32)
     big = by_owner(big_own, big_far, big_near, me, core)
-    rest = jnp.concatenate(by_owner(rest_own, rest_far, rest_near, me, core), axis=1).astype(F32)
     r_up = jnp.concatenate([q[0] for q in big], axis=1).astype(F32)
     r_down = jnp.concatenate([q[1] for q in big], axis=0).astype(F32)
     count = width // PAIR
@@ -1066,9 +1074,9 @@
     order = [unit_of(p, n) for n in range(2) for p in range(count)] + [unit_of(p, 2) for p in range(count // 2)]
     r_qkv = jnp.concatenate(order, axis=1)
     sums = []
-    for entry in small:
-        sums.append(packed[: entry.shape[0]])
-        packed = packed[entry.shape[0] :]
+    for size in (width, width, width, fresh, width, width, width, ff, width):
+        sums.append(packed[:size])
+        packed = packed[size:]
     return (
         layer_out,
         grad_tokens,

time: 336 us -> 330 us (0.982)
  starting transfers between devices: 45.9 us -> 42.5 us
    ppermute x6, waiting for transfers between devices: 0.02 us -> 4.93 us  [plane_swap(): lax.ppermute(array, 'seq', [(s, s ^ (core_one if s & 1 else core_zero)) f...]
    ppermute x26, waiting for transfers between devices: 98.6 us -> 94.5 us  [group_swap(): return lax.ppermute(array, ('seq', 'head'), pairs)]
    convert_element_type x12 -> x13, other arithmetic: 8.26 us -> 5.66 us  [add_up(): return total.astype(BF16)]
  transfers between devices with their start and end apart: 38 -> 38, of which waited for: 14 -> 18; matrix products, arithmetic and copies ran while one was open for 4% -> 4% of each run, Pallas kernels for 31% -> 32%
where the time goes in v4:
time: 330 us; the launch traced here: 325 us
  Pallas kernels  153 us (46%)
  waiting for transfers between devices  99.5 us (30%)
  starting transfers between devices  42.5 us (13%)
  other arithmetic  14.7 us (4%)
  local copies, waits for them, and re-layouts  13.7 us (4%)
    ppermute x26, waiting for transfers between devices, group_swap(): return lax.ppermute(array, ('seq', 'head'), pairs)  94.5 us
    pallas_call x1, Pallas kernels, feed(): call(feed_kernel, 'feed', (4,), [full, once(o_a.shape), once(o_b.shape)]...  48.5 us
    pallas_call x2, Pallas kernels, attend_back(): call(functools.partial(backward_kernel, len(values), before is None, last...  47.8 us
    ppermute x26, starting transfers between devices, group_swap(): return lax.ppermute(array, ('seq', 'head'), pairs)  35.4 us
    pallas_call x2, Pallas kernels, attend(): call(functools.partial(forward_kernel, len(values)), name, (pairs,), [who...  26.7 us
    pallas_call x4, Pallas kernels, project(): call(project_kernel, 'project', (1,), [whole((part + CODE_ROWS, width)),...  19.5 us
    pallas_call x3, Pallas kernels, settle(): call(settle_kernel, name, (2,), specs, pl.BlockSpec((4, rows, width), lam...  10 us
    unnamed x92, local copies, waits for them, and re-layouts  6.63 us
  transfers between devices with their start and end apart: 38, of which 18 were waited for; matrix products, arithmetic and copies ran while one was open for 4% of the time, Pallas kernels for 32%

profile of v4, /device:TPU:0, one launch (start us, length us, event | category | flops | bytes accessed | tf_op | source)
XLA Modules:
  0.0 324.9 jit_solution(8703232498370769771)
XLA Ops:
  1.4 1.5 dynamic-slice_bitcast_fusion.4
  3.0 3.1 collective-permute-start.2
  6.2 2.5 collective-permute-start.1
  12.4 4.8 %project.4 = (bf16[1024,768]{1,0:T(8,128)(2,1)}, bf16[1024,768]{1,0:T(8,128)(2,1)}, bf16[1024,1920]{1,0:T(8,128)(2,1)}, s32[8,1024]{1,0:T(8,128)}) custom-call(s32[3]{0:T(128)} %pad_add_fusion.at_ref.me_ref, bf16[272,768]{1,0:T(8,128)(2,1)} %pad_maximum_fusion.8.x_ref, f32[8,768]{1,0:T(8,128)} %convert_element_type.233.vec_ref.refs_10_, ...), custom_call_target="tpu_custom_call" | custom-call | flops 754974720 | bytes 5111808 | tf_op jit(solution)/shard_map/project/pallas_call | solution.py:140
  17.2 3.0 collective-permute-done.2.x_ref
  21.0 4.9 %project.5 = (bf16[1024,768]{1,0:T(8,128)(2,1)}, bf16[1024,768]{1,0:T(8,128)(2,1)}, bf16[1024,1920]{1,0:T(8,128)(2,1)}, s32[8,1024]{1,0:T(8,128)}) custom-call(s32[3]{0:T(128)} %pad_add_fusion.at_ref.me_ref, bf16[272,768]{1,0:T(8,128)(2,1)} %copy-done.14, ...), custom_call_target="tpu_custom_call", output_to_operand_aliasing={{0}: (5, {}), {1}: (6, {}), {2}: (7, {}), {3}: (8, {})} | custom-call | flops 754974720 | bytes 5111808 | tf_op jit(solution)/shard_map/project/pallas_call | solution.py:140
  25.9 2.3 collective-permute-done.1.x_ref
  28.9 5.0 %project.6 = (bf16[1024,768]{1,0:T(8,128)(2,1)}, bf16[1024,768]{1,0:T(8,128)(2,1)}, bf16[1024,1920]{1,0:T(8,128)(2,1)}, s32[8,1024]{1,0:T(8,128)}) custom-call(s32[3]{0:T(128)} %pad_add_fusion.at_ref.me_ref, bf16[272,768]{1,0:T(8,128)(2,1)} %copy-done.15, ...), custom_call_target="tpu_custom_call", output_to_operand_aliasing={{0}: (5, {}), {1}: (6, {}), {2}: (7, {}), {3}: (8, {})} | custom-call | flops 754974720 | bytes 5111808 | tf_op jit(solution)/shard_map/project/pallas_call | solution.py:140
  34.0 9.9 %collective-permute-done.x_ref = bf16[272,768]{1,0:T(8,128)(2,1)S(1)} collective-permute-done((bf16[272,768]{1,0:T(8,128)(2,1)S(1)}, bf16[272,768]{1,0:T(8,128)(2,1)S(1)}, u32[]{:S(2)}, u32[]{:S(2)}) %collective-permute-start) | collective-permute-done | bytes 417824 | tf_op jit(solution)/shard_map/ppermute | solution.py:875
  43.8 0.8 dynamic-slice_bitcast_fusion.12
  44.6 2.5 collective-permute-start.4
  47.1 1.0 collective-permute-start.5
  48.2 1.0 collective-permute-start.6
  49.2 2.1 collective-permute-start.8
  51.3 4.8 %project.7 = (bf16[1024,768]{1,0:T(8,128)(2,1)}, bf16[1024,768]{1,0:T(8,128)(2,1)}, bf16[1024,1920]{1,0:T(8,128)(2,1)}, s32[8,1024]{1,0:T(8,128)}) custom-call(s32[3]{0:T(128)} %pad_add_fusion.at_ref.me_ref, bf16[272,768]{1,0:T(8,128)(2,1)} %copy-done.13, ...), custom_call_target="tpu_custom_call", output_to_operand_aliasing={{0}: (5, {}), {1}: (6, {}), {2}: (7, {}), {3}: (8, {})} | custom-call | flops 754974720 | bytes 5111808 | tf_op jit(solution)/shard_map/project/pallas_call | solution.py:140
  56.1 13.6 %attend_a.1 = (bf16[1024,384]{1,0:T(8,128)(2,1)}, f32[1024,384]{1,0:T(8,128)}) custom-call(s32[3]{0:T(128)} %pad_add_fusion.at_ref.me_ref, s32[8,1024]{1,0:T(8,128)} %get-tuple-element.144.code_ref, bf16[1024,1920]{1,0:T(8,128)(2,1)} %get-tuple-element.145.q_ref.k_ref.refs_0_, bf16[1024,1920]{1,0:T(8,128)(2,1)} %get-tuple-element.145.q_ref.k_ref.refs_0_, ...), custom_call_target="tpu_custom_call" | custom-call | flops 9663676416 | bytes 4718592 | tf_op jit(solution)/shard_map/attend_a/pallas_call | solution.py:326
  69.7 8.4 %collective-permute-done.5.refs_3_ = bf16[256,384]{1,0:T(8,128)(2,1)S(1)} collective-permute-done((bf16[256,384]{1,0:T(8,128)(2,1)S(1)}, bf16[256,384]{1,0:T(8,128)(2,1)S(1)}, u32[]{:S(2)}, u32[]{:S(2)}) %collective-permute-start.5) | collective-permute-done | bytes 196640 | tf_op jit(solution)/shard_map/ppermute | solution.py:875
  78.1 0.8 dynamic-slice_bitcast_fusion.1
  78.9 1.7 collective-permute-start.7
  80.6 13.2 %attend_b.1 = (bf16[1024,384]{1,0:T(8,128)(2,1)}, f32[1024,384]{1,0:T(8,128)}) custom-call(s32[3]{0:T(128)} %pad_add_fusion.at_ref.me_ref, s32[8,1024]{1,0:T(8,128)} %get-tuple-element.144.code_ref, bf16[1024,1920]{1,0:T(8,128)(2,1)} %get-tuple-element.145.q_ref.k_ref.refs_0_, bf16[1024,1920]{1,0:T(8,128)(2,1)} %get-tuple-element.145.q_ref.k_ref.refs_0_, ...), custom_call_target="tpu_custom_call" | custom-call | flops 9663676416 | bytes 4718592 | tf_op jit(solution)/shard_map/attend_b/pallas_call | solution.py:326
  94.8 48.5 %feed.1 = (bf16[256,768]{1,0:T(8,128)(2,1)}, bf16[2,256,768]{2,1,0:T(8,128)(2,1)}, bf16[256,768]{1,0:T(8,128)(2,1)}, bf16[4,384,768]{2,1,0:T(8,128)(2,1)}, bf16[...) custom-call(s32[3]{0:T(128)} %pad_add_fusion.at_ref.me_ref, ...), custom_call_target="tpu_custom_call" | custom-call | flops 32614907904 | bytes 33423360 | tf_op jit(solution)/shard_map/feed/pallas_call | solution.py:503
  144.0 3.0 collective-permute-start.11
  147.0 20.6 %attend_back_b.1 = (bf16[4,3,2,96,128]{4,3,2,1,0:T(8,128)(2,1)}, bf16[4,3,2,96,128]{4,3,2,1,0:T(8,128)(2,1)}, f32[3,1,256]{2,1,0:T(1,128)}, bf16[256,384]{1,0:T(...) custom-call(s32[3]{0:T(128)} %pad_add_fusion.at_ref.me_ref, ...), custom_call_target="tpu_custom_call" | custom-call | flops 14495514624 | bytes 16515072 | tf_op jit(solution)/shard_map/attend_back_b/pallas_call | solution.py:379
  167.6 0.9 copy-done.3
  169.1 1.1 copy-done.1
  172.0 1.0 pad_maximum_fusion.2
  172.9 1.5 collective-permute-start.13
  174.4 1.4 collective-permute-start.14
  176.3 27.3 %attend_back_a.1 = (bf16[4,3,3,96,128]{4,3,2,1,0:T(8,128)(2,1)}, bf16[4,3,3,96,128]{4,3,2,1,0:T(8,128)(2,1)}, bf16[256,768]{1,0:T(8,128)(2,1)}, bf16[2,256,768]{...) custom-call(s32[3]{0:T(128)} %pad_add_fusion.at_ref.me_ref, s32[8,1024]{1,0:T(8,128)} %get-tuple-element.144.code_ref, ...), custom_call_target="tpu_custom_call" | custom-call | flops 15703474176 | bytes 16515072 | tf_op jit(solution)/shard_map/attend_back_a/pallas_call | solution.py:379
  204.7 1.5 collective-permute-start.17
  206.2 0.8 pad_maximum_fusion.9
  207.0 2.0 collective-permute-start.19
  209.8 1.1 collective-permute-start.20
  210.9 1.4 collective-permute-start.21
  212.3 1.2 add_convert_fusion.10
  213.5 3.2 settle_out.1
  216.8 1.3 add_convert_fusion.9
  218.1 3.1 collective-permute-done.19.refs_2_.refs_3_
  221.1 9.4 %collective-permute-done.20.refs_1_ = bf16[256,768]{1,0:T(8,128)(2,1)S(1)} collective-permute-done((bf16[256,768]{1,0:T(8,128)(2,1)}, bf16[256,768]{1,0:T(8,128)(2,1)S(1)}, u32[]{:S(2)}, u32[]{:S(2)}) %collective-permute-start.20) | collective-permute-done | bytes 393248 | tf_op jit(solution)/shard_map/ppermute | solution.py:875
  230.5 7.1 %collective-permute-done.21.refs_2_ = bf16[256,768]{1,0:T(8,128)(2,1)S(1)} collective-permute-done((bf16[256,768]{1,0:T(8,128)(2,1)}, bf16[256,768]{1,0:T(8,128)(2,1)S(1)}, u32[]{:S(2)}, u32[]{:S(2)}) %collective-permute-start.21) | collective-permute-done | bytes 393248 | tf_op jit(solution)/shard_map/ppermute | solution.py:875
  239.8 1.1 collective-permute-start.23
  241.1 1.1 collective-permute-start.24
  242.4 3.1 settle_skip.1
  245.6 4.1 %collective-permute-done.24 = f32[72,128]{1,0:T(8,128)S(1)} collective-permute-done((f32[72,128]{1,0:T(8,128)S(1)}, f32[72,128]{1,0:T(8,128)S(1)}, u32[]{:S(2)}, u32[]{:S(2)}) %collective-permute-start.24) | collective-permute-done | bytes 36896 | tf_op jit(solution)/shard_map/ppermute | solution.py:875
  249.6 8.3 %collective-permute-done.23.refs_3_ = bf16[256,768]{1,0:T(8,128)(2,1)S(1)} collective-permute-done((bf16[256,768]{1,0:T(8,128)(2,1)S(1)}, bf16[256,768]{1,0:T(8,128)(2,1)S(1)}, u32[]{:S(2)}, u32[]{:S(2)}) %collective-permute-start.23) | collective-permute-done | bytes 393248 | tf_op jit(solution)/shard_map/ppermute | solution.py:875
  258.7 0.8 collective-permute-start.27
  259.5 1.8 collective-permute-start.25
  261.3 3.7 %settle_tokens.1 = f32[4,256,768]{2,1,0:T(8,128)} custom-call(s32[3]{0:T(128)} %pad_add_fusion.at_ref.me_ref, bf16[256,768]{1,0:T(8,128)(2,1)} %get-tuple-element.207.refs_0_, bf16[256,768]{1,0:T(8,128)(2,1)} %copy-done.16, bf16[256,768]{1,0:T(8,128)(2,1)} %copy-done.17, bf16[256,768]{1,0:T(8,128)(2,1)} %copy-done.18), custom_call_target="tpu_custom_call" | custom-call | bytes 4718592 | tf_op jit(solution)/shard_map/settle_tokens/pallas_call | solution.py:544
  265.0 2.8 collective-permute-done.27
  268.1 8.4 %collective-permute-done.26 = bf16[2,2,96,768]{3,2,1,0:T(8,128)(2,1)S(1)} collective-permute-done((bf16[2,2,96,768]{3,2,1,0:T(8,128)(2,1)S(1)}, bf16[2,2,96,768]{3,2,1,0:T(8,128)(2,1)S(1)}, u32[]{:S(2)}, u32[]{:S(2)}) %collective-permute-start.26) | collective-permute-done | bytes 589856 | tf_op jit(solution)/shard_map/ppermute | solution.py:875
  276.8 1.8 collective-permute-start.29
  278.6 4.3 %collective-permute-done.30 = bf16[2,21,24,128]{3,2,1,0:T(8,128)(2,1)S(1)} collective-permute-done((bf16[2,21,24,128]{3,2,1,0:T(8,128)(2,1)S(1)}, bf16[2,21,24,128]{3,2,1,0:T(8,128)(2,1)S(1)}, u32[]{:S(2)}, u32[]{:S(2)}) %collective-permute-start.30) | collective-permute-done | bytes 258080 | tf_op jit(solution)/shard_map/ppermute | solution.py:875
  283.0 5.6 %collective-permute-done.29 = bf16[2,96,768]{2,1,0:T(8,128)(2,1)S(1)} collective-permute-done((bf16[2,96,768]{2,1,0:T(8,128)(2,1)S(1)}, bf16[2,96,768]{2,1,0:T(8,128)(2,1)S(1)}, u32[]{:S(2)}, u32[]{:S(2)}) %collective-permute-start.29) | collective-permute-done | bytes 294944 | tf_op jit(solution)/shard_map/ppermute | solution.py:875
  289.5 1.1 collective-permute-done.32
  290.6 2.1 collective-permute-done.31
  292.7 1.2 collective-permute-start.33
  293.9 1.2 collective-permute-start.36
  295.2 2.6 collective-permute-start.34
  299.0 5.8 %collective-permute-done.34 = bf16[21,24,128]{2,1,0:T(8,128)(2,1)S(1)} collective-permute-done((bf16[21,24,128]{2,1,0:T(8,128)(2,1)S(1)}, bf16[21,24,128]{2,1,0:T(8,128)(2,1)S(1)}, u32[]{:S(2)}, u32[]{:S(2)}) %collective-permute-start.34) | collective-permute-done | bytes 129056 | tf_op jit(solution)/shard_map/ppermute | solution.py:875
  305.6 2.1 collective-permute-start.37
  307.7 8.1 %collective-permute-done.35 = bf16[2,21,24,128]{3,2,1,0:T(8,128)(2,1)S(1)} collective-permute-done((bf16[2,21,24,128]{3,2,1,0:T(8,128)(2,1)S(1)}, bf16[2,21,24,128]{3,2,1,0:T(8,128)(2,1)S(1)}, u32[]{:S(2)}, u32[]{:S(2)}) %collective-permute-start.35) | collective-permute-done | bytes 258080 | tf_op jit(solution)/shard_map/ppermute | solution.py:875
  316.4 5.7 %collective-permute-done.37 = bf16[2,2,96,768]{3,2,1,0:T(8,128)(2,1)S(1)} collective-permute-done((bf16[2,2,96,768]{3,2,1,0:T(8,128)(2,1)S(1)}, bf16[2,2,96,768]{3,2,1,0:T(8,128)(2,1)S(1)}, u32[]{:S(2)}, u32[]{:S(2)}) %collective-permute-start.37) | collective-permute-done | bytes 589856 | tf_op jit(solution)/shard_map/ppermute | solution.py:875
  322.4 1.1 maximum_convert_fusion
  323.6 1.1 maximum_convert_fusion.1
  (198 shorter events, 19.8 us)
Async XLA Ops:
  2.9 6.1 %copy-start.32 = (bf16[384]{0:T(512)(128)(2,1)S(1)}, bf16[384]{0:T(512)(128)(2,1)}, u32[]{:S(2)}) copy-start(bf16[384]{0:T(512)(128)(2,1)} %param.26) | copy-start | bytes 2308
  2.9 6.1 %copy-start.25 = (bf16[768]{0:T(1024)(128)(2,1)S(1)}, bf16[768]{0:T(1024)(128)(2,1)}, u32[]{:S(2)}) copy-start(bf16[768]{0:T(1024)(128)(2,1)} %param.25) | copy-start | bytes 4612
  2.9 7.5 %copy-start.26 = (bf16[768]{0:T(1024)(128)(2,1)S(1)}, bf16[768]{0:T(1024)(128)(2,1)}, u32[]{:S(2)}) copy-start(bf16[768]{0:T(1024)(128)(2,1)} %param.22) | copy-start | bytes 4612
  2.9 7.5 %copy-start.27 = (bf16[768]{0:T(1024)(128)(2,1)S(1)}, bf16[768]{0:T(1024)(128)(2,1)}, u32[]{:S(2)}) copy-start(bf16[768]{0:T(1024)(128)(2,1)} %param.23) | copy-start | bytes 4612
  2.9 7.5 %copy-start.28 = (bf16[768]{0:T(1024)(128)(2,1)S(1)}, bf16[768]{0:T(1024)(128)(2,1)}, u32[]{:S(2)}) copy-start(bf16[768]{0:T(1024)(128)(2,1)} %param.28) | copy-start | bytes 4612
  3.0 7.5 %copy-start.29 = (bf16[768]{0:T(1024)(128)(2,1)S(1)}, bf16[768]{0:T(1024)(128)(2,1)}, u32[]{:S(2)}) copy-start(bf16[768]{0:T(1024)(128)(2,1)} %param.29) | copy-start | bytes 4612
  3.0 7.5 %copy-start.30 = (bf16[768]{0:T(1024)(128)(2,1)S(1)}, bf16[768]{0:T(1024)(128)(2,1)}, u32[]{:S(2)}) copy-start(bf16[768]{0:T(1024)(128)(2,1)} %param.30) | copy-start | bytes 4612
  3.0 7.5 %copy-start.31 = (bf16[768]{0:T(1024)(128)(2,1)S(1)}, bf16[768]{0:T(1024)(128)(2,1)}, u32[]{:S(2)}) copy-start(bf16[768]{0:T(1024)(128)(2,1)} %param.34) | copy-start | bytes 4612
  3.0 8.2 %copy-start.23 = (bf16[3072]{0:T(1024)(128)(2,1)S(1)}, bf16[3072]{0:T(1024)(128)(2,1)}, u32[]{:S(2)}) copy-start(bf16[3072]{0:T(1024)(128)(2,1)} %param.32) | copy-start | bytes 18436
  3.0 17.2 %collective-permute-start.2 = (bf16[272,768]{1,0:T(8,128)(2,1)S(1)}, bf16[272,768]{1,0:T(8,128)(2,1)S(1)}, u32[]{:S(2)}, u32[]{:S(2)}) collective-permute-start(bf16[272,768]{1,0:T(8,128)(2,1)S(1)} %pad_maximum_fusion.7), channel_id=1, source_target_pairs={{0,1},{1,0},{2,3},{3,2},{4,7},{5,6},{6,5},{7,4},{8,9},{9,8},{10,11... | collective-permute-start | bytes 1253384 | tf_op jit(solution)/shard_map/ppermute | solution.py:875
  6.2 22.0 %collective-permute-start.1 = (bf16[272,768]{1,0:T(8,128)(2,1)S(1)}, bf16[272,768]{1,0:T(8,128)(2,1)S(1)}, u32[]{:S(2)}, u32[]{:S(2)}) collective-permute-start(bf16[272,768]{1,0:T(8,128)(2,1)S(1)} %get-tuple-element.125), channel_id=1, source_target_pairs={{0,3},{1,2},{2,1},{3,0},{4,5},{5,4},{6,7},{7,6},{8,11},{9,10},{10,... | collective-permute-start | bytes 1253384 | tf_op jit(solution)/shard_map/ppermute | solution.py:875
  8.8 35.1 %collective-permute-start = (bf16[272,768]{1,0:T(8,128)(2,1)S(1)}, bf16[272,768]{1,0:T(8,128)(2,1)S(1)}, u32[]{:S(2)}, u32[]{:S(2)}) collective-permute-start(bf16[272,768]{1,0:T(8,128)(2,1)S(1)} %get-tuple-element.126), channel_id=1, source_target_pairs={{0,2},{1,3},{2,0},{3,1},{4,6},{5,7},{6,4},{7,5},{8,10},{9,11},{10,... | collective-permute-start | bytes 1253384 | tf_op jit(solution)/shard_map/ppermute | solution.py:875
  28.9 14.9 %copy-start.8 = (bf16[4,256,384]{2,1,0:T(8,128)(2,1)S(1)}, bf16[4,256,384]{2,1,0:T(8,128)(2,1)}, u32[]{:S(2)}) copy-start(bf16[4,256,384]{2,1,0:T(8,128)(2,1)} %param.19) | copy-start | bytes 2359300
  34.0 14.2 %copy-start.5 = (bf16[4,256,768]{2,1,0:T(8,128)(2,1)S(1)}, bf16[4,256,768]{2,1,0:T(8,128)(2,1)}, u32[]{:S(2)}) copy-start(bf16[4,256,768]{2,1,0:T(8,128)(2,1)} %param.35) | copy-start | bytes 4718596
  43.8 4.4 %copy-start.13 = (bf16[272,768]{1,0:T(8,128)(2,1)}, bf16[272,768]{1,0:T(8,128)(2,1)S(1)}, u32[]{:S(2)}) copy-start(bf16[272,768]{1,0:T(8,128)(2,1)S(1)} %collective-permute-done.x_ref) | copy-start | bytes 1253380
  44.6 25.1 %collective-permute-start.3 = (bf16[256,384]{1,0:T(8,128)(2,1)S(1)}, bf16[256,384]{1,0:T(8,128)(2,1)S(1)}, u32[]{:S(2)}, u32[]{:S(2)}) collective-permute-start(bf16[256,384]{1,0:T(8,128)(2,1)S(1)} %get-tuple-element.283), channel_id=1, source_target_pairs={{0,1},{1,0},{2,3},{3,2},{4,7},{5,6},{6,5},{7,4},{8,9},{9,8},{10,11... | collective-permute-start | bytes 589832 | tf_op jit(solution)/shard_map/ppermute | solution.py:875
  44.6 25.1 %collective-permute-start.4 = (bf16[256,384]{1,0:T(8,128)(2,1)S(1)}, bf16[256,384]{1,0:T(8,128)(2,1)S(1)}, u32[]{:S(2)}, u32[]{:S(2)}) collective-permute-start(bf16[256,384]{1,0:T(8,128)(2,1)S(1)} %get-tuple-element.282), channel_id=1, source_target_pairs={{0,3},{1,2},{2,1},{3,0},{4,5},{5,4},{6,7},{7,6},{8,11},{9,10},{10,... | collective-permute-start | bytes 589832 | tf_op jit(solution)/shard_map/ppermute | solution.py:875
  47.1 31.0 %collective-permute-start.5 = (bf16[256,384]{1,0:T(8,128)(2,1)S(1)}, bf16[256,384]{1,0:T(8,128)(2,1)S(1)}, u32[]{:S(2)}, u32[]{:S(2)}) collective-permute-start(bf16[256,384]{1,0:T(8,128)(2,1)S(1)} %get-tuple-element.281), channel_id=1, source_target_pairs={{0,2},{1,3},{2,0},{3,1},{4,6},{5,7},{6,4},{7,5},{8,10},{9,11},{10,... | collective-permute-start | bytes 589832 | tf_op jit(solution)/shard_map/ppermute | solution.py:875
  48.2 45.6 %collective-permute-start.6 = (bf16[256,768]{1,0:T(8,128)(2,1)S(1)}, bf16[256,768]{1,0:T(8,128)(2,1)S(1)}, u32[]{:S(2)}, u32[]{:S(2)}) collective-permute-start(bf16[256,768]{1,0:T(8,128)(2,1)S(1)} %get-tuple-element.251), channel_id=1, source_target_pairs={{0,1},{1,0},{2,3},{3,2},{4,7},{5,6},{6,5},{7,4},{8,9},{9,8},{10,11... | collective-permute-start | bytes 1179656 | tf_op jit(solution)/shard_map/ppermute | solution.py:875
  49.2 44.6 %collective-permute-start.8 = (bf16[256,768]{1,0:T(8,128)(2,1)S(1)}, bf16[256,768]{1,0:T(8,128)(2,1)S(1)}, u32[]{:S(2)}, u32[]{:S(2)}) collective-permute-start(bf16[256,768]{1,0:T(8,128)(2,1)S(1)} %get-tuple-element.250), channel_id=1, source_target_pairs={{0,2},{1,3},{2,0},{3,1},{4,6},{5,7},{6,4},{7,5},{8,10},{9,11},{10,... | collective-permute-start | bytes 1179656 | tf_op jit(solution)/shard_map/ppermute | solution.py:875
  69.7 10.9 %copy-start.36 = (bf16[256,384]{1,0:T(8,128)(2,1)}, bf16[256,384]{1,0:T(8,128)(2,1)S(1)}, u32[]{:S(2)}) copy-start(bf16[256,384]{1,0:T(8,128)(2,1)S(1)} %collective-permute-done.3.refs_1_) | copy-start | bytes 589828
  69.7 10.9 %copy-start.37 = (bf16[256,384]{1,0:T(8,128)(2,1)}, bf16[256,384]{1,0:T(8,128)(2,1)S(1)}, u32[]{:S(2)}) copy-start(bf16[256,384]{1,0:T(8,128)(2,1)S(1)} %collective-permute-done.4.refs_2_) | copy-start | bytes 589828
  78.1 2.5 copy-start.38
  78.9 14.9 %collective-permute-start.7 = (bf16[256,768]{1,0:T(8,128)(2,1)S(1)}, bf16[256,768]{1,0:T(8,128)(2,1)S(1)}, u32[]{:S(2)}, u32[]{:S(2)}) collective-permute-start(bf16[256,768]{1,0:T(8,128)(2,1)S(1)} %get-tuple-element.252), channel_id=1, source_target_pairs={{0,3},{1,2},{2,1},{3,0},{4,5},{5,4},{6,7},{7,6},{8,11},{9,10},{10,... | collective-permute-start | bytes 1179656 | tf_op jit(solution)/shard_map/ppermute | solution.py:875
  143.4 24.2 %collective-permute-start.9 = (bf16[4,384,768]{2,1,0:T(8,128)(2,1)}, bf16[4,384,768]{2,1,0:T(8,128)(2,1)S(1)}, u32[]{:S(2)}, u32[]{:S(2)}) collective-permute-start(bf16[4,384,768]{2,1,0:T(8,128)(2,1)} %get-tuple-element.169), channel_id=1, source_target_pairs={{0,4},{4,0},{8,12},{12,8},{16,20},{20,16},{24,28},{28,24},{1,5},{5... | collective-permute-start | bytes 7077896 | tf_op jit(solution)/shard_map/ppermute | solution.py:870
  143.5 24.2 %collective-permute-start.10 = (bf16[4,4,96,768]{3,2,1,0:T(8,128)(2,1)}, bf16[4,4,96,768]{3,2,1,0:T(8,128)(2,1)S(1)}, u32[]{:S(2)}, u32[]{:S(2)}) collective-permute-start(bf16[4,4,96,768]{3,2,1,0:T(8,128)(2,1)} %get-tuple-element.170), channel_id=1, source_target_pairs={{0,4},{4,0},{8,12},{12,8},{16,20},{20,16},{24,28},{28,24},{1,5},{5... | collective-permute-start | bytes 7077896 | tf_op jit(solution)/shard_map/ppermute | solution.py:870
  144.0 23.6 %collective-permute-start.11 = (bf16[2,256,768]{2,1,0:T(8,128)(2,1)}, bf16[2,256,768]{2,1,0:T(8,128)(2,1)S(1)}, u32[]{:S(2)}, u32[]{:S(2)}) collective-permute-start(bf16[2,256,768]{2,1,0:T(8,128)(2,1)} %get-tuple-element.171), channel_id=1, source_target_pairs={{0,1},{1,0},{2,3},{3,2},{4,7},{5,6},{6,5},{7,4},{8,9},{9,8},{10,11... | collective-permute-start | bytes 2359304 | tf_op jit(solution)/shard_map/ppermute | solution.py:875
  147.0 20.6 %collective-permute-start.12 = (bf16[4,6,96,128]{3,2,1,0:T(8,128)(2,1)}, bf16[4,6,96,128]{3,2,1,0:T(8,128)(2,1)}, u32[]{:S(2)}, u32[]{:S(2)}) collective-permute-start(bf16[4,6,96,128]{3,2,1,0:T(8,128)(2,1)} %get-tuple-element.172), channel_id=1, source_target_pairs={{0,4},{4,0},{8,12},{12,8},{16,20},{20,16},{24,28},{28,24},{1,5},{5... | collective-permute-start | bytes 1769480 | tf_op jit(solution)/shard_map/ppermute | solution.py:870
  147.0 21.5 %copy-start.2 = (bf16[4,384,768]{2,1,0:T(8,128)(2,1)S(1)}, bf16[4,384,768]{2,1,0:T(8,128)(2,1)}, u32[]{:S(2)}) copy-start(bf16[4,384,768]{2,1,0:T(8,128)(2,1)} %get-tuple-element.179) | copy-start | bytes 7077892
  168.5 1.7 copy-start.1
  172.9 30.7 %collective-permute-start.13 = (bf16[2,8,96,768]{3,2,1,0:T(8,128)(2,1)S(1)}, bf16[2,8,96,768]{3,2,1,0:T(8,128)(2,1)S(1)}, u32[]{:S(2)}, u32[]{:S(2)}) collective-permute-start(bf16[2,8,96,768]{3,2,1,0:T(8,128)(2,1)S(1)} %pad_maximum_fusion), channel_id=1, source_target_pairs={{0,8},{4,20},{8,0},{12,28},{16,24},{20,4},{24,16},{28,12},{1,9},{5... | collective-permute-start | bytes 7077896 | tf_op jit(solution)/shard_map/ppermute | solution.py:891
  174.4 29.2 %collective-permute-start.14 = (bf16[2,256,768]{2,1,0:T(8,128)(2,1)}, bf16[2,256,768]{2,1,0:T(8,128)(2,1)S(1)}, u32[]{:S(2)}, u32[]{:S(2)}) collective-permute-start(bf16[2,256,768]{2,1,0:T(8,128)(2,1)} %pad_maximum_fusion.2), channel_id=1, source_target_pairs={{0,3},{1,2},{2,1},{3,0},{4,5},{5,4},{6,7},{7,6},{8,11},{9,10},{10,... | collective-permute-start | bytes 2359304 | tf_op jit(solution)/shard_map/ppermute | solution.py:875
  175.8 27.8 %collective-permute-start.15 = (bf16[2,256,384]{2,1,0:T(8,128)(2,1)}, bf16[2,256,384]{2,1,0:T(8,128)(2,1)S(1)}, u32[]{:S(2)}, u32[]{:S(2)}) collective-permute-start(bf16[2,256,384]{2,1,0:T(8,128)(2,1)} %get-tuple-element.195), channel_id=1, source_target_pairs={{0,1},{1,0},{2,3},{3,2},{4,7},{5,6},{6,5},{7,4},{8,9},{9,8},{10,11... | collective-permute-start | bytes 1179656 | tf_op jit(solution)/shard_map/ppermute | solution.py:875
  176.2 27.4 %collective-permute-start.16 = (bf16[4,3,2,96,128]{4,3,2,1,0:T(8,128)(2,1)}, bf16[4,3,2,96,128]{4,3,2,1,0:T(8,128)(2,1)}, u32[]{:S(2)}, u32[]{:S(2)}) collective-permute-start(bf16[4,3,2,96,128]{4,3,2,1,0:T(8,128)(2,1)} %get-tuple-element.196), channel_id=1, source_target_pairs={{0,4},{4,0},{8,12},{12,8},{16,20},{20,16},{24,28},{28,24},{1,5},{5... | collective-permute-start | bytes 1769480 | tf_op jit(solution)/shard_map/ppermute | solution.py:870
  203.6 2.5 copy-start.6
  204.6 4.4 %copy-start.9 = (bf16[2,256,768]{2,1,0:T(8,128)(2,1)S(1)}, bf16[2,256,768]{2,1,0:T(8,128)(2,1)}, u32[]{:S(2)}) copy-start(bf16[2,256,768]{2,1,0:T(8,128)(2,1)} %get-tuple-element.217) | copy-start | bytes 2359300
  204.7 7.7 %copy-start.11 = (bf16[4,6,96,128]{3,2,1,0:T(8,128)(2,1)S(1)}, bf16[4,6,96,128]{3,2,1,0:T(8,128)(2,1)}, u32[]{:S(2)}) copy-start(bf16[4,6,96,128]{3,2,1,0:T(8,128)(2,1)} %get-tuple-element.212) | copy-start | bytes 1769476
  204.7 33.7 %collective-permute-start.17 = (bf16[8,96,768]{2,1,0:T(8,128)(2,1)S(1)}, bf16[8,96,768]{2,1,0:T(8,128)(2,1)S(1)}, u32[]{:S(2)}, u32[]{:S(2)}) collective-permute-start(bf16[8,96,768]{2,1,0:T(8,128)(2,1)S(1)} %slice_bitcast_fusion.1), channel_id=1, source_target_pairs={{0,16},{4,12},{8,24},{12,4},{16,0},{20,28},{24,8},{28,20},{1,17},{... | collective-permute-start | bytes 3538952 | tf_op jit(solution)/shard_map/ppermute | solution.py:891
  206.2 31.4 %collective-permute-start.18 = (bf16[4,3,3,96,128]{4,3,2,1,0:T(8,128)(2,1)}, bf16[4,3,3,96,128]{4,3,2,1,0:T(8,128)(2,1)S(1)}, u32[]{:S(2)}, u32[]{:S(2)}) collective-permute-start(bf16[4,3,3,96,128]{4,3,2,1,0:T(8,128)(2,1)} %get-tuple-element.198), channel_id=1, source_target_pairs={{0,4},{4,0},{8,12},{12,8},{16,20},{20,16},{24,28},{28,24},{1,5},{5... | collective-permute-start | bytes 2654216 | tf_op jit(solution)/shard_map/ppermute | solution.py:870
  207.0 14.1 %collective-permute-start.19 = (bf16[2,256,384]{2,1,0:T(8,128)(2,1)}, bf16[2,256,384]{2,1,0:T(8,128)(2,1)S(1)}, u32[]{:S(2)}, u32[]{:S(2)}) collective-permute-start(bf16[2,256,384]{2,1,0:T(8,128)(2,1)} %pad_maximum_fusion.9), channel_id=1, source_target_pairs={{0,3},{1,2},{2,1},{3,0},{4,5},{5,4},{6,7},{7,6},{8,11},{9,10},{10,... | collective-permute-start | bytes 1179656 | tf_op jit(solution)/shard_map/ppermute | solution.py:875
  209.8 20.7 %collective-permute-start.20 = (bf16[256,768]{1,0:T(8,128)(2,1)}, bf16[256,768]{1,0:T(8,128)(2,1)S(1)}, u32[]{:S(2)}, u32[]{:S(2)}) collective-permute-start(bf16[256,768]{1,0:T(8,128)(2,1)} %slice_bitcast_fusion.5), channel_id=1, source_target_pairs={{0,1},{1,0},{2,3},{3,2},{4,7},{5,6},{6,5},{7,4},{8,9},{9,8},{10,11... | collective-permute-start | bytes 1179656 | tf_op jit(solution)/shard_map/ppermute | solution.py:875
  210.9 26.7 %collective-permute-start.21 = (bf16[256,768]{1,0:T(8,128)(2,1)}, bf16[256,768]{1,0:T(8,128)(2,1)S(1)}, u32[]{:S(2)}, u32[]{:S(2)}) collective-permute-start(bf16[256,768]{1,0:T(8,128)(2,1)} %get-tuple-element.205), channel_id=1, source_target_pairs={{0,3},{1,2},{2,1},{3,0},{4,5},{5,4},{6,7},{7,6},{8,11},{9,10},{10,... | collective-permute-start | bytes 1179656 | tf_op jit(solution)/shard_map/ppermute | solution.py:875
  213.5 3.2 copy-start.12
  216.8 21.6 %copy-start.7 = (bf16[4,3,3,96,128]{4,3,2,1,0:T(8,128)(2,1)S(1)}, bf16[4,3,3,96,128]{4,3,2,1,0:T(8,128)(2,1)}, u32[]{:S(2)}) copy-start(bf16[4,3,3,96,128]{4,3,2,1,0:T(8,128)(2,1)} %get-tuple-element.216) | copy-start | bytes 2654212
  221.1 17.6 %copy-start.4 = (bf16[2,256,384]{2,1,0:T(8,128)(2,1)}, bf16[2,256,384]{2,1,0:T(8,128)(2,1)S(1)}, u32[]{:S(2)}) copy-start(bf16[2,256,384]{2,1,0:T(8,128)(2,1)S(1)} %collective-permute-done.19.refs_2_.refs_3_) | copy-start | bytes 1179652
  230.5 8.2 %copy-start.16 = (bf16[256,768]{1,0:T(8,128)(2,1)}, bf16[256,768]{1,0:T(8,128)(2,1)S(1)}, u32[]{:S(2)}) copy-start(bf16[256,768]{1,0:T(8,128)(2,1)S(1)} %collective-permute-done.20.refs_1_) | copy-start | bytes 1179652
  238.7 19.2 %collective-permute-start.22 = (bf16[2,21,96,128]{3,2,1,0:T(8,128)(2,1)S(1)}, bf16[2,21,96,128]{3,2,1,0:T(8,128)(2,1)S(1)}, u32[]{:S(2)}, u32[]{:S(2)}) collective-permute-start(bf16[2,21,96,128]{3,2,1,0:T(8,128)(2,1)S(1)} %pad_maximum_fusion.1), channel_id=1, source_target_pairs={{0,8},{4,20},{8,0},{12,28},{16,24},{20,4},{24,16},{28,12},{1,9},{5... | collective-permute-start | bytes 3096584 | tf_op jit(solution)/shard_map/ppermute | solution.py:891
  239.8 18.2 %collective-permute-start.23 = (bf16[256,768]{1,0:T(8,128)(2,1)S(1)}, bf16[256,768]{1,0:T(8,128)(2,1)S(1)}, u32[]{:S(2)}, u32[]{:S(2)}) collective-permute-start(bf16[256,768]{1,0:T(8,128)(2,1)S(1)} %slice_bitcast_fusion.4), channel_id=1, source_target_pairs={{0,2},{1,3},{2,0},{3,1},{4,6},{5,7},{6,4},{7,5},{8,10},{9,11},{10,... | collective-permute-start | bytes 1179656 | tf_op jit(solution)/shard_map/ppermute | solution.py:875
  241.1 8.5 %collective-permute-start.24 = (f32[72,128]{1,0:T(8,128)S(1)}, f32[72,128]{1,0:T(8,128)S(1)}, u32[]{:S(2)}, u32[]{:S(2)}) collective-permute-start(f32[72,128]{1,0:T(8,128)S(1)} %copy-done.21), channel_id=1, source_target_pairs={{0,1},{1,0},{2,3},{3,2},{4,5},{5,4},{6,7},{7,6},{8,9},{9,8},{10,11... | collective-permute-start | bytes 110600 | tf_op jit(solution)/shard_map/ppermute | solution.py:875
  258.7 9.1 %collective-permute-start.27 = (bf16[21,96,128]{2,1,0:T(8,128)(2,1)S(1)}, bf16[21,96,128]{2,1,0:T(8,128)(2,1)S(1)}, u32[]{:S(2)}, u32[]{:S(2)}) collective-permute-start(bf16[21,96,128]{2,1,0:T(8,128)(2,1)S(1)} %slice_bitcast_fusion.3), channel_id=1, source_target_pairs={{0,16},{4,12},{8,24},{12,4},{16,0},{20,28},{24,8},{28,20},{1,17},{... | collective-permute-start | bytes 1548296 | tf_op jit(solution)/shard_map/ppermute | solution.py:891
  259.5 17.0 %collective-permute-start.26 = (bf16[2,2,96,768]{3,2,1,0:T(8,128)(2,1)S(1)}, bf16[2,2,96,768]{3,2,1,0:T(8,128)(2,1)S(1)}, u32[]{:S(2)}, u32[]{:S(2)}) collective-permute-start(bf16[2,2,96,768]{3,2,1,0:T(8,128)(2,1)S(1)} %pad_maximum_fusion.3), channel_id=1, source_target_pairs={{0,1},{1,0},{2,3},{3,2},{4,7},{5,6},{6,5},{7,4},{8,9},{9,8},{10,11... | collective-permute-start | bytes 1769480 | tf_op jit(solution)/shard_map/ppermute | solution.py:875
  259.5 17.1 %collective-permute-start.25 = (f32[72,128]{1,0:T(8,128)S(1)}, f32[72,128]{1,0:T(8,128)S(1)}, u32[]{:S(2)}, u32[]{:S(2)}) collective-permute-start(f32[72,128]{1,0:T(8,128)S(1)} %add.137), channel_id=1, source_target_pairs={{0,3},{1,2},{2,1},{3,0},{4,7},{5,6},{6,5},{7,4},{8,11},{9,10},{10,... | collective-permute-start | bytes 110600 | tf_op jit(solution)/shard_map/ppermute | solution.py:875
  268.0 14.8 %collective-permute-start.30 = (bf16[2,21,24,128]{3,2,1,0:T(8,128)(2,1)S(1)}, bf16[2,21,24,128]{3,2,1,0:T(8,128)(2,1)S(1)}, u32[]{:S(2)}, u32[]{:S(2)}) collective-permute-start(bf16[2,21,24,128]{3,2,1,0:T(8,128)(2,1)S(1)} %pad_maximum_fusion.10), channel_id=1, source_target_pairs={{0,1},{1,0},{2,3},{3,2},{4,7},{5,6},{6,5},{7,4},{8,9},{9,8},{10,11... | collective-permute-start | bytes 774152 | tf_op jit(solution)/shard_map/ppermute | solution.py:875
  276.7 12.0 %collective-permute-start.28 = (f32[72,128]{1,0:T(8,128)S(1)}, f32[72,128]{1,0:T(8,128)S(1)}, u32[]{:S(2)}, u32[]{:S(2)}) collective-permute-start(f32[72,128]{1,0:T(8,128)S(1)} %add.144), channel_id=1, source_target_pairs={{0,4},{4,0},{8,12},{12,8},{16,20},{20,16},{24,28},{28,24},{1,5},{5... | collective-permute-start | bytes 110600 | tf_op jit(solution)/shard_map/ppermute | solution.py:870
  276.8 11.8 %collective-permute-start.29 = (bf16[2,96,768]{2,1,0:T(8,128)(2,1)S(1)}, bf16[2,96,768]{2,1,0:T(8,128)(2,1)S(1)}, u32[]{:S(2)}, u32[]{:S(2)}) collective-permute-start(bf16[2,96,768]{2,1,0:T(8,128)(2,1)S(1)} %slice_bitcast_fusion.9), channel_id=1, source_target_pairs={{0,3},{1,2},{2,1},{3,0},{4,5},{5,4},{6,7},{7,6},{8,11},{9,10},{10,... | collective-permute-start | bytes 884744 | tf_op jit(solution)/shard_map/ppermute | solution.py:875
  282.9 7.6 %collective-permute-start.32 = (bf16[21,24,128]{2,1,0:T(8,128)(2,1)S(1)}, bf16[21,24,128]{2,1,0:T(8,128)(2,1)S(1)}, u32[]{:S(2)}, u32[]{:S(2)}) collective-permute-start(bf16[21,24,128]{2,1,0:T(8,128)(2,1)S(1)} %slice_bitcast_fusion.21), channel_id=1, source_target_pairs={{0,3},{1,2},{2,1},{3,0},{4,5},{5,4},{6,7},{7,6},{8,11},{9,10},{10,... | collective-permute-start | bytes 387080 | tf_op jit(solution)/shard_map/ppermute | solution.py:875
  288.7 4.0 %collective-permute-start.31 = (f32[72,128]{1,0:T(8,128)S(1)}, f32[72,128]{1,0:T(8,128)S(1)}, u32[]{:S(2)}, u32[]{:S(2)}) collective-permute-start(f32[72,128]{1,0:T(8,128)S(1)} %add.147), channel_id=1, source_target_pairs={{0,8},{4,12},{8,0},{12,4},{16,24},{20,28},{24,16},{28,20},{1,9},{5... | collective-permute-start | bytes 110600 | tf_op jit(solution)/shard_map/ppermute | solution.py:891
  292.7 5.0 %collective-permute-start.33 = (f32[72,128]{1,0:T(8,128)S(1)}, f32[72,128]{1,0:T(8,128)S(1)}, u32[]{:S(2)}, u32[]{:S(2)}) collective-permute-start(f32[72,128]{1,0:T(8,128)S(1)} %add.149), channel_id=1, source_target_pairs={{0,16},{4,20},{8,24},{12,28},{16,0},{20,4},{24,8},{28,12},{1,17},{... | collective-permute-start | bytes 110600 | tf_op jit(solution)/shard_map/ppermute | solution.py:891
  293.9 11.6 %collective-permute-start.36 = (bf16[2,96,768]{2,1,0:T(8,128)(2,1)S(1)}, bf16[2,96,768]{2,1,0:T(8,128)(2,1)S(1)}, u32[]{:S(2)}, u32[]{:S(2)}) collective-permute-start(bf16[2,96,768]{2,1,0:T(8,128)(2,1)S(1)} %fusion.2), channel_id=1, source_target_pairs={{0,3},{1,2},{2,1},{3,0},{4,5},{5,4},{6,7},{7,6},{8,11},{9,10},{10,... | collective-permute-start | bytes 884744 | tf_op jit(solution)/shard_map/ppermute | solution.py:875
  295.2 9.7 %collective-permute-start.34 = (bf16[21,24,128]{2,1,0:T(8,128)(2,1)S(1)}, bf16[21,24,128]{2,1,0:T(8,128)(2,1)S(1)}, u32[]{:S(2)}, u32[]{:S(2)}) collective-permute-start(bf16[21,24,128]{2,1,0:T(8,128)(2,1)S(1)} %fusion.3), channel_id=1, source_target_pairs={{0,3},{1,2},{2,1},{3,0},{4,5},{5,4},{6,7},{7,6},{8,11},{9,10},{10,... | collective-permute-start | bytes 387080 | tf_op jit(solution)/shard_map/ppermute | solution.py:875
  304.9 10.9 %collective-permute-start.35 = (bf16[2,21,24,128]{3,2,1,0:T(8,128)(2,1)S(1)}, bf16[2,21,24,128]{3,2,1,0:T(8,128)(2,1)S(1)}, u32[]{:S(2)}, u32[]{:S(2)}) collective-permute-start(bf16[2,21,24,128]{3,2,1,0:T(8,128)(2,1)S(1)} %pad_maximum_fusion.11), channel_id=1, source_target_pairs={{0,1},{1,0},{2,3},{3,2},{4,7},{5,6},{6,5},{7,4},{8,9},{9,8},{10,11... | collective-permute-start | bytes 774152 | tf_op jit(solution)/shard_map/ppermute | solution.py:875
  305.6 16.5 %collective-permute-start.37 = (bf16[2,2,96,768]{3,2,1,0:T(8,128)(2,1)S(1)}, bf16[2,2,96,768]{3,2,1,0:T(8,128)(2,1)S(1)}, u32[]{:S(2)}, u32[]{:S(2)}) collective-permute-start(bf16[2,2,96,768]{3,2,1,0:T(8,128)(2,1)S(1)} %pad_maximum_fusion.4), channel_id=1, source_target_pairs={{0,1},{1,0},{2,3},{3,2},{4,7},{5,6},{6,5},{7,4},{8,9},{9,8},{10,11... | collective-permute-start | bytes 1769480 | tf_op jit(solution)/shard_map/ppermute | solution.py:875
  316.4 5.9 %copy-start.22 = (f32[96,768]{1,0:T(8,128)}, f32[96,768]{1,0:T(8,128)S(1)}, u32[]{:S(2)}) copy-start(f32[96,768]{1,0:T(8,128)S(1)} %get-tuple-element.269) | copy-start | bytes 884740
  316.4 5.9 %copy-start.24 = (f32[96,1920]{1,0:T(8,128)}, f32[96,1920]{1,0:T(8,128)S(1)}, u32[]{:S(2)}) copy-start(f32[96,1920]{1,0:T(8,128)S(1)} %get-tuple-element.270) | copy-start | bytes 2211844
  (14 other events, 13.8 us)

commit v5 on v4

--- a/solution.py
+++ b/solution.py
@@ -440,8 +440,8 @@
 
     @pl.when(step == 0)
     def _():
-        for rows, ref in each_way(at_ref, (d0_ref, d1_ref, d2_ref, d3_ref)):
-            dy_ref[rows, :] = ref[...]
+        for d, ref in enumerate((d0_ref, d1_ref, d2_ref, d3_ref)):
+            dy_ref[block_rows(at_ref[0], d, ref.shape[0]), :] = ref[...]
         half = oa_ref.shape[1]
         middle = (
             x_ref[...].astype(F32)
@@ -978,15 +978,15 @@
     skip_near = near_swap(pick(skip_values, me ^ near))
     skip_far = far_swap(pick(skip_values, me ^ far))
     dy_across = across_swap(pick(cotangent, me ^ 2))
-    dy_near = near_swap(pick(cotangent, me ^ near))
+    dy_three = group_swap(pick(cotangent, me ^ 3), 3, 3)
     x, normed, proj, code_row = pro(3, across_x, so_far)
     skip = [pick(skip_values, me), skip_near, skip_far, skip_across]
 
     from_a = attend(at, code_row, proj, [proj], 0, 6, 12, 3, "attend_a")
     (o_a, lse_a, skip), cotangent = gate((*from_a, skip), cotangent)
-    dy_far = far_swap(pick(cotangent, me ^ far))
+    dy_one = group_swap(pick(cotangent, me ^ 1), 1, 1)
     o_b, lse_b = attend(at, code_row, proj, skip, 3, 9, 0, 3, "attend_b")
-    dy = [pick(cotangent, me), dy_near, dy_far, dy_across]
+    dy = [pick(cotangent, me), dy_one, dy_across, dy_three]
     fed = feed(at, x, o_a, o_b, dy, w_out, vecs, w_up, up_row, w_down)
     y_own, y_away, y_far, down_send, down_keep, up_send, up_keep, g_up_bias, d_att, d_o, mlp_sums, out_send, out_keep = fed
     down_got = across_cores(down_send)
@@ -1034,23 +1034,24 @@
     small_got = group_swap(packed, 1, 1)
     big = add_up([big_got, big_half[1]]).reshape(2, 4, strip, width).transpose(1, 0, 2, 3)
     big_send, big_keep = group_first(big, me, core)
-    (big_send, rest_got), (x_across, small_got, grad_skip) = gate((big_send, rest_got), (x_across, small_got, grad_skip))
-
     big_got = near_swap(big_send)
+    (rest_got, packed), (small_got, grad_skip) = gate((rest_got, packed), (small_got, grad_skip))
+
     packed = packed + small_got
     small_got = group_swap(packed, 3, 3)
     rest_half = add_up([rest_got, plane_stay(rest_pairs)])
     rest_got = second_hop(rest_half[0])
+    (rest_got, big_got), (x_across, small_got) = gate((rest_got, big_got), (x_across, small_got))
     rest = add_up([rest_got, rest_half[1]]).reshape(-1, 4, strip // 4, PAIR).transpose(1, 0, 2, 3)
     rest_send, rest_keep = group_first(rest, me, core)
     rest_got = near_swap(rest_send)
     grad_tokens = settle(at, [x_own, x_near, x_far, x_across], F32, "settle_tokens")
 
-    big_sum = add_up([after(big_got, rest_send, grad_tokens), big_keep])
+    big_sum = add_up([big_got, big_keep])
     big_got = far_swap(big_sum[1])
     packed = packed + after(small_got, big_sum)
     small_got = across_cores(packed)
-    rest_sum = add_up([after(rest_got, big_sum), rest_keep])
+    rest_sum = add_up([after(rest_got, big_sum, grad_tokens), rest_keep])
     rest_got = far_swap(rest_sum[1])
     big_own = add_up([after(big_got, rest_sum), big_sum[0]])
     big_far = far_swap(big_own)
@@ -1058,14 +1059,15 @@
     small_got = plane_swap(packed, 2, 2)
     rest_own = add_up([after(rest_got, big_own), rest_sum[0]])
     rest_far = far_swap(rest_own)
-    big_near = near_swap(jnp.stack([big_own, after(big_far, rest_own)]))
+    big_far = jnp.stack([big_own, big_far])
+    big_near = near_swap(big_far)
     packed = packed + after(small_got, rest_own)
     small_got = plane_swap(packed, 4, 4)
-    rest_near = near_swap(jnp.stack([rest_own, rest_far]))
+    rest_near = near_swap(jnp.stack([rest_own, after(rest_far, big_far)]))
     packed = (packed + small_got).reshape(-1)
 
     rest = jnp.concatenate(by_owner(rest_own, rest_far, rest_near, me, core), axis=1).astype(F32)
-    big = by_owner(big_own, big_far, big_near, me, core)
+    big = by_owner(big_own, big_far[1], big_near, me, core)
     r_up = jnp.concatenate([q[0] for q in big], axis=1).astype(F32)
     r_down = jnp.concatenate([q[1] for q in big], axis=0).astype(F32)
     count = width // PAIR

time: 330 us -> 329 us (level)
    ppermute x6, waiting for transfers between devices: 4.93 us -> 11.2 us  [plane_swap(): lax.ppermute(array, 'seq', [(s, s ^ (core_one if s & 1 else core_zero)) f...]
    ppermute x26, waiting for transfers between devices: 94.5 us -> 89.4 us  [group_swap(): return lax.ppermute(array, ('seq', 'head'), pairs)]
    unnamed x92 -> x90, local copies, waits for them, and re-layouts: 6.63 us -> 5.12 us
  transfers between devices with their start and end apart: 38 -> 38, of which waited for: 18 -> 17; matrix products, arithmetic and copies ran while one was open for 4% -> 4% of each run, Pallas kernels for 32% -> 32%
where the time goes in v5:
time: 329 us; the launch traced here: 323 us
  Pallas kernels  153 us (47%)
  waiting for transfers between devices  101 us (31%)
  starting transfers between devices  41.3 us (13%)
  other arithmetic  14.7 us (4%)
  local copies, waits for them, and re-layouts  12.2 us (4%)
    ppermute x26, waiting for transfers between devices, group_swap(): return lax.ppermute(array, ('seq', 'head'), pairs)  89.4 us
    pallas_call x1, Pallas kernels, feed(): call(feed_kernel, 'feed', (4,), [full, once(o_a.shape), once(o_b.shape)]...  48.5 us
    pallas_call x2, Pallas kernels, attend_back(): call(functools.partial(backward_kernel, len(values), before is None, last...  47.8 us
    ppermute x26, starting transfers between devices, group_swap(): return lax.ppermute(array, ('seq', 'head'), pairs)  34.8 us
    pallas_call x2, Pallas kernels, attend(): call(functools.partial(forward_kernel, len(values)), name, (pairs,), [who...  26.7 us
    pallas_call x4, Pallas kernels, project(): call(project_kernel, 'project', (1,), [whole((part + CODE_ROWS, width)),...  19.5 us
    ppermute x6, waiting for transfers between devices, plane_swap(): lax.ppermute(array, 'seq', [(s, s ^ (core_one if s & 1 else core_zero)) f...  11.2 us
    pallas_call x3, Pallas kernels, settle(): call(settle_kernel, name, (2,), specs, pl.BlockSpec((4, rows, width), lam...  10 us
  transfers between devices with their start and end apart: 38, of which 17 were waited for; matrix products, arithmetic and copies ran while one was open for 4% of the time, Pallas kernels for 32%

profile of v5, /device:TPU:0, one launch (start us, length us, event | category | flops | bytes accessed | tf_op | source)
XLA Modules:
  0.0 323.4 jit_solution(8409735798384108959)
XLA Ops:
  1.4 1.5 dynamic-slice_bitcast_fusion.4
  3.0 3.1 collective-permute-start.2
  6.2 2.5 collective-permute-start.1
  9.0 0.8 pad_maximum_fusion.8.x_ref
  12.4 4.8 %project.4 = (bf16[1024,768]{1,0:T(8,128)(2,1)}, bf16[1024,768]{1,0:T(8,128)(2,1)}, bf16[1024,1920]{1,0:T(8,128)(2,1)}, s32[8,1024]{1,0:T(8,128)}) custom-call(s32[3]{0:T(128)} %pad_add_fusion.at_ref.me_ref, bf16[272,768]{1,0:T(8,128)(2,1)} %pad_maximum_fusion.8.x_ref, f32[8,768]{1,0:T(8,128)} %convert_element_type.233.vec_ref.refs_10_, ...), custom_call_target="tpu_custom_call" | custom-call | flops 754974720 | bytes 5111808 | tf_op jit(solution)/shard_map/project/pallas_call | solution.py:140
  17.3 3.0 collective-permute-done.2.x_ref
  21.0 4.9 %project.5 = (bf16[1024,768]{1,0:T(8,128)(2,1)}, bf16[1024,768]{1,0:T(8,128)(2,1)}, bf16[1024,1920]{1,0:T(8,128)(2,1)}, s32[8,1024]{1,0:T(8,128)}) custom-call(s32[3]{0:T(128)} %pad_add_fusion.at_ref.me_ref, bf16[272,768]{1,0:T(8,128)(2,1)} %copy-done.14, ...), custom_call_target="tpu_custom_call", output_to_operand_aliasing={{0}: (5, {}), {1}: (6, {}), {2}: (7, {}), {3}: (8, {})} | custom-call | flops 754974720 | bytes 5111808 | tf_op jit(solution)/shard_map/project/pallas_call | solution.py:140
  25.9 2.3 collective-permute-done.1.x_ref
  28.9 5.0 %project.6 = (bf16[1024,768]{1,0:T(8,128)(2,1)}, bf16[1024,768]{1,0:T(8,128)(2,1)}, bf16[1024,1920]{1,0:T(8,128)(2,1)}, s32[8,1024]{1,0:T(8,128)}) custom-call(s32[3]{0:T(128)} %pad_add_fusion.at_ref.me_ref, bf16[272,768]{1,0:T(8,128)(2,1)} %copy-done.15, ...), custom_call_target="tpu_custom_call", output_to_operand_aliasing={{0}: (5, {}), {1}: (6, {}), {2}: (7, {}), {3}: (8, {})} | custom-call | flops 754974720 | bytes 5111808 | tf_op jit(solution)/shard_map/project/pallas_call | solution.py:140
  33.9 9.9 %collective-permute-done.x_ref = bf16[272,768]{1,0:T(8,128)(2,1)S(1)} collective-permute-done((bf16[272,768]{1,0:T(8,128)(2,1)S(1)}, bf16[272,768]{1,0:T(8,128)(2,1)S(1)}, u32[]{:S(2)}, u32[]{:S(2)}) %collective-permute-start) | collective-permute-done | bytes 417824 | tf_op jit(solution)/shard_map/ppermute | solution.py:875
  43.8 0.8 dynamic-slice_bitcast_fusion.12
  44.6 2.5 collective-permute-start.4
  47.1 1.0 collective-permute-start.5
  48.2 2.0 collective-permute-start.7
  50.2 1.3 collective-permute-start.8
  51.5 4.8 %project.7 = (bf16[1024,768]{1,0:T(8,128)(2,1)}, bf16[1024,768]{1,0:T(8,128)(2,1)}, bf16[1024,1920]{1,0:T(8,128)(2,1)}, s32[8,1024]{1,0:T(8,128)}) custom-call(s32[3]{0:T(128)} %pad_add_fusion.at_ref.me_ref, bf16[272,768]{1,0:T(8,128)(2,1)} %copy-done.13, ...), custom_call_target="tpu_custom_call", output_to_operand_aliasing={{0}: (5, {}), {1}: (6, {}), {2}: (7, {}), {3}: (8, {})} | custom-call | flops 754974720 | bytes 5111808 | tf_op jit(solution)/shard_map/project/pallas_call | solution.py:140
  56.3 13.6 %attend_a.1 = (bf16[1024,384]{1,0:T(8,128)(2,1)}, f32[1024,384]{1,0:T(8,128)}) custom-call(s32[3]{0:T(128)} %pad_add_fusion.at_ref.me_ref, s32[8,1024]{1,0:T(8,128)} %get-tuple-element.146.code_ref, bf16[1024,1920]{1,0:T(8,128)(2,1)} %get-tuple-element.147.q_ref.k_ref.refs_0_, bf16[1024,1920]{1,0:T(8,128)(2,1)} %get-tuple-element.147.q_ref.k_ref.refs_0_, ...), custom_call_target="tpu_custom_call" | custom-call | flops 9663676416 | bytes 4718592 | tf_op jit(solution)/shard_map/attend_a/pallas_call | solution.py:326
  70.0 12.4 %collective-permute-done.5.refs_3_ = bf16[256,384]{1,0:T(8,128)(2,1)S(1)} collective-permute-done((bf16[256,384]{1,0:T(8,128)(2,1)S(1)}, bf16[256,384]{1,0:T(8,128)(2,1)S(1)}, u32[]{:S(2)}, u32[]{:S(2)}) %collective-permute-start.5) | collective-permute-done | bytes 196640 | tf_op jit(solution)/shard_map/ppermute | solution.py:875
  82.4 0.8 dynamic-slice_bitcast_fusion.2
  83.3 13.1 %attend_b.1 = (bf16[1024,384]{1,0:T(8,128)(2,1)}, f32[1024,384]{1,0:T(8,128)}) custom-call(s32[3]{0:T(128)} %pad_add_fusion.at_ref.me_ref, s32[8,1024]{1,0:T(8,128)} %get-tuple-element.146.code_ref, bf16[1024,1920]{1,0:T(8,128)(2,1)} %get-tuple-element.147.q_ref.k_ref.refs_0_, bf16[1024,1920]{1,0:T(8,128)(2,1)} %get-tuple-element.147.q_ref.k_ref.refs_0_, ...), custom_call_target="tpu_custom_call" | custom-call | flops 9663676416 | bytes 4718592 | tf_op jit(solution)/shard_map/attend_b/pallas_call | solution.py:326
  97.5 48.5 %feed.1 = (bf16[256,768]{1,0:T(8,128)(2,1)}, bf16[2,256,768]{2,1,0:T(8,128)(2,1)}, bf16[256,768]{1,0:T(8,128)(2,1)}, bf16[4,384,768]{2,1,0:T(8,128)(2,1)}, bf16[...) custom-call(s32[3]{0:T(128)} %pad_add_fusion.at_ref.me_ref, ...), custom_call_target="tpu_custom_call" | custom-call | flops 32614907904 | bytes 33423360 | tf_op jit(solution)/shard_map/feed/pallas_call | solution.py:503
  146.6 2.0 collective-permute-start.11
  148.6 20.6 %attend_back_b.1 = (bf16[4,3,2,96,128]{4,3,2,1,0:T(8,128)(2,1)}, bf16[4,3,2,96,128]{4,3,2,1,0:T(8,128)(2,1)}, f32[3,1,256]{2,1,0:T(1,128)}, bf16[256,384]{1,0:T(...) custom-call(s32[3]{0:T(128)} %pad_add_fusion.at_ref.me_ref, ...), custom_call_target="tpu_custom_call" | custom-call | flops 14495514624 | bytes 16515072 | tf_op jit(solution)/shard_map/attend_back_b/pallas_call | solution.py:379
  169.2 0.9 copy-done.3
  170.6 1.1 copy-done.1
  172.7 0.8 slice-done
  173.6 1.0 pad_maximum_fusion.2
  174.5 1.5 collective-permute-start.13
  176.0 1.6 collective-permute-start.14
  177.9 27.3 %attend_back_a.1 = (bf16[4,3,3,96,128]{4,3,2,1,0:T(8,128)(2,1)}, bf16[4,3,3,96,128]{4,3,2,1,0:T(8,128)(2,1)}, bf16[256,768]{1,0:T(8,128)(2,1)}, bf16[2,256,768]{...) custom-call(s32[3]{0:T(128)} %pad_add_fusion.at_ref.me_ref, s32[8,1024]{1,0:T(8,128)} %get-tuple-element.146.code_ref, ...), custom_call_target="tpu_custom_call" | custom-call | flops 15703474176 | bytes 16515072 | tf_op jit(solution)/shard_map/attend_back_a/pallas_call | solution.py:379
  206.2 1.5 collective-permute-start.17
  207.8 0.8 pad_maximum_fusion.9
  208.6 2.0 collective-permute-start.19
  210.6 0.8 slice_bitcast_fusion.5
  211.4 1.1 collective-permute-start.20
  212.5 1.6 collective-permute-start.21
  214.2 1.2 add_convert_fusion.10
  215.4 3.2 settle_out.1
  218.6 1.3 add_convert_fusion.9
  219.9 2.8 collective-permute-done.19.refs_2_.refs_3_
  222.8 9.4 %collective-permute-done.20.refs_1_ = bf16[256,768]{1,0:T(8,128)(2,1)S(1)} collective-permute-done((bf16[256,768]{1,0:T(8,128)(2,1)}, bf16[256,768]{1,0:T(8,128)(2,1)S(1)}, u32[]{:S(2)}, u32[]{:S(2)}) %collective-permute-start.20) | collective-permute-done | bytes 393248 | tf_op jit(solution)/shard_map/ppermute | solution.py:875
  232.1 7.2 %collective-permute-done.21.refs_2_ = bf16[256,768]{1,0:T(8,128)(2,1)} collective-permute-done((bf16[256,768]{1,0:T(8,128)(2,1)}, bf16[256,768]{1,0:T(8,128)(2,1)}, u32[]{:S(2)}, u32[]{:S(2)}) %collective-permute-start.21) | collective-permute-done | bytes 393248 | tf_op jit(solution)/shard_map/ppermute | solution.py:875
  240.8 2.1 collective-permute-start.25
  242.9 3.1 settle_skip.1
  246.0 9.3 %collective-permute-done.22 = bf16[2,21,96,128]{3,2,1,0:T(8,128)(2,1)S(1)} collective-permute-done((bf16[2,21,96,128]{3,2,1,0:T(8,128)(2,1)S(1)}, bf16[2,21,96,128]{3,2,1,0:T(8,128)(2,1)S(1)}, u32[]{:S(2)}, u32[]{:S(2)}) %collective-permute-start.22) | collective-permute-done | bytes 1032224 | tf_op jit(solution)/shard_map/ppermute | solution.py:891
  255.6 0.8 collective-permute-start.24
  256.7 1.1 collective-permute-start.27
  257.8 16.3 %collective-permute-done.26.refs_3_ = bf16[256,768]{1,0:T(8,128)(2,1)S(1)} collective-permute-done((bf16[256,768]{1,0:T(8,128)(2,1)S(1)}, bf16[256,768]{1,0:T(8,128)(2,1)S(1)}, u32[]{:S(2)}, u32[]{:S(2)}) %collective-permute-start.26) | collective-permute-done | bytes 393248 | tf_op jit(solution)/shard_map/ppermute | solution.py:875
  274.4 1.0 collective-permute-start.30
  275.7 1.9 collective-permute-start.29
  277.6 3.7 %settle_tokens.1 = f32[4,256,768]{2,1,0:T(8,128)} custom-call(s32[3]{0:T(128)} %pad_add_fusion.at_ref.me_ref, bf16[256,768]{1,0:T(8,128)(2,1)} %get-tuple-element.209.refs_0_, bf16[256,768]{1,0:T(8,128)(2,1)} %copy-done.16, bf16[256,768]{1,0:T(8,128)(2,1)} %collective-permute-done.21.refs_2_, bf16[256,768]{1,0:T(8,128)(2,1)} %copy-done.17), custom_call_target="tpu_custom_call" | custom-call | bytes 4718592 | tf_op jit(solution)/shard_map/settle_tokens/pallas_call | solution.py:544
  281.3 5.2 %collective-permute-done.30 = bf16[2,21,24,128]{3,2,1,0:T(8,128)(2,1)S(1)} collective-permute-done((bf16[2,21,24,128]{3,2,1,0:T(8,128)(2,1)S(1)}, bf16[2,21,24,128]{3,2,1,0:T(8,128)(2,1)S(1)}, u32[]{:S(2)}, u32[]{:S(2)}) %collective-permute-start.30) | collective-permute-done | bytes 258080 | tf_op jit(solution)/shard_map/ppermute | solution.py:875
  286.5 1.1 collective-permute-start.32
  287.6 3.1 collective-permute-done.29
  290.8 1.4 collective-permute-start.35
  292.8 1.9 collective-permute-done.32
  294.8 1.4 collective-permute-done.31
  296.9 2.7 collective-permute-start.34
  300.8 4.3 %collective-permute-done.34 = bf16[21,24,128]{2,1,0:T(8,128)(2,1)S(1)} collective-permute-done((bf16[21,24,128]{2,1,0:T(8,128)(2,1)S(1)}, bf16[21,24,128]{2,1,0:T(8,128)(2,1)S(1)}, u32[]{:S(2)}, u32[]{:S(2)}) %collective-permute-start.34) | collective-permute-done | bytes 129056 | tf_op jit(solution)/shard_map/ppermute | solution.py:875
  306.5 2.0 collective-permute-start.37
  308.5 5.8 %collective-permute-done.36 = bf16[2,21,24,128]{3,2,1,0:T(8,128)(2,1)S(1)} collective-permute-done((bf16[2,21,24,128]{3,2,1,0:T(8,128)(2,1)S(1)}, bf16[2,21,24,128]{3,2,1,0:T(8,128)(2,1)S(1)}, u32[]{:S(2)}, u32[]{:S(2)}) %collective-permute-start.36) | collective-permute-done | bytes 258080 | tf_op jit(solution)/shard_map/ppermute | solution.py:875
  315.0 5.7 %collective-permute-done.37 = bf16[2,2,96,768]{3,2,1,0:T(8,128)(2,1)S(1)} collective-permute-done((bf16[2,2,96,768]{3,2,1,0:T(8,128)(2,1)S(1)}, bf16[2,2,96,768]{3,2,1,0:T(8,128)(2,1)S(1)}, u32[]{:S(2)}, u32[]{:S(2)}) %collective-permute-start.37) | collective-permute-done | bytes 589856 | tf_op jit(solution)/shard_map/ppermute | solution.py:875
  321.0 1.1 maximum_convert_fusion
  322.1 1.1 maximum_convert_fusion.1
  (196 shorter events, 17.1 us)
Async XLA Ops:
  2.9 6.1 %copy-start.31 = (bf16[384]{0:T(512)(128)(2,1)S(1)}, bf16[384]{0:T(512)(128)(2,1)}, u32[]{:S(2)}) copy-start(bf16[384]{0:T(512)(128)(2,1)} %param.26) | copy-start | bytes 2308
  2.9 6.1 %copy-start.24 = (bf16[768]{0:T(1024)(128)(2,1)S(1)}, bf16[768]{0:T(1024)(128)(2,1)}, u32[]{:S(2)}) copy-start(bf16[768]{0:T(1024)(128)(2,1)} %param.25) | copy-start | bytes 4612
  2.9 7.5 %copy-start.25 = (bf16[768]{0:T(1024)(128)(2,1)S(1)}, bf16[768]{0:T(1024)(128)(2,1)}, u32[]{:S(2)}) copy-start(bf16[768]{0:T(1024)(128)(2,1)} %param.22) | copy-start | bytes 4612
  2.9 7.5 %copy-start.26 = (bf16[768]{0:T(1024)(128)(2,1)S(1)}, bf16[768]{0:T(1024)(128)(2,1)}, u32[]{:S(2)}) copy-start(bf16[768]{0:T(1024)(128)(2,1)} %param.23) | copy-start | bytes 4612
  2.9 7.5 %copy-start.27 = (bf16[768]{0:T(1024)(128)(2,1)S(1)}, bf16[768]{0:T(1024)(128)(2,1)}, u32[]{:S(2)}) copy-start(bf16[768]{0:T(1024)(128)(2,1)} %param.28) | copy-start | bytes 4612
  3.0 7.5 %copy-start.28 = (bf16[768]{0:T(1024)(128)(2,1)S(1)}, bf16[768]{0:T(1024)(128)(2,1)}, u32[]{:S(2)}) copy-start(bf16[768]{0:T(1024)(128)(2,1)} %param.29) | copy-start | bytes 4612
  3.0 7.5 %copy-start.29 = (bf16[768]{0:T(1024)(128)(2,1)S(1)}, bf16[768]{0:T(1024)(128)(2,1)}, u32[]{:S(2)}) copy-start(bf16[768]{0:T(1024)(128)(2,1)} %param.30) | copy-start | bytes 4612
  3.0 7.5 %copy-start.30 = (bf16[768]{0:T(1024)(128)(2,1)S(1)}, bf16[768]{0:T(1024)(128)(2,1)}, u32[]{:S(2)}) copy-start(bf16[768]{0:T(1024)(128)(2,1)} %param.34) | copy-start | bytes 4612
  3.0 8.2 %copy-start.22 = (bf16[3072]{0:T(1024)(128)(2,1)S(1)}, bf16[3072]{0:T(1024)(128)(2,1)}, u32[]{:S(2)}) copy-start(bf16[3072]{0:T(1024)(128)(2,1)} %param.32) | copy-start | bytes 18436
  3.0 17.2 %collective-permute-start.2 = (bf16[272,768]{1,0:T(8,128)(2,1)S(1)}, bf16[272,768]{1,0:T(8,128)(2,1)S(1)}, u32[]{:S(2)}, u32[]{:S(2)}) collective-permute-start(bf16[272,768]{1,0:T(8,128)(2,1)S(1)} %pad_maximum_fusion.7), channel_id=1, source_target_pairs={{0,1},{1,0},{2,3},{3,2},{4,7},{5,6},{6,5},{7,4},{8,9},{9,8},{10,11... | collective-permute-start | bytes 1253384 | tf_op jit(solution)/shard_map/ppermute | solution.py:875
  6.2 22.0 %collective-permute-start.1 = (bf16[272,768]{1,0:T(8,128)(2,1)S(1)}, bf16[272,768]{1,0:T(8,128)(2,1)S(1)}, u32[]{:S(2)}, u32[]{:S(2)}) collective-permute-start(bf16[272,768]{1,0:T(8,128)(2,1)S(1)} %get-tuple-element.127), channel_id=1, source_target_pairs={{0,3},{1,2},{2,1},{3,0},{4,5},{5,4},{6,7},{7,6},{8,11},{9,10},{10,... | collective-permute-start | bytes 1253384 | tf_op jit(solution)/shard_map/ppermute | solution.py:875
  8.8 35.1 %collective-permute-start = (bf16[272,768]{1,0:T(8,128)(2,1)S(1)}, bf16[272,768]{1,0:T(8,128)(2,1)S(1)}, u32[]{:S(2)}, u32[]{:S(2)}) collective-permute-start(bf16[272,768]{1,0:T(8,128)(2,1)S(1)} %get-tuple-element.128), channel_id=1, source_target_pairs={{0,2},{1,3},{2,0},{3,1},{4,6},{5,7},{6,4},{7,5},{8,10},{9,11},{10,... | collective-permute-start | bytes 1253384 | tf_op jit(solution)/shard_map/ppermute | solution.py:875
  28.9 14.9 %copy-start.8 = (bf16[4,256,384]{2,1,0:T(8,128)(2,1)S(1)}, bf16[4,256,384]{2,1,0:T(8,128)(2,1)}, u32[]{:S(2)}) copy-start(bf16[4,256,384]{2,1,0:T(8,128)(2,1)} %param.19) | copy-start | bytes 2359300
  33.9 14.2 %copy-start.5 = (bf16[4,256,768]{2,1,0:T(8,128)(2,1)S(1)}, bf16[4,256,768]{2,1,0:T(8,128)(2,1)}, u32[]{:S(2)}) copy-start(bf16[4,256,768]{2,1,0:T(8,128)(2,1)} %param.35) | copy-start | bytes 4718596
  43.8 4.4 %copy-start.13 = (bf16[272,768]{1,0:T(8,128)(2,1)}, bf16[272,768]{1,0:T(8,128)(2,1)S(1)}, u32[]{:S(2)}) copy-start(bf16[272,768]{1,0:T(8,128)(2,1)S(1)} %collective-permute-done.x_ref) | copy-start | bytes 1253380
  44.6 25.4 %collective-permute-start.3 = (bf16[256,384]{1,0:T(8,128)(2,1)S(1)}, bf16[256,384]{1,0:T(8,128)(2,1)S(1)}, u32[]{:S(2)}, u32[]{:S(2)}) collective-permute-start(bf16[256,384]{1,0:T(8,128)(2,1)S(1)} %get-tuple-element.287), channel_id=1, source_target_pairs={{0,1},{1,0},{2,3},{3,2},{4,7},{5,6},{6,5},{7,4},{8,9},{9,8},{10,11... | collective-permute-start | bytes 589832 | tf_op jit(solution)/shard_map/ppermute | solution.py:875
  44.6 25.4 %collective-permute-start.4 = (bf16[256,384]{1,0:T(8,128)(2,1)S(1)}, bf16[256,384]{1,0:T(8,128)(2,1)S(1)}, u32[]{:S(2)}, u32[]{:S(2)}) collective-permute-start(bf16[256,384]{1,0:T(8,128)(2,1)S(1)} %get-tuple-element.286), channel_id=1, source_target_pairs={{0,3},{1,2},{2,1},{3,0},{4,5},{5,4},{6,7},{7,6},{8,11},{9,10},{10,... | collective-permute-start | bytes 589832 | tf_op jit(solution)/shard_map/ppermute | solution.py:875
  47.1 35.3 %collective-permute-start.5 = (bf16[256,384]{1,0:T(8,128)(2,1)S(1)}, bf16[256,384]{1,0:T(8,128)(2,1)S(1)}, u32[]{:S(2)}, u32[]{:S(2)}) collective-permute-start(bf16[256,384]{1,0:T(8,128)(2,1)S(1)} %get-tuple-element.285), channel_id=1, source_target_pairs={{0,2},{1,3},{2,0},{3,1},{4,6},{5,7},{6,4},{7,5},{8,10},{9,11},{10,... | collective-permute-start | bytes 589832 | tf_op jit(solution)/shard_map/ppermute | solution.py:875
  48.2 48.2 %collective-permute-start.7 = (bf16[256,768]{1,0:T(8,128)(2,1)S(1)}, bf16[256,768]{1,0:T(8,128)(2,1)S(1)}, u32[]{:S(2)}, u32[]{:S(2)}) collective-permute-start(bf16[256,768]{1,0:T(8,128)(2,1)S(1)} %get-tuple-element.255), channel_id=1, source_target_pairs={{0,2},{1,3},{2,0},{3,1},{4,6},{5,7},{6,4},{7,5},{8,10},{9,11},{10,... | collective-permute-start | bytes 1179656 | tf_op jit(solution)/shard_map/ppermute | solution.py:875
  50.2 46.2 %collective-permute-start.8 = (bf16[256,768]{1,0:T(8,128)(2,1)S(1)}, bf16[256,768]{1,0:T(8,128)(2,1)S(1)}, u32[]{:S(2)}, u32[]{:S(2)}) collective-permute-start(bf16[256,768]{1,0:T(8,128)(2,1)S(1)} %get-tuple-element.254), channel_id=1, source_target_pairs={{0,3},{1,2},{2,1},{3,0},{4,7},{5,6},{6,5},{7,4},{8,11},{9,10},{10,... | collective-permute-start | bytes 1179656 | tf_op jit(solution)/shard_map/ppermute | solution.py:875
  70.0 13.3 %copy-start.35 = (bf16[256,384]{1,0:T(8,128)(2,1)}, bf16[256,384]{1,0:T(8,128)(2,1)S(1)}, u32[]{:S(2)}) copy-start(bf16[256,384]{1,0:T(8,128)(2,1)S(1)} %collective-permute-done.3.refs_1_) | copy-start | bytes 589828
  70.0 13.2 %copy-start.36 = (bf16[256,384]{1,0:T(8,128)(2,1)}, bf16[256,384]{1,0:T(8,128)(2,1)S(1)}, u32[]{:S(2)}) copy-start(bf16[256,384]{1,0:T(8,128)(2,1)S(1)} %collective-permute-done.4.refs_2_) | copy-start | bytes 589828
  83.2 13.2 %collective-permute-start.6 = (bf16[256,768]{1,0:T(8,128)(2,1)S(1)}, bf16[256,768]{1,0:T(8,128)(2,1)S(1)}, u32[]{:S(2)}, u32[]{:S(2)}) collective-permute-start(bf16[256,768]{1,0:T(8,128)(2,1)S(1)} %get-tuple-element.256), channel_id=1, source_target_pairs={{0,1},{1,0},{2,3},{3,2},{4,5},{5,4},{6,7},{7,6},{8,9},{9,8},{10,11... | collective-permute-start | bytes 1179656 | tf_op jit(solution)/shard_map/ppermute | solution.py:875
  146.0 23.2 %collective-permute-start.9 = (bf16[4,384,768]{2,1,0:T(8,128)(2,1)}, bf16[4,384,768]{2,1,0:T(8,128)(2,1)S(1)}, u32[]{:S(2)}, u32[]{:S(2)}) collective-permute-start(bf16[4,384,768]{2,1,0:T(8,128)(2,1)} %get-tuple-element.171), channel_id=1, source_target_pairs={{0,4},{4,0},{8,12},{12,8},{16,20},{20,16},{24,28},{28,24},{1,5},{5... | collective-permute-start | bytes 7077896 | tf_op jit(solution)/shard_map/ppermute | solution.py:870
  146.1 23.2 %collective-permute-start.10 = (bf16[4,4,96,768]{3,2,1,0:T(8,128)(2,1)}, bf16[4,4,96,768]{3,2,1,0:T(8,128)(2,1)S(1)}, u32[]{:S(2)}, u32[]{:S(2)}) collective-permute-start(bf16[4,4,96,768]{3,2,1,0:T(8,128)(2,1)} %get-tuple-element.172), channel_id=1, source_target_pairs={{0,4},{4,0},{8,12},{12,8},{16,20},{20,16},{24,28},{28,24},{1,5},{5... | collective-permute-start | bytes 7077896 | tf_op jit(solution)/shard_map/ppermute | solution.py:870
  146.6 22.6 %collective-permute-start.11 = (bf16[2,256,768]{2,1,0:T(8,128)(2,1)}, bf16[2,256,768]{2,1,0:T(8,128)(2,1)S(1)}, u32[]{:S(2)}, u32[]{:S(2)}) collective-permute-start(bf16[2,256,768]{2,1,0:T(8,128)(2,1)} %get-tuple-element.173), channel_id=1, source_target_pairs={{0,1},{1,0},{2,3},{3,2},{4,7},{5,6},{6,5},{7,4},{8,9},{9,8},{10,11... | collective-permute-start | bytes 2359304 | tf_op jit(solution)/shard_map/ppermute | solution.py:875
  148.6 20.6 %collective-permute-start.12 = (bf16[4,6,96,128]{3,2,1,0:T(8,128)(2,1)}, bf16[4,6,96,128]{3,2,1,0:T(8,128)(2,1)}, u32[]{:S(2)}, u32[]{:S(2)}) collective-permute-start(bf16[4,6,96,128]{3,2,1,0:T(8,128)(2,1)} %get-tuple-element.174), channel_id=1, source_target_pairs={{0,4},{4,0},{8,12},{12,8},{16,20},{20,16},{24,28},{28,24},{1,5},{5... | collective-permute-start | bytes 1769480 | tf_op jit(solution)/shard_map/ppermute | solution.py:870
  148.6 21.5 %copy-start.2 = (bf16[4,384,768]{2,1,0:T(8,128)(2,1)S(1)}, bf16[4,384,768]{2,1,0:T(8,128)(2,1)}, u32[]{:S(2)}) copy-start(bf16[4,384,768]{2,1,0:T(8,128)(2,1)} %get-tuple-element.181) | copy-start | bytes 7077892
  170.1 1.7 copy-start.1
  174.5 30.7 %collective-permute-start.13 = (bf16[2,8,96,768]{3,2,1,0:T(8,128)(2,1)S(1)}, bf16[2,8,96,768]{3,2,1,0:T(8,128)(2,1)S(1)}, u32[]{:S(2)}, u32[]{:S(2)}) collective-permute-start(bf16[2,8,96,768]{3,2,1,0:T(8,128)(2,1)S(1)} %pad_maximum_fusion), channel_id=1, source_target_pairs={{0,8},{4,20},{8,0},{12,28},{16,24},{20,4},{24,16},{28,12},{1,9},{5... | collective-permute-start | bytes 7077896 | tf_op jit(solution)/shard_map/ppermute | solution.py:891
  176.0 29.2 %collective-permute-start.14 = (bf16[2,256,768]{2,1,0:T(8,128)(2,1)}, bf16[2,256,768]{2,1,0:T(8,128)(2,1)S(1)}, u32[]{:S(2)}, u32[]{:S(2)}) collective-permute-start(bf16[2,256,768]{2,1,0:T(8,128)(2,1)} %pad_maximum_fusion.2), channel_id=1, source_target_pairs={{0,3},{1,2},{2,1},{3,0},{4,5},{5,4},{6,7},{7,6},{8,11},{9,10},{10,... | collective-permute-start | bytes 2359304 | tf_op jit(solution)/shard_map/ppermute | solution.py:875
  177.7 27.5 %collective-permute-start.15 = (bf16[2,256,384]{2,1,0:T(8,128)(2,1)}, bf16[2,256,384]{2,1,0:T(8,128)(2,1)S(1)}, u32[]{:S(2)}, u32[]{:S(2)}) collective-permute-start(bf16[2,256,384]{2,1,0:T(8,128)(2,1)} %get-tuple-element.197), channel_id=1, source_target_pairs={{0,1},{1,0},{2,3},{3,2},{4,7},{5,6},{6,5},{7,4},{8,9},{9,8},{10,11... | collective-permute-start | bytes 1179656 | tf_op jit(solution)/shard_map/ppermute | solution.py:875
  177.9 27.4 %collective-permute-start.16 = (bf16[4,3,2,96,128]{4,3,2,1,0:T(8,128)(2,1)}, bf16[4,3,2,96,128]{4,3,2,1,0:T(8,128)(2,1)}, u32[]{:S(2)}, u32[]{:S(2)}) collective-permute-start(bf16[4,3,2,96,128]{4,3,2,1,0:T(8,128)(2,1)} %get-tuple-element.198), channel_id=1, source_target_pairs={{0,4},{4,0},{8,12},{12,8},{16,20},{20,16},{24,28},{28,24},{1,5},{5... | collective-permute-start | bytes 1769480 | tf_op jit(solution)/shard_map/ppermute | solution.py:870
  205.2 2.6 copy-start.6
  206.2 1.6 copy-start.19
  206.2 4.5 %copy-start.9 = (bf16[2,256,768]{2,1,0:T(8,128)(2,1)S(1)}, bf16[2,256,768]{2,1,0:T(8,128)(2,1)}, u32[]{:S(2)}) copy-start(bf16[2,256,768]{2,1,0:T(8,128)(2,1)} %get-tuple-element.223) | copy-start | bytes 2359300
  206.2 7.9 %copy-start.11 = (bf16[4,6,96,128]{3,2,1,0:T(8,128)(2,1)S(1)}, bf16[4,6,96,128]{3,2,1,0:T(8,128)(2,1)}, u32[]{:S(2)}) copy-start(bf16[4,6,96,128]{3,2,1,0:T(8,128)(2,1)} %get-tuple-element.213) | copy-start | bytes 1769476
  206.2 33.1 %collective-permute-start.17 = (bf16[8,96,768]{2,1,0:T(8,128)(2,1)S(1)}, bf16[8,96,768]{2,1,0:T(8,128)(2,1)S(1)}, u32[]{:S(2)}, u32[]{:S(2)}) collective-permute-start(bf16[8,96,768]{2,1,0:T(8,128)(2,1)S(1)} %slice_bitcast_fusion.1), channel_id=1, source_target_pairs={{0,16},{4,12},{8,24},{12,4},{16,0},{20,28},{24,8},{28,20},{1,17},{... | collective-permute-start | bytes 3538952 | tf_op jit(solution)/shard_map/ppermute | solution.py:891
  207.8 31.6 %collective-permute-start.18 = (bf16[4,3,3,96,128]{4,3,2,1,0:T(8,128)(2,1)}, bf16[4,3,3,96,128]{4,3,2,1,0:T(8,128)(2,1)S(1)}, u32[]{:S(2)}, u32[]{:S(2)}) collective-permute-start(bf16[4,3,3,96,128]{4,3,2,1,0:T(8,128)(2,1)} %get-tuple-element.200), channel_id=1, source_target_pairs={{0,4},{4,0},{8,12},{12,8},{16,20},{20,16},{24,28},{28,24},{1,5},{5... | collective-permute-start | bytes 2654216 | tf_op jit(solution)/shard_map/ppermute | solution.py:870
  208.6 14.1 %collective-permute-start.19 = (bf16[2,256,384]{2,1,0:T(8,128)(2,1)}, bf16[2,256,384]{2,1,0:T(8,128)(2,1)S(1)}, u32[]{:S(2)}, u32[]{:S(2)}) collective-permute-start(bf16[2,256,384]{2,1,0:T(8,128)(2,1)} %pad_maximum_fusion.9), channel_id=1, source_target_pairs={{0,3},{1,2},{2,1},{3,0},{4,5},{5,4},{6,7},{7,6},{8,11},{9,10},{10,... | collective-permute-start | bytes 1179656 | tf_op jit(solution)/shard_map/ppermute | solution.py:875
  211.4 20.8 %collective-permute-start.20 = (bf16[256,768]{1,0:T(8,128)(2,1)}, bf16[256,768]{1,0:T(8,128)(2,1)S(1)}, u32[]{:S(2)}, u32[]{:S(2)}) collective-permute-start(bf16[256,768]{1,0:T(8,128)(2,1)} %slice_bitcast_fusion.5), channel_id=1, source_target_pairs={{0,1},{1,0},{2,3},{3,2},{4,7},{5,6},{6,5},{7,4},{8,9},{9,8},{10,11... | collective-permute-start | bytes 1179656 | tf_op jit(solution)/shard_map/ppermute | solution.py:875
  212.5 26.8 %collective-permute-start.21 = (bf16[256,768]{1,0:T(8,128)(2,1)}, bf16[256,768]{1,0:T(8,128)(2,1)}, u32[]{:S(2)}, u32[]{:S(2)}) collective-permute-start(bf16[256,768]{1,0:T(8,128)(2,1)} %get-tuple-element.207), channel_id=1, source_target_pairs={{0,3},{1,2},{2,1},{3,0},{4,5},{5,4},{6,7},{7,6},{8,11},{9,10},{10,... | collective-permute-start | bytes 1179656 | tf_op jit(solution)/shard_map/ppermute | solution.py:875
  215.4 3.2 %copy-start.12 = (bf16[4,3,2,96,128]{4,3,2,1,0:T(8,128)(2,1)S(1)}, bf16[4,3,2,96,128]{4,3,2,1,0:T(8,128)(2,1)}, u32[]{:S(2)}) copy-start(bf16[4,3,2,96,128]{4,3,2,1,0:T(8,128)(2,1)} %get-tuple-element.215) | copy-start | bytes 1769476
  218.6 20.7 %copy-start.7 = (bf16[4,3,3,96,128]{4,3,2,1,0:T(8,128)(2,1)S(1)}, bf16[4,3,3,96,128]{4,3,2,1,0:T(8,128)(2,1)}, u32[]{:S(2)}) copy-start(bf16[4,3,3,96,128]{4,3,2,1,0:T(8,128)(2,1)} %get-tuple-element.217) | copy-start | bytes 2654212
  222.8 16.9 %copy-start.4 = (bf16[2,256,384]{2,1,0:T(8,128)(2,1)}, bf16[2,256,384]{2,1,0:T(8,128)(2,1)S(1)}, u32[]{:S(2)}) copy-start(bf16[2,256,384]{2,1,0:T(8,128)(2,1)S(1)} %collective-permute-done.19.refs_2_.refs_3_) | copy-start | bytes 1179652
  232.1 7.6 %copy-start.16 = (bf16[256,768]{1,0:T(8,128)(2,1)}, bf16[256,768]{1,0:T(8,128)(2,1)S(1)}, u32[]{:S(2)}) copy-start(bf16[256,768]{1,0:T(8,128)(2,1)S(1)} %collective-permute-done.20.refs_1_) | copy-start | bytes 1179652
  239.7 15.6 %collective-permute-start.22 = (bf16[2,21,96,128]{3,2,1,0:T(8,128)(2,1)S(1)}, bf16[2,21,96,128]{3,2,1,0:T(8,128)(2,1)S(1)}, u32[]{:S(2)}, u32[]{:S(2)}) collective-permute-start(bf16[2,21,96,128]{3,2,1,0:T(8,128)(2,1)S(1)} %pad_maximum_fusion.1), channel_id=1, source_target_pairs={{0,8},{4,20},{8,0},{12,28},{16,24},{20,4},{24,16},{28,12},{1,9},{5... | collective-permute-start | bytes 3096584 | tf_op jit(solution)/shard_map/ppermute | solution.py:891
  240.3 5.7 %collective-permute-start.23 = (f32[72,128]{1,0:T(8,128)S(1)}, f32[72,128]{1,0:T(8,128)S(1)}, u32[]{:S(2)}, u32[]{:S(2)}) collective-permute-start(f32[72,128]{1,0:T(8,128)S(1)} %copy-done.20), channel_id=1, source_target_pairs={{0,1},{1,0},{2,3},{3,2},{4,5},{5,4},{6,7},{7,6},{8,9},{9,8},{10,11... | collective-permute-start | bytes 110600 | tf_op jit(solution)/shard_map/ppermute | solution.py:875
  240.8 33.3 %collective-permute-start.25 = (bf16[2,2,96,768]{3,2,1,0:T(8,128)(2,1)S(1)}, bf16[2,2,96,768]{3,2,1,0:T(8,128)(2,1)S(1)}, u32[]{:S(2)}, u32[]{:S(2)}) collective-permute-start(bf16[2,2,96,768]{3,2,1,0:T(8,128)(2,1)S(1)} %pad_maximum_fusion.3), channel_id=1, source_target_pairs={{0,1},{1,0},{2,3},{3,2},{4,7},{5,6},{6,5},{7,4},{8,9},{9,8},{10,11... | collective-permute-start | bytes 1769480 | tf_op jit(solution)/shard_map/ppermute | solution.py:875
  255.6 18.5 %collective-permute-start.24 = (bf16[21,96,128]{2,1,0:T(8,128)(2,1)S(1)}, bf16[21,96,128]{2,1,0:T(8,128)(2,1)S(1)}, u32[]{:S(2)}, u32[]{:S(2)}) collective-permute-start(bf16[21,96,128]{2,1,0:T(8,128)(2,1)S(1)} %slice_bitcast_fusion.3), channel_id=1, source_target_pairs={{0,16},{4,12},{8,24},{12,4},{16,0},{20,28},{24,8},{28,20},{1,17},{... | collective-permute-start | bytes 1548296 | tf_op jit(solution)/shard_map/ppermute | solution.py:891
  256.5 17.6 %collective-permute-start.26 = (bf16[256,768]{1,0:T(8,128)(2,1)S(1)}, bf16[256,768]{1,0:T(8,128)(2,1)S(1)}, u32[]{:S(2)}, u32[]{:S(2)}) collective-permute-start(bf16[256,768]{1,0:T(8,128)(2,1)S(1)} %slice_bitcast_fusion.4), channel_id=1, source_target_pairs={{0,2},{1,3},{2,0},{3,1},{4,6},{5,7},{6,4},{7,5},{8,10},{9,11},{10,... | collective-permute-start | bytes 1179656 | tf_op jit(solution)/shard_map/ppermute | solution.py:875
  256.7 17.4 %collective-permute-start.27 = (f32[72,128]{1,0:T(8,128)S(1)}, f32[72,128]{1,0:T(8,128)S(1)}, u32[]{:S(2)}, u32[]{:S(2)}) collective-permute-start(f32[72,128]{1,0:T(8,128)S(1)} %add.147), channel_id=1, source_target_pairs={{0,3},{1,2},{2,1},{3,0},{4,7},{5,6},{6,5},{7,4},{8,11},{9,10},{10,... | collective-permute-start | bytes 110600 | tf_op jit(solution)/shard_map/ppermute | solution.py:875
  274.4 12.0 %collective-permute-start.30 = (bf16[2,21,24,128]{3,2,1,0:T(8,128)(2,1)S(1)}, bf16[2,21,24,128]{3,2,1,0:T(8,128)(2,1)S(1)}, u32[]{:S(2)}, u32[]{:S(2)}) collective-permute-start(bf16[2,21,24,128]{3,2,1,0:T(8,128)(2,1)S(1)} %pad_maximum_fusion.10), channel_id=1, source_target_pairs={{0,1},{1,0},{2,3},{3,2},{4,7},{5,6},{6,5},{7,4},{8,9},{9,8},{10,11... | collective-permute-start | bytes 774152 | tf_op jit(solution)/shard_map/ppermute | solution.py:875
  275.6 16.6 %collective-permute-start.28 = (f32[72,128]{1,0:T(8,128)S(1)}, f32[72,128]{1,0:T(8,128)S(1)}, u32[]{:S(2)}, u32[]{:S(2)}) collective-permute-start(f32[72,128]{1,0:T(8,128)S(1)} %add.149), channel_id=1, source_target_pairs={{0,4},{4,0},{8,12},{12,8},{16,20},{20,16},{24,28},{28,24},{1,5},{5... | collective-permute-start | bytes 110600 | tf_op jit(solution)/shard_map/ppermute | solution.py:870
  275.7 15.0 %collective-permute-start.29 = (bf16[2,96,768]{2,1,0:T(8,128)(2,1)S(1)}, bf16[2,96,768]{2,1,0:T(8,128)(2,1)S(1)}, u32[]{:S(2)}, u32[]{:S(2)}) collective-permute-start(bf16[2,96,768]{2,1,0:T(8,128)(2,1)S(1)} %slice_bitcast_fusion.9), channel_id=1, source_target_pairs={{0,3},{1,2},{2,1},{3,0},{4,5},{5,4},{6,7},{7,6},{8,11},{9,10},{10,... | collective-permute-start | bytes 884744 | tf_op jit(solution)/shard_map/ppermute | solution.py:875
  286.5 8.3 %collective-permute-start.32 = (bf16[21,24,128]{2,1,0:T(8,128)(2,1)S(1)}, bf16[21,24,128]{2,1,0:T(8,128)(2,1)S(1)}, u32[]{:S(2)}, u32[]{:S(2)}) collective-permute-start(bf16[21,24,128]{2,1,0:T(8,128)(2,1)S(1)} %slice_bitcast_fusion.21), channel_id=1, source_target_pairs={{0,3},{1,2},{2,1},{3,0},{4,5},{5,4},{6,7},{7,6},{8,11},{9,10},{10,... | collective-permute-start | bytes 387080 | tf_op jit(solution)/shard_map/ppermute | solution.py:875
  290.8 10.0 %collective-permute-start.35 = (bf16[2,96,768]{2,1,0:T(8,128)(2,1)S(1)}, bf16[2,96,768]{2,1,0:T(8,128)(2,1)S(1)}, u32[]{:S(2)}, u32[]{:S(2)}) collective-permute-start(bf16[2,96,768]{2,1,0:T(8,128)(2,1)S(1)} %fusion.2), channel_id=1, source_target_pairs={{0,3},{1,2},{2,1},{3,0},{4,5},{5,4},{6,7},{7,6},{8,11},{9,10},{10,... | collective-permute-start | bytes 884744 | tf_op jit(solution)/shard_map/ppermute | solution.py:875
  292.2 4.0 %collective-permute-start.31 = (f32[72,128]{1,0:T(8,128)S(1)}, f32[72,128]{1,0:T(8,128)S(1)}, u32[]{:S(2)}, u32[]{:S(2)}) collective-permute-start(f32[72,128]{1,0:T(8,128)S(1)} %add.153), channel_id=1, source_target_pairs={{0,8},{4,12},{8,0},{12,4},{16,24},{20,28},{24,16},{28,20},{1,9},{5... | collective-permute-start | bytes 110600 | tf_op jit(solution)/shard_map/ppermute | solution.py:891
  296.2 4.0 %collective-permute-start.33 = (f32[72,128]{1,0:T(8,128)S(1)}, f32[72,128]{1,0:T(8,128)S(1)}, u32[]{:S(2)}, u32[]{:S(2)}) collective-permute-start(f32[72,128]{1,0:T(8,128)S(1)} %add.155), channel_id=1, source_target_pairs={{0,16},{4,20},{8,24},{12,28},{16,0},{20,4},{24,8},{28,12},{1,17},{... | collective-permute-start | bytes 110600 | tf_op jit(solution)/shard_map/ppermute | solution.py:891
  296.9 8.2 %collective-permute-start.34 = (bf16[21,24,128]{2,1,0:T(8,128)(2,1)S(1)}, bf16[21,24,128]{2,1,0:T(8,128)(2,1)S(1)}, u32[]{:S(2)}, u32[]{:S(2)}) collective-permute-start(bf16[21,24,128]{2,1,0:T(8,128)(2,1)S(1)} %fusion.3), channel_id=1, source_target_pairs={{0,3},{1,2},{2,1},{3,0},{4,5},{5,4},{6,7},{7,6},{8,11},{9,10},{10,... | collective-permute-start | bytes 387080 | tf_op jit(solution)/shard_map/ppermute | solution.py:875
  305.2 9.1 %collective-permute-start.36 = (bf16[2,21,24,128]{3,2,1,0:T(8,128)(2,1)S(1)}, bf16[2,21,24,128]{3,2,1,0:T(8,128)(2,1)S(1)}, u32[]{:S(2)}, u32[]{:S(2)}) collective-permute-start(bf16[2,21,24,128]{3,2,1,0:T(8,128)(2,1)S(1)} %pad_maximum_fusion.11), channel_id=1, source_target_pairs={{0,1},{1,0},{2,3},{3,2},{4,7},{5,6},{6,5},{7,4},{8,9},{9,8},{10,11... | collective-permute-start | bytes 774152 | tf_op jit(solution)/shard_map/ppermute | solution.py:875
  306.5 14.2 %collective-permute-start.37 = (bf16[2,2,96,768]{3,2,1,0:T(8,128)(2,1)S(1)}, bf16[2,2,96,768]{3,2,1,0:T(8,128)(2,1)S(1)}, u32[]{:S(2)}, u32[]{:S(2)}) collective-permute-start(bf16[2,2,96,768]{3,2,1,0:T(8,128)(2,1)S(1)} %pad_maximum_fusion.4), channel_id=1, source_target_pairs={{0,1},{1,0},{2,3},{3,2},{4,7},{5,6},{6,5},{7,4},{8,9},{9,8},{10,11... | collective-permute-start | bytes 1769480 | tf_op jit(solution)/shard_map/ppermute | solution.py:875
  314.9 5.9 %copy-start.21 = (f32[96,768]{1,0:T(8,128)}, f32[96,768]{1,0:T(8,128)S(1)}, u32[]{:S(2)}) copy-start(f32[96,768]{1,0:T(8,128)S(1)} %get-tuple-element.273) | copy-start | bytes 884740
  314.9 5.9 %copy-start.23 = (f32[96,1920]{1,0:T(8,128)}, f32[96,1920]{1,0:T(8,128)S(1)}, u32[]{:S(2)}) copy-start(f32[96,1920]{1,0:T(8,128)S(1)} %get-tuple-element.274) | copy-start | bytes 2211844
  (13 other events, 12.3 us)

commit v6 on v5

--- a/solution.py
+++ b/solution.py
@@ -228,14 +228,16 @@
         *y_refs, packed_ref = take(4)
     else:
         (after_ref,) = take(1)
-    bias_ref, value_ref, dkt_ref, dvt_ref, d_ref, w_ref, acc_ref, stage_ref = refs
+    bias_ref, value_ref, dkt_ref, dvt_ref, d_ref, w_ref, stage_ref = refs[:7]
+    acc_ref = refs[7] if last_call else after_ref
     step = pl.program_id(0)
     lane = lambda n: slice(n * PAIR, (n + 1) * PAIR)
 
     @pl.when(step == 0)
     def _():
         fill_bias(code_ref, bias_ref)
-        acc_ref[...] = jnp.zeros_like(acc_ref) if first_call else before_ref[...]
+        if not first_call:
+            acc_ref[...] = before_ref[...]
 
     length = q_ref.shape[0]
     v_pair = gather_values(me_ref, v_refs, value_ref)
@@ -286,7 +288,19 @@
         packed_ref[pl.ds(V_ROWS + step, 1), :] = sums[:, lane(2)]
     else:
         bias_sums_ref[0] = sums
-    acc_ref[...] += nt(grad, w_ref[...])
+    share = nt(grad, w_ref[...])
+    if first_call:
+
+        @pl.when(step == 0)
+        def _():
+            acc_ref[...] = share
+
+        @pl.when(step > 0)
+        def _():
+            acc_ref[...] += share
+
+    else:
+        acc_ref[...] += share
     store_units(tn(normed_ref[...], grad), me_ref, stage_ref, send_ref, keep_ref, (0,))
 
     @pl.when(step == pl.num_programs(0) - 1)
@@ -306,8 +320,6 @@
                     packed_ref[first_row + n : first_row + n + 1, :] = value
             acc_ref[...] = d_att_ref[...].astype(F32) + standardize_back(total * vec_ref[ATTN_GAIN], unit, rate)
             deal_out(me_ref, acc_ref, *y_refs)
-        else:
-            after_ref[...] = acc_ref[...]
 
 
 def pair_specs(length, offset):
@@ -390,9 +402,9 @@
             pltpu.VMEM((PAIR, length), F32),
             pltpu.VMEM((length, cols), BF16),
             pltpu.VMEM((width, cols), BF16),
-            pltpu.VMEM((length, width), F32),
             pltpu.VMEM((4, 2, strip, cols), BF16),
-        ],
+        ]
+        + ([] if last is None else [pltpu.VMEM((length, width), F32)]),
         flops=pairs * (30 * length * length * PAIR + 4 * length * width * cols),
         moved=pairs * length * PAIR * 18 + 12 * length * width,
     )(at, *args)

time: 329 us -> 332 us (level)
  transfers between devices with their start and end apart: 38 -> 38, of which waited for: 17 -> 17; matrix products, arithmetic and copies ran while one was open for 4% -> 4% of each run, Pallas kernels for 32% -> 33%
where the time goes in v6:
time: 332 us; the launch traced here: 327 us
  Pallas kernels  156 us (47%)
  waiting for transfers between devices  101 us (30%)
  starting transfers between devices  41.4 us (12%)
  other arithmetic  14.7 us (4%)
  local copies, waits for them, and re-layouts  12.2 us (4%)
    ppermute x26, waiting for transfers between devices, group_swap(): return lax.ppermute(array, ('seq', 'head'), pairs)  89.3 us
    pallas_call x2, Pallas kernels, attend_back(): call(functools.partial(backward_kernel, len(values), before is None, last...  50.9 us
    pallas_call x1, Pallas kernels, feed(): call(feed_kernel, 'feed', (4,), [full, once(o_a.shape), once(o_b.shape)]...  48.5 us
    ppermute x26, starting transfers between devices, group_swap(): return lax.ppermute(array, ('seq', 'head'), pairs)  34.8 us
    pallas_call x2, Pallas kernels, attend(): call(functools.partial(forward_kernel, len(values)), name, (pairs,), [who...  26.7 us
    pallas_call x4, Pallas kernels, project(): call(project_kernel, 'project', (1,), [whole((part + CODE_ROWS, width)),...  19.5 us
    ppermute x6, waiting for transfers between devices, plane_swap(): lax.ppermute(array, 'seq', [(s, s ^ (core_one if s & 1 else core_zero)) f...  11.2 us
    pallas_call x3, Pallas kernels, settle(): call(settle_kernel, name, (2,), specs, pl.BlockSpec((4, rows, width), lam...  10 us
  transfers between devices with their start and end apart: 38, of which 17 were waited for; matrix products, arithmetic and copies ran while one was open for 4% of the time, Pallas kernels for 33%

profile of v6, /device:TPU:0, one launch (start us, length us, event | category | flops | bytes accessed | tf_op | source)
XLA Modules:
  0.0 326.5 jit_solution(8260530903111032771)
XLA Ops:
  1.4 1.5 dynamic-slice_bitcast_fusion.4
  3.0 3.1 collective-permute-start.2
  6.2 2.5 collective-permute-start.1
  9.0 0.8 pad_maximum_fusion.8.x_ref
  12.4 4.8 %project.4 = (bf16[1024,768]{1,0:T(8,128)(2,1)}, bf16[1024,768]{1,0:T(8,128)(2,1)}, bf16[1024,1920]{1,0:T(8,128)(2,1)}, s32[8,1024]{1,0:T(8,128)}) custom-call(s32[3]{0:T(128)} %pad_add_fusion.at_ref.me_ref, bf16[272,768]{1,0:T(8,128)(2,1)} %pad_maximum_fusion.8.x_ref, f32[8,768]{1,0:T(8,128)} %convert_element_type.233.vec_ref.refs_10_, ...), custom_call_target="tpu_custom_call" | custom-call | flops 754974720 | bytes 5111808 | tf_op jit(solution)/shard_map/project/pallas_call | solution.py:140
  17.3 3.0 collective-permute-done.2.x_ref
  21.0 4.9 %project.5 = (bf16[1024,768]{1,0:T(8,128)(2,1)}, bf16[1024,768]{1,0:T(8,128)(2,1)}, bf16[1024,1920]{1,0:T(8,128)(2,1)}, s32[8,1024]{1,0:T(8,128)}) custom-call(s32[3]{0:T(128)} %pad_add_fusion.at_ref.me_ref, bf16[272,768]{1,0:T(8,128)(2,1)} %copy-done.14, ...), custom_call_target="tpu_custom_call", output_to_operand_aliasing={{0}: (5, {}), {1}: (6, {}), {2}: (7, {}), {3}: (8, {})} | custom-call | flops 754974720 | bytes 5111808 | tf_op jit(solution)/shard_map/project/pallas_call | solution.py:140
  25.9 2.3 collective-permute-done.1.x_ref
  28.9 5.0 %project.6 = (bf16[1024,768]{1,0:T(8,128)(2,1)}, bf16[1024,768]{1,0:T(8,128)(2,1)}, bf16[1024,1920]{1,0:T(8,128)(2,1)}, s32[8,1024]{1,0:T(8,128)}) custom-call(s32[3]{0:T(128)} %pad_add_fusion.at_ref.me_ref, bf16[272,768]{1,0:T(8,128)(2,1)} %copy-done.15, ...), custom_call_target="tpu_custom_call", output_to_operand_aliasing={{0}: (5, {}), {1}: (6, {}), {2}: (7, {}), {3}: (8, {})} | custom-call | flops 754974720 | bytes 5111808 | tf_op jit(solution)/shard_map/project/pallas_call | solution.py:140
  33.9 9.9 %collective-permute-done.x_ref = bf16[272,768]{1,0:T(8,128)(2,1)S(1)} collective-permute-done((bf16[272,768]{1,0:T(8,128)(2,1)S(1)}, bf16[272,768]{1,0:T(8,128)(2,1)S(1)}, u32[]{:S(2)}, u32[]{:S(2)}) %collective-permute-start) | collective-permute-done | bytes 417824 | tf_op jit(solution)/shard_map/ppermute | solution.py:887
  43.8 0.8 dynamic-slice_bitcast_fusion.12
  44.6 2.5 collective-permute-start.4
  47.1 1.0 collective-permute-start.5
  48.2 2.0 collective-permute-start.7
  50.2 1.3 collective-permute-start.8
  51.5 4.8 %project.7 = (bf16[1024,768]{1,0:T(8,128)(2,1)}, bf16[1024,768]{1,0:T(8,128)(2,1)}, bf16[1024,1920]{1,0:T(8,128)(2,1)}, s32[8,1024]{1,0:T(8,128)}) custom-call(s32[3]{0:T(128)} %pad_add_fusion.at_ref.me_ref, bf16[272,768]{1,0:T(8,128)(2,1)} %copy-done.13, ...), custom_call_target="tpu_custom_call", output_to_operand_aliasing={{0}: (5, {}), {1}: (6, {}), {2}: (7, {}), {3}: (8, {})} | custom-call | flops 754974720 | bytes 5111808 | tf_op jit(solution)/shard_map/project/pallas_call | solution.py:140
  56.3 13.6 %attend_a.1 = (bf16[1024,384]{1,0:T(8,128)(2,1)}, f32[1024,384]{1,0:T(8,128)}) custom-call(s32[3]{0:T(128)} %pad_add_fusion.at_ref.me_ref, s32[8,1024]{1,0:T(8,128)} %get-tuple-element.146.code_ref, bf16[1024,1920]{1,0:T(8,128)(2,1)} %get-tuple-element.147.q_ref.k_ref.refs_0_, bf16[1024,1920]{1,0:T(8,128)(2,1)} %get-tuple-element.147.q_ref.k_ref.refs_0_, ...), custom_call_target="tpu_custom_call" | custom-call | flops 9663676416 | bytes 4718592 | tf_op jit(solution)/shard_map/attend_a/pallas_call | solution.py:338
  70.0 12.4 %collective-permute-done.5.refs_3_ = bf16[256,384]{1,0:T(8,128)(2,1)S(1)} collective-permute-done((bf16[256,384]{1,0:T(8,128)(2,1)S(1)}, bf16[256,384]{1,0:T(8,128)(2,1)S(1)}, u32[]{:S(2)}, u32[]{:S(2)}) %collective-permute-start.5) | collective-permute-done | bytes 196640 | tf_op jit(solution)/shard_map/ppermute | solution.py:887
  82.4 0.8 dynamic-slice_bitcast_fusion.2
  83.3 13.1 %attend_b.1 = (bf16[1024,384]{1,0:T(8,128)(2,1)}, f32[1024,384]{1,0:T(8,128)}) custom-call(s32[3]{0:T(128)} %pad_add_fusion.at_ref.me_ref, s32[8,1024]{1,0:T(8,128)} %get-tuple-element.146.code_ref, bf16[1024,1920]{1,0:T(8,128)(2,1)} %get-tuple-element.147.q_ref.k_ref.refs_0_, bf16[1024,1920]{1,0:T(8,128)(2,1)} %get-tuple-element.147.q_ref.k_ref.refs_0_, ...), custom_call_target="tpu_custom_call" | custom-call | flops 9663676416 | bytes 4718592 | tf_op jit(solution)/shard_map/attend_b/pallas_call | solution.py:338
  97.5 48.5 %feed.1 = (bf16[256,768]{1,0:T(8,128)(2,1)}, bf16[2,256,768]{2,1,0:T(8,128)(2,1)}, bf16[256,768]{1,0:T(8,128)(2,1)}, bf16[4,384,768]{2,1,0:T(8,128)(2,1)}, bf16[...) custom-call(s32[3]{0:T(128)} %pad_add_fusion.at_ref.me_ref, ...), custom_call_target="tpu_custom_call" | custom-call | flops 32614907904 | bytes 33423360 | tf_op jit(solution)/shard_map/feed/pallas_call | solution.py:515
  146.6 2.0 collective-permute-start.11
  148.6 23.7 %attend_back_b.1 = (bf16[4,3,2,96,128]{4,3,2,1,0:T(8,128)(2,1)}, bf16[4,3,2,96,128]{4,3,2,1,0:T(8,128)(2,1)}, f32[3,1,256]{2,1,0:T(1,128)}, bf16[256,384]{1,0:T(...) custom-call(s32[3]{0:T(128)} %pad_add_fusion.at_ref.me_ref, ...), custom_call_target="tpu_custom_call" | custom-call | flops 14495514624 | bytes 16515072 | tf_op jit(solution)/shard_map/attend_back_b/pallas_call | solution.py:391
  172.3 0.9 copy-done.3
  173.7 1.1 copy-done.1
  175.8 0.8 slice-done
  176.6 1.0 pad_maximum_fusion.2
  177.6 1.5 collective-permute-start.13
  179.1 1.6 collective-permute-start.14
  181.0 27.3 %attend_back_a.1 = (bf16[4,3,3,96,128]{4,3,2,1,0:T(8,128)(2,1)}, bf16[4,3,3,96,128]{4,3,2,1,0:T(8,128)(2,1)}, bf16[256,768]{1,0:T(8,128)(2,1)}, bf16[2,256,768]{...) custom-call(s32[3]{0:T(128)} %pad_add_fusion.at_ref.me_ref, s32[8,1024]{1,0:T(8,128)} %get-tuple-element.146.code_ref, ...), custom_call_target="tpu_custom_call" | custom-call | flops 15703474176 | bytes 16515072 | tf_op jit(solution)/shard_map/attend_back_a/pallas_call | solution.py:391
  209.4 1.5 collective-permute-start.17
  210.9 0.8 pad_maximum_fusion.9
  211.7 2.0 collective-permute-start.19
  213.7 0.8 slice_bitcast_fusion.5
  214.5 1.1 collective-permute-start.20
  215.6 1.6 collective-permute-start.21
  217.3 1.2 add_convert_fusion.10
  218.5 3.2 settle_out.1
  221.7 1.3 add_convert_fusion.9
  223.0 2.9 collective-permute-done.19.refs_2_.refs_3_
  225.9 9.4 %collective-permute-done.20.refs_1_ = bf16[256,768]{1,0:T(8,128)(2,1)S(1)} collective-permute-done((bf16[256,768]{1,0:T(8,128)(2,1)}, bf16[256,768]{1,0:T(8,128)(2,1)S(1)}, u32[]{:S(2)}, u32[]{:S(2)}) %collective-permute-start.20) | collective-permute-done | bytes 393248 | tf_op jit(solution)/shard_map/ppermute | solution.py:887
  235.2 7.2 %collective-permute-done.21.refs_2_ = bf16[256,768]{1,0:T(8,128)(2,1)} collective-permute-done((bf16[256,768]{1,0:T(8,128)(2,1)}, bf16[256,768]{1,0:T(8,128)(2,1)}, u32[]{:S(2)}, u32[]{:S(2)}) %collective-permute-start.21) | collective-permute-done | bytes 393248 | tf_op jit(solution)/shard_map/ppermute | solution.py:887
  243.9 2.1 collective-permute-start.25
  246.0 3.1 settle_skip.1
  249.1 9.3 %collective-permute-done.22 = bf16[2,21,96,128]{3,2,1,0:T(8,128)(2,1)S(1)} collective-permute-done((bf16[2,21,96,128]{3,2,1,0:T(8,128)(2,1)S(1)}, bf16[2,21,96,128]{3,2,1,0:T(8,128)(2,1)S(1)}, u32[]{:S(2)}, u32[]{:S(2)}) %collective-permute-start.22) | collective-permute-done | bytes 1032224 | tf_op jit(solution)/shard_map/ppermute | solution.py:903
  258.7 0.8 collective-permute-start.24
  259.8 1.1 collective-permute-start.27
  260.9 16.3 %collective-permute-done.26.refs_3_ = bf16[256,768]{1,0:T(8,128)(2,1)S(1)} collective-permute-done((bf16[256,768]{1,0:T(8,128)(2,1)S(1)}, bf16[256,768]{1,0:T(8,128)(2,1)S(1)}, u32[]{:S(2)}, u32[]{:S(2)}) %collective-permute-start.26) | collective-permute-done | bytes 393248 | tf_op jit(solution)/shard_map/ppermute | solution.py:887
  277.5 1.0 collective-permute-start.30
  278.8 1.9 collective-permute-start.29
  280.7 3.7 %settle_tokens.1 = f32[4,256,768]{2,1,0:T(8,128)} custom-call(s32[3]{0:T(128)} %pad_add_fusion.at_ref.me_ref, bf16[256,768]{1,0:T(8,128)(2,1)} %get-tuple-element.209.refs_0_, bf16[256,768]{1,0:T(8,128)(2,1)} %copy-done.16, bf16[256,768]{1,0:T(8,128)(2,1)} %collective-permute-done.21.refs_2_, bf16[256,768]{1,0:T(8,128)(2,1)} %copy-done.17), custom_call_target="tpu_custom_call" | custom-call | bytes 4718592 | tf_op jit(solution)/shard_map/settle_tokens/pallas_call | solution.py:556
  284.3 5.1 %collective-permute-done.30 = bf16[2,21,24,128]{3,2,1,0:T(8,128)(2,1)S(1)} collective-permute-done((bf16[2,21,24,128]{3,2,1,0:T(8,128)(2,1)S(1)}, bf16[2,21,24,128]{3,2,1,0:T(8,128)(2,1)S(1)}, u32[]{:S(2)}, u32[]{:S(2)}) %collective-permute-start.30) | collective-permute-done | bytes 258080 | tf_op jit(solution)/shard_map/ppermute | solution.py:887
  289.5 1.1 collective-permute-start.32
  290.6 3.1 collective-permute-done.29
  293.9 1.4 collective-permute-start.35
  295.9 1.8 collective-permute-done.32
  297.8 1.4 collective-permute-done.31
  300.0 2.7 collective-permute-start.34
  303.9 4.3 %collective-permute-done.34 = bf16[21,24,128]{2,1,0:T(8,128)(2,1)S(1)} collective-permute-done((bf16[21,24,128]{2,1,0:T(8,128)(2,1)S(1)}, bf16[21,24,128]{2,1,0:T(8,128)(2,1)S(1)}, u32[]{:S(2)}, u32[]{:S(2)}) %collective-permute-start.34) | collective-permute-done | bytes 129056 | tf_op jit(solution)/shard_map/ppermute | solution.py:887
  309.6 2.0 collective-permute-start.37
  311.6 5.8 %collective-permute-done.36 = bf16[2,21,24,128]{3,2,1,0:T(8,128)(2,1)S(1)} collective-permute-done((bf16[2,21,24,128]{3,2,1,0:T(8,128)(2,1)S(1)}, bf16[2,21,24,128]{3,2,1,0:T(8,128)(2,1)S(1)}, u32[]{:S(2)}, u32[]{:S(2)}) %collective-permute-start.36) | collective-permute-done | bytes 258080 | tf_op jit(solution)/shard_map/ppermute | solution.py:887
  318.0 5.7 %collective-permute-done.37 = bf16[2,2,96,768]{3,2,1,0:T(8,128)(2,1)S(1)} collective-permute-done((bf16[2,2,96,768]{3,2,1,0:T(8,128)(2,1)S(1)}, bf16[2,2,96,768]{3,2,1,0:T(8,128)(2,1)S(1)}, u32[]{:S(2)}, u32[]{:S(2)}) %collective-permute-start.37) | collective-permute-done | bytes 589856 | tf_op jit(solution)/shard_map/ppermute | solution.py:887
  324.0 1.1 maximum_convert_fusion
  325.2 1.1 maximum_convert_fusion.1
  (196 shorter events, 17.1 us)
Async XLA Ops:
  2.9 6.1 %copy-start.31 = (bf16[384]{0:T(512)(128)(2,1)S(1)}, bf16[384]{0:T(512)(128)(2,1)}, u32[]{:S(2)}) copy-start(bf16[384]{0:T(512)(128)(2,1)} %param.26) | copy-start | bytes 2308
  2.9 6.1 %copy-start.24 = (bf16[768]{0:T(1024)(128)(2,1)S(1)}, bf16[768]{0:T(1024)(128)(2,1)}, u32[]{:S(2)}) copy-start(bf16[768]{0:T(1024)(128)(2,1)} %param.25) | copy-start | bytes 4612
  2.9 7.5 %copy-start.25 = (bf16[768]{0:T(1024)(128)(2,1)S(1)}, bf16[768]{0:T(1024)(128)(2,1)}, u32[]{:S(2)}) copy-start(bf16[768]{0:T(1024)(128)(2,1)} %param.22) | copy-start | bytes 4612
  2.9 7.5 %copy-start.26 = (bf16[768]{0:T(1024)(128)(2,1)S(1)}, bf16[768]{0:T(1024)(128)(2,1)}, u32[]{:S(2)}) copy-start(bf16[768]{0:T(1024)(128)(2,1)} %param.23) | copy-start | bytes 4612
  2.9 7.5 %copy-start.27 = (bf16[768]{0:T(1024)(128)(2,1)S(1)}, bf16[768]{0:T(1024)(128)(2,1)}, u32[]{:S(2)}) copy-start(bf16[768]{0:T(1024)(128)(2,1)} %param.28) | copy-start | bytes 4612
  3.0 7.5 %copy-start.28 = (bf16[768]{0:T(1024)(128)(2,1)S(1)}, bf16[768]{0:T(1024)(128)(2,1)}, u32[]{:S(2)}) copy-start(bf16[768]{0:T(1024)(128)(2,1)} %param.29) | copy-start | bytes 4612
  3.0 7.5 %copy-start.29 = (bf16[768]{0:T(1024)(128)(2,1)S(1)}, bf16[768]{0:T(1024)(128)(2,1)}, u32[]{:S(2)}) copy-start(bf16[768]{0:T(1024)(128)(2,1)} %param.30) | copy-start | bytes 4612
  3.0 7.5 %copy-start.30 = (bf16[768]{0:T(1024)(128)(2,1)S(1)}, bf16[768]{0:T(1024)(128)(2,1)}, u32[]{:S(2)}) copy-start(bf16[768]{0:T(1024)(128)(2,1)} %param.34) | copy-start | bytes 4612
  3.0 8.2 %copy-start.22 = (bf16[3072]{0:T(1024)(128)(2,1)S(1)}, bf16[3072]{0:T(1024)(128)(2,1)}, u32[]{:S(2)}) copy-start(bf16[3072]{0:T(1024)(128)(2,1)} %param.32) | copy-start | bytes 18436
  3.0 17.2 %collective-permute-start.2 = (bf16[272,768]{1,0:T(8,128)(2,1)S(1)}, bf16[272,768]{1,0:T(8,128)(2,1)S(1)}, u32[]{:S(2)}, u32[]{:S(2)}) collective-permute-start(bf16[272,768]{1,0:T(8,128)(2,1)S(1)} %pad_maximum_fusion.7), channel_id=1, source_target_pairs={{0,1},{1,0},{2,3},{3,2},{4,7},{5,6},{6,5},{7,4},{8,9},{9,8},{10,11... | collective-permute-start | bytes 1253384 | tf_op jit(solution)/shard_map/ppermute | solution.py:887
  6.2 22.0 %collective-permute-start.1 = (bf16[272,768]{1,0:T(8,128)(2,1)S(1)}, bf16[272,768]{1,0:T(8,128)(2,1)S(1)}, u32[]{:S(2)}, u32[]{:S(2)}) collective-permute-start(bf16[272,768]{1,0:T(8,128)(2,1)S(1)} %get-tuple-element.127), channel_id=1, source_target_pairs={{0,3},{1,2},{2,1},{3,0},{4,5},{5,4},{6,7},{7,6},{8,11},{9,10},{10,... | collective-permute-start | bytes 1253384 | tf_op jit(solution)/shard_map/ppermute | solution.py:887
  8.8 35.1 %collective-permute-start = (bf16[272,768]{1,0:T(8,128)(2,1)S(1)}, bf16[272,768]{1,0:T(8,128)(2,1)S(1)}, u32[]{:S(2)}, u32[]{:S(2)}) collective-permute-start(bf16[272,768]{1,0:T(8,128)(2,1)S(1)} %get-tuple-element.128), channel_id=1, source_target_pairs={{0,2},{1,3},{2,0},{3,1},{4,6},{5,7},{6,4},{7,5},{8,10},{9,11},{10,... | collective-permute-start | bytes 1253384 | tf_op jit(solution)/shard_map/ppermute | solution.py:887
  28.9 14.9 %copy-start.8 = (bf16[4,256,384]{2,1,0:T(8,128)(2,1)S(1)}, bf16[4,256,384]{2,1,0:T(8,128)(2,1)}, u32[]{:S(2)}) copy-start(bf16[4,256,384]{2,1,0:T(8,128)(2,1)} %param.19) | copy-start | bytes 2359300
  33.9 14.2 %copy-start.5 = (bf16[4,256,768]{2,1,0:T(8,128)(2,1)S(1)}, bf16[4,256,768]{2,1,0:T(8,128)(2,1)}, u32[]{:S(2)}) copy-start(bf16[4,256,768]{2,1,0:T(8,128)(2,1)} %param.35) | copy-start | bytes 4718596
  43.8 4.4 %copy-start.13 = (bf16[272,768]{1,0:T(8,128)(2,1)}, bf16[272,768]{1,0:T(8,128)(2,1)S(1)}, u32[]{:S(2)}) copy-start(bf16[272,768]{1,0:T(8,128)(2,1)S(1)} %collective-permute-done.x_ref) | copy-start | bytes 1253380
  44.6 25.4 %collective-permute-start.3 = (bf16[256,384]{1,0:T(8,128)(2,1)S(1)}, bf16[256,384]{1,0:T(8,128)(2,1)S(1)}, u32[]{:S(2)}, u32[]{:S(2)}) collective-permute-start(bf16[256,384]{1,0:T(8,128)(2,1)S(1)} %get-tuple-element.287), channel_id=1, source_target_pairs={{0,1},{1,0},{2,3},{3,2},{4,7},{5,6},{6,5},{7,4},{8,9},{9,8},{10,11... | collective-permute-start | bytes 589832 | tf_op jit(solution)/shard_map/ppermute | solution.py:887
  44.6 25.4 %collective-permute-start.4 = (bf16[256,384]{1,0:T(8,128)(2,1)S(1)}, bf16[256,384]{1,0:T(8,128)(2,1)S(1)}, u32[]{:S(2)}, u32[]{:S(2)}) collective-permute-start(bf16[256,384]{1,0:T(8,128)(2,1)S(1)} %get-tuple-element.286), channel_id=1, source_target_pairs={{0,3},{1,2},{2,1},{3,0},{4,5},{5,4},{6,7},{7,6},{8,11},{9,10},{10,... | collective-permute-start | bytes 589832 | tf_op jit(solution)/shard_map/ppermute | solution.py:887
  47.1 35.3 %collective-permute-start.5 = (bf16[256,384]{1,0:T(8,128)(2,1)S(1)}, bf16[256,384]{1,0:T(8,128)(2,1)S(1)}, u32[]{:S(2)}, u32[]{:S(2)}) collective-permute-start(bf16[256,384]{1,0:T(8,128)(2,1)S(1)} %get-tuple-element.285), channel_id=1, source_target_pairs={{0,2},{1,3},{2,0},{3,1},{4,6},{5,7},{6,4},{7,5},{8,10},{9,11},{10,... | collective-permute-start | bytes 589832 | tf_op jit(solution)/shard_map/ppermute | solution.py:887
  48.2 48.2 %collective-permute-start.7 = (bf16[256,768]{1,0:T(8,128)(2,1)S(1)}, bf16[256,768]{1,0:T(8,128)(2,1)S(1)}, u32[]{:S(2)}, u32[]{:S(2)}) collective-permute-start(bf16[256,768]{1,0:T(8,128)(2,1)S(1)} %get-tuple-element.255), channel_id=1, source_target_pairs={{0,2},{1,3},{2,0},{3,1},{4,6},{5,7},{6,4},{7,5},{8,10},{9,11},{10,... | collective-permute-start | bytes 1179656 | tf_op jit(solution)/shard_map/ppermute | solution.py:887
  50.2 46.2 %collective-permute-start.8 = (bf16[256,768]{1,0:T(8,128)(2,1)S(1)}, bf16[256,768]{1,0:T(8,128)(2,1)S(1)}, u32[]{:S(2)}, u32[]{:S(2)}) collective-permute-start(bf16[256,768]{1,0:T(8,128)(2,1)S(1)} %get-tuple-element.254), channel_id=1, source_target_pairs={{0,3},{1,2},{2,1},{3,0},{4,7},{5,6},{6,5},{7,4},{8,11},{9,10},{10,... | collective-permute-start | bytes 1179656 | tf_op jit(solution)/shard_map/ppermute | solution.py:887
  70.0 13.3 %copy-start.35 = (bf16[256,384]{1,0:T(8,128)(2,1)}, bf16[256,384]{1,0:T(8,128)(2,1)S(1)}, u32[]{:S(2)}) copy-start(bf16[256,384]{1,0:T(8,128)(2,1)S(1)} %collective-permute-done.3.refs_1_) | copy-start | bytes 589828
  70.0 13.2 %copy-start.36 = (bf16[256,384]{1,0:T(8,128)(2,1)}, bf16[256,384]{1,0:T(8,128)(2,1)S(1)}, u32[]{:S(2)}) copy-start(bf16[256,384]{1,0:T(8,128)(2,1)S(1)} %collective-permute-done.4.refs_2_) | copy-start | bytes 589828
  83.2 13.2 %collective-permute-start.6 = (bf16[256,768]{1,0:T(8,128)(2,1)S(1)}, bf16[256,768]{1,0:T(8,128)(2,1)S(1)}, u32[]{:S(2)}, u32[]{:S(2)}) collective-permute-start(bf16[256,768]{1,0:T(8,128)(2,1)S(1)} %get-tuple-element.256), channel_id=1, source_target_pairs={{0,1},{1,0},{2,3},{3,2},{4,5},{5,4},{6,7},{7,6},{8,9},{9,8},{10,11... | collective-permute-start | bytes 1179656 | tf_op jit(solution)/shard_map/ppermute | solution.py:887
  146.0 26.3 %collective-permute-start.9 = (bf16[4,384,768]{2,1,0:T(8,128)(2,1)}, bf16[4,384,768]{2,1,0:T(8,128)(2,1)S(1)}, u32[]{:S(2)}, u32[]{:S(2)}) collective-permute-start(bf16[4,384,768]{2,1,0:T(8,128)(2,1)} %get-tuple-element.171), channel_id=1, source_target_pairs={{0,4},{4,0},{8,12},{12,8},{16,20},{20,16},{24,28},{28,24},{1,5},{5... | collective-permute-start | bytes 7077896 | tf_op jit(solution)/shard_map/ppermute | solution.py:882
  146.1 26.2 %collective-permute-start.10 = (bf16[4,4,96,768]{3,2,1,0:T(8,128)(2,1)}, bf16[4,4,96,768]{3,2,1,0:T(8,128)(2,1)S(1)}, u32[]{:S(2)}, u32[]{:S(2)}) collective-permute-start(bf16[4,4,96,768]{3,2,1,0:T(8,128)(2,1)} %get-tuple-element.172), channel_id=1, source_target_pairs={{0,4},{4,0},{8,12},{12,8},{16,20},{20,16},{24,28},{28,24},{1,5},{5... | collective-permute-start | bytes 7077896 | tf_op jit(solution)/shard_map/ppermute | solution.py:882
  146.6 25.7 %collective-permute-start.11 = (bf16[2,256,768]{2,1,0:T(8,128)(2,1)}, bf16[2,256,768]{2,1,0:T(8,128)(2,1)S(1)}, u32[]{:S(2)}, u32[]{:S(2)}) collective-permute-start(bf16[2,256,768]{2,1,0:T(8,128)(2,1)} %get-tuple-element.173), channel_id=1, source_target_pairs={{0,1},{1,0},{2,3},{3,2},{4,7},{5,6},{6,5},{7,4},{8,9},{9,8},{10,11... | collective-permute-start | bytes 2359304 | tf_op jit(solution)/shard_map/ppermute | solution.py:887
  148.6 23.7 %collective-permute-start.12 = (bf16[4,6,96,128]{3,2,1,0:T(8,128)(2,1)}, bf16[4,6,96,128]{3,2,1,0:T(8,128)(2,1)}, u32[]{:S(2)}, u32[]{:S(2)}) collective-permute-start(bf16[4,6,96,128]{3,2,1,0:T(8,128)(2,1)} %get-tuple-element.174), channel_id=1, source_target_pairs={{0,4},{4,0},{8,12},{12,8},{16,20},{20,16},{24,28},{28,24},{1,5},{5... | collective-permute-start | bytes 1769480 | tf_op jit(solution)/shard_map/ppermute | solution.py:882
  148.6 24.6 %copy-start.2 = (bf16[4,384,768]{2,1,0:T(8,128)(2,1)S(1)}, bf16[4,384,768]{2,1,0:T(8,128)(2,1)}, u32[]{:S(2)}) copy-start(bf16[4,384,768]{2,1,0:T(8,128)(2,1)} %get-tuple-element.181) | copy-start | bytes 7077892
  173.2 1.7 copy-start.1
  177.6 30.8 %collective-permute-start.13 = (bf16[2,8,96,768]{3,2,1,0:T(8,128)(2,1)S(1)}, bf16[2,8,96,768]{3,2,1,0:T(8,128)(2,1)S(1)}, u32[]{:S(2)}, u32[]{:S(2)}) collective-permute-start(bf16[2,8,96,768]{3,2,1,0:T(8,128)(2,1)S(1)} %pad_maximum_fusion), channel_id=1, source_target_pairs={{0,8},{4,20},{8,0},{12,28},{16,24},{20,4},{24,16},{28,12},{1,9},{5... | collective-permute-start | bytes 7077896 | tf_op jit(solution)/shard_map/ppermute | solution.py:903
  179.1 29.2 %collective-permute-start.14 = (bf16[2,256,768]{2,1,0:T(8,128)(2,1)}, bf16[2,256,768]{2,1,0:T(8,128)(2,1)S(1)}, u32[]{:S(2)}, u32[]{:S(2)}) collective-permute-start(bf16[2,256,768]{2,1,0:T(8,128)(2,1)} %pad_maximum_fusion.2), channel_id=1, source_target_pairs={{0,3},{1,2},{2,1},{3,0},{4,5},{5,4},{6,7},{7,6},{8,11},{9,10},{10,... | collective-permute-start | bytes 2359304 | tf_op jit(solution)/shard_map/ppermute | solution.py:887
  180.8 27.5 %collective-permute-start.15 = (bf16[2,256,384]{2,1,0:T(8,128)(2,1)}, bf16[2,256,384]{2,1,0:T(8,128)(2,1)S(1)}, u32[]{:S(2)}, u32[]{:S(2)}) collective-permute-start(bf16[2,256,384]{2,1,0:T(8,128)(2,1)} %get-tuple-element.197), channel_id=1, source_target_pairs={{0,1},{1,0},{2,3},{3,2},{4,7},{5,6},{6,5},{7,4},{8,9},{9,8},{10,11... | collective-permute-start | bytes 1179656 | tf_op jit(solution)/shard_map/ppermute | solution.py:887
  181.0 27.4 %collective-permute-start.16 = (bf16[4,3,2,96,128]{4,3,2,1,0:T(8,128)(2,1)}, bf16[4,3,2,96,128]{4,3,2,1,0:T(8,128)(2,1)}, u32[]{:S(2)}, u32[]{:S(2)}) collective-permute-start(bf16[4,3,2,96,128]{4,3,2,1,0:T(8,128)(2,1)} %get-tuple-element.198), channel_id=1, source_target_pairs={{0,4},{4,0},{8,12},{12,8},{16,20},{20,16},{24,28},{28,24},{1,5},{5... | collective-permute-start | bytes 1769480 | tf_op jit(solution)/shard_map/ppermute | solution.py:882
  208.3 2.6 copy-start.6
  209.3 1.6 copy-start.19
  209.3 4.5 %copy-start.9 = (bf16[2,256,768]{2,1,0:T(8,128)(2,1)S(1)}, bf16[2,256,768]{2,1,0:T(8,128)(2,1)}, u32[]{:S(2)}) copy-start(bf16[2,256,768]{2,1,0:T(8,128)(2,1)} %get-tuple-element.223) | copy-start | bytes 2359300
  209.4 7.9 %copy-start.11 = (bf16[4,6,96,128]{3,2,1,0:T(8,128)(2,1)S(1)}, bf16[4,6,96,128]{3,2,1,0:T(8,128)(2,1)}, u32[]{:S(2)}) copy-start(bf16[4,6,96,128]{3,2,1,0:T(8,128)(2,1)} %get-tuple-element.213) | copy-start | bytes 1769476
  209.4 33.1 %collective-permute-start.17 = (bf16[8,96,768]{2,1,0:T(8,128)(2,1)S(1)}, bf16[8,96,768]{2,1,0:T(8,128)(2,1)S(1)}, u32[]{:S(2)}, u32[]{:S(2)}) collective-permute-start(bf16[8,96,768]{2,1,0:T(8,128)(2,1)S(1)} %slice_bitcast_fusion.1), channel_id=1, source_target_pairs={{0,16},{4,12},{8,24},{12,4},{16,0},{20,28},{24,8},{28,20},{1,17},{... | collective-permute-start | bytes 3538952 | tf_op jit(solution)/shard_map/ppermute | solution.py:903
  210.9 31.5 %collective-permute-start.18 = (bf16[4,3,3,96,128]{4,3,2,1,0:T(8,128)(2,1)}, bf16[4,3,3,96,128]{4,3,2,1,0:T(8,128)(2,1)S(1)}, u32[]{:S(2)}, u32[]{:S(2)}) collective-permute-start(bf16[4,3,3,96,128]{4,3,2,1,0:T(8,128)(2,1)} %get-tuple-element.200), channel_id=1, source_target_pairs={{0,4},{4,0},{8,12},{12,8},{16,20},{20,16},{24,28},{28,24},{1,5},{5... | collective-permute-start | bytes 2654216 | tf_op jit(solution)/shard_map/ppermute | solution.py:882
  211.7 14.2 %collective-permute-start.19 = (bf16[2,256,384]{2,1,0:T(8,128)(2,1)}, bf16[2,256,384]{2,1,0:T(8,128)(2,1)S(1)}, u32[]{:S(2)}, u32[]{:S(2)}) collective-permute-start(bf16[2,256,384]{2,1,0:T(8,128)(2,1)} %pad_maximum_fusion.9), channel_id=1, source_target_pairs={{0,3},{1,2},{2,1},{3,0},{4,5},{5,4},{6,7},{7,6},{8,11},{9,10},{10,... | collective-permute-start | bytes 1179656 | tf_op jit(solution)/shard_map/ppermute | solution.py:887
  214.5 20.7 %collective-permute-start.20 = (bf16[256,768]{1,0:T(8,128)(2,1)}, bf16[256,768]{1,0:T(8,128)(2,1)S(1)}, u32[]{:S(2)}, u32[]{:S(2)}) collective-permute-start(bf16[256,768]{1,0:T(8,128)(2,1)} %slice_bitcast_fusion.5), channel_id=1, source_target_pairs={{0,1},{1,0},{2,3},{3,2},{4,7},{5,6},{6,5},{7,4},{8,9},{9,8},{10,11... | collective-permute-start | bytes 1179656 | tf_op jit(solution)/shard_map/ppermute | solution.py:887
  215.6 26.8 %collective-permute-start.21 = (bf16[256,768]{1,0:T(8,128)(2,1)}, bf16[256,768]{1,0:T(8,128)(2,1)}, u32[]{:S(2)}, u32[]{:S(2)}) collective-permute-start(bf16[256,768]{1,0:T(8,128)(2,1)} %get-tuple-element.207), channel_id=1, source_target_pairs={{0,3},{1,2},{2,1},{3,0},{4,5},{5,4},{6,7},{7,6},{8,11},{9,10},{10,... | collective-permute-start | bytes 1179656 | tf_op jit(solution)/shard_map/ppermute | solution.py:887
  218.5 3.2 copy-start.12
  221.7 20.7 %copy-start.7 = (bf16[4,3,3,96,128]{4,3,2,1,0:T(8,128)(2,1)S(1)}, bf16[4,3,3,96,128]{4,3,2,1,0:T(8,128)(2,1)}, u32[]{:S(2)}) copy-start(bf16[4,3,3,96,128]{4,3,2,1,0:T(8,128)(2,1)} %get-tuple-element.217) | copy-start | bytes 2654212
  225.9 16.9 %copy-start.4 = (bf16[2,256,384]{2,1,0:T(8,128)(2,1)}, bf16[2,256,384]{2,1,0:T(8,128)(2,1)S(1)}, u32[]{:S(2)}) copy-start(bf16[2,256,384]{2,1,0:T(8,128)(2,1)S(1)} %collective-permute-done.19.refs_2_.refs_3_) | copy-start | bytes 1179652
  235.2 7.6 %copy-start.16 = (bf16[256,768]{1,0:T(8,128)(2,1)}, bf16[256,768]{1,0:T(8,128)(2,1)S(1)}, u32[]{:S(2)}) copy-start(bf16[256,768]{1,0:T(8,128)(2,1)S(1)} %collective-permute-done.20.refs_1_) | copy-start | bytes 1179652
  242.8 15.6 %collective-permute-start.22 = (bf16[2,21,96,128]{3,2,1,0:T(8,128)(2,1)S(1)}, bf16[2,21,96,128]{3,2,1,0:T(8,128)(2,1)S(1)}, u32[]{:S(2)}, u32[]{:S(2)}) collective-permute-start(bf16[2,21,96,128]{3,2,1,0:T(8,128)(2,1)S(1)} %pad_maximum_fusion.1), channel_id=1, source_target_pairs={{0,8},{4,20},{8,0},{12,28},{16,24},{20,4},{24,16},{28,12},{1,9},{5... | collective-permute-start | bytes 3096584 | tf_op jit(solution)/shard_map/ppermute | solution.py:903
  243.4 5.7 %collective-permute-start.23 = (f32[72,128]{1,0:T(8,128)S(1)}, f32[72,128]{1,0:T(8,128)S(1)}, u32[]{:S(2)}, u32[]{:S(2)}) collective-permute-start(f32[72,128]{1,0:T(8,128)S(1)} %copy-done.20), channel_id=1, source_target_pairs={{0,1},{1,0},{2,3},{3,2},{4,5},{5,4},{6,7},{7,6},{8,9},{9,8},{10,11... | collective-permute-start | bytes 110600 | tf_op jit(solution)/shard_map/ppermute | solution.py:887
  243.9 33.3 %collective-permute-start.25 = (bf16[2,2,96,768]{3,2,1,0:T(8,128)(2,1)S(1)}, bf16[2,2,96,768]{3,2,1,0:T(8,128)(2,1)S(1)}, u32[]{:S(2)}, u32[]{:S(2)}) collective-permute-start(bf16[2,2,96,768]{3,2,1,0:T(8,128)(2,1)S(1)} %pad_maximum_fusion.3), channel_id=1, source_target_pairs={{0,1},{1,0},{2,3},{3,2},{4,7},{5,6},{6,5},{7,4},{8,9},{9,8},{10,11... | collective-permute-start | bytes 1769480 | tf_op jit(solution)/shard_map/ppermute | solution.py:887
  258.7 18.5 %collective-permute-start.24 = (bf16[21,96,128]{2,1,0:T(8,128)(2,1)S(1)}, bf16[21,96,128]{2,1,0:T(8,128)(2,1)S(1)}, u32[]{:S(2)}, u32[]{:S(2)}) collective-permute-start(bf16[21,96,128]{2,1,0:T(8,128)(2,1)S(1)} %slice_bitcast_fusion.3), channel_id=1, source_target_pairs={{0,16},{4,12},{8,24},{12,4},{16,0},{20,28},{24,8},{28,20},{1,17},{... | collective-permute-start | bytes 1548296 | tf_op jit(solution)/shard_map/ppermute | solution.py:903
  259.6 17.6 %collective-permute-start.26 = (bf16[256,768]{1,0:T(8,128)(2,1)S(1)}, bf16[256,768]{1,0:T(8,128)(2,1)S(1)}, u32[]{:S(2)}, u32[]{:S(2)}) collective-permute-start(bf16[256,768]{1,0:T(8,128)(2,1)S(1)} %slice_bitcast_fusion.4), channel_id=1, source_target_pairs={{0,2},{1,3},{2,0},{3,1},{4,6},{5,7},{6,4},{7,5},{8,10},{9,11},{10,... | collective-permute-start | bytes 1179656 | tf_op jit(solution)/shard_map/ppermute | solution.py:887
  259.8 17.4 %collective-permute-start.27 = (f32[72,128]{1,0:T(8,128)S(1)}, f32[72,128]{1,0:T(8,128)S(1)}, u32[]{:S(2)}, u32[]{:S(2)}) collective-permute-start(f32[72,128]{1,0:T(8,128)S(1)} %add.147), channel_id=1, source_target_pairs={{0,3},{1,2},{2,1},{3,0},{4,7},{5,6},{6,5},{7,4},{8,11},{9,10},{10,... | collective-permute-start | bytes 110600 | tf_op jit(solution)/shard_map/ppermute | solution.py:887
  277.5 12.0 %collective-permute-start.30 = (bf16[2,21,24,128]{3,2,1,0:T(8,128)(2,1)S(1)}, bf16[2,21,24,128]{3,2,1,0:T(8,128)(2,1)S(1)}, u32[]{:S(2)}, u32[]{:S(2)}) collective-permute-start(bf16[2,21,24,128]{3,2,1,0:T(8,128)(2,1)S(1)} %pad_maximum_fusion.10), channel_id=1, source_target_pairs={{0,1},{1,0},{2,3},{3,2},{4,7},{5,6},{6,5},{7,4},{8,9},{9,8},{10,11... | collective-permute-start | bytes 774152 | tf_op jit(solution)/shard_map/ppermute | solution.py:887
  278.7 16.6 %collective-permute-start.28 = (f32[72,128]{1,0:T(8,128)S(1)}, f32[72,128]{1,0:T(8,128)S(1)}, u32[]{:S(2)}, u32[]{:S(2)}) collective-permute-start(f32[72,128]{1,0:T(8,128)S(1)} %add.149), channel_id=1, source_target_pairs={{0,4},{4,0},{8,12},{12,8},{16,20},{20,16},{24,28},{28,24},{1,5},{5... | collective-permute-start | bytes 110600 | tf_op jit(solution)/shard_map/ppermute | solution.py:882
  278.8 15.0 %collective-permute-start.29 = (bf16[2,96,768]{2,1,0:T(8,128)(2,1)S(1)}, bf16[2,96,768]{2,1,0:T(8,128)(2,1)S(1)}, u32[]{:S(2)}, u32[]{:S(2)}) collective-permute-start(bf16[2,96,768]{2,1,0:T(8,128)(2,1)S(1)} %slice_bitcast_fusion.9), channel_id=1, source_target_pairs={{0,3},{1,2},{2,1},{3,0},{4,5},{5,4},{6,7},{7,6},{8,11},{9,10},{10,... | collective-permute-start | bytes 884744 | tf_op jit(solution)/shard_map/ppermute | solution.py:887
  289.5 8.3 %collective-permute-start.32 = (bf16[21,24,128]{2,1,0:T(8,128)(2,1)S(1)}, bf16[21,24,128]{2,1,0:T(8,128)(2,1)S(1)}, u32[]{:S(2)}, u32[]{:S(2)}) collective-permute-start(bf16[21,24,128]{2,1,0:T(8,128)(2,1)S(1)} %slice_bitcast_fusion.21), channel_id=1, source_target_pairs={{0,3},{1,2},{2,1},{3,0},{4,5},{5,4},{6,7},{7,6},{8,11},{9,10},{10,... | collective-permute-start | bytes 387080 | tf_op jit(solution)/shard_map/ppermute | solution.py:887
  293.9 10.0 %collective-permute-start.35 = (bf16[2,96,768]{2,1,0:T(8,128)(2,1)S(1)}, bf16[2,96,768]{2,1,0:T(8,128)(2,1)S(1)}, u32[]{:S(2)}, u32[]{:S(2)}) collective-permute-start(bf16[2,96,768]{2,1,0:T(8,128)(2,1)S(1)} %fusion.2), channel_id=1, source_target_pairs={{0,3},{1,2},{2,1},{3,0},{4,5},{5,4},{6,7},{7,6},{8,11},{9,10},{10,... | collective-permute-start | bytes 884744 | tf_op jit(solution)/shard_map/ppermute | solution.py:887
  295.2 4.0 %collective-permute-start.31 = (f32[72,128]{1,0:T(8,128)S(1)}, f32[72,128]{1,0:T(8,128)S(1)}, u32[]{:S(2)}, u32[]{:S(2)}) collective-permute-start(f32[72,128]{1,0:T(8,128)S(1)} %add.153), channel_id=1, source_target_pairs={{0,8},{4,12},{8,0},{12,4},{16,24},{20,28},{24,16},{28,20},{1,9},{5... | collective-permute-start | bytes 110600 | tf_op jit(solution)/shard_map/ppermute | solution.py:903
  299.3 4.0 %collective-permute-start.33 = (f32[72,128]{1,0:T(8,128)S(1)}, f32[72,128]{1,0:T(8,128)S(1)}, u32[]{:S(2)}, u32[]{:S(2)}) collective-permute-start(f32[72,128]{1,0:T(8,128)S(1)} %add.155), channel_id=1, source_target_pairs={{0,16},{4,20},{8,24},{12,28},{16,0},{20,4},{24,8},{28,12},{1,17},{... | collective-permute-start | bytes 110600 | tf_op jit(solution)/shard_map/ppermute | solution.py:903
  300.0 8.2 %collective-permute-start.34 = (bf16[21,24,128]{2,1,0:T(8,128)(2,1)S(1)}, bf16[21,24,128]{2,1,0:T(8,128)(2,1)S(1)}, u32[]{:S(2)}, u32[]{:S(2)}) collective-permute-start(bf16[21,24,128]{2,1,0:T(8,128)(2,1)S(1)} %fusion.3), channel_id=1, source_target_pairs={{0,3},{1,2},{2,1},{3,0},{4,5},{5,4},{6,7},{7,6},{8,11},{9,10},{10,... | collective-permute-start | bytes 387080 | tf_op jit(solution)/shard_map/ppermute | solution.py:887
  308.3 9.1 %collective-permute-start.36 = (bf16[2,21,24,128]{3,2,1,0:T(8,128)(2,1)S(1)}, bf16[2,21,24,128]{3,2,1,0:T(8,128)(2,1)S(1)}, u32[]{:S(2)}, u32[]{:S(2)}) collective-permute-start(bf16[2,21,24,128]{3,2,1,0:T(8,128)(2,1)S(1)} %pad_maximum_fusion.11), channel_id=1, source_target_pairs={{0,1},{1,0},{2,3},{3,2},{4,7},{5,6},{6,5},{7,4},{8,9},{9,8},{10,11... | collective-permute-start | bytes 774152 | tf_op jit(solution)/shard_map/ppermute | solution.py:887
  309.6 14.2 %collective-permute-start.37 = (bf16[2,2,96,768]{3,2,1,0:T(8,128)(2,1)S(1)}, bf16[2,2,96,768]{3,2,1,0:T(8,128)(2,1)S(1)}, u32[]{:S(2)}, u32[]{:S(2)}) collective-permute-start(bf16[2,2,96,768]{3,2,1,0:T(8,128)(2,1)S(1)} %pad_maximum_fusion.4), channel_id=1, source_target_pairs={{0,1},{1,0},{2,3},{3,2},{4,7},{5,6},{6,5},{7,4},{8,9},{9,8},{10,11... | collective-permute-start | bytes 1769480 | tf_op jit(solution)/shard_map/ppermute | solution.py:887
  318.0 5.9 %copy-start.21 = (f32[96,768]{1,0:T(8,128)}, f32[96,768]{1,0:T(8,128)S(1)}, u32[]{:S(2)}) copy-start(f32[96,768]{1,0:T(8,128)S(1)} %get-tuple-element.273) | copy-start | bytes 884740
  318.0 5.9 %copy-start.23 = (f32[96,1920]{1,0:T(8,128)}, f32[96,1920]{1,0:T(8,128)S(1)}, u32[]{:S(2)}) copy-start(f32[96,1920]{1,0:T(8,128)S(1)} %get-tuple-element.274) | copy-start | bytes 2211844
  (13 other events, 12.3 us)

commit v7 on v5

--- a/solution.py
+++ b/solution.py
@@ -16,7 +16,7 @@
 BF16 = jnp.bfloat16
 F32 = jnp.float32
 VMEM_BYTES = 56 << 20
-CODE_ROWS = 16
+CODE_ROWS = 8
 GAIN_ROWS, Q_ROWS, V_ROWS, SUM_ROWS = 6, 12, 18, 72
 ATTN_GAIN, ATTN_SHIFT, OUT_BIAS, MLP_GAIN, MLP_SHIFT, DOWN_BIAS = (slice(n, n + 1) for n in range(6))
 

time: 329 us -> 327 us (level)
  no operation moved by 1% of the time
where the time goes in v7:
time: 327 us; the launch traced here: 322 us
  Pallas kernels  153 us (47%)
  waiting for transfers between devices  99.1 us (30%)
  starting transfers between devices  41.7 us (13%)
  other arithmetic  14.7 us (4%)
  local copies, waits for them, and re-layouts  12.2 us (4%)
    ppermute x26, waiting for transfers between devices, group_swap(): return lax.ppermute(array, ('seq', 'head'), pairs)  87.8 us
    pallas_call x1, Pallas kernels, feed(): call(feed_kernel, 'feed', (4,), [full, once(o_a.shape), once(o_b.shape)]...  48.5 us
    pallas_call x2, Pallas kernels, attend_back(): call(functools.partial(backward_kernel, len(values), before is None, last...  47.8 us
    ppermute x26, starting transfers between devices, group_swap(): return lax.ppermute(array, ('seq', 'head'), pairs)  35.1 us
    pallas_call x2, Pallas kernels, attend(): call(functools.partial(forward_kernel, len(values)), name, (pairs,), [who...  26.8 us
    pallas_call x4, Pallas kernels, project(): call(project_kernel, 'project', (1,), [whole((part + CODE_ROWS, width)),...  19.5 us
    ppermute x6, waiting for transfers between devices, plane_swap(): lax.ppermute(array, 'seq', [(s, s ^ (core_one if s & 1 else core_zero)) f...  11.2 us
    pallas_call x3, Pallas kernels, settle(): call(settle_kernel, name, (2,), specs, pl.BlockSpec((4, rows, width), lam...  10 us
  transfers between devices with their start and end apart: 38, of which 17 were waited for; matrix products, arithmetic and copies ran while one was open for 4% of the time, Pallas kernels for 32%

profile of v7, /device:TPU:0, one launch (start us, length us, event | category | flops | bytes accessed | tf_op | source)
XLA Modules:
  0.0 322.3 jit_solution(6424230995817988026)
XLA Ops:
  1.4 1.5 dynamic-slice_bitcast_fusion.4
  3.0 3.1 collective-permute-start.2
  6.2 2.5 collective-permute-start.1
  9.0 0.8 pad_maximum_fusion.8.x_ref
  12.4 4.8 %project.4 = (bf16[1024,768]{1,0:T(8,128)(2,1)}, bf16[1024,768]{1,0:T(8,128)(2,1)}, bf16[1024,1920]{1,0:T(8,128)(2,1)}, s32[8,1024]{1,0:T(8,128)}) custom-call(s32[3]{0:T(128)} %pad_add_fusion.at_ref.me_ref, bf16[264,768]{1,0:T(8,128)(2,1)} %pad_maximum_fusion.8.x_ref, f32[8,768]{1,0:T(8,128)} %convert_element_type.233.vec_ref.refs_10_, ...), custom_call_target="tpu_custom_call" | custom-call | flops 754974720 | bytes 5111808 | tf_op jit(solution)/shard_map/project/pallas_call | solution.py:140
  17.2 2.5 collective-permute-done.2.x_ref
  20.5 4.9 %project.5 = (bf16[1024,768]{1,0:T(8,128)(2,1)}, bf16[1024,768]{1,0:T(8,128)(2,1)}, bf16[1024,1920]{1,0:T(8,128)(2,1)}, s32[8,1024]{1,0:T(8,128)}) custom-call(s32[3]{0:T(128)} %pad_add_fusion.at_ref.me_ref, bf16[264,768]{1,0:T(8,128)(2,1)} %copy-done.14, ...), custom_call_target="tpu_custom_call", output_to_operand_aliasing={{0}: (5, {}), {1}: (6, {}), {2}: (7, {}), {3}: (8, {})} | custom-call | flops 754974720 | bytes 5111808 | tf_op jit(solution)/shard_map/project/pallas_call | solution.py:140
  25.3 2.3 collective-permute-done.1.x_ref
  28.4 5.0 %project.6 = (bf16[1024,768]{1,0:T(8,128)(2,1)}, bf16[1024,768]{1,0:T(8,128)(2,1)}, bf16[1024,1920]{1,0:T(8,128)(2,1)}, s32[8,1024]{1,0:T(8,128)}) custom-call(s32[3]{0:T(128)} %pad_add_fusion.at_ref.me_ref, bf16[264,768]{1,0:T(8,128)(2,1)} %copy-done.15, ...), custom_call_target="tpu_custom_call", output_to_operand_aliasing={{0}: (5, {}), {1}: (6, {}), {2}: (7, {}), {3}: (8, {})} | custom-call | flops 754974720 | bytes 5111808 | tf_op jit(solution)/shard_map/project/pallas_call | solution.py:140
  33.4 9.4 %collective-permute-done.x_ref = bf16[264,768]{1,0:T(8,128)(2,1)S(1)} collective-permute-done((bf16[264,768]{1,0:T(8,128)(2,1)S(1)}, bf16[264,768]{1,0:T(8,128)(2,1)S(1)}, u32[]{:S(2)}, u32[]{:S(2)}) %collective-permute-start) | collective-permute-done | bytes 405536 | tf_op jit(solution)/shard_map/ppermute | solution.py:875
  42.8 0.8 dynamic-slice_bitcast_fusion.12
  43.6 2.5 collective-permute-start.4
  46.1 1.0 collective-permute-start.5
  47.1 2.0 collective-permute-start.7
  49.1 1.3 collective-permute-start.8
  50.5 4.8 %project.7 = (bf16[1024,768]{1,0:T(8,128)(2,1)}, bf16[1024,768]{1,0:T(8,128)(2,1)}, bf16[1024,1920]{1,0:T(8,128)(2,1)}, s32[8,1024]{1,0:T(8,128)}) custom-call(s32[3]{0:T(128)} %pad_add_fusion.at_ref.me_ref, bf16[264,768]{1,0:T(8,128)(2,1)} %copy-done.13, ...), custom_call_target="tpu_custom_call", output_to_operand_aliasing={{0}: (5, {}), {1}: (6, {}), {2}: (7, {}), {3}: (8, {})} | custom-call | flops 754974720 | bytes 5111808 | tf_op jit(solution)/shard_map/project/pallas_call | solution.py:140
  55.3 13.6 %attend_a.1 = (bf16[1024,384]{1,0:T(8,128)(2,1)}, f32[1024,384]{1,0:T(8,128)}) custom-call(s32[3]{0:T(128)} %pad_add_fusion.at_ref.me_ref, s32[8,1024]{1,0:T(8,128)} %get-tuple-element.146.code_ref, bf16[1024,1920]{1,0:T(8,128)(2,1)} %get-tuple-element.147.q_ref.k_ref.refs_0_, bf16[1024,1920]{1,0:T(8,128)(2,1)} %get-tuple-element.147.q_ref.k_ref.refs_0_, ...), custom_call_target="tpu_custom_call" | custom-call | flops 9663676416 | bytes 4718592 | tf_op jit(solution)/shard_map/attend_a/pallas_call | solution.py:326
  69.0 12.4 %collective-permute-done.5.refs_3_ = bf16[256,384]{1,0:T(8,128)(2,1)S(1)} collective-permute-done((bf16[256,384]{1,0:T(8,128)(2,1)S(1)}, bf16[256,384]{1,0:T(8,128)(2,1)S(1)}, u32[]{:S(2)}, u32[]{:S(2)}) %collective-permute-start.5) | collective-permute-done | bytes 196640 | tf_op jit(solution)/shard_map/ppermute | solution.py:875
  81.4 0.8 dynamic-slice_bitcast_fusion.2
  82.2 13.1 %attend_b.1 = (bf16[1024,384]{1,0:T(8,128)(2,1)}, f32[1024,384]{1,0:T(8,128)}) custom-call(s32[3]{0:T(128)} %pad_add_fusion.at_ref.me_ref, s32[8,1024]{1,0:T(8,128)} %get-tuple-element.146.code_ref, bf16[1024,1920]{1,0:T(8,128)(2,1)} %get-tuple-element.147.q_ref.k_ref.refs_0_, bf16[1024,1920]{1,0:T(8,128)(2,1)} %get-tuple-element.147.q_ref.k_ref.refs_0_, ...), custom_call_target="tpu_custom_call" | custom-call | flops 9663676416 | bytes 4718592 | tf_op jit(solution)/shard_map/attend_b/pallas_call | solution.py:326
  96.4 48.5 %feed.1 = (bf16[256,768]{1,0:T(8,128)(2,1)}, bf16[2,256,768]{2,1,0:T(8,128)(2,1)}, bf16[256,768]{1,0:T(8,128)(2,1)}, bf16[4,384,768]{2,1,0:T(8,128)(2,1)}, bf16[...) custom-call(s32[3]{0:T(128)} %pad_add_fusion.at_ref.me_ref, ...), custom_call_target="tpu_custom_call" | custom-call | flops 32614907904 | bytes 33423360 | tf_op jit(solution)/shard_map/feed/pallas_call | solution.py:503
  145.5 2.0 collective-permute-start.11
  147.5 20.6 %attend_back_b.1 = (bf16[4,3,2,96,128]{4,3,2,1,0:T(8,128)(2,1)}, bf16[4,3,2,96,128]{4,3,2,1,0:T(8,128)(2,1)}, f32[3,1,256]{2,1,0:T(1,128)}, bf16[256,384]{1,0:T(...) custom-call(s32[3]{0:T(128)} %pad_add_fusion.at_ref.me_ref, ...), custom_call_target="tpu_custom_call" | custom-call | flops 14495514624 | bytes 16515072 | tf_op jit(solution)/shard_map/attend_back_b/pallas_call | solution.py:379
  168.2 0.9 copy-done.3
  169.6 1.1 copy-done.1
  172.5 1.0 pad_maximum_fusion.2
  173.5 1.5 collective-permute-start.13
  174.9 1.7 collective-permute-start.14
  176.8 27.3 %attend_back_a.1 = (bf16[4,3,3,96,128]{4,3,2,1,0:T(8,128)(2,1)}, bf16[4,3,3,96,128]{4,3,2,1,0:T(8,128)(2,1)}, bf16[256,768]{1,0:T(8,128)(2,1)}, bf16[2,256,768]{...) custom-call(s32[3]{0:T(128)} %pad_add_fusion.at_ref.me_ref, s32[8,1024]{1,0:T(8,128)} %get-tuple-element.146.code_ref, ...), custom_call_target="tpu_custom_call" | custom-call | flops 15703474176 | bytes 16515072 | tf_op jit(solution)/shard_map/attend_back_a/pallas_call | solution.py:379
  205.1 1.5 collective-permute-start.17
  206.7 0.8 pad_maximum_fusion.9
  207.5 2.0 collective-permute-start.19
  209.5 0.8 slice_bitcast_fusion.5
  210.3 1.1 collective-permute-start.20
  211.4 1.7 collective-permute-start.21
  213.1 1.2 add_convert_fusion.10
  214.3 3.2 %settle_out.1 = bf16[4,256,768]{2,1,0:T(8,128)(2,1)} custom-call(s32[3]{0:T(128)} %pad_add_fusion.at_ref.me_ref, bf16[256,768]{1,0:T(8,128)(2,1)} %get-tuple-element.203.refs_0_, bf16[2,256,768]{2,1,0:T(8,128)(2,1)} %copy-done.3, bf16[2,256,768]{2,1,0:T(8,128)(2,1)} %copy-done, bf16[2,256,768]{2,1,0:T(8,128)(2,1)} %copy-done), custom_call_target="tpu_custom_call" | custom-call | bytes 4718592 | tf_op jit(solution)/shard_map/settle_out/pallas_call | solution.py:544
  217.5 1.3 add_convert_fusion.9
  218.8 2.8 collective-permute-done.19.refs_2_.refs_3_
  221.7 9.4 %collective-permute-done.20.refs_1_ = bf16[256,768]{1,0:T(8,128)(2,1)S(1)} collective-permute-done((bf16[256,768]{1,0:T(8,128)(2,1)}, bf16[256,768]{1,0:T(8,128)(2,1)S(1)}, u32[]{:S(2)}, u32[]{:S(2)}) %collective-permute-start.20) | collective-permute-done | bytes 393248 | tf_op jit(solution)/shard_map/ppermute | solution.py:875
  231.0 7.2 %collective-permute-done.21.refs_2_ = bf16[256,768]{1,0:T(8,128)(2,1)} collective-permute-done((bf16[256,768]{1,0:T(8,128)(2,1)}, bf16[256,768]{1,0:T(8,128)(2,1)}, u32[]{:S(2)}, u32[]{:S(2)}) %collective-permute-start.21) | collective-permute-done | bytes 393248 | tf_op jit(solution)/shard_map/ppermute | solution.py:875
  239.8 2.0 collective-permute-start.25
  241.8 3.1 settle_skip.1
  244.9 9.2 %collective-permute-done.22 = bf16[2,21,96,128]{3,2,1,0:T(8,128)(2,1)S(1)} collective-permute-done((bf16[2,21,96,128]{3,2,1,0:T(8,128)(2,1)S(1)}, bf16[2,21,96,128]{3,2,1,0:T(8,128)(2,1)S(1)}, u32[]{:S(2)}, u32[]{:S(2)}) %collective-permute-start.22) | collective-permute-done | bytes 1032224 | tf_op jit(solution)/shard_map/ppermute | solution.py:891
  254.5 0.8 collective-permute-start.24
  255.6 1.3 collective-permute-start.27
  256.9 16.1 %collective-permute-done.26.refs_3_ = bf16[256,768]{1,0:T(8,128)(2,1)S(1)} collective-permute-done((bf16[256,768]{1,0:T(8,128)(2,1)S(1)}, bf16[256,768]{1,0:T(8,128)(2,1)S(1)}, u32[]{:S(2)}, u32[]{:S(2)}) %collective-permute-start.26) | collective-permute-done | bytes 393248 | tf_op jit(solution)/shard_map/ppermute | solution.py:875
  273.3 1.0 collective-permute-start.30
  274.6 1.9 collective-permute-start.29
  276.5 3.7 %settle_tokens.1 = f32[4,256,768]{2,1,0:T(8,128)} custom-call(s32[3]{0:T(128)} %pad_add_fusion.at_ref.me_ref, bf16[256,768]{1,0:T(8,128)(2,1)} %get-tuple-element.209.refs_0_, bf16[256,768]{1,0:T(8,128)(2,1)} %copy-done.16, bf16[256,768]{1,0:T(8,128)(2,1)} %collective-permute-done.21.refs_2_, bf16[256,768]{1,0:T(8,128)(2,1)} %copy-done.17), custom_call_target="tpu_custom_call" | custom-call | bytes 4718592 | tf_op jit(solution)/shard_map/settle_tokens/pallas_call | solution.py:544
  280.2 5.0 %collective-permute-done.30 = bf16[2,21,24,128]{3,2,1,0:T(8,128)(2,1)S(1)} collective-permute-done((bf16[2,21,24,128]{3,2,1,0:T(8,128)(2,1)S(1)}, bf16[2,21,24,128]{3,2,1,0:T(8,128)(2,1)S(1)}, u32[]{:S(2)}, u32[]{:S(2)}) %collective-permute-start.30) | collective-permute-done | bytes 258080 | tf_op jit(solution)/shard_map/ppermute | solution.py:875
  285.3 1.2 collective-permute-start.32
  286.5 3.1 collective-permute-done.29
  289.7 1.4 collective-permute-start.35
  291.8 1.8 collective-permute-done.32
  293.6 1.5 collective-permute-done.31
  295.1 0.8 collective-permute-start.33
  295.9 2.7 collective-permute-start.34
  299.7 4.4 %collective-permute-done.34 = bf16[21,24,128]{2,1,0:T(8,128)(2,1)S(1)} collective-permute-done((bf16[21,24,128]{2,1,0:T(8,128)(2,1)S(1)}, bf16[21,24,128]{2,1,0:T(8,128)(2,1)S(1)}, u32[]{:S(2)}, u32[]{:S(2)}) %collective-permute-start.34) | collective-permute-done | bytes 129056 | tf_op jit(solution)/shard_map/ppermute | solution.py:875
  305.4 2.0 collective-permute-start.37
  307.4 5.7 %collective-permute-done.36 = bf16[2,21,24,128]{3,2,1,0:T(8,128)(2,1)S(1)} collective-permute-done((bf16[2,21,24,128]{3,2,1,0:T(8,128)(2,1)S(1)}, bf16[2,21,24,128]{3,2,1,0:T(8,128)(2,1)S(1)}, u32[]{:S(2)}, u32[]{:S(2)}) %collective-permute-start.36) | collective-permute-done | bytes 258080 | tf_op jit(solution)/shard_map/ppermute | solution.py:875
  313.8 5.7 %collective-permute-done.37 = bf16[2,2,96,768]{3,2,1,0:T(8,128)(2,1)S(1)} collective-permute-done((bf16[2,2,96,768]{3,2,1,0:T(8,128)(2,1)S(1)}, bf16[2,2,96,768]{3,2,1,0:T(8,128)(2,1)S(1)}, u32[]{:S(2)}, u32[]{:S(2)}) %collective-permute-start.37) | collective-permute-done | bytes 589856 | tf_op jit(solution)/shard_map/ppermute | solution.py:875
  319.8 1.1 maximum_convert_fusion
  320.9 1.1 maximum_convert_fusion.1
  (196 shorter events, 17.1 us)
Async XLA Ops:
  2.9 6.1 %copy-start.31 = (bf16[384]{0:T(512)(128)(2,1)S(1)}, bf16[384]{0:T(512)(128)(2,1)}, u32[]{:S(2)}) copy-start(bf16[384]{0:T(512)(128)(2,1)} %param.26) | copy-start | bytes 2308
  2.9 6.1 %copy-start.24 = (bf16[768]{0:T(1024)(128)(2,1)S(1)}, bf16[768]{0:T(1024)(128)(2,1)}, u32[]{:S(2)}) copy-start(bf16[768]{0:T(1024)(128)(2,1)} %param.25) | copy-start | bytes 4612
  2.9 7.5 %copy-start.25 = (bf16[768]{0:T(1024)(128)(2,1)S(1)}, bf16[768]{0:T(1024)(128)(2,1)}, u32[]{:S(2)}) copy-start(bf16[768]{0:T(1024)(128)(2,1)} %param.22) | copy-start | bytes 4612
  2.9 7.5 %copy-start.26 = (bf16[768]{0:T(1024)(128)(2,1)S(1)}, bf16[768]{0:T(1024)(128)(2,1)}, u32[]{:S(2)}) copy-start(bf16[768]{0:T(1024)(128)(2,1)} %param.23) | copy-start | bytes 4612
  2.9 7.5 %copy-start.27 = (bf16[768]{0:T(1024)(128)(2,1)S(1)}, bf16[768]{0:T(1024)(128)(2,1)}, u32[]{:S(2)}) copy-start(bf16[768]{0:T(1024)(128)(2,1)} %param.28) | copy-start | bytes 4612
  3.0 7.5 %copy-start.28 = (bf16[768]{0:T(1024)(128)(2,1)S(1)}, bf16[768]{0:T(1024)(128)(2,1)}, u32[]{:S(2)}) copy-start(bf16[768]{0:T(1024)(128)(2,1)} %param.29) | copy-start | bytes 4612
  3.0 7.5 %copy-start.29 = (bf16[768]{0:T(1024)(128)(2,1)S(1)}, bf16[768]{0:T(1024)(128)(2,1)}, u32[]{:S(2)}) copy-start(bf16[768]{0:T(1024)(128)(2,1)} %param.30) | copy-start | bytes 4612
  3.0 7.5 %copy-start.30 = (bf16[768]{0:T(1024)(128)(2,1)S(1)}, bf16[768]{0:T(1024)(128)(2,1)}, u32[]{:S(2)}) copy-start(bf16[768]{0:T(1024)(128)(2,1)} %param.34) | copy-start | bytes 4612
  3.0 8.2 %copy-start.22 = (bf16[3072]{0:T(1024)(128)(2,1)S(1)}, bf16[3072]{0:T(1024)(128)(2,1)}, u32[]{:S(2)}) copy-start(bf16[3072]{0:T(1024)(128)(2,1)} %param.32) | copy-start | bytes 18436
  3.0 16.7 %collective-permute-start.2 = (bf16[264,768]{1,0:T(8,128)(2,1)S(1)}, bf16[264,768]{1,0:T(8,128)(2,1)S(1)}, u32[]{:S(2)}, u32[]{:S(2)}) collective-permute-start(bf16[264,768]{1,0:T(8,128)(2,1)S(1)} %pad_maximum_fusion.7), channel_id=1, source_target_pairs={{0,1},{1,0},{2,3},{3,2},{4,7},{5,6},{6,5},{7,4},{8,9},{9,8},{10,11... | collective-permute-start | bytes 1216520 | tf_op jit(solution)/shard_map/ppermute | solution.py:875
  6.2 21.5 %collective-permute-start.1 = (bf16[264,768]{1,0:T(8,128)(2,1)S(1)}, bf16[264,768]{1,0:T(8,128)(2,1)S(1)}, u32[]{:S(2)}, u32[]{:S(2)}) collective-permute-start(bf16[264,768]{1,0:T(8,128)(2,1)S(1)} %get-tuple-element.127), channel_id=1, source_target_pairs={{0,3},{1,2},{2,1},{3,0},{4,5},{5,4},{6,7},{7,6},{8,11},{9,10},{10,... | collective-permute-start | bytes 1216520 | tf_op jit(solution)/shard_map/ppermute | solution.py:875
  8.7 34.0 %collective-permute-start = (bf16[264,768]{1,0:T(8,128)(2,1)S(1)}, bf16[264,768]{1,0:T(8,128)(2,1)S(1)}, u32[]{:S(2)}, u32[]{:S(2)}) collective-permute-start(bf16[264,768]{1,0:T(8,128)(2,1)S(1)} %get-tuple-element.128), channel_id=1, source_target_pairs={{0,2},{1,3},{2,0},{3,1},{4,6},{5,7},{6,4},{7,5},{8,10},{9,11},{10,... | collective-permute-start | bytes 1216520 | tf_op jit(solution)/shard_map/ppermute | solution.py:875
  28.4 14.4 %copy-start.8 = (bf16[4,256,384]{2,1,0:T(8,128)(2,1)S(1)}, bf16[4,256,384]{2,1,0:T(8,128)(2,1)}, u32[]{:S(2)}) copy-start(bf16[4,256,384]{2,1,0:T(8,128)(2,1)} %param.19) | copy-start | bytes 2359300
  33.4 13.7 %copy-start.5 = (bf16[4,256,768]{2,1,0:T(8,128)(2,1)S(1)}, bf16[4,256,768]{2,1,0:T(8,128)(2,1)}, u32[]{:S(2)}) copy-start(bf16[4,256,768]{2,1,0:T(8,128)(2,1)} %param.35) | copy-start | bytes 4718596
  42.8 4.4 %copy-start.13 = (bf16[264,768]{1,0:T(8,128)(2,1)}, bf16[264,768]{1,0:T(8,128)(2,1)S(1)}, u32[]{:S(2)}) copy-start(bf16[264,768]{1,0:T(8,128)(2,1)S(1)} %collective-permute-done.x_ref) | copy-start | bytes 1216516
  43.6 25.4 %collective-permute-start.3 = (bf16[256,384]{1,0:T(8,128)(2,1)S(1)}, bf16[256,384]{1,0:T(8,128)(2,1)S(1)}, u32[]{:S(2)}, u32[]{:S(2)}) collective-permute-start(bf16[256,384]{1,0:T(8,128)(2,1)S(1)} %get-tuple-element.287), channel_id=1, source_target_pairs={{0,1},{1,0},{2,3},{3,2},{4,7},{5,6},{6,5},{7,4},{8,9},{9,8},{10,11... | collective-permute-start | bytes 589832 | tf_op jit(solution)/shard_map/ppermute | solution.py:875
  43.6 25.4 %collective-permute-start.4 = (bf16[256,384]{1,0:T(8,128)(2,1)S(1)}, bf16[256,384]{1,0:T(8,128)(2,1)S(1)}, u32[]{:S(2)}, u32[]{:S(2)}) collective-permute-start(bf16[256,384]{1,0:T(8,128)(2,1)S(1)} %get-tuple-element.286), channel_id=1, source_target_pairs={{0,3},{1,2},{2,1},{3,0},{4,5},{5,4},{6,7},{7,6},{8,11},{9,10},{10,... | collective-permute-start | bytes 589832 | tf_op jit(solution)/shard_map/ppermute | solution.py:875
  46.1 35.3 %collective-permute-start.5 = (bf16[256,384]{1,0:T(8,128)(2,1)S(1)}, bf16[256,384]{1,0:T(8,128)(2,1)S(1)}, u32[]{:S(2)}, u32[]{:S(2)}) collective-permute-start(bf16[256,384]{1,0:T(8,128)(2,1)S(1)} %get-tuple-element.285), channel_id=1, source_target_pairs={{0,2},{1,3},{2,0},{3,1},{4,6},{5,7},{6,4},{7,5},{8,10},{9,11},{10,... | collective-permute-start | bytes 589832 | tf_op jit(solution)/shard_map/ppermute | solution.py:875
  47.1 48.2 %collective-permute-start.7 = (bf16[256,768]{1,0:T(8,128)(2,1)S(1)}, bf16[256,768]{1,0:T(8,128)(2,1)S(1)}, u32[]{:S(2)}, u32[]{:S(2)}) collective-permute-start(bf16[256,768]{1,0:T(8,128)(2,1)S(1)} %get-tuple-element.255), channel_id=1, source_target_pairs={{0,2},{1,3},{2,0},{3,1},{4,6},{5,7},{6,4},{7,5},{8,10},{9,11},{10,... | collective-permute-start | bytes 1179656 | tf_op jit(solution)/shard_map/ppermute | solution.py:875
  49.1 46.2 %collective-permute-start.8 = (bf16[256,768]{1,0:T(8,128)(2,1)S(1)}, bf16[256,768]{1,0:T(8,128)(2,1)S(1)}, u32[]{:S(2)}, u32[]{:S(2)}) collective-permute-start(bf16[256,768]{1,0:T(8,128)(2,1)S(1)} %get-tuple-element.254), channel_id=1, source_target_pairs={{0,3},{1,2},{2,1},{3,0},{4,7},{5,6},{6,5},{7,4},{8,11},{9,10},{10,... | collective-permute-start | bytes 1179656 | tf_op jit(solution)/shard_map/ppermute | solution.py:875
  68.9 13.2 %copy-start.35 = (bf16[256,384]{1,0:T(8,128)(2,1)}, bf16[256,384]{1,0:T(8,128)(2,1)S(1)}, u32[]{:S(2)}) copy-start(bf16[256,384]{1,0:T(8,128)(2,1)S(1)} %collective-permute-done.3.refs_1_) | copy-start | bytes 589828
  69.0 13.2 %copy-start.36 = (bf16[256,384]{1,0:T(8,128)(2,1)}, bf16[256,384]{1,0:T(8,128)(2,1)S(1)}, u32[]{:S(2)}) copy-start(bf16[256,384]{1,0:T(8,128)(2,1)S(1)} %collective-permute-done.4.refs_2_) | copy-start | bytes 589828
  82.2 13.2 %collective-permute-start.6 = (bf16[256,768]{1,0:T(8,128)(2,1)S(1)}, bf16[256,768]{1,0:T(8,128)(2,1)S(1)}, u32[]{:S(2)}, u32[]{:S(2)}) collective-permute-start(bf16[256,768]{1,0:T(8,128)(2,1)S(1)} %get-tuple-element.256), channel_id=1, source_target_pairs={{0,1},{1,0},{2,3},{3,2},{4,5},{5,4},{6,7},{7,6},{8,9},{9,8},{10,11... | collective-permute-start | bytes 1179656 | tf_op jit(solution)/shard_map/ppermute | solution.py:875
  145.0 23.2 %collective-permute-start.9 = (bf16[4,384,768]{2,1,0:T(8,128)(2,1)}, bf16[4,384,768]{2,1,0:T(8,128)(2,1)S(1)}, u32[]{:S(2)}, u32[]{:S(2)}) collective-permute-start(bf16[4,384,768]{2,1,0:T(8,128)(2,1)} %get-tuple-element.171), channel_id=1, source_target_pairs={{0,4},{4,0},{8,12},{12,8},{16,20},{20,16},{24,28},{28,24},{1,5},{5... | collective-permute-start | bytes 7077896 | tf_op jit(solution)/shard_map/ppermute | solution.py:870
  145.0 23.1 %collective-permute-start.10 = (bf16[4,4,96,768]{3,2,1,0:T(8,128)(2,1)}, bf16[4,4,96,768]{3,2,1,0:T(8,128)(2,1)S(1)}, u32[]{:S(2)}, u32[]{:S(2)}) collective-permute-start(bf16[4,4,96,768]{3,2,1,0:T(8,128)(2,1)} %get-tuple-element.172), channel_id=1, source_target_pairs={{0,4},{4,0},{8,12},{12,8},{16,20},{20,16},{24,28},{28,24},{1,5},{5... | collective-permute-start | bytes 7077896 | tf_op jit(solution)/shard_map/ppermute | solution.py:870
  145.5 22.6 %collective-permute-start.11 = (bf16[2,256,768]{2,1,0:T(8,128)(2,1)}, bf16[2,256,768]{2,1,0:T(8,128)(2,1)S(1)}, u32[]{:S(2)}, u32[]{:S(2)}) collective-permute-start(bf16[2,256,768]{2,1,0:T(8,128)(2,1)} %get-tuple-element.173), channel_id=1, source_target_pairs={{0,1},{1,0},{2,3},{3,2},{4,7},{5,6},{6,5},{7,4},{8,9},{9,8},{10,11... | collective-permute-start | bytes 2359304 | tf_op jit(solution)/shard_map/ppermute | solution.py:875
  147.5 20.6 %collective-permute-start.12 = (bf16[4,6,96,128]{3,2,1,0:T(8,128)(2,1)}, bf16[4,6,96,128]{3,2,1,0:T(8,128)(2,1)}, u32[]{:S(2)}, u32[]{:S(2)}) collective-permute-start(bf16[4,6,96,128]{3,2,1,0:T(8,128)(2,1)} %get-tuple-element.174), channel_id=1, source_target_pairs={{0,4},{4,0},{8,12},{12,8},{16,20},{20,16},{24,28},{28,24},{1,5},{5... | collective-permute-start | bytes 1769480 | tf_op jit(solution)/shard_map/ppermute | solution.py:870
  147.5 21.5 %copy-start.2 = (bf16[4,384,768]{2,1,0:T(8,128)(2,1)S(1)}, bf16[4,384,768]{2,1,0:T(8,128)(2,1)}, u32[]{:S(2)}) copy-start(bf16[4,384,768]{2,1,0:T(8,128)(2,1)} %get-tuple-element.181) | copy-start | bytes 7077892
  169.0 1.7 copy-start.1
  173.5 30.7 %collective-permute-start.13 = (bf16[2,8,96,768]{3,2,1,0:T(8,128)(2,1)S(1)}, bf16[2,8,96,768]{3,2,1,0:T(8,128)(2,1)S(1)}, u32[]{:S(2)}, u32[]{:S(2)}) collective-permute-start(bf16[2,8,96,768]{3,2,1,0:T(8,128)(2,1)S(1)} %pad_maximum_fusion), channel_id=1, source_target_pairs={{0,8},{4,20},{8,0},{12,28},{16,24},{20,4},{24,16},{28,12},{1,9},{5... | collective-permute-start | bytes 7077896 | tf_op jit(solution)/shard_map/ppermute | solution.py:891
  174.9 29.2 %collective-permute-start.14 = (bf16[2,256,768]{2,1,0:T(8,128)(2,1)}, bf16[2,256,768]{2,1,0:T(8,128)(2,1)S(1)}, u32[]{:S(2)}, u32[]{:S(2)}) collective-permute-start(bf16[2,256,768]{2,1,0:T(8,128)(2,1)} %pad_maximum_fusion.2), channel_id=1, source_target_pairs={{0,3},{1,2},{2,1},{3,0},{4,5},{5,4},{6,7},{7,6},{8,11},{9,10},{10,... | collective-permute-start | bytes 2359304 | tf_op jit(solution)/shard_map/ppermute | solution.py:875
  176.6 27.5 %collective-permute-start.15 = (bf16[2,256,384]{2,1,0:T(8,128)(2,1)}, bf16[2,256,384]{2,1,0:T(8,128)(2,1)S(1)}, u32[]{:S(2)}, u32[]{:S(2)}) collective-permute-start(bf16[2,256,384]{2,1,0:T(8,128)(2,1)} %get-tuple-element.197), channel_id=1, source_target_pairs={{0,1},{1,0},{2,3},{3,2},{4,7},{5,6},{6,5},{7,4},{8,9},{9,8},{10,11... | collective-permute-start | bytes 1179656 | tf_op jit(solution)/shard_map/ppermute | solution.py:875
  176.8 27.3 %collective-permute-start.16 = (bf16[4,3,2,96,128]{4,3,2,1,0:T(8,128)(2,1)}, bf16[4,3,2,96,128]{4,3,2,1,0:T(8,128)(2,1)}, u32[]{:S(2)}, u32[]{:S(2)}) collective-permute-start(bf16[4,3,2,96,128]{4,3,2,1,0:T(8,128)(2,1)} %get-tuple-element.198), channel_id=1, source_target_pairs={{0,4},{4,0},{8,12},{12,8},{16,20},{20,16},{24,28},{28,24},{1,5},{5... | collective-permute-start | bytes 1769480 | tf_op jit(solution)/shard_map/ppermute | solution.py:870
  204.1 2.6 copy-start.6
  205.0 1.7 copy-start.19
  205.1 4.5 %copy-start.9 = (bf16[2,256,768]{2,1,0:T(8,128)(2,1)S(1)}, bf16[2,256,768]{2,1,0:T(8,128)(2,1)}, u32[]{:S(2)}) copy-start(bf16[2,256,768]{2,1,0:T(8,128)(2,1)} %get-tuple-element.223) | copy-start | bytes 2359300
  205.1 8.0 %copy-start.11 = (bf16[4,6,96,128]{3,2,1,0:T(8,128)(2,1)S(1)}, bf16[4,6,96,128]{3,2,1,0:T(8,128)(2,1)}, u32[]{:S(2)}) copy-start(bf16[4,6,96,128]{3,2,1,0:T(8,128)(2,1)} %get-tuple-element.213) | copy-start | bytes 1769476
  205.1 33.1 %collective-permute-start.17 = (bf16[8,96,768]{2,1,0:T(8,128)(2,1)S(1)}, bf16[8,96,768]{2,1,0:T(8,128)(2,1)S(1)}, u32[]{:S(2)}, u32[]{:S(2)}) collective-permute-start(bf16[8,96,768]{2,1,0:T(8,128)(2,1)S(1)} %slice_bitcast_fusion.1), channel_id=1, source_target_pairs={{0,16},{4,12},{8,24},{12,4},{16,0},{20,28},{24,8},{28,20},{1,17},{... | collective-permute-start | bytes 3538952 | tf_op jit(solution)/shard_map/ppermute | solution.py:891
  206.7 31.6 %collective-permute-start.18 = (bf16[4,3,3,96,128]{4,3,2,1,0:T(8,128)(2,1)}, bf16[4,3,3,96,128]{4,3,2,1,0:T(8,128)(2,1)S(1)}, u32[]{:S(2)}, u32[]{:S(2)}) collective-permute-start(bf16[4,3,3,96,128]{4,3,2,1,0:T(8,128)(2,1)} %get-tuple-element.200), channel_id=1, source_target_pairs={{0,4},{4,0},{8,12},{12,8},{16,20},{20,16},{24,28},{28,24},{1,5},{5... | collective-permute-start | bytes 2654216 | tf_op jit(solution)/shard_map/ppermute | solution.py:870
  207.5 14.2 %collective-permute-start.19 = (bf16[2,256,384]{2,1,0:T(8,128)(2,1)}, bf16[2,256,384]{2,1,0:T(8,128)(2,1)S(1)}, u32[]{:S(2)}, u32[]{:S(2)}) collective-permute-start(bf16[2,256,384]{2,1,0:T(8,128)(2,1)} %pad_maximum_fusion.9), channel_id=1, source_target_pairs={{0,3},{1,2},{2,1},{3,0},{4,5},{5,4},{6,7},{7,6},{8,11},{9,10},{10,... | collective-permute-start | bytes 1179656 | tf_op jit(solution)/shard_map/ppermute | solution.py:875
  210.3 20.7 %collective-permute-start.20 = (bf16[256,768]{1,0:T(8,128)(2,1)}, bf16[256,768]{1,0:T(8,128)(2,1)S(1)}, u32[]{:S(2)}, u32[]{:S(2)}) collective-permute-start(bf16[256,768]{1,0:T(8,128)(2,1)} %slice_bitcast_fusion.5), channel_id=1, source_target_pairs={{0,1},{1,0},{2,3},{3,2},{4,7},{5,6},{6,5},{7,4},{8,9},{9,8},{10,11... | collective-permute-start | bytes 1179656 | tf_op jit(solution)/shard_map/ppermute | solution.py:875
  211.4 26.8 %collective-permute-start.21 = (bf16[256,768]{1,0:T(8,128)(2,1)}, bf16[256,768]{1,0:T(8,128)(2,1)}, u32[]{:S(2)}, u32[]{:S(2)}) collective-permute-start(bf16[256,768]{1,0:T(8,128)(2,1)} %get-tuple-element.207), channel_id=1, source_target_pairs={{0,3},{1,2},{2,1},{3,0},{4,5},{5,4},{6,7},{7,6},{8,11},{9,10},{10,... | collective-permute-start | bytes 1179656 | tf_op jit(solution)/shard_map/ppermute | solution.py:875
  214.3 3.2 %copy-start.12 = (bf16[4,3,2,96,128]{4,3,2,1,0:T(8,128)(2,1)S(1)}, bf16[4,3,2,96,128]{4,3,2,1,0:T(8,128)(2,1)}, u32[]{:S(2)}) copy-start(bf16[4,3,2,96,128]{4,3,2,1,0:T(8,128)(2,1)} %get-tuple-element.215) | copy-start | bytes 1769476
  217.5 20.7 %copy-start.7 = (bf16[4,3,3,96,128]{4,3,2,1,0:T(8,128)(2,1)S(1)}, bf16[4,3,3,96,128]{4,3,2,1,0:T(8,128)(2,1)}, u32[]{:S(2)}) copy-start(bf16[4,3,3,96,128]{4,3,2,1,0:T(8,128)(2,1)} %get-tuple-element.217) | copy-start | bytes 2654212
  221.7 16.9 %copy-start.4 = (bf16[2,256,384]{2,1,0:T(8,128)(2,1)}, bf16[2,256,384]{2,1,0:T(8,128)(2,1)S(1)}, u32[]{:S(2)}) copy-start(bf16[2,256,384]{2,1,0:T(8,128)(2,1)S(1)} %collective-permute-done.19.refs_2_.refs_3_) | copy-start | bytes 1179652
  231.0 7.6 %copy-start.16 = (bf16[256,768]{1,0:T(8,128)(2,1)}, bf16[256,768]{1,0:T(8,128)(2,1)S(1)}, u32[]{:S(2)}) copy-start(bf16[256,768]{1,0:T(8,128)(2,1)S(1)} %collective-permute-done.20.refs_1_) | copy-start | bytes 1179652
  238.6 15.5 %collective-permute-start.22 = (bf16[2,21,96,128]{3,2,1,0:T(8,128)(2,1)S(1)}, bf16[2,21,96,128]{3,2,1,0:T(8,128)(2,1)S(1)}, u32[]{:S(2)}, u32[]{:S(2)}) collective-permute-start(bf16[2,21,96,128]{3,2,1,0:T(8,128)(2,1)S(1)} %pad_maximum_fusion.1), channel_id=1, source_target_pairs={{0,8},{4,20},{8,0},{12,28},{16,24},{20,4},{24,16},{28,12},{1,9},{5... | collective-permute-start | bytes 3096584 | tf_op jit(solution)/shard_map/ppermute | solution.py:891
  239.2 5.7 %collective-permute-start.23 = (f32[72,128]{1,0:T(8,128)S(1)}, f32[72,128]{1,0:T(8,128)S(1)}, u32[]{:S(2)}, u32[]{:S(2)}) collective-permute-start(f32[72,128]{1,0:T(8,128)S(1)} %copy-done.20), channel_id=1, source_target_pairs={{0,1},{1,0},{2,3},{3,2},{4,5},{5,4},{6,7},{7,6},{8,9},{9,8},{10,11... | collective-permute-start | bytes 110600 | tf_op jit(solution)/shard_map/ppermute | solution.py:875
  239.8 33.2 %collective-permute-start.25 = (bf16[2,2,96,768]{3,2,1,0:T(8,128)(2,1)S(1)}, bf16[2,2,96,768]{3,2,1,0:T(8,128)(2,1)S(1)}, u32[]{:S(2)}, u32[]{:S(2)}) collective-permute-start(bf16[2,2,96,768]{3,2,1,0:T(8,128)(2,1)S(1)} %pad_maximum_fusion.3), channel_id=1, source_target_pairs={{0,1},{1,0},{2,3},{3,2},{4,7},{5,6},{6,5},{7,4},{8,9},{9,8},{10,11... | collective-permute-start | bytes 1769480 | tf_op jit(solution)/shard_map/ppermute | solution.py:875
  254.5 18.5 %collective-permute-start.24 = (bf16[21,96,128]{2,1,0:T(8,128)(2,1)S(1)}, bf16[21,96,128]{2,1,0:T(8,128)(2,1)S(1)}, u32[]{:S(2)}, u32[]{:S(2)}) collective-permute-start(bf16[21,96,128]{2,1,0:T(8,128)(2,1)S(1)} %slice_bitcast_fusion.3), channel_id=1, source_target_pairs={{0,16},{4,12},{8,24},{12,4},{16,0},{20,28},{24,8},{28,20},{1,17},{... | collective-permute-start | bytes 1548296 | tf_op jit(solution)/shard_map/ppermute | solution.py:891
  255.3 17.7 %collective-permute-start.26 = (bf16[256,768]{1,0:T(8,128)(2,1)S(1)}, bf16[256,768]{1,0:T(8,128)(2,1)S(1)}, u32[]{:S(2)}, u32[]{:S(2)}) collective-permute-start(bf16[256,768]{1,0:T(8,128)(2,1)S(1)} %slice_bitcast_fusion.4), channel_id=1, source_target_pairs={{0,2},{1,3},{2,0},{3,1},{4,6},{5,7},{6,4},{7,5},{8,10},{9,11},{10,... | collective-permute-start | bytes 1179656 | tf_op jit(solution)/shard_map/ppermute | solution.py:875
  255.6 17.4 %collective-permute-start.27 = (f32[72,128]{1,0:T(8,128)S(1)}, f32[72,128]{1,0:T(8,128)S(1)}, u32[]{:S(2)}, u32[]{:S(2)}) collective-permute-start(f32[72,128]{1,0:T(8,128)S(1)} %add.147), channel_id=1, source_target_pairs={{0,3},{1,2},{2,1},{3,0},{4,7},{5,6},{6,5},{7,4},{8,11},{9,10},{10,... | collective-permute-start | bytes 110600 | tf_op jit(solution)/shard_map/ppermute | solution.py:875
  273.3 11.9 %collective-permute-start.30 = (bf16[2,21,24,128]{3,2,1,0:T(8,128)(2,1)S(1)}, bf16[2,21,24,128]{3,2,1,0:T(8,128)(2,1)S(1)}, u32[]{:S(2)}, u32[]{:S(2)}) collective-permute-start(bf16[2,21,24,128]{3,2,1,0:T(8,128)(2,1)S(1)} %pad_maximum_fusion.10), channel_id=1, source_target_pairs={{0,1},{1,0},{2,3},{3,2},{4,7},{5,6},{6,5},{7,4},{8,9},{9,8},{10,11... | collective-permute-start | bytes 774152 | tf_op jit(solution)/shard_map/ppermute | solution.py:875
  274.5 16.6 %collective-permute-start.28 = (f32[72,128]{1,0:T(8,128)S(1)}, f32[72,128]{1,0:T(8,128)S(1)}, u32[]{:S(2)}, u32[]{:S(2)}) collective-permute-start(f32[72,128]{1,0:T(8,128)S(1)} %add.149), channel_id=1, source_target_pairs={{0,4},{4,0},{8,12},{12,8},{16,20},{20,16},{24,28},{28,24},{1,5},{5... | collective-permute-start | bytes 110600 | tf_op jit(solution)/shard_map/ppermute | solution.py:870
  274.6 15.0 %collective-permute-start.29 = (bf16[2,96,768]{2,1,0:T(8,128)(2,1)S(1)}, bf16[2,96,768]{2,1,0:T(8,128)(2,1)S(1)}, u32[]{:S(2)}, u32[]{:S(2)}) collective-permute-start(bf16[2,96,768]{2,1,0:T(8,128)(2,1)S(1)} %slice_bitcast_fusion.9), channel_id=1, source_target_pairs={{0,3},{1,2},{2,1},{3,0},{4,5},{5,4},{6,7},{7,6},{8,11},{9,10},{10,... | collective-permute-start | bytes 884744 | tf_op jit(solution)/shard_map/ppermute | solution.py:875
  285.3 8.3 %collective-permute-start.32 = (bf16[21,24,128]{2,1,0:T(8,128)(2,1)S(1)}, bf16[21,24,128]{2,1,0:T(8,128)(2,1)S(1)}, u32[]{:S(2)}, u32[]{:S(2)}) collective-permute-start(bf16[21,24,128]{2,1,0:T(8,128)(2,1)S(1)} %slice_bitcast_fusion.21), channel_id=1, source_target_pairs={{0,3},{1,2},{2,1},{3,0},{4,5},{5,4},{6,7},{7,6},{8,11},{9,10},{10,... | collective-permute-start | bytes 387080 | tf_op jit(solution)/shard_map/ppermute | solution.py:875
  289.7 10.0 %collective-permute-start.35 = (bf16[2,96,768]{2,1,0:T(8,128)(2,1)S(1)}, bf16[2,96,768]{2,1,0:T(8,128)(2,1)S(1)}, u32[]{:S(2)}, u32[]{:S(2)}) collective-permute-start(bf16[2,96,768]{2,1,0:T(8,128)(2,1)S(1)} %fusion.2), channel_id=1, source_target_pairs={{0,3},{1,2},{2,1},{3,0},{4,5},{5,4},{6,7},{7,6},{8,11},{9,10},{10,... | collective-permute-start | bytes 884744 | tf_op jit(solution)/shard_map/ppermute | solution.py:875
  291.1 4.0 %collective-permute-start.31 = (f32[72,128]{1,0:T(8,128)S(1)}, f32[72,128]{1,0:T(8,128)S(1)}, u32[]{:S(2)}, u32[]{:S(2)}) collective-permute-start(f32[72,128]{1,0:T(8,128)S(1)} %add.153), channel_id=1, source_target_pairs={{0,8},{4,12},{8,0},{12,4},{16,24},{20,28},{24,16},{28,20},{1,9},{5... | collective-permute-start | bytes 110600 | tf_op jit(solution)/shard_map/ppermute | solution.py:891
  295.1 4.0 %collective-permute-start.33 = (f32[72,128]{1,0:T(8,128)S(1)}, f32[72,128]{1,0:T(8,128)S(1)}, u32[]{:S(2)}, u32[]{:S(2)}) collective-permute-start(f32[72,128]{1,0:T(8,128)S(1)} %add.155), channel_id=1, source_target_pairs={{0,16},{4,20},{8,24},{12,28},{16,0},{20,4},{24,8},{28,12},{1,17},{... | collective-permute-start | bytes 110600 | tf_op jit(solution)/shard_map/ppermute | solution.py:891
  295.9 8.2 %collective-permute-start.34 = (bf16[21,24,128]{2,1,0:T(8,128)(2,1)S(1)}, bf16[21,24,128]{2,1,0:T(8,128)(2,1)S(1)}, u32[]{:S(2)}, u32[]{:S(2)}) collective-permute-start(bf16[21,24,128]{2,1,0:T(8,128)(2,1)S(1)} %fusion.3), channel_id=1, source_target_pairs={{0,3},{1,2},{2,1},{3,0},{4,5},{5,4},{6,7},{7,6},{8,11},{9,10},{10,... | collective-permute-start | bytes 387080 | tf_op jit(solution)/shard_map/ppermute | solution.py:875
  304.1 9.0 %collective-permute-start.36 = (bf16[2,21,24,128]{3,2,1,0:T(8,128)(2,1)S(1)}, bf16[2,21,24,128]{3,2,1,0:T(8,128)(2,1)S(1)}, u32[]{:S(2)}, u32[]{:S(2)}) collective-permute-start(bf16[2,21,24,128]{3,2,1,0:T(8,128)(2,1)S(1)} %pad_maximum_fusion.11), channel_id=1, source_target_pairs={{0,1},{1,0},{2,3},{3,2},{4,7},{5,6},{6,5},{7,4},{8,9},{9,8},{10,11... | collective-permute-start | bytes 774152 | tf_op jit(solution)/shard_map/ppermute | solution.py:875
  305.4 14.1 %collective-permute-start.37 = (bf16[2,2,96,768]{3,2,1,0:T(8,128)(2,1)S(1)}, bf16[2,2,96,768]{3,2,1,0:T(8,128)(2,1)S(1)}, u32[]{:S(2)}, u32[]{:S(2)}) collective-permute-start(bf16[2,2,96,768]{3,2,1,0:T(8,128)(2,1)S(1)} %pad_maximum_fusion.4), channel_id=1, source_target_pairs={{0,1},{1,0},{2,3},{3,2},{4,7},{5,6},{6,5},{7,4},{8,9},{9,8},{10,11... | collective-permute-start | bytes 1769480 | tf_op jit(solution)/shard_map/ppermute | solution.py:875
  313.8 5.9 %copy-start.21 = (f32[96,768]{1,0:T(8,128)}, f32[96,768]{1,0:T(8,128)S(1)}, u32[]{:S(2)}) copy-start(f32[96,768]{1,0:T(8,128)S(1)} %get-tuple-element.273) | copy-start | bytes 884740
  313.8 5.9 %copy-start.23 = (f32[96,1920]{1,0:T(8,128)}, f32[96,1920]{1,0:T(8,128)S(1)}, u32[]{:S(2)}) copy-start(f32[96,1920]{1,0:T(8,128)S(1)} %get-tuple-element.274) | copy-start | bytes 2211844
  (13 other events, 12.3 us)
